TPU v7x, 32 devices: a whole 2x2x4 slice. The times are simulated.
32 devices in a mesh: dp: 8 (over y, x, core), ctx: 4 (over z).
Axes of the slice: x: 2, y: 2, z: 4, core: 2. Of those that a mesh axis runs over, the one named last changes fastest.
Arguments:
- layer_input: bfloat16 [24, 2048, 1024], P('dp', 'ctx'), may hold values from -6 to 6
- segments: int32 [24, 2048], P('dp'), may hold values from 0 to 34, as said below
- positions: int32 [24, 2048], P('dp', 'ctx'), may hold values from 0 to 2047, as said below
- gain_one: bfloat16 [1024], P(('dp', 'ctx')), may hold values from 0.5 to 1.5
- w_in: bfloat16 [1024, 3352], P(('dp', 'ctx')), may hold values from -0.1875 to 0.1875
- conv_w: bfloat16 [4, 1792], P(None, ('dp', 'ctx')), may hold values from -3 to 3
- conv_b: bfloat16 [1792], P(('dp', 'ctx')), may hold values from -3 to 3
- head_params: float32 [3, 24], replicated, as said below
- gain_m: bfloat16 [1536], P(('dp', 'ctx')), may hold values from 0.5 to 1.5
- w_out: bfloat16 [1536, 1024], P(('dp', 'ctx')), may hold values from -0.15625 to 0.15625
- w_q: bfloat16 [1024, 512], P(('dp', 'ctx')), may hold values from -0.1875 to 0.1875
- w_k: bfloat16 [1024, 128], P(('dp', 'ctx')), may hold values from -0.1875 to 0.1875
- w_v: bfloat16 [1024, 128], P(('dp', 'ctx')), may hold values from -0.1875 to 0.1875
- w_o: bfloat16 [512, 1024], P(None, ('dp', 'ctx')), may hold values from -1 to 1
- gain_two: bfloat16 [1024], P(('dp', 'ctx')), may hold values from 0.5 to 1.5
- w_gate: bfloat16 [1024, 2048], P(('dp', 'ctx')), may hold values from -0.1875 to 0.1875
- w_up: bfloat16 [1024, 2048], P(('dp', 'ctx')), may hold values from -0.1875 to 0.1875
- w_down: bfloat16 [2048, 1024], P(('dp', 'ctx')), may hold values from -0.125 to 0.125
- cotangent: bfloat16 [24, 2048, 1024], P('dp', 'ctx'), may hold values from -6 to 6
Outputs:
- block_out: bfloat16 [24, 2048, 1024], P('dp', 'ctx')
- grad_input: bfloat16 [24, 2048, 1024], P('dp', 'ctx')
- grad_gain_one: float32 [1024], P(('dp', 'ctx'))
- grad_w_in: float32 [1024, 3352], P(('dp', 'ctx'))
- grad_conv_w: float32 [4, 1792], P(None, ('dp', 'ctx'))
- grad_conv_b: float32 [1792], P(('dp', 'ctx'))
- grad_head_params: float32 [3, 24], replicated
- grad_gain_m: float32 [1536], P(('dp', 'ctx'))
- grad_w_out: float32 [1536, 1024], P(('dp', 'ctx'))
- grad_w_q: float32 [1024, 512], P(('dp', 'ctx'))
- grad_w_k: float32 [1024, 128], P(('dp', 'ctx'))
- grad_w_v: float32 [1024, 128], P(('dp', 'ctx'))
- grad_w_o: float32 [512, 1024], P(None, ('dp', 'ctx'))
- grad_gain_two: float32 [1024], P(('dp', 'ctx'))
- grad_w_gate: float32 [1024, 2048], P(('dp', 'ctx'))
- grad_w_up: float32 [1024, 2048], P(('dp', 'ctx'))
- grad_w_down: float32 [2048, 1024], P(('dp', 'ctx'))
Inputs may be any that keep to these rules, and one draw needn't show every extreme that they name: `segments`: segment numbers never fall along a sequence and start at 0; documents hold 60 to 800 tokens except a sequence's last one; one sequence among the 3 of each index of dp is a single document; one sequence holds only documents of 60 tokens. Within a document positions rise by one from token to token. `head_params`: row 0 holds logarithms of decay magnitudes, row 1 biases of the step sizes, row 2 skip weights.
All inputs are finite; a program needn't handle non-finite values.
Results may differ from a plain program's by a relative error of at most 0.019.
Values may be sent and summed in bfloat16 or wider, within the bound.
No kernel may reach another device: no remote copies, remote signals or barrier semaphores. Data moves between devices by JAX's collectives and lax.ppermute only.
A program may use at most 512 MiB of HBM per device.

v0:
```python
import jax
import jax.numpy as jnp
from jax import lax
from jax.sharding import PartitionSpec as P

MH = 24
MP = 64
NS = 128
KC = 4
QH = 8
KVH = 2
HD = 64


EPSILON = 1e-05
ROPE_BASE = 10000.0
MASKED = -1e30


def from_behind(block, axis, distance):
    devices = range(lax.axis_size(axis))
    route = [(i - distance, i) for i in devices if i - distance in devices]
    return lax.ppermute(block, axis, route)


def entering(shard, axis, combine, identity, reverse):
    count, place = (lax.axis_size(axis), lax.axis_index(axis))
    everything = jax.tree.map(
        lambda part, kind: lax.all_gather(part.astype(kind), axis),
        shard,
        (jnp.bfloat16, jnp.bfloat16),
    )
    start = jax.tree.map(
        lambda part, zero: jnp.broadcast_to(jnp.asarray(zero, part.dtype), part.shape),
        shard,
        identity,
    )

    def hop(k, before):
        at = count - 1 - k if reverse else k
        reached = at > place if reverse else at < place
        new = combine(
            before, jax.tree.map(lambda part, own: part[at].astype(own.dtype), everything, shard)
        )
        return jax.tree.map(lambda a, b: jnp.where(reached, a, b), new, before)

    return lax.fori_loop(0, count, hop, start)


def rms_scale(values, gain_vec):
    return (
        values * lax.rsqrt(jnp.mean(values * values, axis=-1, keepdims=True) + EPSILON) * gain_vec
    )


def rotary(values, places):
    half_width = values.shape[-1] // 2
    frequency = ROPE_BASE ** (-jnp.arange(half_width, dtype=jnp.float32) / half_width)
    angles = places.astype(jnp.float32)[..., None] * frequency
    cosine = jnp.cos(angles)[..., None, :]
    sine_part = jnp.sin(angles)[..., None, :]
    first_half = values[..., :half_width]
    second_half = values[..., half_width:]
    return jnp.concatenate(
        [
            first_half * cosine - second_half * sine_part,
            second_half * cosine + first_half * sine_part,
        ],
        axis=-1,
    )


def silu_product(gate_lin, up_lin):
    return jax.nn.silu(gate_lin) * up_lin


def gated_norm(mixer_y, gate_vals, gain_vec):
    return rms_scale(mixer_y * jax.nn.silu(gate_vals), gain_vec)


def conv_silu(extended, taps, shift, tap_match):
    out_len = tap_match.shape[2]
    total = shift
    for tap_idx in range(taps.shape[0]):
        total = (
            total
            + extended[:, tap_idx : tap_idx + out_len]
            * taps[tap_idx]
            * tap_match[:, tap_idx, :, None]
        )
    return jax.nn.silu(total)


def decay_terms(rate_raw, decay_log, step_bias, pair_mask, last_same, prev_same, flag_gain):
    step_size = jax.nn.softplus(rate_raw + step_bias)
    log_decay = -step_size * jnp.exp(decay_log)
    cumul = jnp.cumsum(log_decay, axis=1)
    by_head = jnp.swapaxes(cumul, 1, 2)
    differ = by_head[:, :, :, None] - by_head[:, :, None, :]
    inside = pair_mask[:, None]
    mixing = (
        jnp.where(inside, jnp.exp(jnp.where(inside, differ, 0.0)), 0.0)
        * jnp.swapaxes(step_size, 1, 2)[:, :, None, :]
    )
    weight_end = jnp.exp(cumul[:, -1:, :] - cumul) * step_size * last_same[..., None]
    entry = jnp.exp(cumul) * prev_same[..., None]
    carry_gain = jnp.exp(cumul[:, -1, :]) * flag_gain[:, None]
    return (mixing, weight_end, entry, carry_gain)


def combine_states(early_part, later_part):
    return (
        early_part[0] * later_part[0],
        later_part[0][..., None, None] * early_part[1] + later_part[1],
    )


def key_allowed(segments, seg_own, query_index, piece_len):
    key_index = jnp.arange(piece_len, dtype=jnp.int32)
    allowed = (seg_own[:, :, None] == segments[:, None, :]) & (
        key_index[None, None, :] <= query_index[None, :, None]
    )
    return allowed[:, None, None]


def body(
    layer_input,
    segments,
    positions,
    gain_one,
    w_in,
    conv_w,
    conv_b,
    head_params,
    gain_m,
    w_out,
    w_q,
    w_k,
    w_v,
    w_o,
    gain_two,
    w_gate,
    w_up,
    w_down,
    cotangent,
):
    seq_count, span_len, model_width = layer_input.shape
    tok_rows = seq_count * span_len
    inner_width = MH * MP
    channels = inner_width + 2 * NS
    group_size = QH // KVH
    qk_scale = HD ** (-0.5)
    gathered = (
        lax.all_gather(gain_one, ("dp", "ctx"), axis=0, tiled=True),
        lax.all_gather(w_in, ("dp", "ctx"), axis=0, tiled=True),
        lax.all_gather(conv_w, ("dp", "ctx"), axis=1, tiled=True),
        lax.all_gather(conv_b, ("dp", "ctx"), axis=0, tiled=True),
        lax.all_gather(gain_m, ("dp", "ctx"), axis=0, tiled=True),
        lax.all_gather(w_out, ("dp", "ctx"), axis=0, tiled=True),
        lax.all_gather(w_q, ("dp", "ctx"), axis=0, tiled=True),
        lax.all_gather(w_k, ("dp", "ctx"), axis=0, tiled=True),
        lax.all_gather(w_v, ("dp", "ctx"), axis=0, tiled=True),
        lax.all_gather(w_o, ("dp", "ctx"), axis=1, tiled=True),
        lax.all_gather(gain_two, ("dp", "ctx"), axis=0, tiled=True),
        lax.all_gather(w_gate, ("dp", "ctx"), axis=0, tiled=True),
        lax.all_gather(w_up, ("dp", "ctx"), axis=0, tiled=True),
        lax.all_gather(w_down, ("dp", "ctx"), axis=0, tiled=True),
    )
    (
        gain1_all,
        w_in_all,
        conv_w_all,
        conv_b_all,
        gain_m_all,
        w_out_all,
        w_q_all,
        w_k_all,
        w_v_all,
        w_o_all,
        gain2_all,
        w_gate_all,
        w_up_all,
        w_down_all,
    ) = gathered
    span_start = lax.axis_index("ctx") * span_len
    has_prev = lax.axis_index("ctx") > 0
    offsets = jnp.arange(span_len, dtype=jnp.int32)
    query_index = span_start + offsets
    seg_own = lax.dynamic_slice_in_dim(segments, span_start, span_len, 1)
    seg_rim = jnp.where(
        has_prev,
        lax.dynamic_slice_in_dim(segments, jnp.maximum(span_start - (KC - 1), 0), KC - 1, 1),
        -1,
    )
    seg_prev = seg_rim[:, -1]
    tokens_f = layer_input.astype(jnp.float32).reshape(tok_rows, model_width)
    normed_one, norm1_pull = jax.vjp(rms_scale, tokens_f, gain1_all.astype(jnp.float32))
    hidden = normed_one.astype(jnp.bfloat16)
    projected = jnp.dot(hidden, w_in_all, preferred_element_type=jnp.float32).astype(jnp.bfloat16)
    gate_vals = projected[:, :inner_width].astype(jnp.float32)
    pre_conv = projected[:, inner_width : inner_width + channels].reshape(
        seq_count, span_len, channels
    )
    rate_raw = (
        projected[:, inner_width + channels :].astype(jnp.float32).reshape(seq_count, span_len, MH)
    )
    rim_rows = from_behind(pre_conv[:, span_len - (KC - 1) :], "ctx", 1)
    extended = jnp.concatenate([rim_rows, pre_conv], axis=1).astype(jnp.float32)
    seg_ext = jnp.concatenate([seg_rim, seg_own], axis=1)
    tap_match = jnp.stack(
        [seg_ext[:, tap_idx : tap_idx + span_len] == seg_own for tap_idx in range(KC)], axis=1
    ).astype(jnp.float32)
    conv_out, conv_pull = jax.vjp(
        lambda ext_in, taps_in, shift_in: conv_silu(ext_in, taps_in, shift_in, tap_match),
        extended,
        conv_w_all.astype(jnp.float32),
        conv_b_all.astype(jnp.float32),
    )
    conv_act = conv_out.astype(jnp.bfloat16)
    xs_rows = conv_act[..., :inner_width].reshape(seq_count, span_len, MH, MP)
    b_rows = conv_act[..., inner_width : inner_width + NS]
    c_rows = conv_act[..., inner_width + NS :]
    pair_mask = (seg_own[:, :, None] == seg_own[:, None, :]) & (
        offsets[None, :, None] >= offsets[None, None, :]
    )
    last_same = (seg_own == seg_own[:, -1:]).astype(jnp.float32)
    prev_same = (seg_own == seg_prev[:, None]).astype(jnp.float32)
    flag_gain = (seg_own[:, -1] == seg_prev).astype(jnp.float32)
    decays, decay_pull = jax.vjp(
        lambda rate_in, log_in, bias_in: decay_terms(
            rate_in, log_in, bias_in, pair_mask, last_same, prev_same, flag_gain
        ),
        rate_raw,
        head_params[0],
        head_params[1],
    )
    mixing, weight_end, entry, carry_gain = decays
    cross = jnp.einsum("sin,sjn->sij", c_rows, b_rows, preferred_element_type=jnp.float32)
    mix_low = (cross[:, None] * mixing).astype(jnp.bfloat16)
    y_inner = jnp.einsum("shij,sjhp->sihp", mix_low, xs_rows, preferred_element_type=jnp.float32)
    b_scaled = (b_rows[:, :, None, :].astype(jnp.float32) * weight_end[..., None]).astype(
        jnp.bfloat16
    )
    block_state = jnp.einsum(
        "sjhp,sjhn->shpn", xs_rows, b_scaled, preferred_element_type=jnp.float32
    )
    state_identity = (jnp.ones_like(carry_gain), jnp.zeros_like(block_state))
    gain_before, state_in = entering(
        (carry_gain, block_state), "ctx", combine_states, state_identity, False
    )
    state_low = state_in.astype(jnp.bfloat16)
    carried = jnp.einsum("sin,shpn->sihp", c_rows, state_low, preferred_element_type=jnp.float32)
    skip_gain = head_params[2]
    xs_float = xs_rows.astype(jnp.float32)
    mixer_y = y_inner + entry[..., None] * carried + skip_gain[:, None] * xs_float
    normed_mix, gate_pull = jax.vjp(
        gated_norm,
        mixer_y.reshape(tok_rows, inner_width),
        gate_vals,
        gain_m_all.astype(jnp.float32),
    )
    mixer_in = normed_mix.astype(jnp.bfloat16)
    mixer_out = jnp.dot(mixer_in, w_out_all, preferred_element_type=jnp.float32)
    query_lin = jnp.dot(hidden, w_q_all, preferred_element_type=jnp.float32).reshape(
        seq_count, span_len, QH, HD
    )
    key_lin = jnp.dot(hidden, w_k_all, preferred_element_type=jnp.float32).reshape(
        seq_count, span_len, KVH, HD
    )
    query_rot, query_pull = jax.vjp(lambda vals_in: rotary(vals_in, positions), query_lin)
    key_rot, key_pull = jax.vjp(lambda vals_in: rotary(vals_in, positions), key_lin)
    queries = query_rot.astype(jnp.bfloat16).reshape(seq_count, span_len, KVH, group_size, HD)
    key_rows = key_rot.astype(jnp.bfloat16).reshape(seq_count, span_len, KVH * HD)
    value_rows = (
        jnp.dot(hidden, w_v_all, preferred_element_type=jnp.float32)
        .astype(jnp.bfloat16)
        .reshape(seq_count, span_len, KVH * HD)
    )
    block_in = (
        lax.all_gather(key_rows, "ctx", axis=1, tiled=True),
        lax.all_gather(value_rows, "ctx", axis=1, tiled=True),
    )
    run_max = jnp.full((seq_count, KVH, group_size, span_len), MASKED, jnp.float32)
    run_acc = jnp.zeros((seq_count, span_len, KVH, group_size, HD), jnp.float32)
    piece_len = block_in[0].shape[1]
    key_piece = block_in[0].reshape(seq_count, piece_len, KVH, HD)
    value_piece = block_in[1].reshape(seq_count, piece_len, KVH, HD)
    allowed = key_allowed(segments, seg_own, query_index, piece_len)
    scores = (
        jnp.einsum("sigrd,sjgd->sgrij", queries, key_piece, preferred_element_type=jnp.float32)
        * qk_scale
    )
    scores = jnp.where(allowed, scores, MASKED)
    new_max = jnp.maximum(run_max, jnp.max(scores, axis=-1))
    rescale = jnp.exp(run_max - new_max)
    weights = jnp.where(allowed, jnp.exp(scores - new_max[..., None]), 0.0)
    run_sum = jnp.sum(weights, axis=-1)
    run_acc = run_acc * jnp.moveaxis(rescale, 3, 1)[..., None] + jnp.einsum(
        "sgrij,sjgd->sigrd",
        weights.astype(jnp.bfloat16),
        value_piece,
        preferred_element_type=jnp.float32,
    )
    run_max, run_sum, run_acc = (new_max, run_sum, run_acc)
    att_full = run_acc / jnp.moveaxis(run_sum, 3, 1)[..., None]
    log_total = run_max + jnp.log(run_sum)
    att_low = att_full.astype(jnp.bfloat16).reshape(tok_rows, QH * HD)
    attn_branch = jnp.dot(att_low, w_o_all, preferred_element_type=jnp.float32)
    middle = tokens_f + mixer_out + attn_branch
    normed_mid, norm2_pull = jax.vjp(rms_scale, middle, gain2_all.astype(jnp.float32))
    normed_two = normed_mid.astype(jnp.bfloat16)
    gate_lin = jnp.dot(normed_two, w_gate_all, preferred_element_type=jnp.float32)
    up_lin = jnp.dot(normed_two, w_up_all, preferred_element_type=jnp.float32)
    act_float, act_pull = jax.vjp(silu_product, gate_lin, up_lin)
    act_rows = act_float.astype(jnp.bfloat16)
    layer_result = (
        (middle + jnp.dot(act_rows, w_down_all, preferred_element_type=jnp.float32))
        .astype(jnp.bfloat16)
        .reshape(seq_count, span_len, model_width)
    )
    (
        w_in_back,
        w_out_back,
        w_q_back,
        w_k_back,
        w_v_back,
        w_o_back,
        w_gate_back,
        w_up_back,
        w_down_back,
    ) = (
        lax.all_gather(w_in, ("dp", "ctx"), axis=0, tiled=True),
        lax.all_gather(w_out, ("dp", "ctx"), axis=0, tiled=True),
        lax.all_gather(w_q, ("dp", "ctx"), axis=0, tiled=True),
        lax.all_gather(w_k, ("dp", "ctx"), axis=0, tiled=True),
        lax.all_gather(w_v, ("dp", "ctx"), axis=0, tiled=True),
        lax.all_gather(w_o, ("dp", "ctx"), axis=1, tiled=True),
        lax.all_gather(w_gate, ("dp", "ctx"), axis=0, tiled=True),
        lax.all_gather(w_up, ("dp", "ctx"), axis=0, tiled=True),
        lax.all_gather(w_down, ("dp", "ctx"), axis=0, tiled=True),
    )
    cot_rows = cotangent.reshape(tok_rows, model_width)
    grad_down = jnp.einsum("rf,rd->fd", act_rows, cot_rows, preferred_element_type=jnp.float32)
    grad_act = jnp.einsum("rd,fd->rf", cot_rows, w_down_back, preferred_element_type=jnp.float32)
    grad_gate_f, grad_up_f = act_pull(grad_act)
    grad_gate_low = grad_gate_f.astype(jnp.bfloat16)
    grad_up_low = grad_up_f.astype(jnp.bfloat16)
    grad_wgate = jnp.einsum(
        "rd,rf->df", normed_two, grad_gate_low, preferred_element_type=jnp.float32
    )
    grad_wup = jnp.einsum("rd,rf->df", normed_two, grad_up_low, preferred_element_type=jnp.float32)
    grad_normed = jnp.einsum(
        "rf,df->rd", grad_gate_low, w_gate_back, preferred_element_type=jnp.float32
    ) + jnp.einsum("rf,df->rd", grad_up_low, w_up_back, preferred_element_type=jnp.float32)
    grad_mid_norm, grad_gain_second = norm2_pull(grad_normed)
    grad_middle = cot_rows.astype(jnp.float32) + grad_mid_norm
    grad_mid_low = grad_middle.astype(jnp.bfloat16)
    grad_wout = jnp.einsum("ri,rd->id", mixer_in, grad_mid_low, preferred_element_type=jnp.float32)
    grad_wo = jnp.einsum("ra,rd->ad", att_low, grad_mid_low, preferred_element_type=jnp.float32)
    grad_mixer_in = jnp.einsum(
        "rd,id->ri", grad_mid_low, w_out_back, preferred_element_type=jnp.float32
    )
    grad_att = (
        jnp.einsum("rd,ad->ra", grad_mid_low, w_o_back, preferred_element_type=jnp.float32)
        .astype(jnp.bfloat16)
        .reshape(seq_count, span_len, KVH, group_size, HD)
    )
    grad_mixer_y, grad_gate_vals, grad_gain_mix = gate_pull(grad_mixer_in)
    grad_y_low = grad_mixer_y.reshape(seq_count, span_len, MH, MP).astype(jnp.bfloat16)
    grad_y_float = grad_y_low.astype(jnp.float32)
    grad_mix = jnp.einsum(
        "sihp,sjhp->shij", grad_y_low, xs_rows, preferred_element_type=jnp.float32
    )
    grad_xs = (
        jnp.einsum("shij,sihp->sjhp", mix_low, grad_y_low, preferred_element_type=jnp.float32)
        + skip_gain[:, None] * grad_y_float
    )
    grad_carried = (entry[..., None] * grad_y_float).astype(jnp.bfloat16)
    grad_entry = jnp.sum(grad_y_float * carried, axis=-1)
    grad_c = jnp.einsum(
        "sihp,shpn->sin", grad_carried, state_low, preferred_element_type=jnp.float32
    )
    grad_state_local = jnp.einsum(
        "sihp,sin->shpn", grad_carried, c_rows, preferred_element_type=jnp.float32
    )
    grad_skip = jnp.sum(grad_y_float * xs_float, axis=(0, 1, 3))
    gain_after, grad_state_out = entering(
        (carry_gain, grad_state_local), "ctx", combine_states, state_identity, True
    )
    grad_carry_gain = jnp.sum(grad_state_out * state_in, axis=(2, 3))
    grad_state_low = grad_state_out.astype(jnp.bfloat16)
    grad_xs = grad_xs + jnp.einsum(
        "sjhn,shpn->sjhp", b_scaled, grad_state_low, preferred_element_type=jnp.float32
    )
    grad_bscaled = jnp.einsum(
        "sjhp,shpn->sjhn", xs_rows, grad_state_low, preferred_element_type=jnp.float32
    )
    grad_b = jnp.sum(grad_bscaled * weight_end[..., None], axis=2)
    grad_weight_end = jnp.sum(grad_bscaled * b_rows.astype(jnp.float32)[:, :, None, :], axis=-1)
    grad_cross = jnp.sum(grad_mix * mixing, axis=1).astype(jnp.bfloat16)
    grad_mixing = grad_mix * cross[:, None]
    grad_c = grad_c + jnp.einsum(
        "sij,sjn->sin", grad_cross, b_rows, preferred_element_type=jnp.float32
    )
    grad_b = grad_b + jnp.einsum(
        "sij,sin->sjn", grad_cross, c_rows, preferred_element_type=jnp.float32
    )
    grad_rates, grad_decay_log, grad_step_bias = decay_pull(
        (grad_mixing, grad_weight_end, grad_entry, grad_carry_gain)
    )
    grad_conv_out = jnp.concatenate(
        [grad_xs.reshape(seq_count, span_len, inner_width), grad_b, grad_c], axis=-1
    )
    grad_ext, grad_conv_taps, grad_conv_shift = conv_pull(grad_conv_out)
    back_rim = from_behind(grad_ext[:, : KC - 1].astype(jnp.bfloat16), "ctx", -1).astype(
        jnp.float32
    )
    grad_pre = grad_ext[:, KC - 1 :] + jnp.concatenate(
        [jnp.zeros((seq_count, span_len - (KC - 1), channels), jnp.float32), back_rim], axis=1
    )
    grad_proj = jnp.concatenate(
        [grad_gate_vals, grad_pre.reshape(tok_rows, channels), grad_rates.reshape(tok_rows, MH)],
        axis=1,
    ).astype(jnp.bfloat16)
    grad_win = jnp.einsum("rd,rc->dc", hidden, grad_proj, preferred_element_type=jnp.float32)
    grad_hidden = jnp.einsum("rc,dc->rd", grad_proj, w_in_back, preferred_element_type=jnp.float32)
    row_delta = jnp.einsum("sigrd,sigrd->sgri", grad_att.astype(jnp.float32), att_full)
    block_in = (
        lax.all_gather(key_rows, "ctx", axis=1, tiled=True),
        lax.all_gather(value_rows, "ctx", axis=1, tiled=True),
    )
    piece_len = block_in[0].shape[1]
    key_piece = block_in[0].reshape(seq_count, piece_len, KVH, HD)
    value_piece = block_in[1].reshape(seq_count, piece_len, KVH, HD)
    allowed = key_allowed(segments, seg_own, query_index, piece_len)
    scores = (
        jnp.einsum("sigrd,sjgd->sgrij", queries, key_piece, preferred_element_type=jnp.float32)
        * qk_scale
    )
    scores = jnp.where(allowed, scores, MASKED)
    probs = jnp.where(allowed, jnp.exp(scores - log_total[..., None]), 0.0)
    probs_low = probs.astype(jnp.bfloat16)
    grad_probs = jnp.einsum(
        "sigrd,sjgd->sgrij", grad_att, value_piece, preferred_element_type=jnp.float32
    )
    grad_scores = (probs * (grad_probs - row_delta[..., None]) * qk_scale).astype(jnp.bfloat16)
    grad_query = jnp.einsum(
        "sgrij,sjgd->sigrd", grad_scores, key_piece, preferred_element_type=jnp.float32
    )
    part_key = jnp.einsum(
        "sgrij,sigrd->sjgd", grad_scores, queries, preferred_element_type=jnp.float32
    ).reshape(seq_count, piece_len, KVH * HD)
    part_value = jnp.einsum(
        "sgrij,sigrd->sjgd", probs_low, grad_att, preferred_element_type=jnp.float32
    ).reshape(seq_count, piece_len, KVH * HD)
    grad_key_all = part_key
    grad_value_all = part_value
    grad_query, grad_key_all, grad_value_all = (grad_query, grad_key_all, grad_value_all)
    grad_key_rot, grad_value = (
        lax.psum_scatter(
            grad_key_all.astype(jnp.bfloat16), "ctx", scatter_dimension=1, tiled=True
        ).astype(jnp.float32),
        lax.psum_scatter(
            grad_value_all.astype(jnp.bfloat16), "ctx", scatter_dimension=1, tiled=True
        ).astype(jnp.float32),
    )
    grad_query_lin = (
        query_pull(grad_query.reshape(seq_count, span_len, QH, HD))[0]
        .astype(jnp.bfloat16)
        .reshape(tok_rows, QH * HD)
    )
    grad_key_lin = (
        key_pull(grad_key_rot.reshape(seq_count, span_len, KVH, HD))[0]
        .astype(jnp.bfloat16)
        .reshape(tok_rows, KVH * HD)
    )
    grad_value_low = grad_value.astype(jnp.bfloat16).reshape(tok_rows, KVH * HD)
    grad_wq = jnp.einsum("rd,ra->da", hidden, grad_query_lin, preferred_element_type=jnp.float32)
    grad_wk = jnp.einsum("rd,ra->da", hidden, grad_key_lin, preferred_element_type=jnp.float32)
    grad_wv = jnp.einsum("rd,ra->da", hidden, grad_value_low, preferred_element_type=jnp.float32)
    grad_hidden = grad_hidden + jnp.einsum(
        "ra,da->rd", grad_query_lin, w_q_back, preferred_element_type=jnp.float32
    )
    grad_hidden = grad_hidden + jnp.einsum(
        "ra,da->rd", grad_key_lin, w_k_back, preferred_element_type=jnp.float32
    )
    grad_hidden = grad_hidden + jnp.einsum(
        "ra,da->rd", grad_value_low, w_v_back, preferred_element_type=jnp.float32
    )
    grad_tokens_norm, grad_gain_first = norm1_pull(grad_hidden)
    grad_tokens = (
        (grad_middle + grad_tokens_norm)
        .astype(jnp.bfloat16)
        .reshape(seq_count, span_len, model_width)
    )
    summed = (
        lax.psum_scatter(grad_gain_first, ("dp", "ctx"), scatter_dimension=0, tiled=True),
        lax.psum_scatter(grad_win, ("dp", "ctx"), scatter_dimension=0, tiled=True),
        lax.psum_scatter(grad_conv_taps, ("dp", "ctx"), scatter_dimension=1, tiled=True),
        lax.psum_scatter(grad_conv_shift, ("dp", "ctx"), scatter_dimension=0, tiled=True),
        lax.psum_scatter(grad_gain_mix, ("dp", "ctx"), scatter_dimension=0, tiled=True),
        lax.psum_scatter(grad_wout, ("dp", "ctx"), scatter_dimension=0, tiled=True),
        lax.psum_scatter(grad_wq, ("dp", "ctx"), scatter_dimension=0, tiled=True),
        lax.psum_scatter(grad_wk, ("dp", "ctx"), scatter_dimension=0, tiled=True),
        lax.psum_scatter(grad_wv, ("dp", "ctx"), scatter_dimension=0, tiled=True),
        lax.psum_scatter(grad_wo, ("dp", "ctx"), scatter_dimension=1, tiled=True),
        lax.psum_scatter(grad_gain_second, ("dp", "ctx"), scatter_dimension=0, tiled=True),
        lax.psum_scatter(grad_wgate, ("dp", "ctx"), scatter_dimension=0, tiled=True),
        lax.psum_scatter(grad_wup, ("dp", "ctx"), scatter_dimension=0, tiled=True),
        lax.psum_scatter(grad_down, ("dp", "ctx"), scatter_dimension=0, tiled=True),
    )
    head_grad = lax.psum(jnp.stack([grad_decay_log, grad_step_bias, grad_skip]), ("dp", "ctx"))
    return (
        layer_result,
        grad_tokens,
        summed[0],
        summed[1],
        summed[2],
        summed[3],
        head_grad,
        summed[4],
        summed[5],
        summed[6],
        summed[7],
        summed[8],
        summed[9],
        summed[10],
        summed[11],
        summed[12],
        summed[13],
    )


def solution(mesh):
    in_specs = (
        P("dp", "ctx", None),
        P("dp", None),
        P("dp", "ctx"),
        P(("dp", "ctx")),
        P(("dp", "ctx"), None),
        P(None, ("dp", "ctx")),
        P(("dp", "ctx")),
        P(),
        P(("dp", "ctx")),
        P(("dp", "ctx"), None),
        P(("dp", "ctx"), None),
        P(("dp", "ctx"), None),
        P(("dp", "ctx"), None),
        P(None, ("dp", "ctx")),
        P(("dp", "ctx")),
        P(("dp", "ctx"), None),
        P(("dp", "ctx"), None),
        P(("dp", "ctx"), None),
        P("dp", "ctx", None),
    )
    out_specs = (
        P("dp", "ctx", None),
        P("dp", "ctx", None),
        P(("dp", "ctx")),
        P(("dp", "ctx"), None),
        P(None, ("dp", "ctx")),
        P(("dp", "ctx")),
        P(),
        P(("dp", "ctx")),
        P(("dp", "ctx"), None),
        P(("dp", "ctx"), None),
        P(("dp", "ctx"), None),
        P(("dp", "ctx"), None),
        P(None, ("dp", "ctx")),
        P(("dp", "ctx")),
        P(("dp", "ctx"), None),
        P(("dp", "ctx"), None),
        P(("dp", "ctx"), None),
    )
    return jax.shard_map(body, mesh=mesh, in_specs=in_specs, out_specs=out_specs, check_vma=False)
```

profile of v0, /device:TPU:0, one launch (start us, length us, event | category | flops | bytes accessed | tf_op | source)
XLA Modules:
  0.0 2477.5 jit_solution(3140222655763943128)
XLA Ops:
  12.1 42.7 %all-reduce.25 = (bf16[1024]{0:T(1024)(128)(2,1)S(1)}, bf16[1792]{0:T(1024)(128)(2,1)S(1)}, bf16[1536]{0:T(1024)(128)(2,1)}, bf16[1024]{0:T(1024)(128)(2,1)}) all-reduce(bf16[1024]{0:T(1024)(128)(2,1)S(1)} %dynamic-update-slice.1, bf16[1792]{0:T(1024)(128)(2,1)S(1)} %dynamic-update-slice, ...), channel_id=1, replica_groups=mesh['dp'=8,'ctx'=4] {'dp','ctx'}, use_global_device_ids=true, to_apply=%add.16 | all-reduce | flops 5376 | bytes 21504
  54.8 69.7 %all_gather.86 = bf16[1024,128]{1,0:T(8,128)(2,1)S(1)} all-gather(bf16[32,128]{1,0:T(8,128)(2,1)} %param.34), channel_id=1, replica_groups=mesh['dp'=8,'ctx'=4] {'dp','ctx'}, dimensions={0}, use_global_device_ids=true | all-gather | bytes 270336 | tf_op jit(solution)/shard_map/all_gather | solution.py:161
  135.5 67.6 %all_gather.89 = bf16[1024,128]{1,0:T(8,128)(2,1)S(1)} all-gather(bf16[32,128]{1,0:T(8,128)(2,1)} %param.35), channel_id=1, replica_groups=mesh['dp'=8,'ctx'=4] {'dp','ctx'}, dimensions={0}, use_global_device_ids=true | all-gather | bytes 270336 | tf_op jit(solution)/shard_map/all_gather | solution.py:162
  210.3 66.8 %all-gather.2 = bf16[32,56,4]{1,2,0:T(4,128)(2,1)S(1)} all-gather(bf16[1,56,4]{1,2,0:T(4,128)(2,1)} %bitcast.471), channel_id=1, replica_groups=mesh['dp'=8,'ctx'=4] {'dp','ctx'}, dimensions={0}, use_global_device_ids=true | all-gather | bytes 14784 | tf_op jit(solution)/shard_map/all_gather | solution.py:156
  277.9 16.9 convolution_convert_fusion
  301.1 8.1 copy.321
  322.9 12.9 multiply_convert_fusion.8
  340.6 6.6 copy.323
  349.5 6.7 fusion.77
  377.3 38.2 %fusion.10 = (f32[3,2,4,512]{3,2,1,0:T(4,128)S(1)}, f32[3,2,2048,512,4]{3,2,4,1,0:T(8,128)}) fusion(pred[3,512,2048]{1,2,0:T(8,128)(4,1)} %compare_and_fusion, bf16[3,2048,2,64,1]{1,3,4,2,0:T(8,128)(2,1)} %bitcast.456, bf16[3,512,2,4,32]{1,4,3,2,0:T(8,128)(2,1)} %bitcast.444, bf16[3,512,2,4,32]{1,4,3,2,0:T(8,128)(2,1)} %bitcast.442), kind=kOutput, calls=%fused_computation.23 | convolution fusion | flops 3299856384 | bytes 107003904 | tf_op jit(solution)/shard_map/sigrd,sjgd->sgrij/dot_general | solution.py:290
  415.6 31.5 %fusion.5 = f32[3,2,4,512]{3,2,1,0:T(4,128)S(1)} fusion(f32[3,2,2048,512,4]{3,2,4,1,0:T(8,128)} %get-tuple-element.415, f32[3,2,4,512]{3,2,1,0:T(4,128)S(1)} %broadcast_maximum_fusion, pred[3,512,2048]{1,2,0:T(8,128)(4,1)S(1)} %copy-done.18), kind=kLoop, calls=%fused_computation.13 | loop fusion | flops 125816832 | bytes 103907328 | tf_op jit(solution)/shard_map/reduce_sum | solution.py:297
  450.3 37.1 %fusion.150 = (bf16[3,512,2,4,64]{1,4,3,2,0:T(8,128)(2,1)S(1)}, f32[3,512,2,4,64]{1,4,3,2,0:T(8,128)}) fusion(f32[3,512,2,4]{1,3,2,0:T(4,128)S(1)} %bitcast.465, bf16[3,2048,2,64,1]{1,3,4,2,0:T(8,128)(2,1)} %bitcast.452, f32[3,2,2048,512,4]{3,2,4,1,0:T(8,128)} %get-tuple-element.415, f32[3,2,4,512]{3,2,1,0:T(4,128)S(1)} %broadcast_maximum_fusion, ...), kind=kOutput, calls=%fused_computation.299 | convolution fusion | flops 3349413888 | bytes 110247936 | tf_op jit(solution)/shard_map/sgrij,sjgd->sigrd/dot_general | solution.py:298
  490.6 7.6 all_gather.81
  506.8 10.2 copy.365
  517.0 7.7 while.30
  528.4 30.1 %fusion.42 = f32[3,512,24,64]{1,3,2,0:T(8,128)S(1)} fusion(bf16[3,512,24,64]{1,3,2,0:T(8,128)(2,1)} %bitcast.437, f32[3,512,24,64]{1,3,2,0:T(8,128)S(1)} %fusion.90, f32[24]{0:T(128)S(1)} %copy-done.108, f32[3,512,24]{1,2,0:T(8,128)S(1)} %copy-done.61, f32[3,24,512]{2,1,0:T(8,128)S(1)} %copy-done.64, f32[3,24,512]{2,1,0:T(8,128)S(1)} %copy-done.58, ...), kind=kOutput, calls=%fused_computation.89 | convolution fusion | flops 2540961792 | bytes 27967584 | tf_op jit(solution)/shard_map/shij,sjhp->sihp/dot_general | solution.py:240
  558.6 9.3 copy.330
  567.9 9.4 copy.404
  577.4 9.3 multiply_reduce_fusion.9
  587.3 11.6 fusion.139
  608.2 15.8 all-gather.27.cloned.1.call-done
  624.0 11.6 fusion.151
  635.6 52.1 %all-gather.29.cloned.1.call-done = bf16[1024,2048]{1,0:T(8,128)(2,1)} async-done(((bf16[32,2048]{1,0:T(8,128)(2,1)}), bf16[1024,2048]{1,0:T(8,128)(2,1)}) %all-gather.29.cloned.1.call-update) | async-done | bytes 4194320 | tf_op jit(solution)/shard_map/all_gather | solution.py:166
  687.7 12.2 fusion.152
  699.9 51.3 %all-gather.31.cloned.1.call-done = bf16[2048,1024]{1,0:T(8,128)(2,1)} async-done(((bf16[64,1024]{1,0:T(8,128)(2,1)}), bf16[2048,1024]{1,0:T(8,128)(2,1)}) %all-gather.31.cloned.1.call-update) | async-done | bytes 4194320 | tf_op jit(solution)/shard_map/all_gather | solution.py:167
  751.2 22.6 multiply_convert_fusion.6
  773.8 11.8 fusion.153
  785.6 15.3 multiply_reduce_fusion.10
  814.0 59.9 %fusion.4 = bf16[3,2,4,512,2048]{3,4,2,1,0:T(8,128)(2,1)} fusion(f32[3,2,2048,512,4]{3,2,4,1,0:T(8,128)} %get-tuple-element.415, f32[3,2,4,512]{3,2,1,0:T(4,128)S(1)} %multiply_reduce_fusion.13, f32[3,2,4,512]{3,2,1,0:T(4,128)S(1)} %copy-done.97, pred[3,512,2048]{1,2,0:T(8,128)(4,1)S(1)} %copy-done.19, bf16[3,2048,2,64,1]{1,3,4,2,0:T(8,128)(2,1)} %bitcast.453, ...), kind=kOutput, calls=%fused_computation.9 | convolution fusion | flops 3422552064 | bytes 157384704 | tf_op jit(solution)/shard_map/sigrd,sjgd->sgrij/dot_general | solution.py:443
  874.0 22.5 bitcast_convert_fusion.4
  896.6 38.9 %bitcast_convert_fusion.3 = bf16[3,2,64,2048]{3,2,1,0:T(8,128)(2,1)} fusion(f32[3,2,2048,512,4]{3,2,4,1,0:T(8,128)} %get-tuple-element.415, f32[3,2,4,512]{3,2,1,0:T(4,128)S(1)} %copy-done.97, pred[3,512,2048]{1,2,0:T(8,128)(4,1)S(1)} %copy-done.19, bf16[3,512,2,4,64]{1,0,4,3,2:T(4,128)(2,1)} %reshape.546), kind=kOutput, calls=%fused_computation.132 | convolution fusion | flops 3347841024 | bytes 107003904 | tf_op jit(solution)/shard_map/sgrij,sigrd->sjgd/dot_general | solution.py:453
  938.1 12.4 multiply_reduce_fusion.6
  950.6 20.8 multiply_reduce_fusion.7
  971.3 11.9 convert_element_type.293
  994.4 19.5 fusion.154
  1028.6 11.3 fusion.138
  1041.8 10.9 fusion.161
  1052.8 10.9 fusion.162
  1065.6 28.7 %fusion.19 = f32[3,24,64,512]{3,2,1,0:T(8,128)} fusion(f32[3,24,512]{2,1,0:T(8,128)S(1)} %copy-done.65, f32[3,24,512]{2,1,0:T(8,128)S(1)} %copy-done.59, f32[3,512,512]{2,1,0:T(8,128)S(1)} %copy-done.38, pred[3,512,512]{2,1,0:T(8,128)(4,1)} %compare_and_fusion.1, bf16[3,512,24,64]{1,0,3,2:T(4,128)(2,1)} %convert_element_type.293), kind=kOutput, calls=%fused_computation.30 | convolution fusion | flops 2529165312 | bytes 18382848 | tf_op jit(solution)/shard_map/shij,sihp->sjhp/dot_general | solution.py:375
  1094.4 6.8 copy.354
  1101.2 10.9 fusion.163
  1112.0 59.0 %fusion.18 = (f32[3,24,512]{2,1,0:T(8,128)}, f32[3,24,512]{2,1,0:T(8,128)}, f32[3,24,512]{2,1,0:T(8,128)}, bf16[3,512,512]{2,1,0:T(8,128)(2,1)}) fusion(f32[3,24,512]{2,1,0:T(8,128)S(1)} %copy-done.65, f32[3,24,512]{2,1,0:T(8,128)S(1)} %copy-done.59, f32[3,512,512]{2,1,0:T(8,128)} %fusion.95, pred[3,512,512]{2,1,0:T(8,128)(4,1)} %compare_and_fusion.1, ...), kind=kOutput, calls=%fused_computation.29 | convolution fusion | flops 2698137600 | bytes 15679488 | tf_op jit(solution)/shard_map/sihp,sjhp->shij/dot_general | solution.py:371
  1179.4 8.1 fusion.41
  1187.5 17.4 while.31
  1204.9 10.3 fusion.39
  1215.3 9.7 copy.346
  1224.9 7.6 fusion.21
  1237.4 24.3 multiply_reduce_fusion.5
  1261.7 15.2 multiply_multiply_fusion.3
  1277.0 15.8 pad_add_fusion
  1299.9 14.9 reduce-window.16
  1324.0 17.6 fusion.59
  1343.2 6.2 fusion.155
  1349.4 10.1 add_convert_fusion
  1368.8 21.2 fusion.53
  1390.1 40.9 %all-reduce.24 = (f32[1024]{0:T(1024)S(1)}, f32[4,1792]{1,0:T(4,128)S(1)}, f32[1792]{0:T(1024)S(1)}, f32[3,24]{1,0:T(4,128)}, f32[1536]{0:T(1024)S(1)}, /*index=5*/f32[1024]{0:T(1024)S(1)}) all-reduce(f32[1024]{0:T(1024)} %get-tuple-element.326, f32[4,1792]{1,0:T(4,128)} %pad_add_fusion.1, ...), channel_id=6, replica_groups=mesh['dp'=8,'ctx'=4] {'dp','ctx'}, use_global_device_ids=true, to_apply=%region_28.29.clone | all-reduce | flops 12616 | bytes 100928
  1434.7 10.5 fusion.49
  1445.2 45.3 %reduce-scatter.23.cloned.1.call-done = f32[32,128]{1,0:T(8,128)} async-done(((f32[1024,128]{1,0:T(8,128)}), f32[32,128]{1,0:T(8,128)}) %reduce-scatter.23.cloned.1.call-update) | async-done | bytes 16400 | tf_op jit(solution)/shard_map/reduce_scatter | solution.py:504
  1490.5 133.5 %reduce-scatter.25.cloned.1.call-done = f32[32,128]{1,0:T(8,128)} async-done(((f32[1024,128]{1,0:T(8,128)}), f32[32,128]{1,0:T(8,128)}) %reduce-scatter.25.cloned.1.call-update) | async-done | bytes 16400 | tf_op jit(solution)/shard_map/reduce_scatter | solution.py:505
  1624.0 117.5 %reduce-scatter.19.cloned.1.call-done = f32[48,1024]{1,0:T(8,128)} async-done(((f32[1536,1024]{1,0:T(8,128)}), f32[48,1024]{1,0:T(8,128)}) %reduce-scatter.19.cloned.1.call-update) | async-done | bytes 196624 | tf_op jit(solution)/shard_map/reduce_scatter | solution.py:502
  1741.5 188.0 %reduce-scatter.29.cloned.1.call-done = f32[32,2048]{1,0:T(8,128)} async-done(((f32[1024,2048]{1,0:T(8,128)}), f32[32,2048]{1,0:T(8,128)}) %reduce-scatter.29.cloned.1.call-update) | async-done | bytes 262160 | tf_op jit(solution)/shard_map/reduce_scatter | solution.py:508
  1929.5 186.3 %reduce-scatter.31.cloned.1.call-done = f32[32,2048]{1,0:T(8,128)} async-done(((f32[1024,2048]{1,0:T(8,128)}), f32[32,2048]{1,0:T(8,128)}) %reduce-scatter.31.cloned.1.call-update) | async-done | bytes 262160 | tf_op jit(solution)/shard_map/reduce_scatter | solution.py:509
  2115.8 186.5 %reduce-scatter.33.cloned.1.call-done = f32[64,1024]{1,0:T(8,128)} async-done(((f32[2048,1024]{1,0:T(8,128)}), f32[64,1024]{1,0:T(8,128)}) %reduce-scatter.33.cloned.1.call-update) | async-done | bytes 262160 | tf_op jit(solution)/shard_map/reduce_scatter | solution.py:510
  2302.3 168.1 %reduce-scatter.17.cloned.1.call-done = f32[32,3352]{1,0:T(8,128)} async-done(((f32[1024,3352]{1,0:T(8,128)}), f32[32,3352]{1,0:T(8,128)}) %reduce-scatter.17.cloned.1.call-update) | async-done | bytes 429072 | tf_op jit(solution)/shard_map/reduce_scatter | solution.py:498
  (470 shorter events, 213.7 us)
Async XLA Ops:
  7.2 122.9 %copy-start.7 = (bf16[3,512,1024]{2,1,0:T(8,128)(2,1)S(1)}, bf16[3,512,1024]{2,1,0:T(8,128)(2,1)}, u32[]{:S(2)}) copy-start(bf16[3,512,1024]{2,1,0:T(8,128)(2,1)} %param.23) | copy-start | bytes 9437188
  7.2 270.7 %all-gather.15.cloned.1.call-start = ((), (), s32[]{:S(2)}) async-start(), calls=%async_computation.11 | async-start | bytes 7299072 | tf_op jit(solution)/shard_map/all_gather | solution.py:155
  7.9 362.3 %all-gather.21.cloned.1.call-start = ((), (), s32[]{:S(2)}) async-start(), calls=%async_computation.14 | async-start | bytes 1081344 | tf_op jit(solution)/shard_map/all_gather | solution.py:160
  8.7 368.6 %all-gather.19.cloned.1.call-start = ((), (), s32[]{:S(2)}) async-start(), calls=%async_computation.13 | async-start | bytes 1966080 | tf_op jit(solution)/shard_map/all_gather | solution.py:280
  54.8 148.3 %copy-start.93 = (f32[1024]{0:T(1024)}, f32[1024]{0:T(1024)S(1)}, u32[]{:S(2)}) copy-start(f32[1024]{0:T(1024)S(1)} %convert_element_type.259) | copy-start | bytes 12292
  130.1 245.4 %copy-start.29 = (f32[3,512,32]{1,2,0:T(8,128)}, f32[3,512,32]{1,2,0:T(8,128)S(1)}, u32[]{:S(2)}) copy-start(f32[3,512,32]{1,2,0:T(8,128)S(1)} %get-tuple-element.406) | copy-start | bytes 589828
  130.1 245.4 %copy-start.31 = (f32[3,512,32]{1,2,0:T(8,128)}, f32[3,512,32]{1,2,0:T(8,128)S(1)}, u32[]{:S(2)}) copy-start(f32[3,512,32]{1,2,0:T(8,128)S(1)} %get-tuple-element.407) | copy-start | bytes 589828
  134.7 313.0 %all-gather.23.cloned.1.call-start = ((), (), s32[]{:S(2)}) async-start(), calls=%async_computation.15 | async-start | bytes 1966080 | tf_op jit(solution)/shard_map/all_gather | solution.py:281
  135.5 72.9 %copy-start.83 = (f32[1536]{0:T(1024)}, f32[1536]{0:T(1024)S(1)}, u32[]{:S(2)}) copy-start(f32[1536]{0:T(1024)S(1)} %add.292) | copy-start | bytes 18436
  135.5 71.8 %copy-start.78 = (f32[1536]{0:T(1024)}, f32[1536]{0:T(1024)S(1)}, u32[]{:S(2)}) copy-start(f32[1536]{0:T(1024)S(1)} %rsqrt.33) | copy-start | bytes 18436
  205.6 71.8 %copy-start.116 = (f32[3,24]{1,0:T(4,128)S(1)}, f32[3,24]{1,0:T(4,128)}, u32[]{:S(2)}) copy-start(f32[3,24]{1,0:T(4,128)} %param.30) | copy-start | bytes 868
  207.3 309.7 %all-gather.33.cloned.1.call-start = ((), (), s32[]{:S(2)}) async-start(), calls=%async_computation.31 | async-start | bytes 5898240 | tf_op jit(solution)/shard_map/all_gather | solution.py:29
  209.1 109.0 %copy-start.81 = (f32[3,512]{1,0:T(4,128)}, f32[3,512]{1,0:T(4,128)S(1)}, u32[]{:S(2)}) copy-start(f32[3,512]{1,0:T(4,128)S(1)} %get-tuple-element.371) | copy-start | bytes 18436
  210.1 108.0 %copy-start.56 = (f32[3,512]{1,0:T(4,128)}, f32[3,512]{1,0:T(4,128)S(1)}, u32[]{:S(2)}) copy-start(f32[3,512]{1,0:T(4,128)S(1)} %get-tuple-element.410) | copy-start | bytes 18436
  210.3 112.5 %copy-start.68 = (f32[3,512]{1,0:T(4,128)}, f32[3,512]{1,0:T(4,128)S(1)}, u32[]{:S(2)}) copy-start(f32[3,512]{1,0:T(4,128)S(1)} %get-tuple-element.399) | copy-start | bytes 18436
  210.3 112.5 %copy-start.70 = (f32[3,512]{1,0:T(4,128)}, f32[3,512]{1,0:T(4,128)S(1)}, u32[]{:S(2)}) copy-start(f32[3,512]{1,0:T(4,128)S(1)} %get-tuple-element.400) | copy-start | bytes 18436
  210.3 112.5 %copy-start.72 = (f32[3,512]{1,0:T(4,128)}, f32[3,512]{1,0:T(4,128)S(1)}, u32[]{:S(2)}) copy-start(f32[3,512]{1,0:T(4,128)S(1)} %get-tuple-element.401) | copy-start | bytes 18436
  210.3 112.5 %copy-start.74 = (f32[3,512]{1,0:T(4,128)}, f32[3,512]{1,0:T(4,128)S(1)}, u32[]{:S(2)}) copy-start(f32[3,512]{1,0:T(4,128)S(1)} %get-tuple-element.402) | copy-start | bytes 18436
  277.4 45.4 %copy-start.84 = (f32[1792]{0:T(1024)}, f32[1792]{0:T(1024)S(1)}, u32[]{:S(2)}) copy-start(f32[1792]{0:T(1024)S(1)} %get-tuple-element.330) | copy-start | bytes 21508
  277.4 45.4 %copy-start.86 = (f32[1792]{0:T(1024)}, f32[1792]{0:T(1024)S(1)}, u32[]{:S(2)}) copy-start(f32[1792]{0:T(1024)S(1)} %get-tuple-element.331) | copy-start | bytes 21508
  277.4 45.4 %copy-start.88 = (f32[1792]{0:T(1024)}, f32[1792]{0:T(1024)S(1)}, u32[]{:S(2)}) copy-start(f32[1792]{0:T(1024)S(1)} %get-tuple-element.332) | copy-start | bytes 21508
  277.4 45.4 %copy-start.90 = (f32[1792]{0:T(1024)}, f32[1792]{0:T(1024)S(1)}, u32[]{:S(2)}) copy-start(f32[1792]{0:T(1024)S(1)} %get-tuple-element.333) | copy-start | bytes 21508
  277.9 34.7 %copy-start.111 = (f32[24]{0:T(128)}, f32[24]{0:T(128)S(1)}, u32[]{:S(2)}) copy-start(f32[24]{0:T(128)S(1)} %get-tuple-element.413) | copy-start | bytes 292
  277.9 40.2 %copy-start.106 = (f32[24]{0:T(128)}, f32[24]{0:T(128)S(1)}, u32[]{:S(2)}) copy-start(f32[24]{0:T(128)S(1)} %get-tuple-element.412) | copy-start | bytes 292
  310.1 8.9 collective-permute-start
  319.0 29.6 %copy-start.51 = (f32[3,512,24]{1,2,0:T(8,128)}, f32[3,512,24]{1,2,0:T(8,128)S(1)}, u32[]{:S(2)}) copy-start(f32[3,512,24]{1,2,0:T(8,128)S(1)} %get-tuple-element.393) | copy-start | bytes 442372
  356.3 231.0 %all-gather.17.cloned.1.call-start = ((), (), s32[]{:S(2)}) async-start(), calls=%async_computation.12 | async-start | bytes 3244032 | tf_op jit(solution)/shard_map/all_gather | solution.py:159
  356.8 242.0 %all-gather.25.cloned.1.call-start = ((), (), s32[]{:S(2)}) async-start(), calls=%async_computation.16 | async-start | bytes 1081344 | tf_op jit(solution)/shard_map/all_gather | solution.py:163
  357.6 266.4 %all-gather.27.cloned.1.call-start = ((), (), s32[]{:S(2)}) async-start(), calls=%async_computation.17 | async-start | bytes 4325376 | tf_op jit(solution)/shard_map/all_gather | solution.py:165
  358.3 329.3 %all-gather.29.cloned.1.call-start = ((), (), s32[]{:S(2)}) async-start(), calls=%async_computation.18 | async-start | bytes 4325376 | tf_op jit(solution)/shard_map/all_gather | solution.py:166
  359.1 392.1 %all-gather.31.cloned.1.call-start = ((), (), s32[]{:S(2)}) async-start(), calls=%async_computation.19 | async-start | bytes 4325376 | tf_op jit(solution)/shard_map/all_gather | solution.py:167
  359.7 661.4 %reduce-scatter.13.cloned.1.call-start = ((), (), s32[]{:S(2)}) async-start(), calls=%async_computation.20 | async-start | bytes 1966080 | tf_op jit(solution)/shard_map/reduce_scatter | solution.py:460
  360.7 129.8 %copy-start.113 = (f32[3]{0:T(128)}, f32[3]{0:T(128)S(1)}, u32[]{:S(2)}) copy-start(f32[3]{0:T(128)S(1)} %convert_reduce_fusion) | copy-start | bytes 40
  377.3 38.3 %copy-start.18 = (pred[3,512,2048]{1,2,0:T(8,128)(4,1)S(1)}, pred[3,512,2048]{1,2,0:T(8,128)(4,1)}, u32[]{:S(2)}) copy-start(pred[3,512,2048]{1,2,0:T(8,128)(4,1)} %compare_and_fusion) | copy-start | bytes 9437188
  528.2 30.4 %copy-start.13 = (f32[3,512,24,64]{1,3,2,0:T(8,128)}, f32[3,512,24,64]{1,3,2,0:T(8,128)S(1)}, u32[]{:S(2)}) copy-start(f32[3,512,24,64]{1,3,2,0:T(8,128)S(1)} %fusion.90) | copy-start | bytes 28311556
  604.9 196.1 %copy-start.66 = (f32[1536]{0:T(1024)}, f32[1536]{0:T(1024)S(1)}, u32[]{:S(2)}) copy-start(f32[1536]{0:T(1024)S(1)} %fusion.121) | copy-start | bytes 18436
  635.6 115.6 %copy-start.16 = (bf16[3,512,1024]{2,1,0:T(8,128)(2,1)S(1)}, bf16[3,512,1024]{2,1,0:T(8,128)(2,1)}, u32[]{:S(2)}) copy-start(bf16[3,512,1024]{2,1,0:T(8,128)(2,1)} %param.41) | copy-start | bytes 9437188
  773.8 27.2 %slice-start = ((s8[6291456]{0:T(1024)(128)(4,1)}), s8[4194304]{0:T(1024)(128)(4,1)S(1)}, s32[]{:S(2)}) async-start(s8[6291456]{0:T(1024)(128)(4,1)} %bitcast.403), calls=%async_computation.33 | async-start | bytes 8388608
  896.5 41.6 %copy-start.103 = (f32[1536]{0:T(1024)S(1)}, f32[1536]{0:T(1024)}, u32[]{:S(2)}) copy-start(f32[1536]{0:T(1024)} %convert_element_type.276) | copy-start | bytes 18436
  896.5 41.6 %copy-start.105 = (f32[1536]{0:T(1024)S(1)}, f32[1536]{0:T(1024)}, u32[]{:S(2)}) copy-start(f32[1536]{0:T(1024)} %copy-done.104) | copy-start | bytes 18436
  896.5 129.0 %reduce-scatter.15.cloned.1.call-start = ((), (), s32[]{:S(2)}) async-start(), calls=%async_computation.21 | async-start | bytes 1966080 | tf_op jit(solution)/shard_map/reduce_scatter | solution.py:463
  950.5 237.0 %all-gather.35.cloned.1.call-start = ((), (), s32[]{:S(2)}) async-start(), calls=%async_computation.32 | async-start | bytes 5898240 | tf_op jit(solution)/shard_map/all_gather | solution.py:29
  989.0 456.2 %reduce-scatter.27.cloned.1.call-start = ((), (), s32[]{:S(2)}) async-start(), calls=%async_computation.27 | async-start | bytes 2162688 | tf_op jit(solution)/shard_map/reduce_scatter | solution.py:506
  994.4 450.9 %reduce-scatter.21.cloned.1.call-start = ((), (), s32[]{:S(2)}) async-start(), calls=%async_computation.24 | async-start | bytes 2162688 | tf_op jit(solution)/shard_map/reduce_scatter | solution.py:503
  1021.0 469.5 %reduce-scatter.23.cloned.1.call-start = ((), (), s32[]{:S(2)}) async-start(), calls=%async_computation.25 | async-start | bytes 540672 | tf_op jit(solution)/shard_map/reduce_scatter | solution.py:504
  1025.4 598.6 %reduce-scatter.25.cloned.1.call-start = ((), (), s32[]{:S(2)}) async-start(), calls=%async_computation.26 | async-start | bytes 540672 | tf_op jit(solution)/shard_map/reduce_scatter | solution.py:505
  1028.3 713.1 %reduce-scatter.19.cloned.1.call-start = ((), (), s32[]{:S(2)}) async-start(), calls=%async_computation.23 | async-start | bytes 6488064 | tf_op jit(solution)/shard_map/reduce_scatter | solution.py:502
  1039.9 889.5 %reduce-scatter.29.cloned.1.call-start = ((), (), s32[]{:S(2)}) async-start(), calls=%async_computation.28 | async-start | bytes 8650752 | tf_op jit(solution)/shard_map/reduce_scatter | solution.py:508
  1052.7 1063.1 %reduce-scatter.31.cloned.1.call-start = ((), (), s32[]{:S(2)}) async-start(), calls=%async_computation.29 | async-start | bytes 8650752 | tf_op jit(solution)/shard_map/reduce_scatter | solution.py:509
  1063.8 1238.5 %reduce-scatter.33.cloned.1.call-start = ((), (), s32[]{:S(2)}) async-start(), calls=%async_computation.30 | async-start | bytes 8650752 | tf_op jit(solution)/shard_map/reduce_scatter | solution.py:510
  1171.0 1299.4 %reduce-scatter.17.cloned.1.call-start = ((), (), s32[]{:S(2)}) async-start(), calls=%async_computation.22 | async-start | bytes 14598144 | tf_op jit(solution)/shard_map/reduce_scatter | solution.py:498
  1237.4 24.3 copy-start.85
  1237.4 24.3 copy-start.87
  1237.4 24.3 copy-start.89
  1237.4 24.3 copy-start.91
  1277.0 20.2 copy-start.21
  1277.0 20.2 copy-start.26
  1277.0 20.8 copy-start.114
  1277.0 21.7 copy-start.82
  1292.9 22.2 copy-start.60
  1292.9 22.2 copy-start.112
  1293.5 22.7 collective-permute-start.1
  1368.8 65.9 %copy-start.67 = (f32[1536]{0:T(1024)S(1)}, f32[1536]{0:T(1024)}, u32[]{:S(2)}) copy-start(f32[1536]{0:T(1024)} %copy-done.66) | copy-start | bytes 18436
  1368.8 65.9 %copy-start.77 = (f32[1536]{0:T(1024)S(1)}, f32[1536]{0:T(1024)}, u32[]{:S(2)}) copy-start(f32[1536]{0:T(1024)} %copy-done.76) | copy-start | bytes 18436
  (87 other events, 636.2 us)
Sparse Core Ops, SparseCore 0:
  10.8 75.8 all-gather.14
  89.7 52.7 all-gather.20
  144.6 38.4 all-gather.18
  207.4 36.1 all-gather.22
  356.4 87.5 all-gather.32
  446.8 57.5 all-gather.16
  507.3 52.5 all-gather.24
  562.9 61.0 all-gather.26
  627.0 60.6 all-gather.28
  690.5 60.6 all-gather.30
  896.6 33.9 reduce-scatter.12
  950.6 33.7 reduce-scatter.14
  989.2 87.9 all-gather.34
  1079.8 136.6 reduce-scatter.26
  1219.3 136.5 reduce-scatter.20
  1358.5 131.9 reduce-scatter.22
  1493.3 130.6 reduce-scatter.24
  1630.1 111.3 reduce-scatter.18
  1744.4 184.9 reduce-scatter.28
  1932.3 183.4 reduce-scatter.30
  2118.8 183.4 reduce-scatter.32
  2309.9 160.4 reduce-scatter.16
where the time goes:
time: 2490 us; the launch traced here: 2480 us
  waiting for transfers between devices  1150 us (46%)
  matrix products  627 us (25%)
  blocking collectives  295 us (12%)
  other arithmetic  246 us (10%)
  local copies, waits for them, and re-layouts  137 us (6%)
    reduce_scatter x1, waiting for transfers between devices, body(): lax.psum_scatter(grad_wgate, ('dp', 'ctx'), scatter_dimension=0, tiled=True)  188 us
    reduce_scatter x1, waiting for transfers between devices, body(): lax.psum_scatter(grad_down, ('dp', 'ctx'), scatter_dimension=0, tiled=True)  186 us
    reduce_scatter x1, waiting for transfers between devices, body(): lax.psum_scatter(grad_wup, ('dp', 'ctx'), scatter_dimension=0, tiled=True)  186 us
    reduce_scatter x1, waiting for transfers between devices, body(): lax.psum_scatter(grad_win, ('dp', 'ctx'), scatter_dimension=0, tiled=True)  168 us
    reduce_scatter x1, waiting for transfers between devices, body(): lax.psum_scatter(grad_wv, ('dp', 'ctx'), scatter_dimension=0, tiled=True)  133 us
    reduce_scatter x1, waiting for transfers between devices, body(): lax.psum_scatter(grad_wout, ('dp', 'ctx'), scatter_dimension=0, tiled=True)  117 us
    unnamed x2, blocking collectives  83.6 us
    all_gather x1, blocking collectives, body(): lax.all_gather(w_k, ('dp', 'ctx'), axis=0, tiled=True)  69.7 us
  transfers between devices with their start and end apart: 24, of which 10 were waited for; matrix products, arithmetic and copies ran while one was open for 34% of the time, Pallas kernels for 0%

commit v1 on v0

--- a/solution.py
+++ b/solution.py
@@ -94,7 +94,9 @@
 def decay_terms(rate_raw, decay_log, step_bias, pair_mask, last_same, prev_same, flag_gain):
     step_size = jax.nn.softplus(rate_raw + step_bias)
     log_decay = -step_size * jnp.exp(decay_log)
-    cumul = jnp.cumsum(log_decay, axis=1)
+    span_len = log_decay.shape[1]
+    lower = jnp.tril(jnp.ones((span_len, span_len), jnp.float32))
+    cumul = jnp.einsum("ij,sjh->sih", lower, log_decay, precision=lax.Precision.HIGHEST)
     by_head = jnp.swapaxes(cumul, 1, 2)
     differ = by_head[:, :, :, None] - by_head[:, :, None, :]
     inside = pair_mask[:, None]
@@ -150,38 +152,36 @@
     channels = inner_width + 2 * NS
     group_size = QH // KVH
     qk_scale = HD ** (-0.5)
-    gathered = (
-        lax.all_gather(gain_one, ("dp", "ctx"), axis=0, tiled=True),
-        lax.all_gather(w_in, ("dp", "ctx"), axis=0, tiled=True),
-        lax.all_gather(conv_w, ("dp", "ctx"), axis=1, tiled=True),
-        lax.all_gather(conv_b, ("dp", "ctx"), axis=0, tiled=True),
-        lax.all_gather(gain_m, ("dp", "ctx"), axis=0, tiled=True),
-        lax.all_gather(w_out, ("dp", "ctx"), axis=0, tiled=True),
-        lax.all_gather(w_q, ("dp", "ctx"), axis=0, tiled=True),
-        lax.all_gather(w_k, ("dp", "ctx"), axis=0, tiled=True),
-        lax.all_gather(w_v, ("dp", "ctx"), axis=0, tiled=True),
-        lax.all_gather(w_o, ("dp", "ctx"), axis=1, tiled=True),
-        lax.all_gather(gain_two, ("dp", "ctx"), axis=0, tiled=True),
-        lax.all_gather(w_gate, ("dp", "ctx"), axis=0, tiled=True),
-        lax.all_gather(w_up, ("dp", "ctx"), axis=0, tiled=True),
-        lax.all_gather(w_down, ("dp", "ctx"), axis=0, tiled=True),
-    )
-    (
-        gain1_all,
-        w_in_all,
-        conv_w_all,
-        conv_b_all,
-        gain_m_all,
-        w_out_all,
-        w_q_all,
-        w_k_all,
-        w_v_all,
-        w_o_all,
-        gain2_all,
-        w_gate_all,
-        w_up_all,
-        w_down_all,
-    ) = gathered
+    axes = ("dp", "ctx")
+    own_rows = w_q.shape[0]
+    own_small = jnp.concatenate(
+        [gain_one, gain_two, gain_m, conv_b, conv_w.reshape(-1)], axis=0
+    )
+    small_sizes = (gain_one.shape[0], gain_two.shape[0], gain_m.shape[0], conv_b.shape[0])
+    slots = own_rows * 128
+    small_block = jnp.pad(own_small, (0, slots - own_small.shape[0])).reshape(own_rows, 128)
+    first_all = lax.all_gather(
+        jnp.concatenate([w_q, w_k, w_v, small_block], axis=1), axes, axis=0, tiled=True
+    )
+    w_in_all = lax.all_gather(w_in, axes, axis=0, tiled=True)
+    w_out_all = lax.all_gather(w_out, axes, axis=0, tiled=True)
+    w_o_all = lax.all_gather(w_o.T, axes, axis=0, tiled=True).T
+    w_gate_all = lax.all_gather(w_gate, axes, axis=0, tiled=True)
+    w_up_all = lax.all_gather(w_up, axes, axis=0, tiled=True)
+    w_down_all = lax.all_gather(w_down, axes, axis=0, tiled=True)
+    q_width, k_width = w_q.shape[1], w_k.shape[1]
+    w_q_all = first_all[:, :q_width]
+    w_k_all = first_all[:, q_width : q_width + k_width]
+    w_v_all = first_all[:, q_width + k_width : q_width + 2 * k_width]
+    small_all = first_all[:, q_width + 2 * k_width :].reshape(-1, slots)
+    parts, at = [], 0
+    for size in small_sizes:
+        parts.append(small_all[:, at : at + size].reshape(-1))
+        at += size
+    gain1_all, gain2_all, gain_m_all, conv_b_all = parts
+    conv_w_all = jnp.swapaxes(
+        small_all[:, at : at + KC * small_sizes[3]].reshape(-1, KC, small_sizes[3]), 0, 1
+    ).reshape(KC, -1)
     span_start = lax.axis_index("ctx") * span_len
     has_prev = lax.axis_index("ctx") > 0
     offsets = jnp.arange(span_len, dtype=jnp.int32)
@@ -276,10 +276,11 @@
         .astype(jnp.bfloat16)
         .reshape(seq_count, span_len, KVH * HD)
     )
-    block_in = (
-        lax.all_gather(key_rows, "ctx", axis=1, tiled=True),
-        lax.all_gather(value_rows, "ctx", axis=1, tiled=True),
-    )
+    kv_width = KVH * HD
+    kv_all = lax.all_gather(
+        jnp.concatenate([key_rows, value_rows], axis=2), "ctx", axis=1, tiled=True
+    )
+    block_in = (kv_all[..., :kv_width], kv_all[..., kv_width:])
     run_max = jnp.full((seq_count, KVH, group_size, span_len), MASKED, jnp.float32)
     run_acc = jnp.zeros((seq_count, span_len, KVH, group_size, HD), jnp.float32)
     piece_len = block_in[0].shape[1]
@@ -318,30 +319,9 @@
         .astype(jnp.bfloat16)
         .reshape(seq_count, span_len, model_width)
     )
-    (
-        w_in_back,
-        w_out_back,
-        w_q_back,
-        w_k_back,
-        w_v_back,
-        w_o_back,
-        w_gate_back,
-        w_up_back,
-        w_down_back,
-    ) = (
-        lax.all_gather(w_in, ("dp", "ctx"), axis=0, tiled=True),
-        lax.all_gather(w_out, ("dp", "ctx"), axis=0, tiled=True),
-        lax.all_gather(w_q, ("dp", "ctx"), axis=0, tiled=True),
-        lax.all_gather(w_k, ("dp", "ctx"), axis=0, tiled=True),
-        lax.all_gather(w_v, ("dp", "ctx"), axis=0, tiled=True),
-        lax.all_gather(w_o, ("dp", "ctx"), axis=1, tiled=True),
-        lax.all_gather(w_gate, ("dp", "ctx"), axis=0, tiled=True),
-        lax.all_gather(w_up, ("dp", "ctx"), axis=0, tiled=True),
-        lax.all_gather(w_down, ("dp", "ctx"), axis=0, tiled=True),
-    )
     cot_rows = cotangent.reshape(tok_rows, model_width)
     grad_down = jnp.einsum("rf,rd->fd", act_rows, cot_rows, preferred_element_type=jnp.float32)
-    grad_act = jnp.einsum("rd,fd->rf", cot_rows, w_down_back, preferred_element_type=jnp.float32)
+    grad_act = jnp.einsum("rd,fd->rf", cot_rows, w_down_all, preferred_element_type=jnp.float32)
     grad_gate_f, grad_up_f = act_pull(grad_act)
     grad_gate_low = grad_gate_f.astype(jnp.bfloat16)
     grad_up_low = grad_up_f.astype(jnp.bfloat16)
@@ -350,18 +330,18 @@
     )
     grad_wup = jnp.einsum("rd,rf->df", normed_two, grad_up_low, preferred_element_type=jnp.float32)
     grad_normed = jnp.einsum(
-        "rf,df->rd", grad_gate_low, w_gate_back, preferred_element_type=jnp.float32
-    ) + jnp.einsum("rf,df->rd", grad_up_low, w_up_back, preferred_element_type=jnp.float32)
+        "rf,df->rd", grad_gate_low, w_gate_all, preferred_element_type=jnp.float32
+    ) + jnp.einsum("rf,df->rd", grad_up_low, w_up_all, preferred_element_type=jnp.float32)
     grad_mid_norm, grad_gain_second = norm2_pull(grad_normed)
     grad_middle = cot_rows.astype(jnp.float32) + grad_mid_norm
     grad_mid_low = grad_middle.astype(jnp.bfloat16)
     grad_wout = jnp.einsum("ri,rd->id", mixer_in, grad_mid_low, preferred_element_type=jnp.float32)
     grad_wo = jnp.einsum("ra,rd->ad", att_low, grad_mid_low, preferred_element_type=jnp.float32)
     grad_mixer_in = jnp.einsum(
-        "rd,id->ri", grad_mid_low, w_out_back, preferred_element_type=jnp.float32
+        "rd,id->ri", grad_mid_low, w_out_all, preferred_element_type=jnp.float32
     )
     grad_att = (
-        jnp.einsum("rd,ad->ra", grad_mid_low, w_o_back, preferred_element_type=jnp.float32)
+        jnp.einsum("rd,ad->ra", grad_mid_low, w_o_all, preferred_element_type=jnp.float32)
         .astype(jnp.bfloat16)
         .reshape(seq_count, span_len, KVH, group_size, HD)
     )
@@ -423,12 +403,8 @@
         axis=1,
     ).astype(jnp.bfloat16)
     grad_win = jnp.einsum("rd,rc->dc", hidden, grad_proj, preferred_element_type=jnp.float32)
-    grad_hidden = jnp.einsum("rc,dc->rd", grad_proj, w_in_back, preferred_element_type=jnp.float32)
+    grad_hidden = jnp.einsum("rc,dc->rd", grad_proj, w_in_all, preferred_element_type=jnp.float32)
     row_delta = jnp.einsum("sigrd,sigrd->sgri", grad_att.astype(jnp.float32), att_full)
-    block_in = (
-        lax.all_gather(key_rows, "ctx", axis=1, tiled=True),
-        lax.all_gather(value_rows, "ctx", axis=1, tiled=True),
-    )
     piece_len = block_in[0].shape[1]
     key_piece = block_in[0].reshape(seq_count, piece_len, KVH, HD)
     value_piece = block_in[1].reshape(seq_count, piece_len, KVH, HD)
@@ -456,14 +432,13 @@
     grad_key_all = part_key
     grad_value_all = part_value
     grad_query, grad_key_all, grad_value_all = (grad_query, grad_key_all, grad_value_all)
-    grad_key_rot, grad_value = (
-        lax.psum_scatter(
-            grad_key_all.astype(jnp.bfloat16), "ctx", scatter_dimension=1, tiled=True
-        ).astype(jnp.float32),
-        lax.psum_scatter(
-            grad_value_all.astype(jnp.bfloat16), "ctx", scatter_dimension=1, tiled=True
-        ).astype(jnp.float32),
-    )
+    grad_kv = lax.psum_scatter(
+        jnp.concatenate([grad_key_all, grad_value_all], axis=2).astype(jnp.bfloat16),
+        "ctx",
+        scatter_dimension=1,
+        tiled=True,
+    ).astype(jnp.float32)
+    grad_key_rot, grad_value = (grad_kv[..., :kv_width], grad_kv[..., kv_width:])
     grad_query_lin = (
         query_pull(grad_query.reshape(seq_count, span_len, QH, HD))[0]
         .astype(jnp.bfloat16)
@@ -479,13 +454,13 @@
     grad_wk = jnp.einsum("rd,ra->da", hidden, grad_key_lin, preferred_element_type=jnp.float32)
     grad_wv = jnp.einsum("rd,ra->da", hidden, grad_value_low, preferred_element_type=jnp.float32)
     grad_hidden = grad_hidden + jnp.einsum(
-        "ra,da->rd", grad_query_lin, w_q_back, preferred_element_type=jnp.float32
+        "ra,da->rd", grad_query_lin, w_q_all, preferred_element_type=jnp.float32
     )
     grad_hidden = grad_hidden + jnp.einsum(
-        "ra,da->rd", grad_key_lin, w_k_back, preferred_element_type=jnp.float32
+        "ra,da->rd", grad_key_lin, w_k_all, preferred_element_type=jnp.float32
     )
     grad_hidden = grad_hidden + jnp.einsum(
-        "ra,da->rd", grad_value_low, w_v_back, preferred_element_type=jnp.float32
+        "ra,da->rd", grad_value_low, w_v_all, preferred_element_type=jnp.float32
     )
     grad_tokens_norm, grad_gain_first = norm1_pull(grad_hidden)
     grad_tokens = (
@@ -493,41 +468,57 @@
         .astype(jnp.bfloat16)
         .reshape(seq_count, span_len, model_width)
     )
-    summed = (
-        lax.psum_scatter(grad_gain_first, ("dp", "ctx"), scatter_dimension=0, tiled=True),
-        lax.psum_scatter(grad_win, ("dp", "ctx"), scatter_dimension=0, tiled=True),
-        lax.psum_scatter(grad_conv_taps, ("dp", "ctx"), scatter_dimension=1, tiled=True),
-        lax.psum_scatter(grad_conv_shift, ("dp", "ctx"), scatter_dimension=0, tiled=True),
-        lax.psum_scatter(grad_gain_mix, ("dp", "ctx"), scatter_dimension=0, tiled=True),
-        lax.psum_scatter(grad_wout, ("dp", "ctx"), scatter_dimension=0, tiled=True),
-        lax.psum_scatter(grad_wq, ("dp", "ctx"), scatter_dimension=0, tiled=True),
-        lax.psum_scatter(grad_wk, ("dp", "ctx"), scatter_dimension=0, tiled=True),
-        lax.psum_scatter(grad_wv, ("dp", "ctx"), scatter_dimension=0, tiled=True),
-        lax.psum_scatter(grad_wo, ("dp", "ctx"), scatter_dimension=1, tiled=True),
-        lax.psum_scatter(grad_gain_second, ("dp", "ctx"), scatter_dimension=0, tiled=True),
-        lax.psum_scatter(grad_wgate, ("dp", "ctx"), scatter_dimension=0, tiled=True),
-        lax.psum_scatter(grad_wup, ("dp", "ctx"), scatter_dimension=0, tiled=True),
-        lax.psum_scatter(grad_down, ("dp", "ctx"), scatter_dimension=0, tiled=True),
-    )
-    head_grad = lax.psum(jnp.stack([grad_decay_log, grad_step_bias, grad_skip]), ("dp", "ctx"))
+    def scatter(grad):
+        return lax.psum_scatter(
+            grad.astype(jnp.bfloat16), axes, scatter_dimension=0, tiled=True
+        ).astype(jnp.float32)
+
+    devices = w_q_all.shape[0] // own_rows
+    small_grads = jnp.concatenate(
+        [
+            grad_gain_first.reshape(devices, -1),
+            grad_gain_second.reshape(devices, -1),
+            grad_gain_mix.reshape(devices, -1),
+            grad_conv_shift.reshape(devices, -1),
+            jnp.swapaxes(grad_conv_taps.reshape(KC, devices, -1), 0, 1).reshape(devices, -1),
+        ],
+        axis=1,
+    )
+    small_grads = jnp.pad(small_grads, ((0, 0), (0, slots - small_grads.shape[1])))
+    out_down = scatter(grad_down)
+    out_gate = scatter(grad_wgate)
+    out_up = scatter(grad_wup)
+    out_wout = scatter(grad_wout)
+    out_wo = scatter(grad_wo.T).T
+    out_win = scatter(grad_win)
+    out_first = scatter(
+        jnp.concatenate([grad_wq, grad_wk, grad_wv, small_grads.reshape(-1, 128)], axis=1)
+    )
+    out_small = out_first[:, q_width + 2 * k_width :].reshape(-1)
+    pieces, at = [], 0
+    for size in small_sizes:
+        pieces.append(out_small[at : at + size])
+        at += size
+    out_taps = out_small[at : at + KC * small_sizes[3]].reshape(KC, small_sizes[3])
+    head_grad = lax.psum(jnp.stack([grad_decay_log, grad_step_bias, grad_skip]), axes)
     return (
         layer_result,
         grad_tokens,
-        summed[0],
-        summed[1],
-        summed[2],
-        summed[3],
+        pieces[0],
+        out_win,
+        out_taps,
+        pieces[3],
         head_grad,
-        summed[4],
-        summed[5],
-        summed[6],
-        summed[7],
-        summed[8],
-        summed[9],
-        summed[10],
-        summed[11],
-        summed[12],
-        summed[13],
+        pieces[2],
+        out_wout,
+        out_first[:, :q_width],
+        out_first[:, q_width : q_width + k_width],
+        out_first[:, q_width + k_width : q_width + 2 * k_width],
+        out_wo,
+        pieces[1],
+        out_gate,
+        out_up,
+        out_down,
     )
 
 

time: 2490 us -> 1940 us (0.78)
  waiting for transfers between devices: 1150 us -> 786 us
  blocking collectives: 295 us -> 49.9 us
  local copies, waits for them, and re-layouts: 137 us -> 176 us
    reduce_scatter x11 -> x8, waiting for transfers between devices: 1030 us -> 564 us  [the longest x7 564 us: scatter(): lax.psum_scatter(grad.astype(jnp.bfloat16), axes, scatter_dimension=0, ti...]
    all_gather x3 -> x0, blocking collectives: 204 us -> none  [the longest x1 69.7 us: body(): lax.all_gather(w_k, ('dp', 'ctx'), axis=0, tiled=True)]
    all_gather x9 -> x8, waiting for transfers between devices: 119 us -> 216 us  [the longest x1 52.2 us: body(): w_up_all = lax.all_gather(w_up, axes, axis=0, tiled=True)]
    unnamed x2 -> x0, blocking collectives: 83.6 us -> none
    psum x0 -> x1, blocking collectives: none -> 40.3 us  [body(): lax.psum(jnp.stack([grad_decay_log, grad_step_bias, grad_skip]), axes)]
    dot_general x9 -> x11, matrix products: 98.6 us -> 104 us  [the longest x1 22.8 us: body(): jnp.einsum('rd,fd->rf', cot_rows, w_down_all, preferred_element_type=jnp....]
  transfers between devices with their start and end apart: 24 -> 20, of which waited for: 10 -> 11; matrix products, arithmetic and copies ran while one was open for 34% -> 44% of each run, Pallas kernels for 0% -> 0%
where the time goes in v1:
time: 1940 us; the launch traced here: 1920 us
  waiting for transfers between devices  786 us (41%)
  matrix products  630 us (32%)
  other arithmetic  259 us (13%)
  local copies, waits for them, and re-layouts  176 us (9%)
  blocking collectives  49.9 us (3%)
    reduce_scatter x7, waiting for transfers between devices, scatter(): lax.psum_scatter(grad.astype(jnp.bfloat16), axes, scatter_dimension=0, ti...  564 us
    dot_general x1, matrix products, body(): jnp.einsum('sigrd,sjgd->sgrij', grad_att, value_piece, preferred_element_...  59.9 us
    dot_general x1, matrix products, body(): jnp.einsum('sihp,sjhp->shij', grad_y_low, xs_rows, preferred_element_type...  59.3 us
    all_gather x1, waiting for transfers between devices, body(): w_up_all = lax.all_gather(w_up, axes, axis=0, tiled=True)  52.2 us
    all_gather x1, waiting for transfers between devices, body(): w_down_all = lax.all_gather(w_down, axes, axis=0, tiled=True)  51.5 us
    all_gather x1, waiting for transfers between devices, body(): lax.all_gather(jnp.concatenate([w_q, w_k, w_v, small_block], axis=1), axe...  45.2 us
    psum x1, blocking collectives, body(): lax.psum(jnp.stack([grad_decay_log, grad_step_bias, grad_skip]), axes)  40.3 us
    all_gather x1, waiting for transfers between devices, body(): w_in_all = lax.all_gather(w_in, axes, axis=0, tiled=True)  39.6 us
  transfers between devices with their start and end apart: 20, of which 11 were waited for; matrix products, arithmetic and copies ran while one was open for 44% of the time, Pallas kernels for 0%

profile of v1, /device:TPU:0, one launch (start us, length us, event | category | flops | bytes accessed | tf_op | source)
XLA Modules:
  0.0 1924.5 jit_solution(4112604505347065251)
XLA Ops:
  25.8 45.2 %all-gather.13.cloned.1.call-done = bf16[1024,896]{1,0:T(8,128)(2,1)} async-done(((bf16[32,896]{1,0:T(8,128)(2,1)}), bf16[1024,896]{1,0:T(8,128)(2,1)}) %all-gather.13.cloned.1.call-update) | async-done | bytes 1835024 | tf_op jit(solution)/shard_map/all_gather | solution.py:163
  106.0 39.6 %all-gather.15.cloned.1.call-done = bf16[1024,3352]{1,0:T(8,128)(2,1)} async-done(((bf16[32,3352]{1,0:T(8,128)(2,1)}), bf16[1024,3352]{1,0:T(8,128)(2,1)}) %all-gather.15.cloned.1.call-update) | async-done | bytes 6864912 | tf_op jit(solution)/shard_map/all_gather | solution.py:166
  145.5 16.2 convolution_convert_fusion
  167.9 8.1 copy.203
  187.9 12.9 multiply_convert_fusion.8
  205.7 6.7 copy.204
  213.7 7.0 fusion.76
  247.5 37.5 %fusion.10 = (f32[3,2,4,512]{3,2,1,0:T(4,128)S(1)}, f32[3,2,2048,512,4]{3,2,4,1,0:T(8,128)}) fusion(pred[3,512,2048]{1,2,0:T(8,128)(4,1)} %compare_and_fusion, bf16[3,2048,2,64,1]{1,3,4,2,0:T(8,128)(2,1)} %bitcast.382, bf16[3,512,2,4,32]{1,4,3,2,0:T(8,128)(2,1)} %bitcast.394, bf16[3,512,2,4,32]{1,4,3,2,0:T(8,128)(2,1)S(1)} %bitcast.392), kind=kOutput, calls=%fused_computation.23 | convolution fusion | flops 3299856384 | bytes 107003904 | tf_op jit(solution)/shard_map/sigrd,sjgd->sgrij/dot_general | solution.py:291
  285.1 32.3 %fusion.5 = f32[3,2,4,512]{3,2,1,0:T(4,128)S(1)} fusion(f32[3,2,2048,512,4]{3,2,4,1,0:T(8,128)} %get-tuple-element.466, f32[3,2,4,512]{3,2,1,0:T(4,128)S(1)} %broadcast_maximum_fusion, pred[3,512,2048]{1,2,0:T(8,128)(4,1)} %compare_and_fusion), kind=kLoop, calls=%fused_computation.13 | loop fusion | flops 125816832 | bytes 103907328 | tf_op jit(solution)/shard_map/reduce_sum | solution.py:298
  318.1 37.3 %fusion.185 = (bf16[3,512,2,4,64]{1,4,3,2,0:T(8,128)(2,1)S(1)}, f32[3,512,2,4,64]{1,4,3,2,0:T(8,128)}) fusion(f32[3,512,2,4]{1,3,2,0:T(4,128)S(1)} %bitcast.418, bf16[3,2048,2,64,1]{1,3,4,2,0:T(8,128)(2,1)} %bitcast.402, f32[3,2,2048,512,4]{3,2,4,1,0:T(8,128)} %get-tuple-element.466, f32[3,2,4,512]{3,2,1,0:T(4,128)S(1)} %broadcast_maximum_fusion, ...), kind=kOutput, calls=%fused_computation.347 | convolution fusion | flops 3349413888 | bytes 110247936 | tf_op jit(solution)/shard_map/sgrij,sjgd->sigrd/dot_general | solution.py:299
  358.6 9.6 all_gather.44
  371.6 7.9 while.30
  383.3 30.1 %fusion.42 = f32[3,512,24,64]{1,3,2,0:T(8,128)S(1)} fusion(bf16[3,512,24,64]{1,3,2,0:T(8,128)(2,1)} %bitcast.389, f32[3,512,24,64]{1,3,2,0:T(8,128)S(1)} %fusion.97, f32[24]{0:T(128)S(1)} %copy-done.108, f32[3,512,24]{1,2,0:T(8,128)S(1)} %copy-done.59, f32[3,24,512]{2,1,0:T(8,128)S(1)} %copy-done.57, f32[3,24,512]{2,1,0:T(8,128)S(1)} %copy-done.50, ...), kind=kOutput, calls=%fused_computation.89 | convolution fusion | flops 2540961792 | bytes 27967584 | tf_op jit(solution)/shard_map/shij,sjhp->sihp/dot_general | solution.py:240
  413.5 9.7 copy.209
  423.1 9.4 copy.273
  432.5 9.1 multiply_reduce_fusion.9
  442.3 11.6 fusion.170
  453.9 6.0 multiply_reduce_fusion.12
  463.1 27.5 %all-gather.23.cloned.1.call-done = bf16[1024,2048]{1,0:T(8,128)(2,1)} async-done(((bf16[32,2048]{1,0:T(8,128)(2,1)}), bf16[1024,2048]{1,0:T(8,128)(2,1)}) %all-gather.23.cloned.1.call-update) | async-done | bytes 4194320 | tf_op jit(solution)/shard_map/all_gather | solution.py:169
  490.7 11.4 fusion.186
  502.1 52.2 %all-gather.25.cloned.1.call-done = bf16[1024,2048]{1,0:T(8,128)(2,1)} async-done(((bf16[32,2048]{1,0:T(8,128)(2,1)}), bf16[1024,2048]{1,0:T(8,128)(2,1)}) %all-gather.25.cloned.1.call-update) | async-done | bytes 4194320 | tf_op jit(solution)/shard_map/all_gather | solution.py:170
  554.3 12.2 fusion.187
  566.5 51.5 %all-gather.27.cloned.1.call-done = bf16[2048,1024]{1,0:T(8,128)(2,1)} async-done(((bf16[64,1024]{1,0:T(8,128)(2,1)}), bf16[2048,1024]{1,0:T(8,128)(2,1)}) %all-gather.27.cloned.1.call-update) | async-done | bytes 4194320 | tf_op jit(solution)/shard_map/all_gather | solution.py:171
  618.0 22.8 %multiply_convert_fusion.6 = (bf16[1536,2048]{1,0:T(8,128)(2,1)}, bf16[1536,2048]{1,0:T(8,128)(2,1)}, bf16[1536,2048]{1,0:T(8,128)(2,1)}) fusion(f32[1536,2048]{1,0:T(8,128)} %fusion.186, f32[1536,2048]{1,0:T(8,128)} %fusion.187, bf16[1536,1024]{1,0:T(8,128)(2,1)S(1)} %bitcast.371, bf16[2048,1024]{1,0:T(8,128)(2,1)} %all-gather.27.cloned.1.call-done), kind=kOutput, calls=%fused_computation.53 | convolution fusion | flops 6492782592 | bytes 51380224 | tf_op jit(solution)/shard_map/rd,fd->rf/dot_general | solution.py:324
  640.8 12.0 fusion.188
  652.8 15.3 multiply_reduce_fusion.10
  678.2 5.6 reshape.603
  688.0 38.2 %bitcast_convert_fusion.3 = bf16[3,2,64,2048]{3,2,1,0:T(8,128)(2,1)} fusion(f32[3,2,2048,512,4]{3,2,4,1,0:T(8,128)} %get-tuple-element.466, f32[3,2,4,512]{3,2,1,0:T(4,128)S(1)} %copy-done.88, pred[3,512,2048]{1,2,0:T(8,128)(4,1)S(1)} %copy-done.19, bf16[3,512,2,4,64]{1,0,4,3,2:T(4,128)(2,1)} %reshape.603), kind=kOutput, calls=%fused_computation.137 | convolution fusion | flops 3347841024 | bytes 107003904 | tf_op jit(solution)/shard_map/sgrij,sigrd->sjgd/dot_general | solution.py:429
  730.6 59.9 %fusion.4 = bf16[3,2,4,512,2048]{3,4,2,1,0:T(8,128)(2,1)} fusion(f32[3,2,2048,512,4]{3,2,4,1,0:T(8,128)} %get-tuple-element.466, f32[3,2,4,512]{3,2,1,0:T(4,128)S(1)} %multiply_reduce_fusion.13, f32[3,2,4,512]{3,2,1,0:T(4,128)S(1)} %copy-done.88, pred[3,512,2048]{1,2,0:T(8,128)(4,1)S(1)} %copy-done.19, bf16[3,2048,2,64,1]{1,3,4,2,0:T(8,128)(2,1)} %bitcast.403, ...), kind=kOutput, calls=%fused_computation.9 | convolution fusion | flops 3422552064 | bytes 157384704 | tf_op jit(solution)/shard_map/sigrd,sjgd->sgrij/dot_general | solution.py:419
  790.5 21.6 %bitcast_convert_fusion.4 = bf16[3,2,64,2048]{3,2,1,0:T(8,128)(2,1)S(1)} fusion(bf16[3,2,4,512,2048]{3,4,2,1,0:T(8,128)(2,1)} %fusion.4, bf16[3,512,2,4,32]{1,4,3,2,0:T(8,128)(2,1)} %bitcast.395, bf16[3,512,2,4,32]{1,4,3,2,0:T(8,128)(2,1)} %bitcast.393), kind=kOutput, calls=%fused_computation.138 | convolution fusion | flops 3225157632 | bytes 53477376 | tf_op jit(solution)/shard_map/sgrij,sigrd->sjgd/dot_general | solution.py:426
  814.1 7.4 bitcast_convert_fusion.2
  821.5 9.9 copy.243
  831.4 12.6 multiply_reduce_fusion.7
  844.1 18.3 multiply_reduce_fusion.6
  862.4 11.9 convert_element_type.358
  879.9 19.8 %fusion.189 = f32[3,2,64,4,512]{4,2,3,1,0:T(8,128)S(1)} fusion(bf16[3,2048,2,64,1]{1,3,4,2,0:T(8,128)(2,1)} %bitcast.383, bf16[3,2,4,512,2048]{3,4,2,1,0:T(8,128)(2,1)} %fusion.4), kind=kOutput, calls=%fused_computation.351 | convolution fusion | flops 3221225472 | bytes 55050240 | tf_op jit(solution)/shard_map/sgrij,sjgd->sigrd/dot_general | solution.py:423
  906.2 5.9 fusion.77
  917.4 9.0 fusion.41
  926.4 9.0 convolution_convert_fusion.5
  939.8 11.4 convolution_convert_fusion.4
  951.3 11.2 convolution_convert_fusion.3
  962.6 59.3 %fusion.18 = (f32[3,24,512]{2,1,0:T(8,128)}, f32[3,24,512]{2,1,0:T(8,128)}, f32[3,24,512]{2,1,0:T(8,128)}, bf16[3,512,512]{2,1,0:T(8,128)(2,1)}) fusion(f32[3,24,512]{2,1,0:T(8,128)S(1)} %copy-done.58, f32[3,24,512]{2,1,0:T(8,128)S(1)} %copy-done.51, f32[3,512,512]{2,1,0:T(8,128)} %fusion.106, pred[3,512,512]{2,1,0:T(8,128)(4,1)} %compare_and_fusion.1, ...), kind=kOutput, calls=%fused_computation.29 | convolution fusion | flops 2698137600 | bytes 15679488 | tf_op jit(solution)/shard_map/sihp,sjhp->shij/dot_general | solution.py:351
  1025.4 6.8 copy.229
  1033.5 11.2 convolution_convert_fusion.2
  1044.7 29.2 %fusion.19 = f32[3,24,64,512]{3,2,1,0:T(8,128)} fusion(f32[3,24,512]{2,1,0:T(8,128)S(1)} %copy-done.58, f32[3,24,512]{2,1,0:T(8,128)S(1)} %copy-done.51, f32[3,512,512]{2,1,0:T(8,128)} %fusion.106, pred[3,512,512]{2,1,0:T(8,128)(4,1)} %compare_and_fusion.1, bf16[3,512,24,64]{1,0,3,2:T(4,128)(2,1)} %convert_element_type.358), kind=kOutput, calls=%fused_computation.30 | convolution fusion | flops 2529165312 | bytes 18382848 | tf_op jit(solution)/shard_map/shij,sihp->sjhp/dot_general | solution.py:355
  1074.2 5.9 fusion.89
  1096.1 12.9 while.31
  1109.1 6.9 fusion.21
  1116.0 7.8 fusion.39
  1123.8 9.8 copy.225
  1138.4 29.1 %multiply_reduce_fusion.5 = (f32[1792]{0:T(1024)}, f32[1792]{0:T(1024)}, f32[1792]{0:T(1024)}, f32[1792]{0:T(1024)}, bf16[1792]{0:T(1024)(128)(2,1)}, /*index=5*/f32[3,512,1792]{2,1,0:T(8,128)}) fusion(f32[3,515,1792]{2,1,0:T(8,128)} %copy-done, f32[3,512]{1,0:T(4,128)} %get-tuple-element.449, f32[3,512]{1,0:T(4,128)} %get-tuple-element.450, ...), kind=kLoop, calls=%fused_computation.67 | loop fusion | flops 66051328 | bytes 77127168 | tf_op jit(solution)/shard_map/transpose(jvp())/reduce_sum | solution.py:87
  1169.4 18.8 multiply_multiply_fusion.3
  1188.4 15.3 pad_add_fusion
  1214.8 7.8 fusion.31
  1222.6 20.9 %fusion.53 = (bf16[1024]{0:T(1024)(128)(2,1)S(1)}, f32[1536]{0:T(1024)S(1)}, f32[1536,1024]{1,0:T(8,128)}) fusion(bf16[3,512,1024]{2,1,0:T(8,128)(2,1)S(1)} %copy-done.9, f32[1536]{0:T(1024)S(1)} %copy-done.73, f32[1024]{0:T(1024)S(1)} %copy-done.86, f32[1536,1024]{1,0:T(8,128)} %fusion.112, f32[1536,1024]{1,0:T(8,128)} %fusion.115, ...), kind=kOutput, calls=%fused_computation.113 | convolution fusion | flops 10591098880 | bytes 45492224 | tf_op jit(solution)/shard_map/rc,dc->rd/dot_general | solution.py:406
  1254.6 18.2 convolution_convert_fusion.1
  1273.8 12.1 add_convert_fusion
  1289.5 40.3 %psum.7 = f32[3,24]{1,0:T(4,128)} all-reduce(f32[3,24]{1,0:T(4,128)S(1)} %pad_maximum_fusion.12), channel_id=1, replica_groups=mesh['dp'=8,'ctx'=4] {'dp','ctx'}, use_global_device_ids=true, to_apply=%region_36.37 | all-reduce | flops 72 | bytes 576 | tf_op jit(solution)/shard_map/psum | solution.py:503
  1329.9 10.5 fusion.49
  1340.4 17.1 reduce-scatter.19.cloned.1.call-done
  1359.0 146.9 %reduce-scatter.21.cloned.1.call-done = bf16[32,2048]{1,0:T(8,128)(2,1)} async-done(((bf16[1024,2048]{1,0:T(8,128)(2,1)}), bf16[32,2048]{1,0:T(8,128)(2,1)}) %reduce-scatter.21.cloned.1.call-update) | async-done | bytes 131088 | tf_op jit(solution)/shard_map/reduce_scatter | solution.py:472
  1507.6 147.3 %reduce-scatter.23.cloned.1.call-done = bf16[64,1024]{1,0:T(8,128)(2,1)} async-done(((bf16[2048,1024]{1,0:T(8,128)(2,1)}), bf16[64,1024]{1,0:T(8,128)(2,1)}) %reduce-scatter.23.cloned.1.call-update) | async-done | bytes 131088 | tf_op jit(solution)/shard_map/reduce_scatter | solution.py:472
  1656.6 137.3 %reduce-scatter.25.cloned.1.call-done = bf16[32,896]{1,0:T(8,128)(2,1)} async-done(((bf16[1024,896]{1,0:T(8,128)(2,1)}), bf16[32,896]{1,0:T(8,128)(2,1)}) %reduce-scatter.25.cloned.1.call-update) | async-done | bytes 57360 | tf_op jit(solution)/shard_map/reduce_scatter | solution.py:472
  1799.9 115.9 %reduce-scatter.13.cloned.1.call-done = bf16[32,3352]{1,0:T(8,128)(2,1)} async-done(((bf16[1024,3352]{1,0:T(8,128)(2,1)}), bf16[32,3352]{1,0:T(8,128)(2,1)}) %reduce-scatter.13.cloned.1.call-update) | async-done | bytes 214544 | tf_op jit(solution)/shard_map/reduce_scatter | solution.py:472
  (485 shorter events, 248.1 us)
Async XLA Ops:
  7.2 85.2 %copy-start.7 = (bf16[3,512,1024]{2,1,0:T(8,128)(2,1)S(1)}, bf16[3,512,1024]{2,1,0:T(8,128)(2,1)}, u32[]{:S(2)}) copy-start(bf16[3,512,1024]{2,1,0:T(8,128)(2,1)} %param.23) | copy-start | bytes 9437188
  7.2 63.8 %all-gather.13.cloned.1.call-start = ((), (), s32[]{:S(2)}) async-start(), calls=%async_computation.8 | async-start | bytes 1892352 | tf_op jit(solution)/shard_map/all_gather | solution.py:163
  12.4 133.1 %all-gather.15.cloned.1.call-start = ((), (), s32[]{:S(2)}) async-start(), calls=%async_computation.9 | async-start | bytes 7299072 | tf_op jit(solution)/shard_map/all_gather | solution.py:166
  13.1 230.5 %all-gather.19.cloned.1.call-start = ((), (), s32[]{:S(2)}) async-start(), calls=%async_computation.11 | async-start | bytes 3932160 | tf_op jit(solution)/shard_map/all_gather | solution.py:280
  24.3 163.5 %copy-start.65 = (f32[3,512]{1,0:T(4,128)}, f32[3,512]{1,0:T(4,128)S(1)}, u32[]{:S(2)}) copy-start(f32[3,512]{1,0:T(4,128)S(1)} %get-tuple-element.448) | copy-start | bytes 18436
  25.8 215.5 %copy-start.21 = (f32[3,512,32]{1,2,0:T(8,128)}, f32[3,512,32]{1,2,0:T(8,128)S(1)}, u32[]{:S(2)}) copy-start(f32[3,512,32]{1,2,0:T(8,128)S(1)} %get-tuple-element.457) | copy-start | bytes 589828
  25.8 215.5 %copy-start.24 = (f32[3,512,32]{1,2,0:T(8,128)}, f32[3,512,32]{1,2,0:T(8,128)S(1)}, u32[]{:S(2)}) copy-start(f32[3,512,32]{1,2,0:T(8,128)S(1)} %get-tuple-element.458) | copy-start | bytes 589828
  101.9 43.7 %copy-start.33 = (bf16[1536,1024]{1,0:T(8,128)(2,1)S(1)}, bf16[1536,1024]{1,0:T(8,128)(2,1)}, u32[]{:S(2)}) copy-start(bf16[1536,1024]{1,0:T(8,128)(2,1)} %copy-done.32) | copy-start | bytes 9437188
  105.9 265.7 %all-gather.29.cloned.1.call-start = ((), (), s32[]{:S(2)}) async-start(), calls=%async_computation.23 | async-start | bytes 5898240 | tf_op jit(solution)/shard_map/all_gather | solution.py:29
  167.9 16.0 copy-start.45
  177.0 7.1 collective-permute-start
  183.9 29.8 %copy-start.54 = (f32[3,512,24]{1,2,0:T(8,128)}, f32[3,512,24]{1,2,0:T(8,128)S(1)}, u32[]{:S(2)}) copy-start(f32[3,512,24]{1,2,0:T(8,128)S(1)} %get-tuple-element.442) | copy-start | bytes 442372
  220.8 221.5 %all-gather.17.cloned.1.call-start = ((), (), s32[]{:S(2)}) async-start(), calls=%async_computation.10 | async-start | bytes 3244032 | tf_op jit(solution)/shard_map/all_gather | solution.py:167
  221.4 232.5 %all-gather.21.cloned.1.call-start = ((), (), s32[]{:S(2)}) async-start(), calls=%async_computation.12 | async-start | bytes 1081344 | tf_op jit(solution)/shard_map/all_gather | solution.py:168
  222.0 268.7 %all-gather.23.cloned.1.call-start = ((), (), s32[]{:S(2)}) async-start(), calls=%async_computation.13 | async-start | bytes 4325376 | tf_op jit(solution)/shard_map/all_gather | solution.py:169
  222.7 331.6 %all-gather.25.cloned.1.call-start = ((), (), s32[]{:S(2)}) async-start(), calls=%async_computation.14 | async-start | bytes 4325376 | tf_op jit(solution)/shard_map/all_gather | solution.py:170
  223.5 394.6 %all-gather.27.cloned.1.call-start = ((), (), s32[]{:S(2)}) async-start(), calls=%async_computation.15 | async-start | bytes 4325376 | tf_op jit(solution)/shard_map/all_gather | solution.py:171
  224.2 855.9 %reduce-scatter.11.cloned.1.call-start = ((), (), s32[]{:S(2)}) async-start(), calls=%async_computation.16 | async-start | bytes 3932160 | tf_op jit(solution)/shard_map/reduce_scatter | solution.py:435
  242.8 42.3 %copy-start.27 = (bf16[3,512,8,32]{1,3,2,0:T(8,128)(2,1)}, bf16[3,512,8,32]{1,3,2,0:T(8,128)(2,1)S(1)}, u32[]{:S(2)}) copy-start(bf16[3,512,8,32]{1,3,2,0:T(8,128)(2,1)S(1)} %get-tuple-element.426) | copy-start | bytes 2359300
  383.1 30.4 %copy-start.13 = (f32[3,512,24,64]{1,3,2,0:T(8,128)}, f32[3,512,24,64]{1,3,2,0:T(8,128)S(1)}, u32[]{:S(2)}) copy-start(f32[3,512,24,64]{1,3,2,0:T(8,128)S(1)} %fusion.97) | copy-start | bytes 28311556
  460.0 208.2 %copy-start.63 = (f32[1536]{0:T(1024)}, f32[1536]{0:T(1024)S(1)}, u32[]{:S(2)}) copy-start(f32[1536]{0:T(1024)S(1)} %fusion.148) | copy-start | bytes 18436
  463.1 27.5 %copy-start.29 = (bf16[1536,1024]{1,0:T(8,128)(2,1)}, bf16[1536,1024]{1,0:T(8,128)(2,1)S(1)}, u32[]{:S(2)}) copy-start(bf16[1536,1024]{1,0:T(8,128)(2,1)S(1)} %multiply_convert_fusion.11) | copy-start | bytes 9437188
  502.1 115.9 %copy-start.17 = (bf16[3,512,1024]{2,1,0:T(8,128)(2,1)S(1)}, bf16[3,512,1024]{2,1,0:T(8,128)(2,1)}, u32[]{:S(2)}) copy-start(bf16[3,512,1024]{2,1,0:T(8,128)(2,1)} %param.41) | copy-start | bytes 9437188
  640.8 27.3 %slice-start = ((s8[6291456]{0:T(1024)(128)(4,1)}), s8[4194304]{0:T(1024)(128)(4,1)S(1)}, s32[]{:S(2)}) async-start(s8[6291456]{0:T(1024)(128)(4,1)} %bitcast.358), calls=%async_computation.26 | async-start | bytes 8388608
  652.8 15.4 slice-start.1
  790.5 21.6 %copy-start.44 = (bf16[3,2,64,2048]{3,2,1,0:T(8,128)(2,1)S(1)}, bf16[3,2,64,2048]{3,2,1,0:T(8,128)(2,1)}, u32[]{:S(2)}) copy-start(bf16[3,2,64,2048]{3,2,1,0:T(8,128)(2,1)} %bitcast_convert_fusion.3) | copy-start | bytes 4718596
  814.0 282.1 %all-gather.31.cloned.1.call-start = ((), (), s32[]{:S(2)}) async-start(), calls=%async_computation.24 | async-start | bytes 5898240 | tf_op jit(solution)/shard_map/all_gather | solution.py:29
  879.8 406.0 %reduce-scatter.17.cloned.1.call-start = ((), (), s32[]{:S(2)}) async-start(), calls=%async_computation.19 | async-start | bytes 1081344 | tf_op jit(solution)/shard_map/reduce_scatter | solution.py:472
  879.9 19.9 %copy-start.22 = (f32[3,512,32]{1,2,0:T(8,128)S(1)}, f32[3,512,32]{1,2,0:T(8,128)}, u32[]{:S(2)}) copy-start(f32[3,512,32]{1,2,0:T(8,128)} %copy-done.21) | copy-start | bytes 589828
  879.9 19.9 %copy-start.25 = (f32[3,512,32]{1,2,0:T(8,128)S(1)}, f32[3,512,32]{1,2,0:T(8,128)}, u32[]{:S(2)}) copy-start(f32[3,512,32]{1,2,0:T(8,128)} %copy-done.24) | copy-start | bytes 589828
  912.1 375.1 %reduce-scatter.15.cloned.1.call-start = ((), (), s32[]{:S(2)}) async-start(), calls=%async_computation.18 | async-start | bytes 3244032 | tf_op jit(solution)/shard_map/reduce_scatter | solution.py:472
  935.4 422.0 %reduce-scatter.19.cloned.1.call-start = ((), (), s32[]{:S(2)}) async-start(), calls=%async_computation.20 | async-start | bytes 4325376 | tf_op jit(solution)/shard_map/reduce_scatter | solution.py:472
  962.5 543.5 %reduce-scatter.21.cloned.1.call-start = ((), (), s32[]{:S(2)}) async-start(), calls=%async_computation.21 | async-start | bytes 4325376 | tf_op jit(solution)/shard_map/reduce_scatter | solution.py:472
  1021.9 633.1 %reduce-scatter.23.cloned.1.call-start = ((), (), s32[]{:S(2)}) async-start(), calls=%async_computation.22 | async-start | bytes 4325376 | tf_op jit(solution)/shard_map/reduce_scatter | solution.py:472
  1044.7 29.5 %copy-start.41 = (bf16[1024,896]{1,0:T(8,128)(2,1)S(1)}, bf16[1024,896]{1,0:T(8,128)(2,1)}, u32[]{:S(2)}) copy-start(bf16[1024,896]{1,0:T(8,128)(2,1)} %all-gather.13.cloned.1.call-done) | copy-start | bytes 5505028
  1074.0 719.9 %reduce-scatter.25.cloned.1.call-start = ((), (), s32[]{:S(2)}) async-start(), calls=%async_computation.25 | async-start | bytes 1892352 | tf_op jit(solution)/shard_map/reduce_scatter | solution.py:472
  1138.4 29.1 %copy-start.3 = (f32[3,24,64,128]{3,2,1,0:T(8,128)S(1)}, f32[3,24,64,128]{3,2,1,0:T(8,128)}, u32[]{:S(2)}) copy-start(f32[3,24,64,128]{3,2,1,0:T(8,128)} %copy-done.1) | copy-start | bytes 7077892
  1138.4 29.6 %copy-start.46 = (f32[1536,24]{0,1:T(8,128)S(1)}, f32[1536,24]{0,1:T(8,128)}, u32[]{:S(2)}) copy-start(f32[1536,24]{0,1:T(8,128)} %copy-done.45) | copy-start | bytes 442372
  1188.2 21.6 %copy-start.95 = (f32[1792]{0:T(1024)S(1)}, f32[1792]{0:T(1024)}, u32[]{:S(2)}) copy-start(f32[1792]{0:T(1024)} %get-tuple-element.366) | copy-start | bytes 21508
  1188.2 21.6 %copy-start.94 = (f32[1792]{0:T(1024)S(1)}, f32[1792]{0:T(1024)}, u32[]{:S(2)}) copy-start(f32[1792]{0:T(1024)} %get-tuple-element.367) | copy-start | bytes 21508
  1188.3 21.6 %copy-start.93 = (f32[1792]{0:T(1024)S(1)}, f32[1792]{0:T(1024)}, u32[]{:S(2)}) copy-start(f32[1792]{0:T(1024)} %get-tuple-element.368) | copy-start | bytes 21508
  1188.3 21.6 %copy-start.92 = (f32[1792]{0:T(1024)S(1)}, f32[1792]{0:T(1024)}, u32[]{:S(2)}) copy-start(f32[1792]{0:T(1024)} %get-tuple-element.369) | copy-start | bytes 21508
  1188.3 21.6 %copy-start.52 = (f32[3,24,512]{2,1,0:T(8,128)S(1)}, f32[3,24,512]{2,1,0:T(8,128)}, u32[]{:S(2)}) copy-start(f32[3,24,512]{2,1,0:T(8,128)} %copy-done.49) | copy-start | bytes 442372
  1188.3 21.6 %copy-start.112 = (f32[3]{0:T(128)S(1)}, f32[3]{0:T(128)}, u32[]{:S(2)}) copy-start(f32[3]{0:T(128)} %convert_reduce_fusion) | copy-start | bytes 40
  1188.3 21.7 %copy-start.56 = (f32[3,512,24]{1,2,0:T(8,128)S(1)}, f32[3,512,24]{1,2,0:T(8,128)}, u32[]{:S(2)}) copy-start(f32[3,512,24]{1,2,0:T(8,128)} %fusion.41) | copy-start | bytes 442372
  1188.3 21.7 %copy-start.62 = (f32[3,512,24]{1,2,0:T(8,128)S(1)}, f32[3,512,24]{1,2,0:T(8,128)}, u32[]{:S(2)}) copy-start(f32[3,512,24]{1,2,0:T(8,128)} %get-tuple-element.373) | copy-start | bytes 442372
  1188.3 21.7 %copy-start.70 = (f32[3,512]{1,0:T(4,128)S(1)}, f32[3,512]{1,0:T(4,128)}, u32[]{:S(2)}) copy-start(f32[3,512]{1,0:T(4,128)} %get-tuple-element.461) | copy-start | bytes 18436
  1188.3 21.7 %copy-start.90 = (f32[3,512]{1,0:T(4,128)S(1)}, f32[3,512]{1,0:T(4,128)}, u32[]{:S(2)}) copy-start(f32[3,512]{1,0:T(4,128)} %get-tuple-element.412) | copy-start | bytes 18436
  1188.3 21.7 %copy-start.106 = (f32[3,24]{1,0:T(4,128)S(1)}, f32[3,24]{1,0:T(4,128)}, u32[]{:S(2)}) copy-start(f32[3,24]{1,0:T(4,128)} %copy-done.105) | copy-start | bytes 868
  1188.4 21.7 %copy-start.114 = (f32[24]{0:T(128)S(1)}, f32[24]{0:T(128)}, u32[]{:S(2)}) copy-start(f32[24]{0:T(128)} %get-tuple-element.463) | copy-start | bytes 292
  1188.4 21.7 %copy-start.119 = (f32[24]{0:T(128)S(1)}, f32[24]{0:T(128)}, u32[]{:S(2)}) copy-start(f32[24]{0:T(128)} %get-tuple-element.464) | copy-start | bytes 292
  1188.4 21.7 %copy-start.121 = (f32[3,24,512]{2,1,0:T(8,128)S(1)}, f32[3,24,512]{2,1,0:T(8,128)}, u32[]{:S(2)}) copy-start(f32[3,24,512]{2,1,0:T(8,128)} %get-tuple-element.362) | copy-start | bytes 442372
  1188.4 21.7 %copy-start.122 = (f32[3,24,512]{2,1,0:T(8,128)S(1)}, f32[3,24,512]{2,1,0:T(8,128)}, u32[]{:S(2)}) copy-start(f32[3,24,512]{2,1,0:T(8,128)} %get-tuple-element.363) | copy-start | bytes 442372
  1188.4 21.7 %copy-start.123 = (f32[3,24,512]{2,1,0:T(8,128)S(1)}, f32[3,24,512]{2,1,0:T(8,128)}, u32[]{:S(2)}) copy-start(f32[3,24,512]{2,1,0:T(8,128)} %get-tuple-element.364) | copy-start | bytes 442372
  1188.4 24.4 %copy-start.107 = (bf16[1792]{0:T(1024)(128)(2,1)S(1)}, bf16[1792]{0:T(1024)(128)(2,1)}, u32[]{:S(2)}) copy-start(bf16[1792]{0:T(1024)(128)(2,1)} %get-tuple-element.376) | copy-start | bytes 10756
  1208.5 6.2 collective-permute-start.1
  1222.6 21.0 %copy-start.96 = (bf16[32,32]{1,0:T(8,128)(2,1)S(1)}, bf16[32,32]{1,0:T(8,128)(2,1)}, u32[]{:S(2)}) copy-start(bf16[32,32]{1,0:T(8,128)(2,1)} %reshape.614) | copy-start | bytes 6148
  1222.6 21.0 %copy-start.97 = (bf16[32,48]{1,0:T(8,128)(2,1)S(1)}, bf16[32,48]{1,0:T(8,128)(2,1)}, u32[]{:S(2)}) copy-start(bf16[32,48]{1,0:T(8,128)(2,1)} %reshape.615) | copy-start | bytes 9220
  1254.6 661.2 %reduce-scatter.13.cloned.1.call-start = ((), (), s32[]{:S(2)}) async-start(), calls=%async_computation.17 | async-start | bytes 7299072 | tf_op jit(solution)/shard_map/reduce_scatter | solution.py:472
  1273.7 15.8 copy-start.117
  1273.7 56.1 %copy-start.77 = (f32[1536]{0:T(1024)S(1)}, f32[1536]{0:T(1024)}, u32[]{:S(2)}) copy-start(f32[1536]{0:T(1024)} %copy-done.76) | copy-start | bytes 18436
  1273.7 56.1 %copy-start.64 = (f32[1536]{0:T(1024)S(1)}, f32[1536]{0:T(1024)}, u32[]{:S(2)}) copy-start(f32[1536]{0:T(1024)} %copy-done.63) | copy-start | bytes 18436
  1273.7 56.1 %copy-start.72 = (f32[1536]{0:T(1024)S(1)}, f32[1536]{0:T(1024)}, u32[]{:S(2)}) copy-start(f32[1536]{0:T(1024)} %copy-done.71) | copy-start | bytes 18436
  1273.7 56.1 %copy-start.84 = (f32[1024]{0:T(1024)S(1)}, f32[1024]{0:T(1024)}, u32[]{:S(2)}) copy-start(f32[1024]{0:T(1024)} %reshape.632) | copy-start | bytes 12292
  (88 other events, 624.5 us)
Sparse Core Ops, SparseCore 0:
  12.5 58.4 all-gather.12
  73.8 71.6 all-gather.14
  147.1 62.0 all-gather.18
  220.9 89.8 all-gather.28
  313.5 57.5 all-gather.16
  374.0 52.5 all-gather.20
  429.6 61.0 all-gather.22
  493.7 60.6 all-gather.24
  557.3 60.6 all-gather.26
  814.2 58.7 reduce-scatter.10
  880.0 87.9 all-gather.30
  970.1 134.0 reduce-scatter.16
  1110.5 98.0 reduce-scatter.14
  1210.8 146.5 reduce-scatter.18
  1359.6 146.2 reduce-scatter.20
  1508.2 146.6 reduce-scatter.22
  1657.1 136.6 reduce-scatter.24
  1799.4 116.3 reduce-scatter.12

commit v2 on v1

v2 whole, which is shorter than its diff:
```python
import jax
import jax.numpy as jnp
from jax import lax
from jax.experimental import pallas as pl
from jax.experimental.pallas import tpu as pltpu
from jax.sharding import PartitionSpec as P

MH = 24
MP = 64
NS = 128
KC = 4
QH = 8
KVH = 2
HD = 64
EPSILON = 1e-05
ROPE_BASE = 10000.0
MASKED = -1e30
LOG2E = 1.4426950408889634
KEY_TILE = 256
VMEM_BYTES = 56 * 1024 * 1024

F32 = jnp.float32
BF16 = jnp.bfloat16


def contract(left, right, left_dim, right_dim):
    return lax.dot_general(
        left, right, (((left_dim,), (right_dim,)), ((), ())), preferred_element_type=F32
    )


def lanes(shape):
    return lax.broadcasted_iota(jnp.int32, shape, len(shape) - 1)


def swap_halves(values):
    lane = lanes(values.shape)
    return jnp.where(lane < 32, pltpu.roll(values, 96, 1), pltpu.roll(values, 32, 1))


def project_kernel(x_ref, gain_ref, w_ref, cos_ref, sin_ref, hidden_ref, q_ref, kv_ref):
    x = x_ref[...].astype(F32)
    scale = lax.rsqrt(jnp.mean(x * x, axis=-1, keepdims=True) + EPSILON)
    hidden = (x * scale * gain_ref[...]).astype(BF16)
    hidden_ref[...] = hidden
    lin = contract(hidden, w_ref[...], 1, 0)
    cosine, sine = cos_ref[...], sin_ref[...]
    lane = lanes(cosine.shape)
    for pair in range(QH // 2):
        both = lin[:, pair * 128 : (pair + 1) * 128]
        other = pltpu.roll(both, 64, 1)
        even = both * cosine + swap_halves(both) * sine
        odd = other * cosine + swap_halves(other) * sine
        q_ref[:, pair * 128 : (pair + 1) * 128] = jnp.where(
            lane < 64, even, pltpu.roll(odd, 64, 1)
        ).astype(BF16)
    for group in range(KVH):
        at = QH * HD + group * 128
        part = lin[:, at : at + 128]
        kv_ref[:, group * 128 : (group + 1) * 128] = (
            part * cosine + swap_halves(part) * sine
        ).astype(BF16)


def project(x, gain, w_first, cosine, sine):
    rows, width = x.shape
    tile = 256
    block = lambda cols: pl.BlockSpec((tile, cols), lambda i: (i, 0))
    fixed = lambda shape: pl.BlockSpec(shape, lambda i: (0, 0))
    kv_width = 2 * KVH * HD
    return pl.pallas_call(
        project_kernel,
        grid=(rows // tile,),
        in_specs=[
            block(width),
            fixed((1, width)),
            fixed((width, QH * HD + kv_width)),
            block(128),
            block(128),
        ],
        out_specs=[block(width), block(QH * HD), block(kv_width)],
        out_shape=[
            jax.ShapeDtypeStruct((rows, width), BF16),
            jax.ShapeDtypeStruct((rows, QH * HD), BF16),
            jax.ShapeDtypeStruct((rows, kv_width), BF16),
        ],
        compiler_params=pltpu.CompilerParams(vmem_limit_bytes=VMEM_BYTES),
        name="project",
    )(x, gain, w_first, cosine, sine)


def visible(segk_ref, segq, query_row, at):
    segk = segk_ref[0, pl.ds(at, KEY_TILE), :]
    key_col = at + lax.broadcasted_iota(jnp.int32, (KEY_TILE, 1), 0)
    return jnp.where((segk == segq) & (key_col <= query_row), 0.0, MASKED)


def attend_kernel(
    low_ref, high_ref, base_ref, q_ref, kv_ref, segk_ref, segq_ref, out_ref, lse_ref,
    q_s, m_s, l_s, acc_s,
):
    seq, tile = pl.program_id(0), pl.program_id(1)
    rows = q_ref.shape[1]
    place = seq * pl.num_programs(1) + tile
    lane = lanes((rows, 128))
    for pair in range(QH // 2):
        both = q_ref[0, :, pair * 128 : (pair + 1) * 128].astype(F32)
        q_s[2 * pair] = jnp.where(lane < 64, both, 0.0).astype(BF16)
        q_s[2 * pair + 1] = jnp.where(lane < 64, pltpu.roll(both, 64, 1), 0.0).astype(BF16)
    m_s[...] = jnp.full(m_s.shape, MASKED, F32)
    l_s[...] = jnp.zeros(l_s.shape, F32)
    acc_s[...] = jnp.zeros(acc_s.shape, F32)
    query_row = base_ref[0] + tile * rows + lanes((1, rows))
    segq = segq_ref[0]
    factor = HD ** (-0.5) * LOG2E

    def step(key_tile, carry):
        at = pl.multiple_of(key_tile * KEY_TILE, KEY_TILE)
        bias = visible(segk_ref, segq, query_row, at)
        for group in range(KVH):
            kv = kv_ref[0, pl.ds(at, KEY_TILE), group * 128 : (group + 1) * 128]
            kv_t = kv.astype(F32).T.astype(BF16)
            for member in range(QH // KVH):
                head = group * (QH // KVH) + member
                scores = contract(kv, q_s[head], 1, 1) * factor + bias
                before = m_s[head : head + 1, :]
                top = jnp.maximum(before, jnp.max(scores, axis=0, keepdims=True))
                weights = jnp.exp2(scores - top)
                fade = jnp.exp2(before - top)
                l_s[head : head + 1, :] = l_s[head : head + 1, :] * fade + jnp.sum(
                    weights, axis=0, keepdims=True
                )
                acc_s[head] = acc_s[head] * fade + contract(kv_t, weights.astype(BF16), 1, 0)
                m_s[head : head + 1, :] = top
        return carry

    lax.fori_loop(low_ref[place], high_ref[place], step, 0)
    lse_ref[0] = m_s[...] + jnp.log2(l_s[...])
    for pair in range(QH // 2):
        even = (acc_s[2 * pair] / l_s[2 * pair : 2 * pair + 1, :]).T
        odd = (acc_s[2 * pair + 1] / l_s[2 * pair + 1 : 2 * pair + 2, :]).T
        out_ref[0, :, pair * 128 : (pair + 1) * 128] = jnp.where(
            lane < 64, pltpu.roll(even, 64, 1), odd
        ).astype(BF16)


def attend_back_kernel(
    low_ref, high_ref, base_ref, q_ref, kv_ref, segk_ref, segq_ref, att_ref, gatt_ref, lse_ref,
    cos_ref, sin_ref, dq_ref, dkv_ref,
    q_s, g_s, delta_s, dq_s, dkv_s,
):
    seq, tile = pl.program_id(0), pl.program_id(1)
    rows = q_ref.shape[1]
    place = seq * pl.num_programs(1) + tile
    lane = lanes((rows, 128))

    @pl.when(tile == 0)
    def _():
        dkv_s[...] = jnp.zeros(dkv_s.shape, F32)

    for pair in range(QH // 2):
        cols = slice(pair * 128, (pair + 1) * 128)
        both = q_ref[0, :, cols].astype(F32)
        q_s[2 * pair] = jnp.where(lane < 64, both, 0.0).astype(BF16)
        q_s[2 * pair + 1] = jnp.where(lane < 64, pltpu.roll(both, 64, 1), 0.0).astype(BF16)
        grad = gatt_ref[0, :, cols].astype(F32)
        g_s[2 * pair] = jnp.where(lane >= 64, pltpu.roll(grad, 64, 1), 0.0).astype(BF16)
        g_s[2 * pair + 1] = jnp.where(lane >= 64, grad, 0.0).astype(BF16)
        product = (grad * att_ref[0, :, cols].astype(F32)).T
        delta_s[2 * pair : 2 * pair + 1, :] = jnp.sum(product[:64], axis=0, keepdims=True)
        delta_s[2 * pair + 1 : 2 * pair + 2, :] = jnp.sum(product[64:], axis=0, keepdims=True)
    dq_s[...] = jnp.zeros(dq_s.shape, F32)
    query_row = base_ref[0] + tile * rows + lanes((1, rows))
    segq = segq_ref[0]
    qk_scale = HD ** (-0.5)
    factor = qk_scale * LOG2E

    def step(key_tile, carry):
        at = pl.multiple_of(key_tile * KEY_TILE, KEY_TILE)
        bias = visible(segk_ref, segq, query_row, at)
        for group in range(KVH):
            kv = kv_ref[0, pl.ds(at, KEY_TILE), group * 128 : (group + 1) * 128]
            kv_t = kv.astype(F32).T.astype(BF16)
            total = jnp.zeros((KEY_TILE, 128), F32)
            for member in range(QH // KVH):
                head = group * (QH // KVH) + member
                q, g = q_s[head], g_s[head]
                scores = contract(kv, q, 1, 1) * factor + bias
                probs = jnp.exp2(scores - lse_ref[0, head : head + 1, :])
                d_probs = contract(kv, g, 1, 1)
                d_scores = (probs * (d_probs - delta_s[head : head + 1, :]) * qk_scale).astype(BF16)
                total = total + contract(d_scores, q, 1, 0) + contract(probs.astype(BF16), g, 1, 0)
                dq_s[head] += contract(kv_t, d_scores, 1, 0)
            cols = slice(group * 128, (group + 1) * 128)
            dkv_s[pl.ds(at, KEY_TILE), cols] += total
        return carry

    lax.fori_loop(low_ref[place], high_ref[place], step, 0)
    cosine, sine = cos_ref[0], sin_ref[0]
    for pair in range(QH // 2):
        even, odd = dq_s[2 * pair].T, dq_s[2 * pair + 1].T
        even = even * cosine + swap_halves(even * sine)
        odd = odd * cosine + swap_halves(odd * sine)
        dq_ref[0, :, pair * 128 : (pair + 1) * 128] = jnp.where(
            lane < 64, even, pltpu.roll(odd, 64, 1)
        ).astype(BF16)

    @pl.when(tile == pl.num_programs(1) - 1)
    def _():
        dkv_ref[0] = dkv_s[...].astype(BF16)


def attention_specs(seqs, span, length, rows):
    tile = lambda cols: pl.BlockSpec((1, rows, cols), lambda s, t, *_: (s, t, 0))
    whole = lambda cols: pl.BlockSpec((1, length, cols), lambda s, t, *_: (s, 0, 0))
    row = lambda n: pl.BlockSpec((1, n, rows), lambda s, t, *_: (s, 0, t))
    return tile, whole, row


def attend(bounds, q, kv_all, segk, segq):
    seqs, span, q_width = q.shape
    length, kv_width = kv_all.shape[1:]
    rows = min(256, span)
    tile, whole, row = attention_specs(seqs, span, length, rows)
    return pl.pallas_call(
        attend_kernel,
        grid_spec=pltpu.PrefetchScalarGridSpec(
            num_scalar_prefetch=3,
            grid=(seqs, span // rows),
            in_specs=[tile(q_width), whole(kv_width), whole(1), row(1)],
            out_specs=[tile(q_width), row(QH)],
            scratch_shapes=[
                pltpu.VMEM((QH, rows, 128), BF16),
                pltpu.VMEM((QH, rows), F32),
                pltpu.VMEM((QH, rows), F32),
                pltpu.VMEM((QH, 128, rows), F32),
            ],
        ),
        out_shape=[
            jax.ShapeDtypeStruct(q.shape, BF16),
            jax.ShapeDtypeStruct((seqs, QH, span), F32),
        ],
        compiler_params=pltpu.CompilerParams(vmem_limit_bytes=VMEM_BYTES),
        name="attend",
    )(*bounds, q, kv_all, segk, segq)


def attend_back(bounds, q, kv_all, segk, segq, att, grad_att, lse, cosine, sine):
    seqs, span, q_width = q.shape
    length, kv_width = kv_all.shape[1:]
    rows = min(256, span)
    tile, whole, row = attention_specs(seqs, span, length, rows)
    return pl.pallas_call(
        attend_back_kernel,
        grid_spec=pltpu.PrefetchScalarGridSpec(
            num_scalar_prefetch=3,
            grid=(seqs, span // rows),
            in_specs=[
                tile(q_width), whole(kv_width), whole(1), row(1), tile(q_width), tile(q_width),
                row(QH), tile(128), tile(128),
            ],
            out_specs=[tile(q_width), whole(kv_width)],
            scratch_shapes=[
                pltpu.VMEM((QH, rows, 128), BF16),
                pltpu.VMEM((QH, rows, 128), BF16),
                pltpu.VMEM((QH, rows), F32),
                pltpu.VMEM((QH, 128, rows), F32),
                pltpu.VMEM((length, kv_width), F32),
            ],
        ),
        out_shape=[
            jax.ShapeDtypeStruct(q.shape, BF16),
            jax.ShapeDtypeStruct(kv_all.shape, BF16),
        ],
        compiler_params=pltpu.CompilerParams(vmem_limit_bytes=VMEM_BYTES),
        name="attend_back",
    )(*bounds, q, kv_all, segk, segq, att, grad_att, lse, cosine, sine)


def rope_tables(positions):
    half = HD // 2
    frequency = ROPE_BASE ** (-jnp.arange(half, dtype=F32) / half)
    angles = positions.astype(F32)[..., None] * frequency
    cosine, sine = jnp.cos(angles), jnp.sin(angles)
    one, zero = jnp.ones(cosine.shape[:-1] + (HD,), F32), jnp.zeros(cosine.shape[:-1] + (HD,), F32)
    return (
        jnp.concatenate([cosine, cosine, one], axis=-1),
        jnp.concatenate([-sine, sine, zero], axis=-1),
    )


def attention_bounds(segments, seg_own, span_start):
    seqs, span = seg_own.shape
    rows = min(256, span)
    first = seg_own[:, ::rows]
    begin = jnp.sum((segments[:, None, :] < first[:, :, None]).astype(jnp.int32), axis=2)
    tiles = jnp.arange(span // rows, dtype=jnp.int32)
    high = (span_start + (tiles + 1) * rows + KEY_TILE - 1) // KEY_TILE
    high = jnp.broadcast_to(high[None], first.shape)
    return (
        (begin // KEY_TILE).reshape(-1),
        high.reshape(-1).astype(jnp.int32),
        jnp.full((1,), span_start, jnp.int32),
    )


CHUNK = 128
DI = MH * MP
CC = DI + 2 * NS
TAP_LANES, PREV_LANE, LAST_LANE, SEG_LANE = 0, 4, 5, 6


def split_three(values):
    high = values.astype(BF16)
    rest = values - high.astype(F32)
    middle = rest.astype(BF16)
    return high, middle, (rest - middle.astype(F32)).astype(BF16)


def product_exact(matrix, values):
    return sum(contract(matrix, part, 1, 0) for part in split_three(values))


def widen(values, spread):
    kept = jnp.where(lanes(values.shape) < 32, values, 0.0)
    high, middle, rest = (part.astype(F32) for part in split_three(kept))
    packed = high + pltpu.roll(middle, 32, 1) + pltpu.roll(rest, 64, 1)
    return contract(packed.astype(BF16), spread, 1, 0)


def gather_heads(values, spread_first):
    high = values.astype(BF16)
    rest = (values - high.astype(F32)).astype(BF16)
    return contract(high, spread_first, 1, 1) + contract(rest, spread_first, 1, 1)


def spread_matrix():
    row = lax.broadcasted_iota(jnp.int32, (128, DI), 0)
    col = lax.broadcasted_iota(jnp.int32, (128, DI), 1)
    return ((row % 32 == col // MP) & (row < 96)).astype(BF16)


def spread_first_matrix():
    row = lax.broadcasted_iota(jnp.int32, (32, DI), 0)
    col = lax.broadcasted_iota(jnp.int32, (32, DI), 1)
    return (row == col // MP).astype(BF16)


def lower_mask():
    row = lax.broadcasted_iota(jnp.int32, (CHUNK, CHUNK), 0)
    return row >= lanes((CHUNK, CHUNK))


def decay_rows(rate, head_ref, token):
    raw = rate.astype(F32) + head_ref[1:2, :]
    step = jnp.maximum(raw, 0.0) + jnp.log1p(jnp.exp(-jnp.abs(raw)))
    log_decay = -step * jnp.exp(head_ref[0:1, :])
    running = product_exact(lower_mask().astype(BF16), log_decay)
    last = running[CHUNK - 1 :, :]
    weight_end = jnp.exp(last - running) * step * token[:, LAST_LANE : LAST_LANE + 1]
    entry = jnp.exp(running) * token[:, PREV_LANE : PREV_LANE + 1]
    gain = jnp.exp(last) * token[CHUNK - 1 :, PREV_LANE : PREV_LANE + 1]
    return raw, step, log_decay, running, weight_end, entry, gain


def conv_total(ext_s, token, taps_ref, shift_ref):
    total = shift_ref[...] + ext_s[8 : 8 + CHUNK, :] * taps_ref[KC - 1 : KC, :]
    for tap in range(KC - 1):
        total = total + ext_s[5 + tap : 5 + tap + CHUNK, :] * (
            taps_ref[tap : tap + 1, :] * token[:, TAP_LANES + tap : TAP_LANES + tap + 1]
        )
    return total


def mixer_scan_kernel(
    proj_ref, rim_ref, token_ref, head_ref, taps_ref, shift_ref, spread_ref,
    act_ref, states_ref, gains_ref, final_ref, final_gain_ref,
    ext_s, state_s, gain_s,
):
    chunk = pl.program_id(1)

    @pl.when(chunk == 0)
    def _():
        ext_s[0:8, :] = rim_ref[0].astype(F32)
        state_s[...] = jnp.zeros(state_s.shape, F32)
        gain_s[...] = jnp.ones(gain_s.shape, F32)

    @pl.when(chunk > 0)
    def _():
        ext_s[0:8, :] = ext_s[CHUNK : CHUNK + 8, :]

    token = token_ref[0]
    ext_s[8 : 8 + CHUNK, :] = proj_ref[0, :, DI : DI + CC].astype(F32)
    total = conv_total(ext_s, token, taps_ref, shift_ref)
    act = (total * jax.nn.sigmoid(total)).astype(BF16)
    act_ref[0] = act
    weight_end, _, gain = decay_rows(proj_ref[0, :, DI + CC :], head_ref, token)[-3:]
    states_ref[0, 0] = state_s[...].astype(BF16)
    before = gain_s[...]
    gains_ref[0, 0] = before
    spread = spread_ref[...]
    scaled = (act[:, :DI].astype(F32) * widen(weight_end, spread)).astype(BF16)
    gain_rows = jnp.broadcast_to(gain, (8, 128))
    state = state_s[...] * widen(gain_rows, spread)[0:1, :] + contract(
        act[:, DI : DI + NS], scaled, 0, 0
    )
    state_s[...] = state
    gain_s[...] = before * gain_rows

    @pl.when(chunk == pl.num_programs(1) - 1)
    def _():
        final_ref[0] = state
        final_gain_ref[0] = before * gain_rows


def entering_state(local_ref, gains_ref, state_ref, spread):
    factor = widen(gains_ref[0, 0], spread)[0:1, :]
    return (local_ref[0, 0].astype(F32) + factor * state_ref[0].astype(F32)).astype(BF16)


def pair_decay(running, rest_t, bias, head):
    parts = []
    for at in (head, head + 1):
        column = jnp.broadcast_to(running[:, at : at + 1], (CHUNK, CHUNK))
        parts.append(jnp.exp2(column + (rest_t[at : at + 1, :] + bias)))
    return parts


def stack_pair(values):
    lane = lanes(values.shape)
    wide = values.astype(F32)
    return jnp.concatenate(
        [jnp.where(lane < 64, wide, 0.0), jnp.where(lane >= 64, wide, 0.0)], axis=0
    ).astype(BF16)


def inside_terms(running, step, token):
    seg = jnp.broadcast_to(token[:, SEG_LANE : SEG_LANE + 1], (CHUNK, CHUNK))
    bias = jnp.where((seg == seg.T) & lower_mask(), 0.0, MASKED)
    running_two = running * LOG2E
    rest_t = (jnp.log2(step) - running_two).T
    return running_two, rest_t, bias


def mixer_out_kernel(
    proj_ref, act_ref, token_ref, states_ref, gains_ref, state_ref, head_ref, skip_ref, gain_ref,
    spread_ref, y_ref, out_ref,
):
    token, spread = token_ref[0], spread_ref[...]
    _, step, _, running, _, entry, _ = decay_rows(proj_ref[0, :, DI + CC :], head_ref, token)
    b_rows, c_rows = act_ref[0, :, DI : DI + NS], act_ref[0, :, DI + NS :]
    state = entering_state(states_ref, gains_ref, state_ref, spread)
    carried = contract(c_rows, state, 1, 0) * widen(entry, spread)
    cross = contract(c_rows, b_rows, 1, 1)
    running_two, rest_t, bias = inside_terms(running, step, token)
    square = jnp.zeros((CHUNK, 128), F32)
    for pair in range(MH // 2):
        cols = slice(pair * 128, (pair + 1) * 128)
        xs = act_ref[0, :, cols]
        mix = jnp.concatenate(
            [
                (cross * part).astype(BF16)
                for part in pair_decay(running_two, rest_t, bias, 2 * pair)
            ],
            axis=1,
        )
        y = (
            contract(mix, stack_pair(xs), 1, 0)
            + carried[:, cols]
            + skip_ref[:, cols] * xs.astype(F32)
        )
        y_ref[0, :, cols] = y
        gate = proj_ref[0, :, cols].astype(F32)
        gated = y * (gate * jax.nn.sigmoid(gate))
        square = square + gated * gated
    scale = lax.rsqrt(jnp.sum(square, axis=1, keepdims=True) * (1.0 / DI) + EPSILON)
    for pair in range(MH // 2):
        cols = slice(pair * 128, (pair + 1) * 128)
        gate = proj_ref[0, :, cols].astype(F32)
        gated = y_ref[0, :, cols] * (gate * jax.nn.sigmoid(gate))
        out_ref[0, :, cols] = (gated * scale * gain_ref[:, cols]).astype(BF16)


def mixer_gate_back_kernel(
    gmix_ref, y_ref, proj_ref, act_ref, token_ref, head_ref, gain_ref, spread_ref,
    gy_ref, dgate_ref, gstates_ref, gains_ref, final_ref, dgain_ref, dskip_ref,
    state_s, gain_s, dgain_s, dskip_s,
):
    seq, chunk = pl.program_id(0), pl.program_id(1)

    @pl.when((seq == 0) & (chunk == 0))
    def _():
        dgain_s[...] = jnp.zeros(dgain_s.shape, F32)
        dskip_s[...] = jnp.zeros(dskip_s.shape, F32)

    @pl.when(chunk == 0)
    def _():
        state_s[...] = jnp.zeros(state_s.shape, F32)
        gain_s[...] = jnp.ones(gain_s.shape, F32)

    token, spread = token_ref[0], spread_ref[...]
    entry, gain = decay_rows(proj_ref[0, :, DI + CC :], head_ref, token)[-2:]
    y = y_ref[0]
    gate = proj_ref[0, :, :DI].astype(F32)
    sig = jax.nn.sigmoid(gate)
    swish = gate * sig
    gated = y * swish
    scale = lax.rsqrt(jnp.mean(gated * gated, axis=1, keepdims=True) + EPSILON)
    grad = gmix_ref[0].astype(F32)
    scaled = grad * gain_ref[...]
    shrink = jnp.mean(scaled * gated, axis=1, keepdims=True) * (scale * scale * scale)
    d_gated = scaled * scale - gated * shrink
    gy = (d_gated * swish).astype(BF16)
    gy_ref[0] = gy
    dgate_ref[0] = (d_gated * y * (sig * (1.0 + gate * (1.0 - sig)))).astype(BF16)
    dgain_s[0:1, :] += jnp.sum(grad * gated * scale, axis=0, keepdims=True)
    gy_float = gy.astype(F32)
    dskip_s[0:1, :] += jnp.sum(gy_float * act_ref[0, :, :DI].astype(F32), axis=0, keepdims=True)
    gstates_ref[0, 0] = state_s[...].astype(BF16)
    after = gain_s[...]
    gains_ref[0, 0] = after
    gain_rows = jnp.broadcast_to(gain, (8, 128))
    carried = (gy_float * widen(entry, spread)).astype(BF16)
    state = state_s[...] * widen(gain_rows, spread)[0:1, :] + contract(
        act_ref[0, :, DI + NS :], carried, 0, 0
    )
    state_s[...] = state
    gain_s[...] = after * gain_rows

    @pl.when(chunk == pl.num_programs(1) - 1)
    def _():
        final_ref[0] = state

    dgain_ref[...] = dgain_s[...]
    dskip_ref[...] = dskip_s[...]


def mixer_back_kernel(
    gy_ref, y_ref, dgate_ref, proj_ref, halo_ref, rim_ref, act_ref, token_ref,
    states_ref, gains_ref, state_ref, gstates_ref, ggains_ref, gstate_ref,
    head_ref, skip_ref, taps_ref, shift_ref, spread_ref, spread_first_ref,
    dproj_ref, drim_ref, dconv_ref, dhead_ref,
    ext_s, grad_s, carry_s, dconv_s, dhead_s,
):
    seq, step_index = pl.program_id(0), pl.program_id(1)
    last_step = pl.num_programs(1) - 1

    @pl.when((seq == 0) & (step_index == 0))
    def _():
        dconv_s[...] = jnp.zeros(dconv_s.shape, F32)
        dhead_s[...] = jnp.zeros(dhead_s.shape, F32)

    @pl.when(step_index == 0)
    def _():
        carry_s[...] = jnp.zeros(carry_s.shape, F32)

    @pl.when(step_index == last_step)
    def _():
        ext_s[0:8, :] = rim_ref[0].astype(F32)

    @pl.when(step_index < last_step)
    def _():
        ext_s[0:8, :] = halo_ref[0, :, DI : DI + CC].astype(F32)[8:16]

    ext_s[8 : 8 + CHUNK, :] = proj_ref[0, :, DI : DI + CC].astype(F32)
    token, spread, spread_first = token_ref[0], spread_ref[...], spread_first_ref[...]
    raw, step, log_decay, running, weight_end, entry, gain = decay_rows(
        proj_ref[0, :, DI + CC :], head_ref, token
    )
    b_rows, c_rows = act_ref[0, :, DI : DI + NS], act_ref[0, :, DI + NS :]
    state = entering_state(states_ref, gains_ref, state_ref, spread)
    gstate = entering_state(gstates_ref, ggains_ref, gstate_ref, spread)
    wide_end = widen(weight_end, spread)
    gy = gy_ref[0]
    gy_float = gy.astype(F32)
    gcarried = (gy_float * widen(entry, spread)).astype(BF16)
    xs_float = act_ref[0, :, :DI].astype(F32)
    grad_c = contract(gcarried, state, 1, 1)
    grad_b = contract((xs_float * wide_end).astype(BF16), gstate, 1, 1)
    from_end = contract(b_rows, gstate, 1, 0) * wide_end
    dgain_row = jnp.sum(gstate.astype(F32) * state.astype(F32), axis=0, keepdims=True)
    cross = contract(c_rows, b_rows, 1, 1)
    running_two, rest_t, bias = inside_terms(running, step, token)
    grad_cross = jnp.zeros((CHUNK, CHUNK), F32)
    lane = lanes((CHUNK, 128))
    for pair in range(MH // 2):
        cols = slice(pair * 128, (pair + 1) * 128)
        stacked = stack_pair(act_ref[0, :, cols])
        gy_pair = gy_ref[0, :, cols]
        first, second = pair_decay(running_two, rest_t, bias, 2 * pair)
        mix = jnp.concatenate([(cross * first).astype(BF16), (cross * second).astype(BF16)], axis=1)
        grad_mix = contract(gy_pair, stacked, 1, 1)
        grad_cross = grad_cross + grad_mix[:, :CHUNK] * first + grad_mix[:, CHUNK:] * second
        both = contract(mix, gy_pair, 0, 0)
        grad_s[8 : 8 + CHUNK, cols] = jnp.where(lane < 64, both[:CHUNK], both[CHUNK:])
    inner = grad_s[8 : 8 + CHUNK, :DI]
    skip = skip_ref[...]
    cross_low = grad_cross.astype(BF16)
    grad_c = grad_c + contract(cross_low, b_rows, 1, 0)
    grad_b = grad_b + contract(cross_low, c_rows, 0, 0)
    narrow = lambda values: jnp.concatenate(
        [gather_heads(values, spread_first), jnp.zeros((values.shape[0], 96), F32)], axis=1
    )
    query_part = narrow(gy_float * (y_ref[0] - skip * xs_float))
    key_inner = narrow(xs_float * inner)
    key_end = narrow(xs_float * from_end)
    extra = jnp.sum(key_end, axis=0, keepdims=True) + gain * narrow(
        jnp.broadcast_to(dgain_row, (8, DI))
    )[0:1, :]
    upper = (~lower_mask() | (lax.broadcasted_iota(jnp.int32, (CHUNK, CHUNK), 0) == lanes((CHUNK, CHUNK))))
    grad_log = product_exact(upper.astype(BF16), query_part - key_inner - key_end) + extra
    sig = jax.nn.sigmoid(raw)
    ratio = jnp.where(raw < -15.0, 1.0, sig / jnp.maximum(step, 1e-30))
    grad_rate = (key_inner + key_end) * ratio - grad_log * jnp.exp(head_ref[0:1, :]) * sig
    dhead_s[0:1, :] += jnp.sum(grad_log * log_decay, axis=0, keepdims=True)
    dhead_s[1:2, :] += jnp.sum(grad_rate, axis=0, keepdims=True)
    total = conv_total(ext_s, token, taps_ref, shift_ref)
    grad_act = jnp.concatenate([inner + from_end + skip * gy_float, grad_b, grad_c], axis=1)
    csig = jax.nn.sigmoid(total)
    grad_total = grad_act * (csig * (1.0 + total * (1.0 - csig)))
    dconv_s[KC : KC + 1, :] += jnp.sum(grad_total, axis=0, keepdims=True)
    grad_s[0:8, :] = jnp.zeros((8, CC), F32)
    grad_s[8 : 8 + CHUNK, :] = grad_total * taps_ref[KC - 1 : KC, :]
    dconv_s[KC - 1 : KC, :] += jnp.sum(grad_total * ext_s[8 : 8 + CHUNK, :], axis=0, keepdims=True)
    for tap in range(KC - 1):
        part = grad_total * token[:, TAP_LANES + tap : TAP_LANES + tap + 1]
        dconv_s[tap : tap + 1, :] += jnp.sum(
            part * ext_s[5 + tap : 5 + tap + CHUNK, :], axis=0, keepdims=True
        )
        grad_s[5 + tap : 5 + tap + CHUNK, :] += part * taps_ref[tap : tap + 1, :]
    grad_s[CHUNK : CHUNK + 8, :] += carry_s[...]
    carry_s[...] = grad_s[0:8, :]
    dproj_ref[0, :, :DI] = dgate_ref[0]
    dproj_ref[0, :, DI : DI + CC] = grad_s[8 : 8 + CHUNK, :].astype(BF16)
    dproj_ref[0, :, DI + CC :] = grad_rate.astype(BF16)

    @pl.when(step_index == last_step)
    def _():
        drim_ref[0] = carry_s[...]

    dconv_ref[...] = dconv_s[...]
    dhead_ref[...] = dhead_s[...]


def mixer_specs(chunks, reverse):
    place = (lambda c: chunks - 1 - c) if reverse else (lambda c: c)
    block = lambda cols: pl.BlockSpec((1, CHUNK, cols), lambda s, c: (s, place(c), 0))
    per_chunk = lambda rows, cols: pl.BlockSpec(
        (1, 1, rows, cols), lambda s, c: (s, place(c), 0, 0)
    )
    per_seq = lambda rows, cols: pl.BlockSpec((1, rows, cols), lambda s, c: (s, 0, 0))
    fixed = lambda rows, cols: pl.BlockSpec((rows, cols), lambda s, c: (0, 0))
    return block, per_chunk, per_seq, fixed


MIXER_PARAMS = pltpu.CompilerParams(vmem_limit_bytes=VMEM_BYTES)


def mixer_scan(proj, rim, token, heads, taps, shift, spread):
    seqs, span, width = proj.shape
    chunks = span // CHUNK
    block, per_chunk, per_seq, fixed = mixer_specs(chunks, False)
    return pl.pallas_call(
        mixer_scan_kernel,
        grid=(seqs, chunks),
        in_specs=[
            block(width), per_seq(8, CC), block(128), fixed(8, 128), fixed(8, CC), fixed(1, CC),
            fixed(128, DI),
        ],
        out_specs=[
            block(CC), per_chunk(NS, DI), per_chunk(8, 128), per_seq(NS, DI), per_seq(8, 128),
        ],
        out_shape=[
            jax.ShapeDtypeStruct((seqs, span, CC), BF16),
            jax.ShapeDtypeStruct((seqs, chunks, NS, DI), BF16),
            jax.ShapeDtypeStruct((seqs, chunks, 8, 128), F32),
            jax.ShapeDtypeStruct((seqs, NS, DI), F32),
            jax.ShapeDtypeStruct((seqs, 8, 128), F32),
        ],
        scratch_shapes=[
            pltpu.VMEM((CHUNK + 8, CC), F32), pltpu.VMEM((NS, DI), F32), pltpu.VMEM((8, 128), F32),
        ],
        compiler_params=MIXER_PARAMS,
        name="mixer_scan",
    )(proj, rim, token, heads, taps, shift, spread)


def mixer_out(proj, act, token, states, gains, state, heads, skip, gain, spread):
    seqs, span, width = proj.shape
    block, per_chunk, per_seq, fixed = mixer_specs(span // CHUNK, False)
    return pl.pallas_call(
        mixer_out_kernel,
        grid=(seqs, span // CHUNK),
        in_specs=[
            block(width), block(CC), block(128), per_chunk(NS, DI), per_chunk(8, 128),
            per_seq(NS, DI), fixed(8, 128), fixed(1, DI), fixed(1, DI), fixed(128, DI),
        ],
        out_specs=[block(DI), block(DI)],
        out_shape=[
            jax.ShapeDtypeStruct((seqs, span, DI), F32),
            jax.ShapeDtypeStruct((seqs, span, DI), BF16),
        ],
        compiler_params=MIXER_PARAMS,
        name="mixer_out",
    )(proj, act, token, states, gains, state, heads, skip, gain, spread)


def mixer_gate_back(gmix, y, proj, act, token, heads, gain, spread):
    seqs, span, width = proj.shape
    chunks = span // CHUNK
    block, per_chunk, per_seq, fixed = mixer_specs(chunks, True)
    return pl.pallas_call(
        mixer_gate_back_kernel,
        grid=(seqs, chunks),
        in_specs=[
            block(DI), block(DI), block(width), block(CC), block(128), fixed(8, 128),
            fixed(1, DI), fixed(128, DI),
        ],
        out_specs=[
            block(DI), block(DI), per_chunk(NS, DI), per_chunk(8, 128), per_seq(NS, DI),
            fixed(8, DI), fixed(8, DI),
        ],
        out_shape=[
            jax.ShapeDtypeStruct((seqs, span, DI), BF16),
            jax.ShapeDtypeStruct((seqs, span, DI), BF16),
            jax.ShapeDtypeStruct((seqs, chunks, NS, DI), BF16),
            jax.ShapeDtypeStruct((seqs, chunks, 8, 128), F32),
            jax.ShapeDtypeStruct((seqs, NS, DI), F32),
            jax.ShapeDtypeStruct((8, DI), F32),
            jax.ShapeDtypeStruct((8, DI), F32),
        ],
        scratch_shapes=[
            pltpu.VMEM((NS, DI), F32), pltpu.VMEM((8, 128), F32),
            pltpu.VMEM((8, DI), F32), pltpu.VMEM((8, DI), F32),
        ],
        compiler_params=MIXER_PARAMS,
        name="mixer_gate_back",
    )(gmix, y, proj, act, token, heads, gain, spread)


def mixer_back(
    gy, y, dgate, proj, rim, act, token, states, gains, state, gstates, ggains, gstate,
    heads, skip, taps, shift, spread, spread_first,
):
    seqs, span, width = proj.shape
    chunks = span // CHUNK
    block, per_chunk, per_seq, fixed = mixer_specs(chunks, True)
    steps = CHUNK // 16
    halo = pl.BlockSpec(
        (1, 16, width), lambda s, c: (s, jnp.maximum((chunks - 1 - c) * steps - 1, 0), 0)
    )
    return pl.pallas_call(
        mixer_back_kernel,
        grid=(seqs, chunks),
        in_specs=[
            block(DI), block(DI), block(DI), block(width), halo, per_seq(8, CC), block(CC),
            block(128), per_chunk(NS, DI), per_chunk(8, 128), per_seq(NS, DI),
            per_chunk(NS, DI), per_chunk(8, 128), per_seq(NS, DI),
            fixed(8, 128), fixed(1, DI), fixed(8, CC), fixed(1, CC), fixed(128, DI), fixed(32, DI),
        ],
        out_specs=[block(width), per_seq(8, CC), fixed(8, CC), fixed(8, 128)],
        out_shape=[
            jax.ShapeDtypeStruct((seqs, span, width), BF16),
            jax.ShapeDtypeStruct((seqs, 8, CC), F32),
            jax.ShapeDtypeStruct((8, CC), F32),
            jax.ShapeDtypeStruct((8, 128), F32),
        ],
        scratch_shapes=[
            pltpu.VMEM((CHUNK + 8, CC), F32), pltpu.VMEM((CHUNK + 8, CC), F32),
            pltpu.VMEM((8, CC), F32), pltpu.VMEM((8, CC), F32), pltpu.VMEM((8, 128), F32),
        ],
        compiler_params=MIXER_PARAMS,
        name="mixer_back",
    )(
        gy, y, dgate, proj, proj, rim, act, token, states, gains, state, gstates, ggains, gstate,
        heads, skip, taps, shift, spread, spread_first,
    )


def token_table(seg_own, seg_rim):
    seqs, span = seg_own.shape
    extended = jnp.concatenate([seg_rim, seg_own], axis=1)
    matches = [extended[:, tap : tap + span] == seg_own for tap in range(KC - 1)]
    by_chunk = seg_own.reshape(seqs, -1, CHUNK)
    last = by_chunk[:, :, -1:]
    before = jnp.concatenate([seg_rim[:, None, -1:], last[:, :-1]], axis=1)
    spare = jnp.zeros((seqs, span), F32)
    rows = [match.astype(F32) for match in matches] + [
        spare,
        (by_chunk == before).reshape(seqs, span).astype(F32),
        (by_chunk == last).reshape(seqs, span).astype(F32),
        seg_own.astype(F32),
        spare,
    ]
    return jnp.pad(jnp.stack(rows, axis=-1), ((0, 0), (0, 0), (0, 120)))


def from_behind(block, axis, distance):
    devices = range(lax.axis_size(axis))
    route = [(i - distance, i) for i in devices if i - distance in devices]
    return lax.ppermute(block, axis, route)


def chain_states(local, gain, reverse):
    count, place = lax.axis_size("ctx"), lax.axis_index("ctx")
    state = jnp.zeros(local.shape, BF16)
    for hop in range(count - 1):
        source = count - 1 - hop if reverse else hop
        target = source - 1 if reverse else source + 1
        sent = (gain * state.astype(F32) + local).astype(BF16)
        received = lax.ppermute(sent, "ctx", [(source, target)])
        state = jnp.where(place == target, received, state)
    return state


def sum_everywhere(values, axes):
    for axis in axes:
        count, distance = lax.axis_size(axis), 1
        while distance < count:
            route = [(i, i ^ distance) for i in range(count)]
            values = values + lax.ppermute(values, axis, route)
            distance *= 2
    return values


def rms_scale(values, gain_vec):
    return (
        values * lax.rsqrt(jnp.mean(values * values, axis=-1, keepdims=True) + EPSILON) * gain_vec
    )


def silu_product(gate_lin, up_lin):
    return jax.nn.silu(gate_lin) * up_lin


def body(
    layer_input, segments, positions, gain_one, w_in, conv_w, conv_b, head_params, gain_m, w_out,
    w_q, w_k, w_v, w_o, gain_two, w_gate, w_up, w_down, cotangent,
):
    seqs, span, width = layer_input.shape
    rows = seqs * span
    axes = ("dp", "ctx")
    own_rows = w_q.shape[0]
    q_width, kv_width = QH * HD, 2 * KVH * HD
    low_dot = lambda a, b: jnp.dot(a, b, preferred_element_type=F32)

    small_parts = [gain_one, gain_two, gain_m, conv_b, conv_w.reshape(-1)]
    small_sizes = [part.shape[0] for part in small_parts]
    slots = own_rows * 128
    small_block = jnp.concatenate(small_parts, axis=0)
    small_block = jnp.pad(small_block, (0, slots - sum(small_sizes))).reshape(own_rows, 128)
    w_kv = jnp.stack(
        [w_k.reshape(own_rows, KVH, HD), w_v.reshape(own_rows, KVH, HD)], axis=2
    ).reshape(own_rows, kv_width)
    gather = lambda shard: lax.all_gather(shard, axes, axis=0, tiled=True)
    first_all = gather(jnp.concatenate([w_q, w_kv, small_block], axis=1))
    in_width = DI + CC + 128
    w_in_all = gather(jnp.pad(w_in, ((0, 0), (0, in_width - w_in.shape[1]))))
    w_out_all = gather(w_out)
    w_o_all = gather(w_o.T)
    w_gate_all = gather(w_gate)
    w_up_all = gather(w_up)
    w_down_all = gather(w_down)
    small_all = first_all[:, q_width + kv_width :].reshape(-1, slots).astype(F32)
    parts, at = [], 0
    for size in small_sizes:
        parts.append(small_all[:, at : at + size])
        at += size
    gain1_all, gain2_all, gain_m_all, shift_all = [part.reshape(1, -1) for part in parts[:4]]
    taps_all = jnp.swapaxes(parts[4].reshape(-1, KC, small_sizes[3]), 0, 1).reshape(KC, CC)
    taps_all = jnp.pad(taps_all, ((0, 8 - KC), (0, 0)))

    place = lax.axis_index("ctx")
    span_start = place * span
    seg_own = lax.dynamic_slice_in_dim(segments, span_start, span, 1)
    seg_rim = jnp.where(
        place > 0,
        lax.dynamic_slice_in_dim(segments, jnp.maximum(span_start - (KC - 1), 0), KC - 1, 1),
        -1,
    )
    token = token_table(seg_own, seg_rim)
    bounds = attention_bounds(segments, seg_own, span_start)
    segk, segq = segments[:, :, None], seg_own[:, None, :]
    cosine, sine = rope_tables(positions)
    heads = jnp.pad(head_params, ((0, 5), (0, 128 - MH)))
    skip = jnp.repeat(head_params[2], MP)[None]
    spread, spread_first = spread_matrix(), spread_first_matrix()

    tokens = layer_input.reshape(rows, width)
    hidden, q, kv = project(
        tokens, gain1_all, first_all, cosine.reshape(rows, 128), sine.reshape(rows, 128)
    )
    q = q.reshape(seqs, span, q_width)
    kv_all = lax.all_gather(kv.reshape(seqs, span, kv_width), "ctx", axis=1, tiled=True)
    proj = low_dot(hidden, w_in_all).astype(BF16).reshape(seqs, span, in_width)
    rim = from_behind(proj[:, span - (KC - 1) :, DI : DI + CC], "ctx", 1)
    rim = jnp.pad(rim, ((0, 0), (8 - (KC - 1), 0), (0, 0)))
    act, states, gains, local_state, local_gain = mixer_scan(
        proj, rim, token, heads, taps_all, shift_all, spread
    )
    wide_gain = jnp.repeat(local_gain[:, :1, :MH], MP, axis=2)
    state_in = chain_states(local_state, wide_gain, False)
    att, lse = attend(bounds, q, kv_all, segk, segq)
    mixer_y, mixer_in = mixer_out(
        proj, act, token, states, gains, state_in, heads, skip, gain_m_all, spread
    )
    mixer_in = mixer_in.reshape(rows, DI)
    att_rows = att.reshape(rows, q_width)
    middle = (
        tokens.astype(F32)
        + low_dot(mixer_in, w_out_all)
        + jnp.einsum("ra,da->rd", att_rows, w_o_all, preferred_element_type=F32)
    )
    normed_mid, norm2_pull = jax.vjp(rms_scale, middle, gain2_all)
    normed_two = normed_mid.astype(BF16)
    gate_lin = low_dot(normed_two, w_gate_all)
    up_lin = low_dot(normed_two, w_up_all)
    act_float, act_pull = jax.vjp(silu_product, gate_lin, up_lin)
    act_rows = act_float.astype(BF16)
    layer_result = (middle + low_dot(act_rows, w_down_all)).astype(BF16)

    def scatter(grad):
        part = lax.psum_scatter(grad, "dp", scatter_dimension=0, tiled=True)
        return lax.psum_scatter(part, "ctx", scatter_dimension=0, tiled=True).astype(F32)

    def weight_grad(left, right):
        return jnp.einsum("ri,ro->io", left, right, preferred_element_type=F32).astype(BF16)

    def back_dot(grad, weight):
        return jnp.einsum("ro,io->ri", grad, weight, preferred_element_type=F32)

    cot_rows = cotangent.reshape(rows, width)
    grad_down = weight_grad(act_rows, cot_rows)
    grad_gate_f, grad_up_f = act_pull(back_dot(cot_rows, w_down_all))
    grad_gate_low, grad_up_low = grad_gate_f.astype(BF16), grad_up_f.astype(BF16)
    grad_wgate = weight_grad(normed_two, grad_gate_low)
    grad_wup = weight_grad(normed_two, grad_up_low)
    grad_normed = back_dot(grad_gate_low, w_gate_all) + back_dot(grad_up_low, w_up_all)
    grad_normed, grad_down, grad_wgate, grad_wup = lax.optimization_barrier(
        (grad_normed, grad_down, grad_wgate, grad_wup)
    )
    out_down, out_gate, out_up = scatter(grad_down), scatter(grad_wgate), scatter(grad_wup)
    grad_mid_norm, grad_gain_second = norm2_pull(grad_normed)
    grad_middle = cot_rows.astype(F32) + grad_mid_norm
    grad_mid_low = grad_middle.astype(BF16)
    grad_wout = weight_grad(mixer_in, grad_mid_low)
    grad_wo = weight_grad(grad_mid_low, att_rows)
    grad_mixer_in = back_dot(grad_mid_low, w_out_all).astype(BF16).reshape(seqs, span, DI)
    grad_att = low_dot(grad_mid_low, w_o_all).astype(BF16).reshape(seqs, span, q_width)
    grad_mixer_in, grad_att, grad_wout, grad_wo = lax.optimization_barrier(
        (grad_mixer_in, grad_att, grad_wout, grad_wo)
    )
    out_wout, out_wo = scatter(grad_wout), scatter(grad_wo)
    grad_y, grad_gate, gstates, ggains, local_gstate, grad_gain_mix, grad_skip = mixer_gate_back(
        grad_mixer_in, mixer_y, proj, act, token, heads, gain_m_all, spread
    )
    gstate_out = chain_states(local_gstate, wide_gain, True)
    dq, dkv_all = attend_back(
        bounds, q, kv_all, segk, segq, att, grad_att, lse, cosine, sine
    )
    dkv = lax.psum_scatter(dkv_all, "ctx", scatter_dimension=1, tiled=True)
    grad_proj, grad_rim, grad_conv, grad_heads = mixer_back(
        grad_y, mixer_y, grad_gate, proj, rim, act, token, states, gains, state_in,
        gstates, ggains, gstate_out, heads, skip, taps_all, shift_all, spread, spread_first,
    )
    back_rim = from_behind(grad_rim[:, 8 - (KC - 1) :].astype(BF16), "ctx", -1)
    edge = grad_proj[:, span - (KC - 1) :, DI : DI + CC].astype(F32) + back_rim.astype(F32)
    grad_proj = lax.dynamic_update_slice(
        grad_proj, edge.astype(BF16), (0, span - (KC - 1), DI)
    ).reshape(rows, in_width)
    grad_win = weight_grad(hidden, grad_proj)
    out_win = scatter(grad_win)[:, : w_in.shape[1]]
    grad_kv = dkv.astype(F32).reshape(seqs, span, KVH, 2 * HD)
    turned = grad_kv[..., :HD] * sine[:, :, None, :HD]
    turned = jnp.concatenate([turned[..., HD // 2 :], turned[..., : HD // 2]], axis=-1)
    grad_key = grad_kv[..., :HD] * cosine[:, :, None, :HD] + turned
    grad_kv = jnp.concatenate([grad_key, grad_kv[..., HD:]], axis=-1).astype(BF16)
    grad_first = jnp.concatenate(
        [dq.reshape(rows, q_width), grad_kv.reshape(rows, kv_width)], axis=1
    )
    grad_wfirst = weight_grad(hidden, grad_first)
    grad_hidden = back_dot(grad_proj, w_in_all) + back_dot(
        grad_first, first_all[:, : q_width + kv_width]
    )
    tokens_f = tokens.astype(F32)
    _, norm1_pull = jax.vjp(rms_scale, tokens_f, gain1_all)
    grad_tokens_norm, grad_gain_first = norm1_pull(grad_hidden)
    grad_tokens = (grad_middle + grad_tokens_norm).astype(BF16)

    devices = first_all.shape[0] // own_rows
    small_grads = jnp.concatenate(
        [
            grad_gain_first.reshape(devices, -1),
            grad_gain_second.reshape(devices, -1),
            grad_gain_mix[0].reshape(devices, -1),
            grad_conv[KC].reshape(devices, -1),
            jnp.swapaxes(grad_conv[:KC].reshape(KC, devices, -1), 0, 1).reshape(devices, -1),
        ],
        axis=1,
    )
    small_grads = jnp.pad(small_grads, ((0, 0), (0, slots - small_grads.shape[1])))
    out_first = scatter(
        jnp.concatenate([grad_wfirst, small_grads.reshape(-1, 128).astype(BF16)], axis=1)
    )
    out_small = out_first[:, q_width + kv_width :].reshape(-1)
    pieces, at = [], 0
    for size in small_sizes:
        pieces.append(out_small[at : at + size])
        at += size
    out_kv = out_first[:, q_width : q_width + kv_width].reshape(own_rows, KVH, 2, HD)
    head_grad = sum_everywhere(
        jnp.concatenate(
            [grad_heads[:2, :MH], grad_skip[0].reshape(MH, MP).sum(axis=1)[None]], axis=0
        ),
        axes,
    )
    return (
        layer_result.reshape(layer_input.shape),
        grad_tokens.reshape(layer_input.shape),
        pieces[0],
        out_win,
        pieces[4].reshape(KC, -1),
        pieces[3],
        head_grad,
        pieces[2],
        out_wout,
        out_first[:, :q_width],
        out_kv[:, :, 0].reshape(own_rows, -1),
        out_kv[:, :, 1].reshape(own_rows, -1),
        out_wo.T,
        pieces[1],
        out_gate,
        out_up,
        out_down,
    )


def solution(mesh):
    in_specs = (
        P("dp", "ctx", None),
        P("dp", None),
        P("dp", "ctx"),
        P(("dp", "ctx")),
        P(("dp", "ctx"), None),
        P(None, ("dp", "ctx")),
        P(("dp", "ctx")),
        P(),
        P(("dp", "ctx")),
        P(("dp", "ctx"), None),
        P(("dp", "ctx"), None),
        P(("dp", "ctx"), None),
        P(("dp", "ctx"), None),
        P(None, ("dp", "ctx")),
        P(("dp", "ctx")),
        P(("dp", "ctx"), None),
        P(("dp", "ctx"), None),
        P(("dp", "ctx"), None),
        P("dp", "ctx", None),
    )
    out_specs = (
        P("dp", "ctx", None),
        P("dp", "ctx", None),
        P(("dp", "ctx")),
        P(("dp", "ctx"), None),
        P(None, ("dp", "ctx")),
        P(("dp", "ctx")),
        P(),
        P(("dp", "ctx")),
        P(("dp", "ctx"), None),
        P(("dp", "ctx"), None),
        P(("dp", "ctx"), None),
        P(("dp", "ctx"), None),
        P(None, ("dp", "ctx")),
        P(("dp", "ctx")),
        P(("dp", "ctx"), None),
        P(("dp", "ctx"), None),
        P(("dp", "ctx"), None),
    )
    return jax.shard_map(body, mesh=mesh, in_specs=in_specs, out_specs=out_specs, check_vma=False)
```

time: 1940 us -> 1320 us (0.68)
  matrix products: 630 us -> 218 us
  Pallas kernels: 0 us -> 207 us
  other arithmetic: 259 us -> 75.3 us
  local copies, waits for them, and re-layouts: 176 us -> 70.6 us
  waiting for transfers between devices: 786 us -> 702 us
  blocking collectives: 49.9 us -> 0 us
    dot_general x47 -> x20, matrix products: 630 us -> 218 us  [the longest x6 77.4 us: back_dot(): return jnp.einsum('ro,io->ri', grad, weight, preferred_element_type=F32)]
    reduce_scatter x8 -> x14, waiting for transfers between devices: 564 us -> 239 us  [the longest x6 122 us: scatter(): part = lax.psum_scatter(grad, 'dp', scatter_dimension=0, tiled=True)]
    pallas_call x0 -> x7, Pallas kernels: none -> 207 us  [the longest x1 65.2 us: mixer_back(): pl.pallas_call(mixer_back_kernel, grid=(seqs, chunks), in_specs=[block(DI...]
    ppermute x0 -> x11, waiting for transfers between devices: none -> 159 us  [the longest x6 153 us: chain_states(): received = lax.ppermute(sent, 'ctx', [(source, target)])]
    reduce_sum x7 -> x3, other arithmetic: 90.5 us -> 3.18 us  [the longest x1 2.06 us: rms_scale(): values * lax.rsqrt(jnp.mean(values * values, axis=-1, keepdims=True) + EP...]
    all_gather x10 -> x8, waiting for transfers between devices: 216 us -> 263 us  [the longest x7 263 us: body(): gather = lambda shard: lax.all_gather(shard, axes, axis=0, tiled=True)]
    psum x1 -> x0, blocking collectives: 40.3 us -> none  [body(): lax.psum(jnp.stack([grad_decay_log, grad_step_bias, grad_skip]), axes)]
    unnamed x18 -> x24, waiting for transfers between devices: 4.02 us -> 37.7 us
  transfers between devices with their start and end apart: 20 -> 36, of which waited for: 11 -> 23; matrix products, arithmetic and copies ran while one was open for 44% -> 18% of each run, Pallas kernels for 0% -> 13%
where the time goes in v2:
time: 1320 us; the launch traced here: 1310 us
  waiting for transfers between devices  702 us (53%)
  matrix products  218 us (17%)
  Pallas kernels  207 us (16%)
  other arithmetic  75.3 us (6%)
  local copies, waits for them, and re-layouts  70.6 us (5%)
  starting transfers between devices  22.1 us (2%)
  between operations  15.4 us (1%)
    all_gather x7, waiting for transfers between devices, body(): gather = lambda shard: lax.all_gather(shard, axes, axis=0, tiled=True)  263 us
    ppermute x6, waiting for transfers between devices, chain_states(): received = lax.ppermute(sent, 'ctx', [(source, target)])  153 us
    reduce_scatter x6, waiting for transfers between devices, scatter(): part = lax.psum_scatter(grad, 'dp', scatter_dimension=0, tiled=True)  122 us
    reduce_scatter x7, waiting for transfers between devices, scatter(): lax.psum_scatter(part, 'ctx', scatter_dimension=0, tiled=True).astype(F32)  117 us
    dot_general x6, matrix products, back_dot(): return jnp.einsum('ro,io->ri', grad, weight, preferred_element_type=F32)  77.4 us
    dot_general x7, matrix products, weight_grad(): jnp.einsum('ri,ro->io', left, right, preferred_element_type=F32)  69 us
    dot_general x6, matrix products, body(): low_dot = lambda a, b: jnp.dot(a, b, preferred_element_type=F32)  65.7 us
    pallas_call x1, Pallas kernels, mixer_back(): pl.pallas_call(mixer_back_kernel, grid=(seqs, chunks), in_specs=[block(DI...  65.2 us
  transfers between devices with their start and end apart: 36, of which 23 were waited for; matrix products, arithmetic and copies ran while one was open for 18% of the time, Pallas kernels for 13%

profile of v2, /device:TPU:0, one launch (start us, length us, event | category | flops | bytes accessed | tf_op | source)
XLA Modules:
  0.0 1310.4 jit_solution(1063019260852259703)
XLA Ops:
  9.8 2.8 concatenate.50
  16.6 2.8 fusion.17
  21.1 51.5 %all-gather.9.cloned.1.call-done.w_ref = bf16[1024,896]{1,0:T(8,128)(2,1)} async-done(((bf16[32,896]{1,0:T(8,128)(2,1)}), bf16[1024,896]{1,0:T(8,128)(2,1)}) %all-gather.9.cloned.1.call-update) | async-done | bytes 1835024 | tf_op jit(solution)/shard_map/all_gather | solution.py:855
  75.2 11.1 project.1
  92.7 54.9 %all-gather.11.cloned.1.call-done = bf16[1024,3456]{1,0:T(8,128)(2,1)} async-done(((bf16[32,3456]{1,0:T(8,128)(2,1)}), bf16[1024,3456]{1,0:T(8,128)(2,1)}) %all-gather.11.cloned.1.call-update) | async-done | bytes 7077904 | tf_op jit(solution)/shard_map/all_gather | solution.py:855
  147.5 14.8 %convolution_convert_fusion = bf16[1536,3456]{1,0:T(8,128)(2,1)S(1)} fusion(bf16[1536,1024]{1,0:T(8,128)(2,1)} %get-tuple-element.50, bf16[1024,3456]{1,0:T(8,128)(2,1)} %all-gather.11.cloned.1.call-done), kind=kOutput, calls=%fused_computation.1 | convolution fusion | flops 10876944384 | bytes 20840448 | tf_op jit(solution)/shard_map/dot_general | solution.py:845
  162.4 3.9 copy-done
  166.4 3.6 collective-permute-start
  174.6 4.4 stack.51
  185.7 23.3 %mixer_scan.1 = (bf16[3,512,1792]{2,1,0:T(8,128)(2,1)}, bf16[3,4,128,1536]{3,2,1,0:T(8,128)(2,1)}, f32[3,4,8,128]{3,2,1,0:T(8,128)}, f32[3,128,1536]{2,1,0:T(8,128)}, f32[3,8,128]{2,1,0:T(8,128)}) custom-call(bf16[3,512,3456]{2,1,0:T(8,128)(2,1)} %bitcast.114, bf16[3,8,1792]{2,1,0:T(8,128)(2,1)} %pad.31.rim_ref, f32[3,512,128]{2,1,0:T(8,128)} %pad.32.token_ref, ...), custom_call_target="tpu_custom_call" | custom-call | tf_op jit(solution)/shard_map/mixer_scan/pallas_call | solution.py:663
  210.6 3.0 add_convert_fusion.6
  213.6 2.9 collective-permute-start.1
  216.5 27.1 %collective-permute-done.1 = bf16[3,128,1536]{2,1,0:T(8,128)(2,1)S(1)} collective-permute-done((bf16[3,128,1536]{2,1,0:T(8,128)(2,1)}, bf16[3,128,1536]{2,1,0:T(8,128)(2,1)S(1)}, u32[]{:S(2)}, u32[]{:S(2)}) %collective-permute-start.1) | collective-permute-done | bytes 1179680 | tf_op jit(solution)/shard_map/ppermute | solution.py:811
  253.7 2.9 copy.196.segk_ref
  256.6 2.3 add_convert_fusion.4
  259.8 2.8 fusion.18
  266.7 27.8 %attend.1 = (bf16[3,512,512]{2,1,0:T(8,128)(2,1)}, f32[3,8,512]{2,1,0:T(8,128)}) custom-call(s32[6]{0:T(128)} %and_select_fusion.1.low_ref, s32[6]{0:T(128)} %reshape.252.high_ref, s32[1]{0:T(128)} %bitcast.12.base_ref, bf16[3,512,512]{2,1,0:T(8,128)(2,1)} %bitcast.125, bf16[3,2048,256]{2,1,0:T(8,128)(2,1)} %all-gather.15.cloned.1.call-done.kv_ref, ...), custom_call_target="tpu_custom_call" | custom-call | tf_op jit(solution)/shard_map/attend/pallas_call | solution.py:225
  294.5 6.2 fusion.38
  301.9 22.0 %mixer_out.1 = (f32[3,512,1536]{2,1,0:T(8,128)}, bf16[3,512,1536]{2,1,0:T(8,128)(2,1)}) custom-call(bf16[3,512,3456]{2,1,0:T(8,128)(2,1)} %bitcast.115, bf16[3,512,1792]{2,1,0:T(8,128)(2,1)} %get-tuple-element.51.act_ref, f32[3,512,128]{2,1,0:T(8,128)} %pad.32.token_ref, bf16[3,4,128,1536]{3,2,1,0:T(8,128)(2,1)} %get-tuple-element.52.states_ref, ...), custom_call_target="tpu_custom_call" | custom-call | tf_op jit(solution)/shard_map/mixer_out/pallas_call | solution.py:691
  323.9 4.8 all-gather.13.cloned.1.call-done
  328.7 12.0 multiply_reduce_fusion.3
  340.7 2.6 copy-done.1
  343.9 48.6 %all-gather.19.cloned.1.call-done = bf16[1024,2048]{1,0:T(8,128)(2,1)} async-done(((bf16[32,2048]{1,0:T(8,128)(2,1)}), bf16[1024,2048]{1,0:T(8,128)(2,1)}) %all-gather.19.cloned.1.call-update) | async-done | bytes 4194320 | tf_op jit(solution)/shard_map/all_gather | solution.py:855
  392.5 11.3 fusion.39
  403.8 52.4 %all-gather.21.cloned.1.call-done = bf16[1024,2048]{1,0:T(8,128)(2,1)} async-done(((bf16[32,2048]{1,0:T(8,128)(2,1)}), bf16[1024,2048]{1,0:T(8,128)(2,1)}) %all-gather.21.cloned.1.call-update) | async-done | bytes 4194320 | tf_op jit(solution)/shard_map/all_gather | solution.py:855
  456.2 12.6 fusion.40
  468.8 51.1 %all-gather.23.cloned.1.call-done = bf16[2048,1024]{1,0:T(8,128)(2,1)} async-done(((bf16[64,1024]{1,0:T(8,128)(2,1)}), bf16[2048,1024]{1,0:T(8,128)(2,1)}) %all-gather.23.cloned.1.call-update) | async-done | bytes 4194320 | tf_op jit(solution)/shard_map/all_gather | solution.py:855
  519.9 22.7 %multiply_convert_fusion = (bf16[1536,2048]{1,0:T(8,128)(2,1)}, bf16[1536,2048]{1,0:T(8,128)(2,1)}, bf16[1536,2048]{1,0:T(8,128)(2,1)}) fusion(f32[1536,2048]{1,0:T(8,128)} %fusion.39, f32[1536,2048]{1,0:T(8,128)} %fusion.40, bf16[1536,1024]{1,0:T(8,128)(2,1)S(1)} %bitcast.123, bf16[2048,1024]{1,0:T(8,128)(2,1)} %all-gather.23.cloned.1.call-done), kind=kOutput, calls=%fused_computation.5 | convolution fusion | flops 6492782592 | bytes 51380224 | tf_op jit(solution)/shard_map/ro,io->ri/dot_general | solution.py:930
  542.5 11.2 convolution_convert_fusion.3
  553.8 11.4 convolution_convert_fusion.4
  565.2 11.2 convolution_convert_fusion.5
  576.3 11.9 fusion.41
  588.2 10.3 convolution_add_fusion.1
  604.9 2.8 convolution_convert_fusion.9
  607.7 9.5 convolution_convert_fusion.6
  617.2 8.7 convolution_convert_fusion.1
  625.9 3.0 convolution_convert_fusion.7
  628.9 33.0 %attend_back.1 = (bf16[3,512,512]{2,1,0:T(8,128)(2,1)}, bf16[3,2048,256]{2,1,0:T(8,128)(2,1)}) custom-call(s32[6]{0:T(128)} %and_select_fusion.1.low_ref, s32[6]{0:T(128)} %reshape.252.high_ref, s32[1]{0:T(128)} %bitcast.12.base_ref, bf16[3,512,512]{2,1,0:T(8,128)(2,1)} %bitcast.126, bf16[3,2048,256]{2,1,0:T(8,128)(2,1)} %all-gather.15.cloned.1.call-done.kv_ref, ...), custom_call_target="tpu_custom_call" | custom-call | tf_op jit(solution)/shard_map/attend_back/pallas_call | solution.py:253
  664.5 24.7 %mixer_gate_back.1 = (bf16[3,512,1536]{2,1,0:T(8,128)(2,1)}, bf16[3,512,1536]{2,1,0:T(8,128)(2,1)}, bf16[3,4,128,1536]{3,2,1,0:T(8,128)(2,1)}, f32[3,4,8,128]{3,...) custom-call(bf16[3,512,1536]{2,1,0:T(8,128)(2,1)} %bitcast.127, ...), custom_call_target="tpu_custom_call" | custom-call | tf_op jit(solution)/shard_map/mixer_gate_back/pallas_call | solution.py:712
  695.4 3.3 add_convert_fusion.1
  700.8 3.5 pad_maximum_fusion.4
  706.2 126.0 %collective-permute-done.6 = bf16[3,128,1536]{2,1,0:T(8,128)(2,1)} collective-permute-done((bf16[3,128,1536]{2,1,0:T(8,128)(2,1)}, bf16[3,128,1536]{2,1,0:T(8,128)(2,1)}, u32[]{:S(2)}, u32[]{:S(2)}) %collective-permute-start.6) | collective-permute-done | bytes 1179680 | tf_op jit(solution)/shard_map/ppermute | solution.py:811
  832.2 2.5 broadcast_select_fusion.gstate_ref
  834.7 65.2 %mixer_back.1 = (bf16[3,512,3456]{2,1,0:T(8,128)(2,1)}, f32[3,8,1792]{2,1,0:T(8,128)}, f32[8,1792]{1,0:T(8,128)}, f32[8,128]{1,0:T(8,128)}) custom-call(bf16[3,512,1536]{2,1,0:T(8,128)(2,1)} %get-tuple-element.63.gy_ref, f32[3,512,1536]{2,1,0:T(8,128)} %get-tuple-element.62.y_ref, bf16[3,512,1536]{2,1,0:T(8,128)(2,1)} %get-tuple-element.64.dgate_ref, ...), custom_call_target="tpu_custom_call" | custom-call | tf_op jit(solution)/shard_map/mixer_back/pallas_call | solution.py:752
  903.3 3.4 collective-permute-done.7
  909.8 2.7 reshape.262
  922.9 4.6 fusion.13
  927.5 19.2 %fusion.10 = (bf16[1024]{0:T(1024)(128)(2,1)S(1)}, f32[1536]{0:T(1024)S(1)}, f32[1536,1024]{1,0:T(8,128)}) fusion(f32[1536]{0:T(1024)S(1)} %rsqrt.21, bf16[3,512,1024]{2,1,0:T(8,128)(2,1)S(1)} %copy-done.4, f32[1024]{0:T(1024)S(1)} %mul.264, f32[1536,1024]{1,0:T(8,128)} %fusion.13, bf16[1536,3456]{1,0:T(8,128)(2,1)} %bitcast.144, ...), kind=kOutput, calls=%fused_computation.23 | convolution fusion | flops 10884216832 | bytes 33441792 | tf_op jit(solution)/shard_map/ro,io->ri/dot_general | solution.py:930
  948.9 5.3 convolution_convert_fusion.8
  955.5 3.8 copy.201
  960.6 17.6 %convolution_convert_fusion.2 = bf16[1024,3456]{1,0:T(8,128)(2,1)} fusion(bf16[1536,1024]{1,0:T(8,128)(2,1)} %get-tuple-element.50, bf16[1536,3456]{1,0:T(8,128)(2,1)} %bitcast.145), kind=kOutput, calls=%fused_computation.16 | convolution fusion | flops 10875174912 | bytes 20840448 | tf_op jit(solution)/shard_map/ri,ro->io/dot_general | solution.py:927
  980.5 54.9 %reduce-scatter.42.cloned.1.call-done = bf16[256,1024]{1,0:T(8,128)(2,1)} async-done(((bf16[2048,1024]{1,0:T(8,128)(2,1)}), bf16[256,1024]{1,0:T(8,128)(2,1)}) %reduce-scatter.42.cloned.1.call-update) | async-done | bytes 524304 | tf_op jit(solution)/shard_map/reduce_scatter | solution.py:923
  1047.1 31.1 %reduce-scatter.46.cloned.1.call-done = bf16[128,896]{1,0:T(8,128)(2,1)} async-done(((bf16[1024,896]{1,0:T(8,128)(2,1)}), bf16[128,896]{1,0:T(8,128)(2,1)}) %reduce-scatter.46.cloned.1.call-update) | async-done | bytes 229392
  1078.3 12.1 add_convert_fusion
  1090.3 2.5 collective-permute-start.12
  1092.8 6.7 reduce-scatter.32.cloned.1.call-done
  1101.5 19.0 %reduce-scatter.28.cloned.1.call-done = bf16[48,1024]{1,0:T(8,128)(2,1)} async-done(((bf16[192,1024]{1,0:T(8,128)(2,1)}), bf16[48,1024]{1,0:T(8,128)(2,1)}) %reduce-scatter.28.cloned.1.call-update) | async-done | bytes 98320 | tf_op jit(solution)/shard_map/reduce_scatter | solution.py:924
  1122.1 65.6 %reduce-scatter.22.cloned.1.call-done = bf16[128,3456]{1,0:T(8,128)(2,1)} async-done(((bf16[1024,3456]{1,0:T(8,128)(2,1)}), bf16[128,3456]{1,0:T(8,128)(2,1)}) %reduce-scatter.22.cloned.1.call-update) | async-done | bytes 884752 | tf_op jit(solution)/shard_map/reduce_scatter | solution.py:923
  1187.7 10.8 fusion.6
  1198.5 13.2 %reduce-scatter.36.cloned.1.call-done = bf16[32,2048]{1,0:T(8,128)(2,1)} async-done(((bf16[128,2048]{1,0:T(8,128)(2,1)}), bf16[32,2048]{1,0:T(8,128)(2,1)}) %reduce-scatter.36.cloned.1.call-update) | async-done | bytes 131088 | tf_op jit(solution)/shard_map/reduce_scatter | solution.py:924
  1213.4 20.5 %reduce-scatter.40.cloned.1.call-done = bf16[32,2048]{1,0:T(8,128)(2,1)} async-done(((bf16[128,2048]{1,0:T(8,128)(2,1)}), bf16[32,2048]{1,0:T(8,128)(2,1)}) %reduce-scatter.40.cloned.1.call-update) | async-done | bytes 131088 | tf_op jit(solution)/shard_map/reduce_scatter | solution.py:924
  1235.5 20.8 %reduce-scatter.44.cloned.1.call-done = bf16[64,1024]{1,0:T(8,128)(2,1)} async-done(((bf16[256,1024]{1,0:T(8,128)(2,1)}), bf16[64,1024]{1,0:T(8,128)(2,1)}) %reduce-scatter.44.cloned.1.call-update) | async-done | bytes 131088 | tf_op jit(solution)/shard_map/reduce_scatter | solution.py:924
  1257.9 18.5 %reduce-scatter.48.cloned.1.call-done = bf16[32,896]{1,0:T(8,128)(2,1)} async-done(((bf16[128,896]{1,0:T(8,128)(2,1)}), bf16[32,896]{1,0:T(8,128)(2,1)}) %reduce-scatter.48.cloned.1.call-update) | async-done | bytes 57360 | tf_op jit(solution)/shard_map/reduce_scatter | solution.py:924
  1283.6 18.1 %reduce-scatter.24.cloned.1.call-done = bf16[32,3456]{1,0:T(8,128)(2,1)} async-done(((bf16[128,3456]{1,0:T(8,128)(2,1)}), bf16[32,3456]{1,0:T(8,128)(2,1)}) %reduce-scatter.24.cloned.1.call-update) | async-done | bytes 221200 | tf_op jit(solution)/shard_map/reduce_scatter | solution.py:924
  (311 shorter events, 118.4 us)
Async XLA Ops:
  7.2 65.4 %all-gather.9.cloned.1.call-start = ((), (), s32[]{:S(2)}) async-start(), calls=%async_computation.15 | async-start | bytes 1892352 | tf_op jit(solution)/shard_map/all_gather | solution.py:855
  13.9 133.6 %all-gather.11.cloned.1.call-start = ((), (), s32[]{:S(2)}) async-start(), calls=%async_computation.16 | async-start | bytes 7299072 | tf_op jit(solution)/shard_map/all_gather | solution.py:855
  15.7 251.1 %all-gather.15.cloned.1.call-start = ((), (), s32[]{:S(2)}) async-start(), calls=%async_computation.18 | async-start | bytes 3932160 | tf_op jit(solution)/shard_map/all_gather | solution.py:894
  16.5 4.6 copy-start.34
  16.6 4.5 copy-start.36
  16.6 4.5 copy-start.39
  73.7 12.6 copy-start.22
  74.5 11.7 copy-start.25
  86.3 208.2 %all-gather.17.cloned.1.call-start = ((), (), s32[]{:S(2)}) async-start(), calls=%async_computation.19 | async-start | bytes 1081344 | tf_op jit(solution)/shard_map/all_gather | solution.py:855
  86.9 241.8 %all-gather.13.cloned.1.call-start = ((), (), s32[]{:S(2)}) async-start(), calls=%async_computation.17 | async-start | bytes 3244032 | tf_op jit(solution)/shard_map/all_gather | solution.py:855
  87.5 305.1 %all-gather.19.cloned.1.call-start = ((), (), s32[]{:S(2)}) async-start(), calls=%async_computation.20 | async-start | bytes 4325376 | tf_op jit(solution)/shard_map/all_gather | solution.py:855
  88.0 368.2 %all-gather.21.cloned.1.call-start = ((), (), s32[]{:S(2)}) async-start(), calls=%async_computation.21 | async-start | bytes 4325376 | tf_op jit(solution)/shard_map/all_gather | solution.py:855
  88.8 431.1 %all-gather.23.cloned.1.call-start = ((), (), s32[]{:S(2)}) async-start(), calls=%async_computation.22 | async-start | bytes 4325376 | tf_op jit(solution)/shard_map/all_gather | solution.py:855
  90.9 71.5 %copy-start.32 = (pred[1536]{0:T(1024)(128)(4,1)}, pred[1536]{0:T(1024)(128)(4,1)S(1)}, u32[]{:S(2)}) copy-start(pred[1536]{0:T(1024)(128)(4,1)S(1)} %fusion.28) | copy-start | bytes 4612
  162.4 3.9 copy-start
  166.4 18.6 %collective-permute-start = (bf16[3,3,1792]{2,1,0:T(4,128)(2,1)S(1)}, bf16[3,3,1792]{2,1,0:T(4,128)(2,1)S(1)}, u32[]{:S(2)}, u32[]{:S(2)}) collective-permute-start(bf16[3,3,1792]{2,1,0:T(4,128)(2,1)S(1)} %slice.180), channel_id=1, source_target_pairs={{0,1},{1,2},{2,3},{4,5},{5,6},{6,7},{8,9},{9,10},{10,11},{12,13},{... | collective-permute-start | bytes 96776 | tf_op jit(solution)/shard_map/ppermute | solution.py:801
  174.6 6.5 copy-start.38
  209.0 34.6 %copy-start.5 = (f32[3,128,1536]{2,1,0:T(8,128)S(1)}, f32[3,128,1536]{2,1,0:T(8,128)}, u32[]{:S(2)}) copy-start(f32[3,128,1536]{2,1,0:T(8,128)} %get-tuple-element.55) | copy-start | bytes 7077892
  213.6 30.0 %collective-permute-start.1 = (bf16[3,128,1536]{2,1,0:T(8,128)(2,1)}, bf16[3,128,1536]{2,1,0:T(8,128)(2,1)S(1)}, u32[]{:S(2)}, u32[]{:S(2)}) collective-permute-start(bf16[3,128,1536]{2,1,0:T(8,128)(2,1)} %add_convert_fusion.6), channel_id=1, source_target_pairs={{0,1},{4,5},{8,9},{12,13},{16,17},{20,21},{24,25},{28,29}} | collective-permute-start | bytes 3538952 | tf_op jit(solution)/shard_map/ppermute | solution.py:811
  245.7 10.9 collective-permute-start.2
  247.4 662.3 %reduce-scatter.20.cloned.1.call-start = ((), (), s32[]{:S(2)}) async-start(), calls=%async_computation.23 | async-start | bytes 3932160 | tf_op jit(solution)/shard_map/reduce_scatter | solution.py:961
  256.6 6.0 copy-start.41
  256.6 6.9 copy-start.35
  256.6 6.9 copy-start.37
  258.9 7.7 copy-start.31
  258.9 41.8 %collective-permute-start.3 = (bf16[3,128,1536]{2,1,0:T(8,128)(2,1)}, bf16[3,128,1536]{2,1,0:T(8,128)(2,1)S(1)}, u32[]{:S(2)}, u32[]{:S(2)}) collective-permute-start(bf16[3,128,1536]{2,1,0:T(8,128)(2,1)} %add_convert_fusion.4), channel_id=1, source_target_pairs={{2,3},{6,7},{10,11},{14,15},{18,19},{22,23},{26,27},{30,31}} | collective-permute-start | bytes 3538952 | tf_op jit(solution)/shard_map/ppermute | solution.py:811
  301.9 26.8 %copy-start.3 = (bf16[3,512,1024]{2,1,0:T(8,128)(2,1)S(1)}, bf16[3,512,1024]{2,1,0:T(8,128)(2,1)}, u32[]{:S(2)}) copy-start(bf16[3,512,1024]{2,1,0:T(8,128)(2,1)} %param.19) | copy-start | bytes 9437188
  343.9 48.6 %copy-start.13 = (bf16[1536,1024]{1,0:T(8,128)(2,1)}, bf16[1536,1024]{1,0:T(8,128)(2,1)S(1)}, u32[]{:S(2)}) copy-start(bf16[1536,1024]{1,0:T(8,128)(2,1)S(1)} %multiply_convert_fusion.2) | copy-start | bytes 9437188
  403.8 116.0 %copy-start.7 = (bf16[3,512,1024]{2,1,0:T(8,128)(2,1)S(1)}, bf16[3,512,1024]{2,1,0:T(8,128)(2,1)}, u32[]{:S(2)}) copy-start(bf16[3,512,1024]{2,1,0:T(8,128)(2,1)} %param.37) | copy-start | bytes 9437188
  576.3 11.9 copy-start.42
  576.3 22.2 %slice-start = ((s8[6291456]{0:T(1024)(128)(4,1)}), s8[4194304]{0:T(1024)(128)(4,1)S(1)}, s32[]{:S(2)}) async-start(s8[6291456]{0:T(1024)(128)(4,1)} %bitcast.119), calls=%async_computation.38 | async-start | bytes 8388608
  588.2 10.4 slice-start.1
  607.7 9.5 copy-start.15
  617.2 8.7 copy-start.44
  661.8 297.6 %reduce-scatter.30.cloned.1.call-start = ((), (), s32[]{:S(2)}) async-start(), calls=%async_computation.28 | async-start | bytes 1179648 | tf_op jit(solution)/shard_map/reduce_scatter | solution.py:923
  662.4 297.6 %reduce-scatter.26.cloned.1.call-start = ((), (), s32[]{:S(2)}) async-start(), calls=%async_computation.26 | async-start | bytes 3538944 | tf_op jit(solution)/shard_map/reduce_scatter | solution.py:923
  663.2 315.2 %reduce-scatter.34.cloned.1.call-start = ((), (), s32[]{:S(2)}) async-start(), calls=%async_computation.30 | async-start | bytes 4718592 | tf_op jit(solution)/shard_map/reduce_scatter | solution.py:923
  663.7 316.6 %reduce-scatter.38.cloned.1.call-start = ((), (), s32[]{:S(2)}) async-start(), calls=%async_computation.32 | async-start | bytes 4718592 | tf_op jit(solution)/shard_map/reduce_scatter | solution.py:923
  664.5 370.8 %reduce-scatter.42.cloned.1.call-start = ((), (), s32[]{:S(2)}) async-start(), calls=%async_computation.34 | async-start | bytes 4718592 | tf_op jit(solution)/shard_map/reduce_scatter | solution.py:923
  664.5 24.8 %copy-start.24 = (f32[3,1536]{1,0:T(4,128)S(1)}, f32[3,1536]{1,0:T(4,128)}, u32[]{:S(2)}) copy-start(f32[3,1536]{1,0:T(4,128)} %copy-done.23) | copy-start | bytes 55300
  691.3 0.7 collective-permute-start.4
  693.6 6.5 copy-start.4
  693.6 1.8 collective-permute-start.5
  698.7 5.7 copy-start.28
  698.7 5.7 copy-start.30
  698.7 5.7 copy-start.33
  698.7 6.4 copy-start.26
  698.7 133.5 %collective-permute-start.6 = (bf16[3,128,1536]{2,1,0:T(8,128)(2,1)}, bf16[3,128,1536]{2,1,0:T(8,128)(2,1)}, u32[]{:S(2)}, u32[]{:S(2)}) collective-permute-start(bf16[3,128,1536]{2,1,0:T(8,128)(2,1)} %add_convert_fusion.1), channel_id=1, source_target_pairs={{1,0},{5,4},{9,8},{13,12},{17,16},{21,20},{25,24},{29,28}} | collective-permute-start | bytes 3538952 | tf_op jit(solution)/shard_map/ppermute | solution.py:811
  705.1 373.1 %reduce-scatter.46.cloned.1.call-start = ((), (), s32[]{:S(2)}) async-start(), calls=%async_computation.36 | async-start | bytes 2064384
  900.8 5.9 collective-permute-start.7
  922.9 4.6 copy-start.21
  959.4 140.2 %reduce-scatter.32.cloned.1.call-start = ((), (), s32[]{:S(2)}) async-start(), calls=%async_computation.29 | async-start | bytes 163840 | tf_op jit(solution)/shard_map/reduce_scatter | solution.py:924
  960.0 160.6 %reduce-scatter.28.cloned.1.call-start = ((), (), s32[]{:S(2)}) async-start(), calls=%async_computation.27 | async-start | bytes 491520 | tf_op jit(solution)/shard_map/reduce_scatter | solution.py:924
  960.5 227.2 %reduce-scatter.22.cloned.1.call-start = ((), (), s32[]{:S(2)}) async-start(), calls=%async_computation.24 | async-start | bytes 7962624 | tf_op jit(solution)/shard_map/reduce_scatter | solution.py:923
  978.2 233.5 %reduce-scatter.36.cloned.1.call-start = ((), (), s32[]{:S(2)}) async-start(), calls=%async_computation.31 | async-start | bytes 655360 | tf_op jit(solution)/shard_map/reduce_scatter | solution.py:924
  979.0 254.9 %reduce-scatter.40.cloned.1.call-start = ((), (), s32[]{:S(2)}) async-start(), calls=%async_computation.33 | async-start | bytes 655360 | tf_op jit(solution)/shard_map/reduce_scatter | solution.py:924
  980.4 275.9 %reduce-scatter.44.cloned.1.call-start = ((), (), s32[]{:S(2)}) async-start(), calls=%async_computation.35 | async-start | bytes 655360 | tf_op jit(solution)/shard_map/reduce_scatter | solution.py:924
  1035.3 241.1 %reduce-scatter.48.cloned.1.call-start = ((), (), s32[]{:S(2)}) async-start(), calls=%async_computation.37 | async-start | bytes 286720 | tf_op jit(solution)/shard_map/reduce_scatter | solution.py:924
  1037.1 1.2 collective-permute-start.8
  1038.3 3.7 collective-permute-start.9
  1042.0 3.6 collective-permute-start.10
  1045.6 44.8 %collective-permute-start.11 = (f32[3,24]{1,0:T(4,128)S(1)}, f32[3,24]{1,0:T(4,128)S(1)}, u32[]{:S(2)}, u32[]{:S(2)}) collective-permute-start(f32[3,24]{1,0:T(4,128)S(1)} %add.212), channel_id=1, source_target_pairs={{0,1},{1,0},{2,3},{3,2},{4,5},{5,4},{6,7},{7,6},{8,9},{9,8},{10,11... | collective-permute-start | bytes 872 | tf_op jit(solution)/shard_map/ppermute | solution.py:821
  1078.2 223.4 %reduce-scatter.24.cloned.1.call-start = ((), (), s32[]{:S(2)}) async-start(), calls=%async_computation.25 | async-start | bytes 1105920 | tf_op jit(solution)/shard_map/reduce_scatter | solution.py:924
  1090.3 10.6 collective-permute-start.12
  (19 other events, 40.2 us)
Sparse Core Ops, SparseCore 0:
  14.1 58.4 all-gather.8
  76.0 71.5 all-gather.10
  149.1 62.0 all-gather.14
  214.0 53.2 all-gather.16
  270.1 58.5 all-gather.12
  331.5 60.9 all-gather.18
  395.5 60.6 all-gather.20
  459.2 60.6 all-gather.22
  662.0 119.9 reduce-scatter.19
  785.0 36.0 reduce-scatter.29
  824.5 46.2 reduce-scatter.25
  874.4 51.2 reduce-scatter.33
  929.1 51.2 reduce-scatter.37
  984.0 51.3 reduce-scatter.41
  1038.5 39.6 reduce-scatter.45
  1080.3 19.1 reduce-scatter.31
  1101.8 18.7 reduce-scatter.27
  1123.9 63.7 reduce-scatter.21
  1190.1 21.6 reduce-scatter.35
  1214.0 19.8 reduce-scatter.39
  1236.3 19.9 reduce-scatter.43
  1258.7 17.7 reduce-scatter.47
  1278.8 22.8 reduce-scatter.23

commit v3 on v2

--- a/solution.py
+++ b/solution.py
@@ -1,3 +1,4 @@
+import functools
 import jax
 import jax.numpy as jnp
 from jax import lax
@@ -89,24 +90,26 @@
     )(x, gain, w_first, cosine, sine)
 
 
-def visible(segk_ref, segq, query_row, at):
-    segk = segk_ref[0, pl.ds(at, KEY_TILE), :]
-    key_col = at + lax.broadcasted_iota(jnp.int32, (KEY_TILE, 1), 0)
+def visible(segk_ref, segq, query_row, at, key_rows):
+    segk = segk_ref[0, pl.ds(at, key_rows), :]
+    key_col = at + lax.broadcasted_iota(jnp.int32, (key_rows, 1), 0)
     return jnp.where((segk == segq) & (key_col <= query_row), 0.0, MASKED)
 
 
 def attend_kernel(
-    low_ref, high_ref, base_ref, q_ref, kv_ref, segk_ref, segq_ref, out_ref, lse_ref,
+    place_at, low_ref, high_ref, base_ref, q_ref, kv_ref, segk_ref, segq_ref, out_ref, lse_ref,
     q_s, m_s, l_s, acc_s,
 ):
-    seq, tile = pl.program_id(0), pl.program_id(1)
+    tile = pl.program_id(0)
     rows = q_ref.shape[1]
-    place = seq * pl.num_programs(1) + tile
+    place = place_at + tile
     lane = lanes((rows, 128))
     for pair in range(QH // 2):
         both = q_ref[0, :, pair * 128 : (pair + 1) * 128].astype(F32)
         q_s[2 * pair] = jnp.where(lane < 64, both, 0.0).astype(BF16)
         q_s[2 * pair + 1] = jnp.where(lane < 64, pltpu.roll(both, 64, 1), 0.0).astype(BF16)
+    key_rows = min(KEY_TILE, kv_ref.shape[2])
+    tiles_each = kv_ref.shape[2] // key_rows
     m_s[...] = jnp.full(m_s.shape, MASKED, F32)
     l_s[...] = jnp.zeros(l_s.shape, F32)
     acc_s[...] = jnp.zeros(acc_s.shape, F32)
@@ -115,23 +118,28 @@
     factor = HD ** (-0.5) * LOG2E
 
     def step(key_tile, carry):
-        at = pl.multiple_of(key_tile * KEY_TILE, KEY_TILE)
-        bias = visible(segk_ref, segq, query_row, at)
+        at = pl.multiple_of(key_tile * key_rows, key_rows)
+        source = key_tile // tiles_each
+        offset = pl.multiple_of((key_tile % tiles_each) * key_rows, key_rows)
+        bias = visible(segk_ref, segq, query_row, at, key_rows)
         for group in range(KVH):
-            kv = kv_ref[0, pl.ds(at, KEY_TILE), group * 128 : (group + 1) * 128]
+            kv = kv_ref[source, 0, pl.ds(offset, key_rows), group * 128 : (group + 1) * 128]
             kv_t = kv.astype(F32).T.astype(BF16)
-            for member in range(QH // KVH):
-                head = group * (QH // KVH) + member
-                scores = contract(kv, q_s[head], 1, 1) * factor + bias
-                before = m_s[head : head + 1, :]
-                top = jnp.maximum(before, jnp.max(scores, axis=0, keepdims=True))
-                weights = jnp.exp2(scores - top)
-                fade = jnp.exp2(before - top)
-                l_s[head : head + 1, :] = l_s[head : head + 1, :] * fade + jnp.sum(
-                    weights, axis=0, keepdims=True
-                )
-                acc_s[head] = acc_s[head] * fade + contract(kv_t, weights.astype(BF16), 1, 0)
-                m_s[head : head + 1, :] = top
+            members = range(group * (QH // KVH), (group + 1) * (QH // KVH))
+            scores = [contract(kv, q_s[head], 1, 1) * factor + bias for head in members]
+            before = [m_s[head : head + 1, :] for head in members]
+            tops = [
+                jnp.maximum(old, jnp.max(part, axis=0, keepdims=True))
+                for old, part in zip(before, scores)
+            ]
+            weights = [jnp.exp2(part - top) for part, top in zip(scores, tops)]
+            sums = [jnp.sum(part, axis=0, keepdims=True) for part in weights]
+            outs = [contract(kv_t, part.astype(BF16), 1, 0) for part in weights]
+            for at_head, head in enumerate(members):
+                fade = jnp.exp2(before[at_head] - tops[at_head])
+                l_s[head : head + 1, :] = l_s[head : head + 1, :] * fade + sums[at_head]
+                acc_s[head] = acc_s[head] * fade + outs[at_head]
+                m_s[head : head + 1, :] = tops[at_head]
         return carry
 
     lax.fori_loop(low_ref[place], high_ref[place], step, 0)
@@ -145,13 +153,13 @@
 
 
 def attend_back_kernel(
-    low_ref, high_ref, base_ref, q_ref, kv_ref, segk_ref, segq_ref, att_ref, gatt_ref, lse_ref,
+    place_at, low_ref, high_ref, base_ref, q_ref, kv_ref, segk_ref, segq_ref, att_ref, gatt_ref, lse_ref,
     cos_ref, sin_ref, dq_ref, dkv_ref,
     q_s, g_s, delta_s, dq_s, dkv_s,
 ):
-    seq, tile = pl.program_id(0), pl.program_id(1)
+    tile = pl.program_id(0)
     rows = q_ref.shape[1]
-    place = seq * pl.num_programs(1) + tile
+    place = place_at + tile
     lane = lanes((rows, 128))
 
     @pl.when(tile == 0)
@@ -169,6 +177,8 @@
         product = (grad * att_ref[0, :, cols].astype(F32)).T
         delta_s[2 * pair : 2 * pair + 1, :] = jnp.sum(product[:64], axis=0, keepdims=True)
         delta_s[2 * pair + 1 : 2 * pair + 2, :] = jnp.sum(product[64:], axis=0, keepdims=True)
+    key_rows = min(KEY_TILE, kv_ref.shape[2])
+    tiles_each = kv_ref.shape[2] // key_rows
     dq_s[...] = jnp.zeros(dq_s.shape, F32)
     query_row = base_ref[0] + tile * rows + lanes((1, rows))
     segq = segq_ref[0]
@@ -176,12 +186,14 @@
     factor = qk_scale * LOG2E
 
     def step(key_tile, carry):
-        at = pl.multiple_of(key_tile * KEY_TILE, KEY_TILE)
-        bias = visible(segk_ref, segq, query_row, at)
+        at = pl.multiple_of(key_tile * key_rows, key_rows)
+        source = key_tile // tiles_each
+        offset = pl.multiple_of((key_tile % tiles_each) * key_rows, key_rows)
+        bias = visible(segk_ref, segq, query_row, at, key_rows)
         for group in range(KVH):
-            kv = kv_ref[0, pl.ds(at, KEY_TILE), group * 128 : (group + 1) * 128]
+            kv = kv_ref[source, 0, pl.ds(offset, key_rows), group * 128 : (group + 1) * 128]
             kv_t = kv.astype(F32).T.astype(BF16)
-            total = jnp.zeros((KEY_TILE, 128), F32)
+            total = jnp.zeros((key_rows, 128), F32)
             for member in range(QH // KVH):
                 head = group * (QH // KVH) + member
                 q, g = q_s[head], g_s[head]
@@ -192,7 +204,7 @@
                 total = total + contract(d_scores, q, 1, 0) + contract(probs.astype(BF16), g, 1, 0)
                 dq_s[head] += contract(kv_t, d_scores, 1, 0)
             cols = slice(group * 128, (group + 1) * 128)
-            dkv_s[pl.ds(at, KEY_TILE), cols] += total
+            dkv_s[source, 0, pl.ds(offset, key_rows), cols] += total
         return carry
 
     lax.fori_loop(low_ref[place], high_ref[place], step, 0)
@@ -205,30 +217,33 @@
             lane < 64, even, pltpu.roll(odd, 64, 1)
         ).astype(BF16)
 
-    @pl.when(tile == pl.num_programs(1) - 1)
+    @pl.when(tile == pl.num_programs(0) - 1)
     def _():
-        dkv_ref[0] = dkv_s[...].astype(BF16)
-
-
-def attention_specs(seqs, span, length, rows):
-    tile = lambda cols: pl.BlockSpec((1, rows, cols), lambda s, t, *_: (s, t, 0))
-    whole = lambda cols: pl.BlockSpec((1, length, cols), lambda s, t, *_: (s, 0, 0))
-    row = lambda n: pl.BlockSpec((1, n, rows), lambda s, t, *_: (s, 0, t))
-    return tile, whole, row
-
-
-def attend(bounds, q, kv_all, segk, segq):
-    seqs, span, q_width = q.shape
-    length, kv_width = kv_all.shape[1:]
+        dkv_ref[...] = dkv_s[...].astype(BF16)
+
+
+def attention_specs(seq, length, rows):
+    tile = lambda cols, at=seq: pl.BlockSpec((1, rows, cols), lambda t, *_: (at, t, 0))
+    whole = lambda cols, at=seq: pl.BlockSpec((1, length, cols), lambda t, *_: (at, 0, 0))
+    keys = lambda array, at=seq: pl.BlockSpec(
+        (array.shape[0], 1) + array.shape[2:], lambda t, *_: (0, at, 0, 0)
+    )
+    row = lambda n, at=seq: pl.BlockSpec((1, n, rows), lambda t, *_: (at, 0, t))
+    return tile, whole, keys, row
+
+
+def attend(seq, bounds, q, kv_all, segk, segq):
+    _, span, q_width = q.shape
     rows = min(256, span)
-    tile, whole, row = attention_specs(seqs, span, length, rows)
+    tile, whole, keys, row = attention_specs(seq, segk.shape[1], rows)
+    own_keys = kv_all.shape[:1] + (1,) + kv_all.shape[2:]
     return pl.pallas_call(
-        attend_kernel,
+        functools.partial(attend_kernel, seq * (span // rows)),
         grid_spec=pltpu.PrefetchScalarGridSpec(
             num_scalar_prefetch=3,
-            grid=(seqs, span // rows),
-            in_specs=[tile(q_width), whole(kv_width), whole(1), row(1)],
-            out_specs=[tile(q_width), row(QH)],
+            grid=(span // rows,),
+            in_specs=[tile(q_width), keys(kv_all), whole(1), row(1)],
+            out_specs=[tile(q_width, 0), row(QH, 0)],
             scratch_shapes=[
                 pltpu.VMEM((QH, rows, 128), BF16),
                 pltpu.VMEM((QH, rows), F32),
@@ -237,40 +252,40 @@
             ],
         ),
         out_shape=[
-            jax.ShapeDtypeStruct(q.shape, BF16),
-            jax.ShapeDtypeStruct((seqs, QH, span), F32),
+            jax.ShapeDtypeStruct((1, span, q_width), BF16),
+            jax.ShapeDtypeStruct((1, QH, span), F32),
         ],
         compiler_params=pltpu.CompilerParams(vmem_limit_bytes=VMEM_BYTES),
         name="attend",
     )(*bounds, q, kv_all, segk, segq)
 
 
-def attend_back(bounds, q, kv_all, segk, segq, att, grad_att, lse, cosine, sine):
-    seqs, span, q_width = q.shape
-    length, kv_width = kv_all.shape[1:]
+def attend_back(seq, bounds, q, kv_all, segk, segq, att, grad_att, lse, cosine, sine):
+    _, span, q_width = q.shape
     rows = min(256, span)
-    tile, whole, row = attention_specs(seqs, span, length, rows)
+    tile, whole, keys, row = attention_specs(seq, segk.shape[1], rows)
+    own_keys = kv_all.shape[:1] + (1,) + kv_all.shape[2:]
     return pl.pallas_call(
-        attend_back_kernel,
+        functools.partial(attend_back_kernel, seq * (span // rows)),
         grid_spec=pltpu.PrefetchScalarGridSpec(
             num_scalar_prefetch=3,
-            grid=(seqs, span // rows),
+            grid=(span // rows,),
             in_specs=[
-                tile(q_width), whole(kv_width), whole(1), row(1), tile(q_width), tile(q_width),
-                row(QH), tile(128), tile(128),
+                tile(q_width), keys(kv_all), whole(1), row(1), tile(q_width, 0), tile(q_width),
+                row(QH, 0), tile(128), tile(128),
             ],
-            out_specs=[tile(q_width), whole(kv_width)],
+            out_specs=[tile(q_width, 0), keys(kv_all, 0)],
             scratch_shapes=[
                 pltpu.VMEM((QH, rows, 128), BF16),
                 pltpu.VMEM((QH, rows, 128), BF16),
                 pltpu.VMEM((QH, rows), F32),
                 pltpu.VMEM((QH, 128, rows), F32),
-                pltpu.VMEM((length, kv_width), F32),
+                pltpu.VMEM(own_keys, F32),
             ],
         ),
         out_shape=[
-            jax.ShapeDtypeStruct(q.shape, BF16),
-            jax.ShapeDtypeStruct(kv_all.shape, BF16),
+            jax.ShapeDtypeStruct((1, span, q_width), BF16),
+            jax.ShapeDtypeStruct(own_keys, BF16),
         ],
         compiler_params=pltpu.CompilerParams(vmem_limit_bytes=VMEM_BYTES),
         name="attend_back",
@@ -291,14 +306,14 @@
 
 def attention_bounds(segments, seg_own, span_start):
     seqs, span = seg_own.shape
-    rows = min(256, span)
+    rows, key_rows = min(256, span), min(KEY_TILE, span)
     first = seg_own[:, ::rows]
     begin = jnp.sum((segments[:, None, :] < first[:, :, None]).astype(jnp.int32), axis=2)
     tiles = jnp.arange(span // rows, dtype=jnp.int32)
-    high = (span_start + (tiles + 1) * rows + KEY_TILE - 1) // KEY_TILE
+    high = (span_start + (tiles + 1) * rows + key_rows - 1) // key_rows
     high = jnp.broadcast_to(high[None], first.shape)
     return (
-        (begin // KEY_TILE).reshape(-1),
+        (begin // key_rows).reshape(-1),
         high.reshape(-1).astype(jnp.int32),
         jnp.full((1,), span_start, jnp.int32),
     )
@@ -377,7 +392,7 @@
     act_ref, states_ref, gains_ref, final_ref, final_gain_ref,
     ext_s, state_s, gain_s,
 ):
-    chunk = pl.program_id(1)
+    chunk = pl.program_id(0)
 
     @pl.when(chunk == 0)
     def _():
@@ -407,7 +422,7 @@
     state_s[...] = state
     gain_s[...] = before * gain_rows
 
-    @pl.when(chunk == pl.num_programs(1) - 1)
+    @pl.when(chunk == pl.num_programs(0) - 1)
     def _():
         final_ref[0] = state
         final_gain_ref[0] = before * gain_rows
@@ -486,9 +501,9 @@
     gy_ref, dgate_ref, gstates_ref, gains_ref, final_ref, dgain_ref, dskip_ref,
     state_s, gain_s, dgain_s, dskip_s,
 ):
-    seq, chunk = pl.program_id(0), pl.program_id(1)
-
-    @pl.when((seq == 0) & (chunk == 0))
+    chunk = pl.program_id(0)
+
+    @pl.when(chunk == 0)
     def _():
         dgain_s[...] = jnp.zeros(dgain_s.shape, F32)
         dskip_s[...] = jnp.zeros(dskip_s.shape, F32)
@@ -527,7 +542,7 @@
     state_s[...] = state
     gain_s[...] = after * gain_rows
 
-    @pl.when(chunk == pl.num_programs(1) - 1)
+    @pl.when(chunk == pl.num_programs(0) - 1)
     def _():
         final_ref[0] = state
 
@@ -542,10 +557,10 @@
     dproj_ref, drim_ref, dconv_ref, dhead_ref,
     ext_s, grad_s, carry_s, dconv_s, dhead_s,
 ):
-    seq, step_index = pl.program_id(0), pl.program_id(1)
-    last_step = pl.num_programs(1) - 1
-
-    @pl.when((seq == 0) & (step_index == 0))
+    step_index = pl.program_id(0)
+    last_step = pl.num_programs(0) - 1
+
+    @pl.when(step_index == 0)
     def _():
         dconv_s[...] = jnp.zeros(dconv_s.shape, F32)
         dhead_s[...] = jnp.zeros(dhead_s.shape, F32)
@@ -642,138 +657,135 @@
     dhead_ref[...] = dhead_s[...]
 
 
-def mixer_specs(chunks, reverse):
+def mixer_call(kernel, name, seq, chunks, reverse, inputs, outputs, scratch, earlier):
     place = (lambda c: chunks - 1 - c) if reverse else (lambda c: c)
-    block = lambda cols: pl.BlockSpec((1, CHUNK, cols), lambda s, c: (s, place(c), 0))
-    per_chunk = lambda rows, cols: pl.BlockSpec(
-        (1, 1, rows, cols), lambda s, c: (s, place(c), 0, 0)
-    )
-    per_seq = lambda rows, cols: pl.BlockSpec((1, rows, cols), lambda s, c: (s, 0, 0))
-    fixed = lambda rows, cols: pl.BlockSpec((rows, cols), lambda s, c: (0, 0))
-    return block, per_chunk, per_seq, fixed
-
-
-MIXER_PARAMS = pltpu.CompilerParams(vmem_limit_bytes=VMEM_BYTES)
-
-
-def mixer_scan(proj, rim, token, heads, taps, shift, spread):
-    seqs, span, width = proj.shape
+    kinds = {
+        "block": lambda array, at: pl.BlockSpec(
+            (1, CHUNK, array.shape[2]), lambda c: (at, place(c), 0)
+        ),
+        "chunk": lambda array, at: pl.BlockSpec(
+            (1, 1) + array.shape[2:], lambda c: (at, place(c), 0, 0)
+        ),
+        "seq": lambda array, at: pl.BlockSpec((1,) + array.shape[1:], lambda c: (at, 0, 0)),
+        "own": lambda array, at: pl.BlockSpec((1,) + array.shape[1:], lambda c: (0, 0, 0)),
+        "fixed": lambda array, at: pl.BlockSpec(array.shape, lambda c: (0, 0)),
+        "halo": lambda array, at: pl.BlockSpec(
+            (1, 16, array.shape[2]),
+            lambda c: (at, jnp.maximum(place(c) * (CHUNK // 16) - 1, 0), 0),
+        ),
+    }
+    arrays = [array for _, array in inputs]
+    in_specs = [kinds[kind](array, seq) for kind, array in inputs]
+    out_specs = [kinds[kind](shape, seq) for kind, shape in outputs]
+    count = len(inputs)
+    aliases, kept = {}, 0
+    if earlier is not None:
+        shared = [i for i, (kind, _) in enumerate(outputs) if kind in ("block", "chunk")]
+        aliases = {count + i: out for i, out in enumerate(shared)}
+        arrays += [earlier[out] for out in shared]
+        in_specs += [pl.BlockSpec(memory_space=pl.ANY)] * len(shared)
+        kept = len(shared)
+
+    def run(*refs):
+        kernel(*refs[:count], *refs[count + kept :])
+
+    return pl.pallas_call(
+        run,
+        grid=(chunks,),
+        in_specs=in_specs,
+        out_specs=out_specs,
+        out_shape=[shape for _, shape in outputs],
+        scratch_shapes=[pltpu.VMEM(shape, F32) for shape in scratch],
+        input_output_aliases=aliases,
+        compiler_params=pltpu.CompilerParams(vmem_limit_bytes=VMEM_BYTES),
+        name=name,
+    )(*arrays)
+
+
+def mixer_scan(seq, earlier, proj, rim, token, heads, taps, shift, spread):
+    seqs, span, _ = proj.shape
     chunks = span // CHUNK
-    block, per_chunk, per_seq, fixed = mixer_specs(chunks, False)
-    return pl.pallas_call(
-        mixer_scan_kernel,
-        grid=(seqs, chunks),
-        in_specs=[
-            block(width), per_seq(8, CC), block(128), fixed(8, 128), fixed(8, CC), fixed(1, CC),
-            fixed(128, DI),
-        ],
-        out_specs=[
-            block(CC), per_chunk(NS, DI), per_chunk(8, 128), per_seq(NS, DI), per_seq(8, 128),
-        ],
-        out_shape=[
-            jax.ShapeDtypeStruct((seqs, span, CC), BF16),
-            jax.ShapeDtypeStruct((seqs, chunks, NS, DI), BF16),
-            jax.ShapeDtypeStruct((seqs, chunks, 8, 128), F32),
-            jax.ShapeDtypeStruct((seqs, NS, DI), F32),
-            jax.ShapeDtypeStruct((seqs, 8, 128), F32),
-        ],
-        scratch_shapes=[
-            pltpu.VMEM((CHUNK + 8, CC), F32), pltpu.VMEM((NS, DI), F32), pltpu.VMEM((8, 128), F32),
-        ],
-        compiler_params=MIXER_PARAMS,
-        name="mixer_scan",
-    )(proj, rim, token, heads, taps, shift, spread)
-
-
-def mixer_out(proj, act, token, states, gains, state, heads, skip, gain, spread):
-    seqs, span, width = proj.shape
-    block, per_chunk, per_seq, fixed = mixer_specs(span // CHUNK, False)
-    return pl.pallas_call(
-        mixer_out_kernel,
-        grid=(seqs, span // CHUNK),
-        in_specs=[
-            block(width), block(CC), block(128), per_chunk(NS, DI), per_chunk(8, 128),
-            per_seq(NS, DI), fixed(8, 128), fixed(1, DI), fixed(1, DI), fixed(128, DI),
-        ],
-        out_specs=[block(DI), block(DI)],
-        out_shape=[
-            jax.ShapeDtypeStruct((seqs, span, DI), F32),
-            jax.ShapeDtypeStruct((seqs, span, DI), BF16),
-        ],
-        compiler_params=MIXER_PARAMS,
-        name="mixer_out",
-    )(proj, act, token, states, gains, state, heads, skip, gain, spread)
-
-
-def mixer_gate_back(gmix, y, proj, act, token, heads, gain, spread):
-    seqs, span, width = proj.shape
+    return mixer_call(
+        mixer_scan_kernel, "mixer_scan", seq, chunks, False,
+        [
+            ("block", proj), ("seq", rim), ("block", token), ("fixed", heads), ("fixed", taps),
+            ("fixed", shift), ("fixed", spread),
+        ],
+        [
+            ("block", jax.ShapeDtypeStruct((seqs, span, CC), BF16)),
+            ("chunk", jax.ShapeDtypeStruct((seqs, chunks, NS, DI), BF16)),
+            ("chunk", jax.ShapeDtypeStruct((seqs, chunks, 8, 128), F32)),
+            ("own", jax.ShapeDtypeStruct((1, NS, DI), F32)),
+            ("own", jax.ShapeDtypeStruct((1, 8, 128), F32)),
+        ],
+        [(CHUNK + 8, CC), (NS, DI), (8, 128)],
+        earlier,
+    )
+
+
+def mixer_out(seq, earlier, proj, act, token, states, gains, state, heads, skip, gain, spread):
+    seqs, span, _ = proj.shape
+    return mixer_call(
+        mixer_out_kernel, "mixer_out", seq, span // CHUNK, False,
+        [
+            ("block", proj), ("block", act), ("block", token), ("chunk", states),
+            ("chunk", gains), ("own", state), ("fixed", heads), ("fixed", skip),
+            ("fixed", gain), ("fixed", spread),
+        ],
+        [
+            ("block", jax.ShapeDtypeStruct((seqs, span, DI), F32)),
+            ("block", jax.ShapeDtypeStruct((seqs, span, DI), BF16)),
+        ],
+        [],
+        earlier,
+    )
+
+
+def mixer_gate_back(seq, earlier, gmix, y, proj, act, token, heads, gain, spread):
+    seqs, span, _ = proj.shape
     chunks = span // CHUNK
-    block, per_chunk, per_seq, fixed = mixer_specs(chunks, True)
-    return pl.pallas_call(
-        mixer_gate_back_kernel,
-        grid=(seqs, chunks),
-        in_specs=[
-            block(DI), block(DI), block(width), block(CC), block(128), fixed(8, 128),
-            fixed(1, DI), fixed(128, DI),
-        ],
-        out_specs=[
-            block(DI), block(DI), per_chunk(NS, DI), per_chunk(8, 128), per_seq(NS, DI),
-            fixed(8, DI), fixed(8, DI),
-        ],
-        out_shape=[
-            jax.ShapeDtypeStruct((seqs, span, DI), BF16),
-            jax.ShapeDtypeStruct((seqs, span, DI), BF16),
-            jax.ShapeDtypeStruct((seqs, chunks, NS, DI), BF16),
-            jax.ShapeDtypeStruct((seqs, chunks, 8, 128), F32),
-            jax.ShapeDtypeStruct((seqs, NS, DI), F32),
-            jax.ShapeDtypeStruct((8, DI), F32),
-            jax.ShapeDtypeStruct((8, DI), F32),
-        ],
-        scratch_shapes=[
-            pltpu.VMEM((NS, DI), F32), pltpu.VMEM((8, 128), F32),
-            pltpu.VMEM((8, DI), F32), pltpu.VMEM((8, DI), F32),
-        ],
-        compiler_params=MIXER_PARAMS,
-        name="mixer_gate_back",
-    )(gmix, y, proj, act, token, heads, gain, spread)
+    return mixer_call(
+        mixer_gate_back_kernel, "mixer_gate_back", seq, chunks, True,
+        [
+            ("block", gmix), ("block", y), ("block", proj), ("block", act), ("block", token),
+            ("fixed", heads), ("fixed", gain), ("fixed", spread),
+        ],
+        [
+            ("block", jax.ShapeDtypeStruct((seqs, span, DI), BF16)),
+            ("block", jax.ShapeDtypeStruct((seqs, span, DI), BF16)),
+            ("chunk", jax.ShapeDtypeStruct((seqs, chunks, NS, DI), BF16)),
+            ("chunk", jax.ShapeDtypeStruct((seqs, chunks, 8, 128), F32)),
+            ("own", jax.ShapeDtypeStruct((1, NS, DI), F32)),
+            ("fixed", jax.ShapeDtypeStruct((8, DI), F32)),
+            ("fixed", jax.ShapeDtypeStruct((8, DI), F32)),
+        ],
+        [(NS, DI), (8, 128), (8, DI), (8, DI)],
+        earlier,
+    )
 
 
 def mixer_back(
-    gy, y, dgate, proj, rim, act, token, states, gains, state, gstates, ggains, gstate,
-    heads, skip, taps, shift, spread, spread_first,
+    seq, earlier, gy, y, dgate, proj, rim, act, token, states, gains, state, gstates, ggains,
+    gstate, heads, skip, taps, shift, spread, spread_first,
 ):
     seqs, span, width = proj.shape
-    chunks = span // CHUNK
-    block, per_chunk, per_seq, fixed = mixer_specs(chunks, True)
-    steps = CHUNK // 16
-    halo = pl.BlockSpec(
-        (1, 16, width), lambda s, c: (s, jnp.maximum((chunks - 1 - c) * steps - 1, 0), 0)
-    )
-    return pl.pallas_call(
-        mixer_back_kernel,
-        grid=(seqs, chunks),
-        in_specs=[
-            block(DI), block(DI), block(DI), block(width), halo, per_seq(8, CC), block(CC),
-            block(128), per_chunk(NS, DI), per_chunk(8, 128), per_seq(NS, DI),
-            per_chunk(NS, DI), per_chunk(8, 128), per_seq(NS, DI),
-            fixed(8, 128), fixed(1, DI), fixed(8, CC), fixed(1, CC), fixed(128, DI), fixed(32, DI),
-        ],
-        out_specs=[block(width), per_seq(8, CC), fixed(8, CC), fixed(8, 128)],
-        out_shape=[
-            jax.ShapeDtypeStruct((seqs, span, width), BF16),
-            jax.ShapeDtypeStruct((seqs, 8, CC), F32),
-            jax.ShapeDtypeStruct((8, CC), F32),
-            jax.ShapeDtypeStruct((8, 128), F32),
-        ],
-        scratch_shapes=[
-            pltpu.VMEM((CHUNK + 8, CC), F32), pltpu.VMEM((CHUNK + 8, CC), F32),
-            pltpu.VMEM((8, CC), F32), pltpu.VMEM((8, CC), F32), pltpu.VMEM((8, 128), F32),
-        ],
-        compiler_params=MIXER_PARAMS,
-        name="mixer_back",
-    )(
-        gy, y, dgate, proj, proj, rim, act, token, states, gains, state, gstates, ggains, gstate,
-        heads, skip, taps, shift, spread, spread_first,
+    return mixer_call(
+        mixer_back_kernel, "mixer_back", seq, span // CHUNK, True,
+        [
+            ("block", gy), ("block", y), ("block", dgate), ("block", proj), ("halo", proj),
+            ("seq", rim), ("block", act), ("block", token), ("chunk", states), ("chunk", gains),
+            ("own", state), ("chunk", gstates), ("chunk", ggains), ("own", gstate),
+            ("fixed", heads), ("fixed", skip), ("fixed", taps), ("fixed", shift),
+            ("fixed", spread), ("fixed", spread_first),
+        ],
+        [
+            ("block", jax.ShapeDtypeStruct((seqs, span, width), BF16)),
+            ("own", jax.ShapeDtypeStruct((1, 8, CC), F32)),
+            ("fixed", jax.ShapeDtypeStruct((8, CC), F32)),
+            ("fixed", jax.ShapeDtypeStruct((8, 128), F32)),
+        ],
+        [(CHUNK + 8, CC), (CHUNK + 8, CC), (8, CC), (8, CC), (8, 128)],
+        earlier,
     )
 
 
@@ -801,16 +813,37 @@
     return lax.ppermute(block, axis, route)
 
 
-def chain_states(local, gain, reverse):
-    count, place = lax.axis_size("ctx"), lax.axis_index("ctx")
-    state = jnp.zeros(local.shape, BF16)
-    for hop in range(count - 1):
-        source = count - 1 - hop if reverse else hop
-        target = source - 1 if reverse else source + 1
-        sent = (gain * state.astype(F32) + local).astype(BF16)
-        received = lax.ppermute(sent, "ctx", [(source, target)])
-        state = jnp.where(place == target, received, state)
-    return state
+def after(value, *earlier):
+    return lax.optimization_barrier((value, earlier))[0]
+
+
+class Chain:
+    def __init__(self, local, gain, reverse):
+        self.local, self.gain, self.reverse = local, gain, reverse
+        self.state, self.hop, self.flying = jnp.zeros(local.shape, BF16), 0, None
+        self.count, self.place = lax.axis_size("ctx"), lax.axis_index("ctx")
+
+    def send(self, *earlier):
+        if self.hop == self.count - 1:
+            return
+        source = self.count - 1 - self.hop if self.reverse else self.hop
+        target = source - 1 if self.reverse else source + 1
+        sent = after((self.gain * self.state.astype(F32) + self.local).astype(BF16), *earlier)
+        self.flying = (lax.ppermute(sent, "ctx", [(source, target)]), target)
+        self.hop += 1
+
+    def take(self):
+        if self.flying is None:
+            return
+        received, target = self.flying
+        self.state, self.flying = jnp.where(self.place == target, received, self.state), None
+
+    def finish(self):
+        self.take()
+        while self.hop < self.count - 1:
+            self.send()
+            self.take()
+        return self.state
 
 
 def sum_everywhere(values, axes):
@@ -821,6 +854,48 @@
             values = values + lax.ppermute(values, axis, route)
             distance *= 2
     return values
+
+
+def gather_all(shard):
+    count, place = lax.axis_size("ctx"), lax.axis_index("ctx")
+    devices, me = lax.axis_size("dp"), lax.axis_index("dp")
+    relative = [shard] + [
+        lax.ppermute(shard, "ctx", [(i, (i + d) % count) for i in range(count)])
+        for d in range(1, count)
+    ]
+    ordered = jnp.stack([relative[-k % count] for k in range(count)])
+    whole = lax.dynamic_slice_in_dim(
+        jnp.concatenate([ordered, ordered]), (count - place) % count, count, 0
+    )
+    bits = devices.bit_length() - 1
+    for bit in list(range(1, bits)) + [0]:
+        other = lax.ppermute(whole, "dp", [(i, i ^ (1 << bit)) for i in range(devices)])
+        low = ((me >> bit) & 1) == 0
+        whole = jnp.stack(
+            [jnp.where(low, whole, other), jnp.where(low, other, whole)],
+            axis=0 if bit else bits - 1,
+        )
+    return whole.reshape((-1,) + shard.shape[1:])
+
+
+def scatter_all(grad):
+    count, place = lax.axis_size("ctx"), lax.axis_index("ctx")
+    devices, me = lax.axis_size("dp"), lax.axis_index("dp")
+    bits = devices.bit_length() - 1
+    part = grad.reshape((2,) * bits + (count, -1, grad.shape[1]))
+    for bit in [0] + list(range(bits - 1, 0, -1)):
+        at = 0 if bit else bits - 1
+        first, second = (lax.index_in_dim(part, side, at, False) for side in range(2))
+        low = ((me >> bit) & 1) == 0
+        sent = jnp.where(low, second, first).astype(BF16)
+        received = lax.ppermute(sent, "dp", [(i, i ^ (1 << bit)) for i in range(devices)])
+        part = jnp.where(low, first, second).astype(F32) + received.astype(F32)
+    relative = lax.dynamic_slice_in_dim(jnp.concatenate([part, part]), place, count, 0)
+    total, rounded = relative[0], relative.astype(BF16)
+    for d in range(1, count):
+        route = [(i, (i + d) % count) for i in range(count)]
+        total = total + lax.ppermute(rounded[d], "ctx", route).astype(F32)
+    return total
 
 
 def rms_scale(values, gain_vec):
@@ -853,14 +928,24 @@
         [w_k.reshape(own_rows, KVH, HD), w_v.reshape(own_rows, KVH, HD)], axis=2
     ).reshape(own_rows, kv_width)
     gather = lambda shard: lax.all_gather(shard, axes, axis=0, tiled=True)
-    first_all = gather(jnp.concatenate([w_q, w_kv, small_block], axis=1))
+    first_all = gather_all(jnp.concatenate([w_q, w_kv, small_block], axis=1))
     in_width = DI + CC + 128
     w_in_all = gather(jnp.pad(w_in, ((0, 0), (0, in_width - w_in.shape[1]))))
-    w_out_all = gather(w_out)
-    w_o_all = gather(w_o.T)
-    w_gate_all = gather(w_gate)
-    w_up_all = gather(w_up)
-    w_down_all = gather(w_down)
+    turned_o = w_o.T
+    half_rows, ff = own_rows // 2, w_gate.shape[1]
+    rest = [w_down, w_out, jnp.concatenate([turned_o[:half_rows], turned_o[half_rows:]], axis=1)]
+    for matrix in (w_gate, w_up):
+        rest += [matrix[:, at : at + width] for at in range(0, ff, width)]
+    rest_sizes = [part.shape[0] for part in rest]
+    rest_all = gather(jnp.concatenate(rest, axis=0)).reshape(-1, sum(rest_sizes), width)
+    cuts, at = [], 0
+    for size in rest_sizes:
+        cuts.append(rest_all[:, at : at + size])
+        at += size
+    w_down_all, w_out_all = cuts[0].reshape(-1, width), cuts[1].reshape(-1, width)
+    w_o_all = jnp.stack([cuts[2][..., :q_width], cuts[2][..., q_width:]], axis=1)
+    w_o_all = w_o_all.reshape(width, q_width)
+    w_gu_all = jnp.concatenate([cut.reshape(width, width) for cut in cuts[3:]], axis=1)
     small_all = first_all[:, q_width + kv_width :].reshape(-1, slots).astype(F32)
     parts, at = [], 0
     for size in small_sizes:
@@ -879,6 +964,7 @@
         -1,
     )
     token = token_table(seg_own, seg_rim)
+    count = lax.axis_size("ctx")
     bounds = attention_bounds(segments, seg_own, span_start)
     segk, segq = segments[:, :, None], seg_own[:, None, :]
     cosine, sine = rope_tables(positions)
@@ -887,25 +973,50 @@
     spread, spread_first = spread_matrix(), spread_first_matrix()
 
     tokens = layer_input.reshape(rows, width)
+    small = (token, bounds, segk, segq, cosine, sine, heads, skip, spread, spread_first)
+    first_all, small = lax.optimization_barrier((first_all, small))
+    token, bounds, segk, segq, cosine, sine, heads, skip, spread, spread_first = small
     hidden, q, kv = project(
         tokens, gain1_all, first_all, cosine.reshape(rows, 128), sine.reshape(rows, 128)
     )
     q = q.reshape(seqs, span, q_width)
-    kv_all = lax.all_gather(kv.reshape(seqs, span, kv_width), "ctx", axis=1, tiled=True)
+    kv = kv.reshape(seqs, span, kv_width)
+    exchange = lambda blocks: lax.all_to_all(blocks, "ctx", 0, 0, tiled=True)
+    kv_all = exchange(jnp.broadcast_to(kv[None], (count,) + kv.shape))
+    edge = from_behind(hidden.reshape(seqs, span, width)[:, span - (KC - 1) :], "ctx", 1)
     proj = low_dot(hidden, w_in_all).astype(BF16).reshape(seqs, span, in_width)
-    rim = from_behind(proj[:, span - (KC - 1) :, DI : DI + CC], "ctx", 1)
-    rim = jnp.pad(rim, ((0, 0), (8 - (KC - 1), 0), (0, 0)))
-    act, states, gains, local_state, local_gain = mixer_scan(
-        proj, rim, token, heads, taps_all, shift_all, spread
-    )
-    wide_gain = jnp.repeat(local_gain[:, :1, :MH], MP, axis=2)
-    state_in = chain_states(local_state, wide_gain, False)
-    att, lse = attend(bounds, q, kv_all, segk, segq)
-    mixer_y, mixer_in = mixer_out(
-        proj, act, token, states, gains, state_in, heads, skip, gain_m_all, spread
-    )
+    rim = low_dot(edge.reshape(-1, width), w_in_all[:, DI : DI + CC]).astype(BF16)
+    rim = jnp.pad(rim.reshape(seqs, KC - 1, CC), ((0, 0), (8 - (KC - 1), 0), (0, 0)))
+    wide = lambda gain: jnp.repeat(gain[:, :1, :MH], MP, axis=2)
+    scanned, chains, wide_gains = None, [], []
+    for seq in range(seqs):
+        scanned = mixer_scan(
+            seq, scanned, proj, rim, token, heads, taps_all,
+            shift_all, spread,
+        )
+        wide_gains.append(wide(scanned[4]))
+        chains.append(Chain(scanned[3], wide_gains[seq], False))
+        chains[seq].send()
+    act, states, gains = scanned[:3]
+    atts, lses, mixed = [], [], None
+    for seq in range(seqs):
+        for chain in chains[: seq + 1]:
+            chain.take()
+            chain.send()
+        taken = [chain.state for chain in chains[: seq + 1]]
+        att, lse = attend(seq, bounds, after(q, act, *taken), kv_all, segk, segq)
+        atts.append(att)
+        lses.append(lse)
+    states_in = []
+    for seq in range(seqs):
+        states_in.append(chains[seq].finish())
+        mixed = mixer_out(
+            seq, mixed, proj, act, token, states, gains, states_in[seq], heads, skip, gain_m_all,
+            spread,
+        )
+    mixer_y, mixer_in = mixed
     mixer_in = mixer_in.reshape(rows, DI)
-    att_rows = att.reshape(rows, q_width)
+    att_rows = jnp.concatenate(atts, axis=0).reshape(rows, q_width)
     middle = (
         tokens.astype(F32)
         + low_dot(mixer_in, w_out_all)
@@ -913,15 +1024,15 @@
     )
     normed_mid, norm2_pull = jax.vjp(rms_scale, middle, gain2_all)
     normed_two = normed_mid.astype(BF16)
-    gate_lin = low_dot(normed_two, w_gate_all)
-    up_lin = low_dot(normed_two, w_up_all)
-    act_float, act_pull = jax.vjp(silu_product, gate_lin, up_lin)
+    gate_up = low_dot(normed_two, w_gu_all).astype(BF16)
+    act_float, act_pull = jax.vjp(
+        silu_product, gate_up[:, :ff].astype(F32), gate_up[:, ff:].astype(F32)
+    )
     act_rows = act_float.astype(BF16)
     layer_result = (middle + low_dot(act_rows, w_down_all)).astype(BF16)
 
     def scatter(grad):
-        part = lax.psum_scatter(grad, "dp", scatter_dimension=0, tiled=True)
-        return lax.psum_scatter(part, "ctx", scatter_dimension=0, tiled=True).astype(F32)
+        return lax.psum_scatter(grad, "dp", scatter_dimension=0, tiled=True)
 
     def weight_grad(left, right):
         return jnp.einsum("ri,ro->io", left, right, preferred_element_type=F32).astype(BF16)
@@ -931,15 +1042,12 @@
 
     cot_rows = cotangent.reshape(rows, width)
     grad_down = weight_grad(act_rows, cot_rows)
-    grad_gate_f, grad_up_f = act_pull(back_dot(cot_rows, w_down_all))
-    grad_gate_low, grad_up_low = grad_gate_f.astype(BF16), grad_up_f.astype(BF16)
-    grad_wgate = weight_grad(normed_two, grad_gate_low)
-    grad_wup = weight_grad(normed_two, grad_up_low)
-    grad_normed = back_dot(grad_gate_low, w_gate_all) + back_dot(grad_up_low, w_up_all)
-    grad_normed, grad_down, grad_wgate, grad_wup = lax.optimization_barrier(
-        (grad_normed, grad_down, grad_wgate, grad_wup)
-    )
-    out_down, out_gate, out_up = scatter(grad_down), scatter(grad_wgate), scatter(grad_wup)
+    grad_gate_up = jnp.concatenate(act_pull(back_dot(cot_rows, w_down_all)), axis=1).astype(BF16)
+    grad_wgu = weight_grad(normed_two, grad_gate_up)
+    grad_normed = back_dot(grad_gate_up, w_gu_all)
+    grad_normed, grad_down, grad_wgu = lax.optimization_barrier((grad_normed, grad_down, grad_wgu))
+    part_down = scatter(grad_down)
+    part_gu = scatter(grad_wgu)
     grad_mid_norm, grad_gain_second = norm2_pull(grad_normed)
     grad_middle = cot_rows.astype(F32) + grad_mid_norm
     grad_mid_low = grad_middle.astype(BF16)
@@ -950,27 +1058,66 @@
     grad_mixer_in, grad_att, grad_wout, grad_wo = lax.optimization_barrier(
         (grad_mixer_in, grad_att, grad_wout, grad_wo)
     )
-    out_wout, out_wo = scatter(grad_wout), scatter(grad_wo)
-    grad_y, grad_gate, gstates, ggains, local_gstate, grad_gain_mix, grad_skip = mixer_gate_back(
-        grad_mixer_in, mixer_y, proj, act, token, heads, gain_m_all, spread
-    )
-    gstate_out = chain_states(local_gstate, wide_gain, True)
-    dq, dkv_all = attend_back(
-        bounds, q, kv_all, segk, segq, att, grad_att, lse, cosine, sine
-    )
-    dkv = lax.psum_scatter(dkv_all, "ctx", scatter_dimension=1, tiled=True)
-    grad_proj, grad_rim, grad_conv, grad_heads = mixer_back(
-        grad_y, mixer_y, grad_gate, proj, rim, act, token, states, gains, state_in,
-        gstates, ggains, gstate_out, heads, skip, taps_all, shift_all, spread, spread_first,
-    )
+    grad_wo = grad_wo.reshape(-1, own_rows, q_width)
+    gated, chains, grad_gain_mix, grad_skip = None, [], 0.0, 0.0
+    for seq in range(seqs):
+        gated = mixer_gate_back(
+            seq, gated, grad_mixer_in, mixer_y, proj, act, token, heads, gain_m_all, spread
+        )
+        grad_gain_mix, grad_skip = grad_gain_mix + gated[5], grad_skip + gated[6]
+        chains.append(Chain(gated[4], wide_gains[seq], True))
+        chains[seq].send()
+    grad_y, grad_gate, gstates, ggains = gated[:4]
+    grad_wgates = weight_grad(hidden, grad_gate.reshape(rows, DI)).reshape(-1, own_rows, DI)
+    blocks = grad_wo.shape[0]
+    grad_out = jnp.concatenate(
+        [
+            grad_wout.reshape(blocks, -1, width),
+            jnp.concatenate([grad_wo[:, :half_rows], grad_wo[:, half_rows:]], axis=2),
+            grad_wgates[..., :width],
+            jnp.concatenate(
+                [grad_wgates[:, :half_rows, width:], grad_wgates[:, half_rows:, width:]], axis=2
+            ),
+        ],
+        axis=1,
+    )
+    part_out = scatter(after(grad_out.reshape(-1, width), part_gu))
+    dqs, dkvs = [], []
+    for seq in range(seqs):
+        for chain in chains[: seq + 1]:
+            chain.take()
+            chain.send(*dqs[-1:])
+        taken = [chain.state for chain in chains[: seq + 1]]
+        dq, dkv = attend_back(
+            seq, bounds, after(q, part_down if seq < seqs - 1 else part_gu, *taken), kv_all, segk,
+            segq, atts[seq], grad_att, lses[seq], cosine, sine,
+        )
+        dqs.append(dq)
+        dkvs.append(dkv)
+    dkv_all = exchange(jnp.concatenate(dkvs, axis=1))
+    dq = jnp.concatenate(dqs, axis=0)
+    last, rims, grad_conv, grad_heads = None, [], 0.0, 0.0
+    waits = [(grad_out,)] + [()] * (seqs - 1)
+    for seq in range(seqs):
+        gstate = chains[seq].finish()
+        last = mixer_back(
+            seq, last, after(grad_y, dqs[-1], *waits[seq]), mixer_y, grad_gate, proj, rim, act, token, states,
+            gains, states_in[seq], gstates, ggains, gstate, heads, skip, taps_all, shift_all,
+            spread, spread_first,
+        )
+        rims.append(last[1])
+        grad_conv, grad_heads = grad_conv + last[2], grad_heads + last[3]
+    grad_proj, grad_rim = last[0], jnp.concatenate(rims, axis=0)
     back_rim = from_behind(grad_rim[:, 8 - (KC - 1) :].astype(BF16), "ctx", -1)
     edge = grad_proj[:, span - (KC - 1) :, DI : DI + CC].astype(F32) + back_rim.astype(F32)
     grad_proj = lax.dynamic_update_slice(
-        grad_proj, edge.astype(BF16), (0, span - (KC - 1), DI)
+        grad_proj, after(edge.astype(BF16), part_out), (0, span - (KC - 1), DI)
     ).reshape(rows, in_width)
-    grad_win = weight_grad(hidden, grad_proj)
-    out_win = scatter(grad_win)[:, : w_in.shape[1]]
-    grad_kv = dkv.astype(F32).reshape(seqs, span, KVH, 2 * HD)
+    grad_wconv = weight_grad(hidden, grad_proj[:, DI:])
+    part_conv = scatter(grad_wconv)
+    grad_kv = jnp.sum(after(dkv_all, grad_wconv).astype(F32), axis=0)
+    out_conv = lax.psum_scatter(part_conv, "ctx", scatter_dimension=0, tiled=True).astype(F32)
+    grad_kv = grad_kv.reshape(seqs, span, KVH, 2 * HD)
     turned = grad_kv[..., :HD] * sine[:, :, None, :HD]
     turned = jnp.concatenate([turned[..., HD // 2 :], turned[..., : HD // 2]], axis=-1)
     grad_key = grad_kv[..., :HD] * cosine[:, :, None, :HD] + turned
@@ -979,7 +1126,7 @@
         [dq.reshape(rows, q_width), grad_kv.reshape(rows, kv_width)], axis=1
     )
     grad_wfirst = weight_grad(hidden, grad_first)
-    grad_hidden = back_dot(grad_proj, w_in_all) + back_dot(
+    grad_hidden = back_dot(after(grad_proj, grad_wconv), w_in_all) + back_dot(
         grad_first, first_all[:, : q_width + kv_width]
     )
     tokens_f = tokens.astype(F32)
@@ -999,9 +1146,36 @@
         axis=1,
     )
     small_grads = jnp.pad(small_grads, ((0, 0), (0, slots - small_grads.shape[1])))
-    out_first = scatter(
+    out_first = scatter_all(
         jnp.concatenate([grad_wfirst, small_grads.reshape(-1, 128).astype(BF16)], axis=1)
     )
+    parts = [part_down.reshape(count, -1, width), part_out.reshape(count, -1, width)]
+    rest_sizes = rest_sizes[:3] + [own_rows, half_rows] + rest_sizes[3:]
+    part_gu = part_gu.reshape(count, own_rows, 2 * ff)
+    parts += [part_gu[..., at : at + width] for at in range(0, 2 * ff, width)]
+    rest_out = lax.psum_scatter(
+        after(jnp.concatenate(parts, axis=1).reshape(-1, width), part_conv),
+        "ctx",
+        scatter_dimension=0,
+        tiled=True,
+    ).astype(F32)
+    outs, at = [], 0
+    for size in rest_sizes:
+        outs.append(rest_out[at : at + size])
+        at += size
+    out_down, out_wout = outs[0], outs[1]
+    out_wo = jnp.concatenate([outs[2][:, :q_width], outs[2][:, q_width:]], axis=0)
+    out_win = jnp.concatenate(
+        [
+            outs[3],
+            jnp.concatenate([outs[4][:, : DI - width], outs[4][:, DI - width :]], axis=0),
+            out_conv[:, : w_in.shape[1] - DI],
+        ],
+        axis=1,
+    )
+    halves = ff // width
+    out_gate = jnp.concatenate(outs[5 : 5 + halves], axis=1)
+    out_up = jnp.concatenate(outs[5 + halves :], axis=1)
     out_small = out_first[:, q_width + kv_width :].reshape(-1)
     pieces, at = [], 0
     for size in small_sizes:

time: 1320 us -> 987 us (0.75)
  waiting for transfers between devices: 702 us -> 220 us
  starting transfers between devices: 22.1 us -> 95.5 us
  local copies, waits for them, and re-layouts: 70.6 us -> 102 us
  other arithmetic: 75.3 us -> 106 us
  Pallas kernels: 207 us -> 234 us
  matrix products: 218 us -> 202 us
    all_gather x7 -> x2, waiting for transfers between devices: 263 us -> 0.04 us  [body(): gather = lambda shard: lax.all_gather(shard, axes, axis=0, tiled=True)]
    reduce_scatter x14 -> x6, waiting for transfers between devices: 239 us -> 114 us  [the longest x4 83 us: scatter(): return lax.psum_scatter(grad, 'dp', scatter_dimension=0, tiled=True)]
    ppermute x6 -> x30, waiting for transfers between devices: 153 us -> 100 us  [the longest x18 79.5 us: send(): self.flying = (lax.ppermute(sent, 'ctx', [(source, target)]), target)]
    unnamed x24 -> x8, waiting for transfers between devices: 37.7 us -> 0.13 us
    all_to_all x0 -> x2, starting transfers between devices: none -> 35.9 us  [body(): exchange = lambda blocks: lax.all_to_all(blocks, 'ctx', 0, 0, tiled=True)]
    ppermute x6 -> x30, starting transfers between devices: 9.38 us -> 41.1 us  [the longest x18 24.5 us: send(): self.flying = (lax.ppermute(sent, 'ctx', [(source, target)]), target)]
    pallas_call x6 -> x18, Pallas kernels: 196 us -> 223 us  [the longest x12 159 us: mixer_call(): pl.pallas_call(run, grid=(chunks,), in_specs=in_specs, out_specs=out_spec...]
    slice x5 -> x15, local copies, waits for them, and re-layouts: 3.48 us -> 23.5 us  [the longest x3 14.5 us: body(): cuts.append(rest_all[:, at:at + size])]
  transfers between devices with their start and end apart: 36 -> 47, of which waited for: 23 -> 13; matrix products, arithmetic and copies ran while one was open for 18% -> 28% of each run, Pallas kernels for 13% -> 24%
where the time goes in v3:
time: 987 us; the launch traced here: 976 us
  Pallas kernels  234 us (24%)
  waiting for transfers between devices  220 us (22%)
  matrix products  202 us (20%)
  other arithmetic  106 us (11%)
  local copies, waits for them, and re-layouts  102 us (10%)
  starting transfers between devices  95.5 us (10%)
  between operations  16 us (2%)
    pallas_call x12, Pallas kernels, mixer_call(): pl.pallas_call(run, grid=(chunks,), in_specs=in_specs, out_specs=out_spec...  159 us
    reduce_scatter x4, waiting for transfers between devices, scatter(): return lax.psum_scatter(grad, 'dp', scatter_dimension=0, tiled=True)  83 us
    ppermute x18, waiting for transfers between devices, send(): self.flying = (lax.ppermute(sent, 'ctx', [(source, target)]), target)  79.5 us
    dot_general x5, matrix products, back_dot(): return jnp.einsum('ro,io->ri', grad, weight, preferred_element_type=F32)  71 us
    dot_general x7, matrix products, weight_grad(): jnp.einsum('ri,ro->io', left, right, preferred_element_type=F32)  64.7 us
    dot_general x6, matrix products, body(): low_dot = lambda a, b: jnp.dot(a, b, preferred_element_type=F32)  64.2 us
    pallas_call x3, Pallas kernels, attend_back(): pl.pallas_call(functools.partial(attend_back_kernel, seq * (span // rows)...  40.9 us
    all_to_all x2, starting transfers between devices, body(): exchange = lambda blocks: lax.all_to_all(blocks, 'ctx', 0, 0, tiled=True)  35.9 us
  transfers between devices with their start and end apart: 47, of which 13 were waited for; matrix products, arithmetic and copies ran while one was open for 28% of the time, Pallas kernels for 24%

profile of v3, /device:TPU:0, one launch (start us, length us, event | category | flops | bytes accessed | tf_op | source)
XLA Modules:
  0.0 975.6 jit_solution(9234941121556850269)
XLA Ops:
  21.8 5.1 collective-permute-start
  33.4 2.8 fusion.37
  38.3 4.8 collective-permute-done.3
  47.0 10.1 %collective-permute-done.4 = bf16[2,4,32,896]{3,2,1,0:T(8,128)(2,1)S(1)} collective-permute-done((bf16[2,4,32,896]{3,2,1,0:T(8,128)(2,1)S(1)}, bf16[2,4,32,896]{3,2,1,0:T(8,128)(2,1)S(1)}, u32[]{:S(2)}, u32[]{:S(2)}) %collective-permute-start.4) | collective-permute-done | bytes 458784 | tf_op jit(solution)/shard_map/ppermute | solution.py:872
  64.9 4.9 stack.113
  77.9 11.1 %project.1 = (bf16[1536,1024]{1,0:T(8,128)(2,1)}, bf16[1536,512]{1,0:T(8,128)(2,1)}, bf16[1536,256]{1,0:T(8,128)(2,1)}) custom-call(bf16[1536,1024]{1,0:T(8,128)(2,1)} %bitcast.238, f32[1,1024]{1,0:T(1,128)} %reshape.350.gain_ref, bf16[1024,896]{1,0:T(8,128)(2,1)} %bitcast.262, f32[1536,128]{1,0:T(8,128)} %bitcast.240, f32[1536,128]{1,0:T(8,128)} %bitcast.242), custom_call_target="tpu_custom_call" | custom-call | tf_op jit(solution)/shard_map/project/pallas_call | solution.py:72
  89.8 4.0 collective-permute-start.6
  95.6 3.1 broadcast_in_dim.86
  98.7 3.8 all-to-all-start
  106.6 17.7 %convolution_convert_fusion.1 = bf16[1536,3456]{1,0:T(8,128)(2,1)} fusion(bf16[1536,1024]{1,0:T(8,128)(2,1)} %get-tuple-element.126, bf16[1024,3456]{1,0:T(8,128)(2,1)} %all-gather.3.cloned.1.call-done), kind=kOutput, calls=%fused_computation.7 | convolution fusion | flops 10876944384 | bytes 20840448 | tf_op jit(solution)/shard_map/dot_general | solution.py:920
  125.6 9.3 mixer_scan.3
  138.3 3.9 collective-permute-start.13
  142.1 9.3 mixer_scan.4
  157.5 9.2 mixer_scan.5
  172.0 23.5 %collective-permute-done.13 = bf16[1,128,1536]{2,1,0:T(8,128)(2,1)S(1)} collective-permute-done((bf16[1,128,1536]{2,1,0:T(8,128)(2,1)}, bf16[1,128,1536]{2,1,0:T(8,128)(2,1)S(1)}, u32[]{:S(2)}, u32[]{:S(2)}) %collective-permute-start.13) | collective-permute-done | bytes 393248 | tf_op jit(solution)/shard_map/ppermute | solution.py:832
  199.2 4.8 collective-permute-done.10
  207.5 10.6 %collective-permute-done.7 = bf16[1,128,1536]{2,1,0:T(8,128)(2,1)S(1)} collective-permute-done((bf16[1,128,1536]{2,1,0:T(8,128)(2,1)S(1)}, bf16[1,128,1536]{2,1,0:T(8,128)(2,1)S(1)}, u32[]{:S(2)}, u32[]{:S(2)}) %collective-permute-start.7) | collective-permute-done | bytes 393248 | tf_op jit(solution)/shard_map/ppermute | solution.py:832
  222.2 7.7 attend.3
  232.7 7.4 attend.4
  241.0 8.9 mixer_out.3
  250.7 9.3 mixer_out.4
  260.9 8.9 mixer_out.5
  269.8 7.6 attend.5
  282.8 7.3 fusion.65
  290.1 4.9 slice.418
  298.5 7.6 multiply_reduce_fusion.3
  306.2 20.8 %convolution_convert_fusion = bf16[1536,4096]{1,0:T(8,128)(2,1)} fusion(bf16[1024,1024]{1,0:T(8,128)(2,1)} %bitcast.276, bf16[1024,1024]{1,0:T(8,128)(2,1)} %bitcast.278, bf16[1024,1024]{1,0:T(8,128)(2,1)} %bitcast.280, bf16[1024,1024]{1,0:T(8,128)(2,1)} %bitcast.274, f32[1536,1024]{1,0:T(8,128)} %get-tuple-element.310, f32[1024]{0:T(1024)S(1)} %copy-done.67, ...), kind=kOutput, calls=%fused_computation.6 | convolution fusion | flops 12929466368 | bytes 27273216 | tf_op jit(solution)/shard_map/dot_general | solution.py:920
  327.0 19.1 %fusion.6 = (bf16[1536,2048]{1,0:T(8,128)(2,1)}, bf16[1536,2048]{1,0:T(8,128)(2,1)}, bf16[1536,2048]{1,0:T(8,128)(2,1)}) fusion(bf16[1536,4096]{1,0:T(8,128)(2,1)} %convolution_convert_fusion, bf16[2048,1024]{1,0:T(8,128)(2,1)} %bitcast.264, bf16[1536,1024]{1,0:T(8,128)(2,1)S(1)} %bitcast.259), kind=kOutput, calls=%fused_computation.14 | convolution fusion | flops 6499074048 | bytes 38797312 | tf_op jit(solution)/shard_map/ro,io->ri/dot_general | solution.py:1041
  346.1 20.6 %fusion.9 = f32[1536,1024]{1,0:T(8,128)} fusion(bf16[1536,2048]{1,0:T(8,128)(2,1)} %get-tuple-element.260, bf16[1536,2048]{1,0:T(8,128)(2,1)} %get-tuple-element.259, bf16[1024,1024]{1,0:T(8,128)(2,1)S(1)} %bitcast.277, bf16[1024,1024]{1,0:T(8,128)(2,1)S(1)} %bitcast.279, bf16[1024,1024]{1,0:T(8,128)(2,1)} %bitcast.281, bf16[1024,1024]{1,0:T(8,128)(2,1)S(1)} %bitcast.275), kind=kOutput, calls=%fused_computation.26 | convolution fusion | flops 12943622144 | bytes 27262976 | tf_op jit(solution)/shard_map/ro,io->ri/dot_general | solution.py:1041
  366.7 21.8 %fusion.10 = bf16[1024,4096]{1,0:T(8,128)(2,1)} fusion(bf16[1536,2048]{1,0:T(8,128)(2,1)} %get-tuple-element.260, bf16[1536,2048]{1,0:T(8,128)(2,1)} %get-tuple-element.259, f32[1536,1024]{1,0:T(8,128)} %get-tuple-element.310, f32[1024]{0:T(1024)S(1)} %copy-done.67, f32[1536]{0:T(1024)S(1)} %fusion.52), kind=kOutput, calls=%fused_computation.28 | convolution fusion | flops 12918980608 | bytes 27273216 | tf_op jit(solution)/shard_map/ri,ro->io/dot_general | solution.py:1038
  388.4 11.2 %convolution_convert_fusion.3 = bf16[2048,1024]{1,0:T(8,128)(2,1)} fusion(bf16[1536,2048]{1,0:T(8,128)(2,1)} %get-tuple-element.267, bf16[1536,1024]{1,0:T(8,128)(2,1)S(1)} %bitcast.260), kind=kOutput, calls=%fused_computation.47 | convolution fusion | flops 6444548096 | bytes 13631488 | tf_op jit(solution)/shard_map/ri,ro->io/dot_general | solution.py:1038
  399.7 6.2 multiply_reduce_fusion
  406.5 6.7 fusion.62
  413.5 5.3 convolution_convert_fusion.6
  420.7 6.9 convolution_convert_fusion.2
  427.6 5.4 convolution_convert_fusion.5
  433.0 10.0 %mixer_gate_back.3 = (bf16[3,512,1536]{2,1,0:T(8,128)(2,1)}, bf16[3,512,1536]{2,1,0:T(8,128)(2,1)}, bf16[3,4,128,1536]{3,2,1,0:T(8,128)(2,1)}, f32[3,4,8,128]{3,...) custom-call(bf16[3,512,1536]{2,1,0:T(8,128)(2,1)} %bitcast.234, ...), custom_call_target="tpu_custom_call" | custom-call | tf_op jit(solution)/shard_map/mixer_gate_back/pallas_call | solution.py:692
  443.0 10.0 %mixer_gate_back.4 = (bf16[3,512,1536]{2,1,0:T(8,128)(2,1)}, bf16[3,512,1536]{2,1,0:T(8,128)(2,1)}, bf16[3,4,128,1536]{3,2,1,0:T(8,128)(2,1)}, f32[3,4,8,128]{3,...) custom-call(bf16[3,512,1536]{2,1,0:T(8,128)(2,1)} %bitcast.235, ...), custom_call_target="tpu_custom_call", output_to_operand_aliasing={{0}: (8, {}), {1}: (9, {}), {2}: (10, {}), {3}: (11, {})} | custom-call | tf_op jit(solution)/shard_map/mixer_gate_back/pallas_call | solution.py:692
  453.0 10.2 %mixer_gate_back.5 = (bf16[3,512,1536]{2,1,0:T(8,128)(2,1)}, bf16[3,512,1536]{2,1,0:T(8,128)(2,1)}, bf16[3,4,128,1536]{3,2,1,0:T(8,128)(2,1)}, f32[3,4,8,128]{3,...) custom-call(bf16[3,512,1536]{2,1,0:T(8,128)(2,1)} %bitcast.236, ...), custom_call_target="tpu_custom_call", output_to_operand_aliasing={{0}: (8, {}), {1}: (9, {}), {2}: (10, {}), {3}: (11, {})} | custom-call | tf_op jit(solution)/shard_map/mixer_gate_back/pallas_call | solution.py:692
  463.3 7.7 convolution_convert_fusion.4
  471.4 4.6 maximum_maximum_fusion
  476.0 55.9 %reduce-scatter.7.cloned.1.call-done = bf16[128,4096]{1,0:T(8,128)(2,1)} async-done(((bf16[1024,4096]{1,0:T(8,128)(2,1)}), bf16[128,4096]{1,0:T(8,128)(2,1)}) %reduce-scatter.7.cloned.1.call-update) | async-done | bytes 1048592 | tf_op jit(solution)/shard_map/reduce_scatter | solution.py:1035
  559.8 27.0 %reduce-scatter.9.cloned.1.call-done = bf16[256,1024]{1,0:T(8,128)(2,1)} async-done(((bf16[2048,1024]{1,0:T(8,128)(2,1)}), bf16[256,1024]{1,0:T(8,128)(2,1)}) %reduce-scatter.9.cloned.1.call-update) | async-done | bytes 524304 | tf_op jit(solution)/shard_map/reduce_scatter | solution.py:1035
  586.8 13.4 %attend_back.3 = (bf16[1,512,512]{2,1,0:T(8,128)(2,1)}, bf16[4,1,512,256]{3,2,1,0:T(8,128)(2,1)}) custom-call(s32[6]{0:T(128)} %and_select_fusion.1.low_ref, s32[6]{0:T(128)} %reshape.352.high_ref, s32[1]{0:T(128)} %bitcast.19.base_ref, bf16[3,512,512]{2,1,0:T(8,128)(2,1)} %bitcast.227, bf16[4,3,512,256]{3,2,1,0:T(8,128)(2,1)} %copy-done, ...), custom_call_target="tpu_custom_call" | custom-call | tf_op jit(solution)/shard_map/attend_back/pallas_call | solution.py:268
  602.5 13.9 %attend_back.5 = (bf16[1,512,512]{2,1,0:T(8,128)(2,1)}, bf16[4,1,512,256]{3,2,1,0:T(8,128)(2,1)}) custom-call(s32[6]{0:T(128)} %and_select_fusion.1.low_ref, s32[6]{0:T(128)} %reshape.352.high_ref, s32[1]{0:T(128)} %bitcast.19.base_ref, bf16[3,512,512]{2,1,0:T(8,128)(2,1)} %bitcast.228, bf16[4,3,512,256]{3,2,1,0:T(8,128)(2,1)} %copy-done, ...), custom_call_target="tpu_custom_call" | custom-call | tf_op jit(solution)/shard_map/attend_back/pallas_call | solution.py:268
  620.9 13.7 %attend_back.4 = (bf16[1,512,512]{2,1,0:T(8,128)(2,1)}, bf16[4,1,512,256]{3,2,1,0:T(8,128)(2,1)}) custom-call(s32[6]{0:T(128)} %and_select_fusion.1.low_ref, s32[6]{0:T(128)} %reshape.352.high_ref, s32[1]{0:T(128)} %bitcast.19.base_ref, bf16[3,512,512]{2,1,0:T(8,128)(2,1)} %bitcast.229, bf16[4,3,512,256]{3,2,1,0:T(8,128)(2,1)} %copy-done, ...), custom_call_target="tpu_custom_call" | custom-call | tf_op jit(solution)/shard_map/attend_back/pallas_call | solution.py:268
  634.6 3.2 pad_maximum_fusion.6
  637.8 32.1 %all-to-all-start.1 = ((bf16[4,3,512,256]{3,2,1,0:T(8,128)(2,1)}), bf16[4,3,512,256]{3,2,1,0:T(8,128)(2,1)}, u32[]{:S(2)}, u32[]{:S(2)}) async-start(bf16[4,3,512,256]{3,2,1,0:T(8,128)(2,1)} %pad_maximum_fusion.6), calls=%async_computation.4 | async-start | bytes 6291456 | tf_op jit(solution)/shard_map/all_to_all | solution.py:984
  674.4 40.5 %collective-permute-done.23 = bf16[1,128,1536]{2,1,0:T(8,128)(2,1)S(1)} collective-permute-done((bf16[1,128,1536]{2,1,0:T(8,128)(2,1)S(1)}, bf16[1,128,1536]{2,1,0:T(8,128)(2,1)S(1)}, u32[]{:S(2)}, u32[]{:S(2)}) %collective-permute-start.23) | collective-permute-done | bytes 393248 | tf_op jit(solution)/shard_map/ppermute | solution.py:832
  715.7 24.5 %mixer_back.3 = (bf16[3,512,3456]{2,1,0:T(8,128)(2,1)}, f32[1,8,1792]{2,1,0:T(8,128)}, f32[8,1792]{1,0:T(8,128)}, f32[8,128]{1,0:T(8,128)}) custom-call(bf16[3,512,1536]{2,1,0:T(8,128)(2,1)} %get-tuple-element.202.refs_0_, f32[3,512,1536]{2,1,0:T(8,128)} %get-tuple-element.166.refs_1_, bf16[3,512,1536]{2,1,0:T(8,128)(2,1)} %get-tuple-element.191.refs_2_, ...), custom_call_target="tpu_custom_call" | custom-call | tf_op jit(solution)/shard_map/mixer_back/pallas_call | solution.py:692
  740.2 24.6 %mixer_back.4 = (bf16[3,512,3456]{2,1,0:T(8,128)(2,1)}, f32[1,8,1792]{2,1,0:T(8,128)}, f32[8,1792]{1,0:T(8,128)}, f32[8,128]{1,0:T(8,128)}) custom-call(bf16[3,512,1536]{2,1,0:T(8,128)(2,1)} %get-tuple-element.202.refs_0_, f32[3,512,1536]{2,1,0:T(8,128)} %get-tuple-element.166.refs_1_, ...), custom_call_target="tpu_custom_call", output_to_operand_aliasing={{0}: (20, {})} | custom-call | tf_op jit(solution)/shard_map/mixer_back/pallas_call | solution.py:692
  764.9 24.9 %mixer_back.5 = (bf16[3,512,3456]{2,1,0:T(8,128)(2,1)}, f32[1,8,1792]{2,1,0:T(8,128)}, f32[8,1792]{1,0:T(8,128)}, f32[8,128]{1,0:T(8,128)}) custom-call(bf16[3,512,1536]{2,1,0:T(8,128)(2,1)} %get-tuple-element.202.refs_0_, f32[3,512,1536]{2,1,0:T(8,128)} %get-tuple-element.166.refs_1_, ...), custom_call_target="tpu_custom_call", output_to_operand_aliasing={{0}: (20, {})} | custom-call | tf_op jit(solution)/shard_map/mixer_back/pallas_call | solution.py:692
  800.5 11.4 %fusion.20 = bf16[1024,1920]{1,0:T(8,128)(2,1)} fusion(bf16[1536,1024]{1,0:T(8,128)(2,1)} %get-tuple-element.126, bf16[1536,3456]{1,0:T(8,128)(2,1)} %bitcast.232), kind=kOutput, calls=%fused_computation.48 | convolution fusion | flops 6041763840 | bytes 12976128 | tf_op jit(solution)/shard_map/ri,ro->io/dot_general | solution.py:1038
  811.9 3.7 convert_reduce_fusion
  815.6 3.3 reshape.385
  829.7 4.6 fusion.29
  834.3 19.8 %fusion.17 = (bf16[1024]{0:T(1024)(128)(2,1)S(1)}, f32[1536]{0:T(1024)S(1)}, f32[1536,1024]{1,0:T(8,128)}) fusion(f32[1536]{0:T(1024)S(1)} %copy-done.73, bf16[3,512,1024]{2,1,0:T(8,128)(2,1)S(1)} %copy-done.2, f32[1024]{0:T(1024)S(1)} %copy-done.76, f32[1536,1024]{1,0:T(8,128)} %fusion.29, bf16[1536,3456]{1,0:T(8,128)(2,1)} %bitcast.233, ...), kind=kOutput, calls=%fused_computation.36 | convolution fusion | flops 10884216832 | bytes 33441792 | tf_op jit(solution)/shard_map/ro,io->ri/dot_general | solution.py:1041
  854.6 5.6 convolution_convert_fusion.7
  861.6 3.1 copy.263
  865.8 2.9 collective-permute-start.33
  889.6 6.1 collective-permute-done.27
  899.2 12.2 %add_convert_fusion = bf16[1536,1024]{1,0:T(8,128)(2,1)} fusion(f32[1536,1024]{1,0:T(8,128)} %get-tuple-element.310, bf16[1536,2048]{1,0:T(8,128)(2,1)} %get-tuple-element.267, bf16[2048,1024]{1,0:T(8,128)(2,1)} %bitcast.265), kind=kOutput, calls=%fused_computation.41 | convolution fusion | flops 6445596672 | bytes 19922944 | tf_op jit(solution)/shard_map/dot_general | solution.py:920
  915.8 7.8 fusion.13
  929.4 31.3 %reduce-scatter.15.cloned.1.call-done = bf16[304,1024]{1,0:T(8,128)(2,1)} async-done(((bf16[1216,1024]{1,0:T(8,128)(2,1)}), bf16[304,1024]{1,0:T(8,128)(2,1)}) %reduce-scatter.15.cloned.1.call-update) | async-done | bytes 622608 | tf_op jit(solution)/shard_map/reduce_scatter | solution.py:1156
  (493 shorter events, 200.1 us)
Async XLA Ops:
  7.2 29.1 %copy-start.47 = (bf16[32,512]{1,0:T(8,128)(2,1)S(1)}, bf16[32,512]{1,0:T(8,128)(2,1)}, u32[]{:S(2)}) copy-start(bf16[32,512]{1,0:T(8,128)(2,1)} %param.29) | copy-start | bytes 98308
  7.2 99.3 %all-gather.3.cloned.1.call-start = ((), (), s32[]{:S(2)}) async-start(), calls=%async_computation.8 | async-start | bytes 7299072 | tf_op jit(solution)/shard_map/all_gather | solution.py:930
  8.9 269.7 %all-gather.5.cloned.1.call-start = ((), (), s32[]{:S(2)}) async-start(), calls=%async_computation.9 | async-start | bytes 17301504 | tf_op jit(solution)/shard_map/all_gather | solution.py:930
  21.8 14.5 %collective-permute-start = (bf16[32,896]{1,0:T(8,128)(2,1)S(1)}, bf16[32,896]{1,0:T(8,128)(2,1)S(1)}, u32[]{:S(2)}, u32[]{:S(2)}) collective-permute-start(bf16[32,896]{1,0:T(8,128)(2,1)S(1)} %pad_maximum_fusion.23), channel_id=1, source_target_pairs={{0,3},{1,0},{2,1},{3,2},{4,7},{5,4},{6,5},{7,6},{8,11},{9,8},{10,9... | collective-permute-start | bytes 172040 | tf_op jit(solution)/shard_map/ppermute | solution.py:863
  26.8 9.4 collective-permute-start.1
  26.8 9.5 collective-permute-start.2
  36.4 6.7 collective-permute-start.3
  43.2 13.8 %collective-permute-start.4 = (bf16[2,4,32,896]{3,2,1,0:T(8,128)(2,1)S(1)}, bf16[2,4,32,896]{3,2,1,0:T(8,128)(2,1)S(1)}, u32[]{:S(2)}, u32[]{:S(2)}) collective-permute-start(bf16[2,4,32,896]{3,2,1,0:T(8,128)(2,1)S(1)} %pad_maximum_fusion.19), channel_id=1, source_target_pairs={{0,16},{4,20},{8,24},{12,28},{16,0},{20,4},{24,8},{28,12},{1,17},{... | collective-permute-start | bytes 1376264 | tf_op jit(solution)/shard_map/ppermute | solution.py:872
  58.2 16.7 %collective-permute-start.5 = (bf16[2,2,4,32,896]{4,3,2,1,0:T(8,128)(2,1)}, bf16[2,2,4,32,896]{4,3,2,1,0:T(8,128)(2,1)}, u32[]{:S(2)}, u32[]{:S(2)}) collective-permute-start(bf16[2,2,4,32,896]{4,3,2,1,0:T(8,128)(2,1)} %pad_maximum_fusion.17), channel_id=1, source_target_pairs={{0,4},{4,0},{8,12},{12,8},{16,20},{20,16},{24,28},{28,24},{1,5},{5... | collective-permute-start | bytes 2752520 | tf_op jit(solution)/shard_map/ppermute | solution.py:872
  89.8 16.7 %collective-permute-start.6 = (bf16[3,3,1024]{2,1,0:T(4,128)(2,1)S(1)}, bf16[3,3,1024]{2,1,0:T(4,128)(2,1)S(1)}, u32[]{:S(2)}, u32[]{:S(2)}) collective-permute-start(bf16[3,3,1024]{2,1,0:T(4,128)(2,1)S(1)} %slice.401), channel_id=1, source_target_pairs={{0,1},{1,2},{2,3},{4,5},{5,6},{6,7},{8,9},{9,10},{10,11},{12,13},{... | collective-permute-start | bytes 55304 | tf_op jit(solution)/shard_map/ppermute | solution.py:813
  98.7 121.8 %all-to-all-start = ((bf16[4,3,512,256]{3,2,1,0:T(8,128)(2,1)}), bf16[4,3,512,256]{3,2,1,0:T(8,128)(2,1)S(1)}, u32[]{:S(2)}, u32[]{:S(2)}) async-start(bf16[4,3,512,256]{3,2,1,0:T(8,128)(2,1)} %broadcast_in_dim.86), calls=%async_computation | async-start | bytes 6291456 | tf_op jit(solution)/shard_map/all_to_all | solution.py:984
  102.5 429.4 %reduce-scatter.7.cloned.1.call-start = ((), (), s32[]{:S(2)}) async-start(), calls=%async_computation.10 | async-start | bytes 9437184 | tf_op jit(solution)/shard_map/reduce_scatter | solution.py:1035
  138.3 57.3 %collective-permute-start.13 = (bf16[1,128,1536]{2,1,0:T(8,128)(2,1)}, bf16[1,128,1536]{2,1,0:T(8,128)(2,1)S(1)}, u32[]{:S(2)}, u32[]{:S(2)}) collective-permute-start(bf16[1,128,1536]{2,1,0:T(8,128)(2,1)} %add_convert_fusion.12), channel_id=1, source_target_pairs={{0,1},{4,5},{8,9},{12,13},{16,17},{20,21},{24,25},{28,29}} | collective-permute-start | bytes 1179656 | tf_op jit(solution)/shard_map/ppermute | solution.py:832
  153.5 78.1 %copy-start.48 = (f32[1536]{0:T(1024)}, f32[1536]{0:T(1024)S(1)}, u32[]{:S(2)}) copy-start(f32[1536]{0:T(1024)S(1)} %broadcast_in_dim.82) | copy-start | bytes 18436
  155.5 48.5 %collective-permute-start.10 = (bf16[1,128,1536]{2,1,0:T(8,128)(2,1)}, bf16[1,128,1536]{2,1,0:T(8,128)(2,1)}, u32[]{:S(2)}, u32[]{:S(2)}) collective-permute-start(bf16[1,128,1536]{2,1,0:T(8,128)(2,1)} %add_convert_fusion.15), channel_id=1, source_target_pairs={{0,1},{4,5},{8,9},{12,13},{16,17},{20,21},{24,25},{28,29}} | collective-permute-start | bytes 1179656 | tf_op jit(solution)/shard_map/ppermute | solution.py:832
  168.9 61.8 %copy-start.45 = (f32[1536]{0:T(1024)}, f32[1536]{0:T(1024)S(1)}, u32[]{:S(2)}) copy-start(f32[1536]{0:T(1024)S(1)} %broadcast_in_dim.80) | copy-start | bytes 18436
  168.9 49.2 %copy-start.11 = (f32[1,128,1536]{2,1,0:T(8,128)S(1)}, f32[1,128,1536]{2,1,0:T(8,128)}, u32[]{:S(2)}) copy-start(f32[1,128,1536]{2,1,0:T(8,128)} %get-tuple-element.140) | copy-start | bytes 2359300
  170.7 47.4 %collective-permute-start.7 = (bf16[1,128,1536]{2,1,0:T(8,128)(2,1)S(1)}, bf16[1,128,1536]{2,1,0:T(8,128)(2,1)S(1)}, u32[]{:S(2)}, u32[]{:S(2)}) collective-permute-start(bf16[1,128,1536]{2,1,0:T(8,128)(2,1)S(1)} %add_convert_fusion.18), channel_id=1, source_target_pairs={{0,1},{4,5},{8,9},{12,13},{16,17},{20,21},{24,25},{28,29}} | collective-permute-start | bytes 1179656 | tf_op jit(solution)/shard_map/ppermute | solution.py:832
  197.7 32.1 %collective-permute-start.14 = (bf16[1,128,1536]{2,1,0:T(8,128)(2,1)}, bf16[1,128,1536]{2,1,0:T(8,128)(2,1)}, u32[]{:S(2)}, u32[]{:S(2)}) collective-permute-start(bf16[1,128,1536]{2,1,0:T(8,128)(2,1)} %get-tuple-element.255), channel_id=1, source_target_pairs={{1,2},{5,6},{9,10},{13,14},{17,18},{21,22},{25,26},{29,30}} | collective-permute-start | bytes 1179656 | tf_op jit(solution)/shard_map/ppermute | solution.py:832
  206.1 25.5 %collective-permute-start.11 = (bf16[1,128,1536]{2,1,0:T(8,128)(2,1)}, bf16[1,128,1536]{2,1,0:T(8,128)(2,1)}, u32[]{:S(2)}, u32[]{:S(2)}) collective-permute-start(bf16[1,128,1536]{2,1,0:T(8,128)(2,1)} %get-tuple-element.251), channel_id=1, source_target_pairs={{1,2},{5,6},{9,10},{13,14},{17,18},{21,22},{25,26},{29,30}} | collective-permute-start | bytes 1179656 | tf_op jit(solution)/shard_map/ppermute | solution.py:832
  219.1 11.7 %collective-permute-start.8 = (bf16[1,128,1536]{2,1,0:T(8,128)(2,1)}, bf16[1,128,1536]{2,1,0:T(8,128)(2,1)}, u32[]{:S(2)}, u32[]{:S(2)}) collective-permute-start(bf16[1,128,1536]{2,1,0:T(8,128)(2,1)} %get-tuple-element.249), channel_id=1, source_target_pairs={{1,2},{5,6},{9,10},{13,14},{17,18},{21,22},{25,26},{29,30}} | collective-permute-start | bytes 1179656 | tf_op jit(solution)/shard_map/ppermute | solution.py:832
  230.0 10.1 %collective-permute-start.15 = (bf16[1,128,1536]{2,1,0:T(8,128)(2,1)S(1)}, bf16[1,128,1536]{2,1,0:T(8,128)(2,1)S(1)}, u32[]{:S(2)}, u32[]{:S(2)}) collective-permute-start(bf16[1,128,1536]{2,1,0:T(8,128)(2,1)S(1)} %get-tuple-element.253), channel_id=1, source_target_pairs={{2,3},{6,7},{10,11},{14,15},{18,19},{22,23},{26,27},{30,31}} | collective-permute-start | bytes 1179656 | tf_op jit(solution)/shard_map/ppermute | solution.py:832
  230.9 29.1 %collective-permute-start.9 = (bf16[1,128,1536]{2,1,0:T(8,128)(2,1)S(1)}, bf16[1,128,1536]{2,1,0:T(8,128)(2,1)S(1)}, u32[]{:S(2)}, u32[]{:S(2)}) collective-permute-start(bf16[1,128,1536]{2,1,0:T(8,128)(2,1)S(1)} %add_convert_fusion.16), channel_id=1, source_target_pairs={{2,3},{6,7},{10,11},{14,15},{18,19},{22,23},{26,27},{30,31}} | collective-permute-start | bytes 1179656 | tf_op jit(solution)/shard_map/ppermute | solution.py:832
  231.8 18.1 %collective-permute-start.12 = (bf16[1,128,1536]{2,1,0:T(8,128)(2,1)S(1)}, bf16[1,128,1536]{2,1,0:T(8,128)(2,1)S(1)}, u32[]{:S(2)}, u32[]{:S(2)}) collective-permute-start(bf16[1,128,1536]{2,1,0:T(8,128)(2,1)S(1)} %get-tuple-element.247), channel_id=1, source_target_pairs={{2,3},{6,7},{10,11},{14,15},{18,19},{22,23},{26,27},{30,31}} | collective-permute-start | bytes 1179656 | tf_op jit(solution)/shard_map/ppermute | solution.py:832
  306.2 99.7 %copy-start.56 = (f32[1536]{0:T(1024)}, f32[1536]{0:T(1024)S(1)}, u32[]{:S(2)}) copy-start(f32[1536]{0:T(1024)S(1)} %fusion.52) | copy-start | bytes 18436
  399.6 187.2 %reduce-scatter.9.cloned.1.call-start = ((), (), s32[]{:S(2)}) async-start(), calls=%async_computation.11 | async-start | bytes 4718592 | tf_op jit(solution)/shard_map/reduce_scatter | solution.py:1035
  413.2 385.4 %reduce-scatter.11.cloned.1.call-start = ((), (), s32[]{:S(2)}) async-start(), calls=%async_computation.12 | async-start | bytes 8257536 | tf_op jit(solution)/shard_map/reduce_scatter | solution.py:1035
  476.0 56.0 %copy-start.2 = (bf16[3,512,1024]{2,1,0:T(8,128)(2,1)S(1)}, bf16[3,512,1024]{2,1,0:T(8,128)(2,1)}, u32[]{:S(2)}) copy-start(bf16[3,512,1024]{2,1,0:T(8,128)(2,1)} %param.19) | copy-start | bytes 9437188
  532.0 25.7 %copy-start.46 = (f32[1536]{0:T(1024)S(1)}, f32[1536]{0:T(1024)}, u32[]{:S(2)}) copy-start(f32[1536]{0:T(1024)} %copy-done.45) | copy-start | bytes 18436
  535.9 16.0 %collective-permute-start.16 = (bf16[1,128,1536]{2,1,0:T(8,128)(2,1)}, bf16[1,128,1536]{2,1,0:T(8,128)(2,1)}, u32[]{:S(2)}, u32[]{:S(2)}) collective-permute-start(bf16[1,128,1536]{2,1,0:T(8,128)(2,1)} %add_convert_fusion.9), channel_id=1, source_target_pairs={{3,2},{7,6},{11,10},{15,14},{19,18},{23,22},{27,26},{31,30}} | collective-permute-start | bytes 1179656 | tf_op jit(solution)/shard_map/ppermute | solution.py:832
  539.3 16.2 %collective-permute-start.19 = (bf16[1,128,1536]{2,1,0:T(8,128)(2,1)}, bf16[1,128,1536]{2,1,0:T(8,128)(2,1)S(1)}, u32[]{:S(2)}, u32[]{:S(2)}) collective-permute-start(bf16[1,128,1536]{2,1,0:T(8,128)(2,1)} %add_convert_fusion.6), channel_id=1, source_target_pairs={{3,2},{7,6},{11,10},{15,14},{19,18},{23,22},{27,26},{31,30}} | collective-permute-start | bytes 1179656 | tf_op jit(solution)/shard_map/ppermute | solution.py:832
  542.1 15.6 %collective-permute-start.21 = (bf16[1,128,1536]{2,1,0:T(8,128)(2,1)}, bf16[1,128,1536]{2,1,0:T(8,128)(2,1)}, u32[]{:S(2)}, u32[]{:S(2)}) collective-permute-start(bf16[1,128,1536]{2,1,0:T(8,128)(2,1)} %add_convert_fusion.4), channel_id=1, source_target_pairs={{3,2},{7,6},{11,10},{15,14},{19,18},{23,22},{27,26},{31,30}} | collective-permute-start | bytes 1179656 | tf_op jit(solution)/shard_map/ppermute | solution.py:832
  554.1 46.9 %collective-permute-start.17 = (bf16[1,128,1536]{2,1,0:T(8,128)(2,1)}, bf16[1,128,1536]{2,1,0:T(8,128)(2,1)}, u32[]{:S(2)}, u32[]{:S(2)}) collective-permute-start(bf16[1,128,1536]{2,1,0:T(8,128)(2,1)} %get-tuple-element.245), channel_id=1, source_target_pairs={{2,1},{6,5},{10,9},{14,13},{18,17},{22,21},{26,25},{30,29}} | collective-permute-start | bytes 1179656 | tf_op jit(solution)/shard_map/ppermute | solution.py:832
  600.2 17.5 %collective-permute-start.20 = (bf16[1,128,1536]{2,1,0:T(8,128)(2,1)S(1)}, bf16[1,128,1536]{2,1,0:T(8,128)(2,1)S(1)}, u32[]{:S(2)}, u32[]{:S(2)}) collective-permute-start(bf16[1,128,1536]{2,1,0:T(8,128)(2,1)S(1)} %copy-done.44), channel_id=1, source_target_pairs={{2,1},{6,5},{10,9},{14,13},{18,17},{22,21},{26,25},{30,29}} | collective-permute-start | bytes 1179656 | tf_op jit(solution)/shard_map/ppermute | solution.py:832
  601.1 18.9 %collective-permute-start.18 = (bf16[1,128,1536]{2,1,0:T(8,128)(2,1)S(1)}, bf16[1,128,1536]{2,1,0:T(8,128)(2,1)S(1)}, u32[]{:S(2)}, u32[]{:S(2)}) collective-permute-start(bf16[1,128,1536]{2,1,0:T(8,128)(2,1)S(1)} %get-tuple-element.183), channel_id=1, source_target_pairs={{1,0},{5,4},{9,8},{13,12},{17,16},{21,20},{25,24},{29,28}} | collective-permute-start | bytes 1179656 | tf_op jit(solution)/shard_map/ppermute | solution.py:832
  616.3 53.6 %collective-permute-start.22 = (bf16[1,128,1536]{2,1,0:T(8,128)(2,1)}, bf16[1,128,1536]{2,1,0:T(8,128)(2,1)}, u32[]{:S(2)}, u32[]{:S(2)}) collective-permute-start(bf16[1,128,1536]{2,1,0:T(8,128)(2,1)} %get-tuple-element.197), channel_id=1, source_target_pairs={{2,1},{6,5},{10,9},{14,13},{18,17},{22,21},{26,25},{30,29}} | collective-permute-start | bytes 1179656 | tf_op jit(solution)/shard_map/ppermute | solution.py:832
  618.8 53.7 %collective-permute-start.24 = (bf16[1,128,1536]{2,1,0:T(8,128)(2,1)}, bf16[1,128,1536]{2,1,0:T(8,128)(2,1)}, u32[]{:S(2)}, u32[]{:S(2)}) collective-permute-start(bf16[1,128,1536]{2,1,0:T(8,128)(2,1)} %get-tuple-element.199), channel_id=1, source_target_pairs={{1,0},{5,4},{9,8},{13,12},{17,16},{21,20},{25,24},{29,28}} | collective-permute-start | bytes 1179656 | tf_op jit(solution)/shard_map/ppermute | solution.py:832
  637.8 174.1 %all-to-all-start.1 = ((bf16[4,3,512,256]{3,2,1,0:T(8,128)(2,1)}), bf16[4,3,512,256]{3,2,1,0:T(8,128)(2,1)}, u32[]{:S(2)}, u32[]{:S(2)}) async-start(bf16[4,3,512,256]{3,2,1,0:T(8,128)(2,1)} %pad_maximum_fusion.6), calls=%async_computation.4 | async-start | bytes 6291456 | tf_op jit(solution)/shard_map/all_to_all | solution.py:984
  669.9 218.1 %reduce-scatter.13.cloned.1.call-start = ((), (), s32[]{:S(2)}) async-start(), calls=%async_computation.13 | async-start | bytes 4423680 | tf_op jit(solution)/shard_map/reduce_scatter | solution.py:1035
  671.2 43.6 %collective-permute-start.23 = (bf16[1,128,1536]{2,1,0:T(8,128)(2,1)S(1)}, bf16[1,128,1536]{2,1,0:T(8,128)(2,1)S(1)}, u32[]{:S(2)}, u32[]{:S(2)}) collective-permute-start(bf16[1,128,1536]{2,1,0:T(8,128)(2,1)S(1)} %add_convert_fusion.2), channel_id=1, source_target_pairs={{1,0},{5,4},{9,8},{13,12},{17,16},{21,20},{25,24},{29,28}} | collective-permute-start | bytes 1179656 | tf_op jit(solution)/shard_map/ppermute | solution.py:832
  764.8 25.9 %copy-start.72 = (f32[1,8,1792]{2,1,0:T(8,128)S(1)}, f32[1,8,1792]{2,1,0:T(8,128)}, u32[]{:S(2)}) copy-start(f32[1,8,1792]{2,1,0:T(8,128)} %get-tuple-element.207) | copy-start | bytes 172036
  764.8 25.9 %copy-start.71 = (f32[1,8,1792]{2,1,0:T(8,128)S(1)}, f32[1,8,1792]{2,1,0:T(8,128)}, u32[]{:S(2)}) copy-start(f32[1,8,1792]{2,1,0:T(8,128)} %get-tuple-element.206) | copy-start | bytes 172036
  764.8 27.2 %copy-start.78 = (f32[8,128]{1,0:T(8,128)S(1)}, f32[8,128]{1,0:T(8,128)}, u32[]{:S(2)}) copy-start(f32[8,128]{1,0:T(8,128)} %get-tuple-element.223) | copy-start | bytes 12292
  764.8 27.2 %copy-start.79 = (f32[8,128]{1,0:T(8,128)S(1)}, f32[8,128]{1,0:T(8,128)}, u32[]{:S(2)}) copy-start(f32[8,128]{1,0:T(8,128)} %get-tuple-element.224) | copy-start | bytes 12292
  764.8 27.9 %copy-start.69 = (f32[8,1792]{1,0:T(8,128)S(1)}, f32[8,1792]{1,0:T(8,128)}, u32[]{:S(2)}) copy-start(f32[8,1792]{1,0:T(8,128)} %get-tuple-element.219) | copy-start | bytes 172036
  764.8 27.9 %copy-start.70 = (f32[8,1792]{1,0:T(8,128)S(1)}, f32[8,1792]{1,0:T(8,128)}, u32[]{:S(2)}) copy-start(f32[8,1792]{1,0:T(8,128)} %get-tuple-element.220) | copy-start | bytes 172036
  764.9 28.8 %copy-start.41 = (bf16[1,512,512]{2,1,0:T(8,128)(2,1)S(1)}, bf16[1,512,512]{2,1,0:T(8,128)(2,1)}, u32[]{:S(2)}) copy-start(bf16[1,512,512]{2,1,0:T(8,128)(2,1)} %get-tuple-element.182) | copy-start | bytes 1572868
  764.9 28.8 %copy-start.42 = (bf16[1,512,512]{2,1,0:T(8,128)(2,1)S(1)}, bf16[1,512,512]{2,1,0:T(8,128)(2,1)}, u32[]{:S(2)}) copy-start(bf16[1,512,512]{2,1,0:T(8,128)(2,1)} %get-tuple-element.196) | copy-start | bytes 1572868
  764.9 28.8 %copy-start.43 = (bf16[1,512,512]{2,1,0:T(8,128)(2,1)S(1)}, bf16[1,512,512]{2,1,0:T(8,128)(2,1)}, u32[]{:S(2)}) copy-start(bf16[1,512,512]{2,1,0:T(8,128)(2,1)} %get-tuple-element.189) | copy-start | bytes 1572868
  764.9 30.1 %copy-start.77 = (f32[24]{0:T(128)S(1)}, f32[24]{0:T(128)}, u32[]{:S(2)}) copy-start(f32[24]{0:T(128)} %reduce_sum.100) | copy-start | bytes 292
  790.7 6.9 collective-permute-start.25
  795.3 70.4 %collective-permute-start.32 = (f32[3,24]{1,0:T(4,128)S(1)}, f32[3,24]{1,0:T(4,128)S(1)}, u32[]{:S(2)}, u32[]{:S(2)}) collective-permute-start(f32[3,24]{1,0:T(4,128)S(1)} %pad_maximum_fusion.27), channel_id=1, source_target_pairs={{0,4},{4,0},{8,12},{12,8},{16,20},{20,16},{24,28},{28,24},{1,5},{5... | collective-permute-start | bytes 872 | tf_op jit(solution)/shard_map/ppermute | solution.py:854
  811.8 116.6 %reduce-scatter.17.cloned.1.call-start = ((), (), s32[]{:S(2)}) async-start(), calls=%async_computation.15 | async-start | bytes 614400 | tf_op jit(solution)/shard_map/reduce_scatter | solution.py:1119
  865.7 17.4 %collective-permute-start.26 = (bf16[2,2,4,32,896]{4,3,2,1,0:T(8,128)(2,1)}, bf16[2,2,4,32,896]{4,3,2,1,0:T(8,128)(2,1)}, u32[]{:S(2)}, u32[]{:S(2)}) collective-permute-start(bf16[2,2,4,32,896]{4,3,2,1,0:T(8,128)(2,1)} %fusion.31), channel_id=1, source_target_pairs={{0,4},{4,0},{8,12},{12,8},{16,20},{20,16},{24,28},{28,24},{1,5},{5... | collective-permute-start | bytes 2752520 | tf_op jit(solution)/shard_map/ppermute | solution.py:891
  865.8 4.5 collective-permute-start.33
  870.3 4.2 collective-permute-start.34
  874.5 4.0 collective-permute-start.35
  878.4 33.0 %collective-permute-start.36 = (f32[3,24]{1,0:T(4,128)S(1)}, f32[3,24]{1,0:T(4,128)S(1)}, u32[]{:S(2)}, u32[]{:S(2)}) collective-permute-start(f32[3,24]{1,0:T(4,128)S(1)} %add.302), channel_id=1, source_target_pairs={{0,2},{1,3},{2,0},{3,1},{4,6},{5,7},{6,4},{7,5},{8,10},{9,11},{10,... | collective-permute-start | bytes 872 | tf_op jit(solution)/shard_map/ppermute | solution.py:854
  885.9 9.7 collective-permute-start.27
  888.1 72.6 %reduce-scatter.15.cloned.1.call-start = ((), (), s32[]{:S(2)}) async-start(), calls=%async_computation.14 | async-start | bytes 3112960 | tf_op jit(solution)/shard_map/reduce_scatter | solution.py:1156
  897.3 14.8 %collective-permute-start.28 = (bf16[4,32,896]{2,1,0:T(8,128)(2,1)S(1)}, bf16[4,32,896]{2,1,0:T(8,128)(2,1)S(1)}, u32[]{:S(2)}, u32[]{:S(2)}) collective-permute-start(bf16[4,32,896]{2,1,0:T(8,128)(2,1)S(1)} %fusion.38), channel_id=1, source_target_pairs={{0,8},{4,12},{8,0},{12,4},{16,24},{20,28},{24,16},{28,20},{1,9},{5... | collective-permute-start | bytes 688136 | tf_op jit(solution)/shard_map/ppermute | solution.py:891
  912.3 11.3 %collective-permute-start.31 = (bf16[32,896]{1,0:T(8,128)(2,1)S(1)}, bf16[32,896]{1,0:T(8,128)(2,1)S(1)}, u32[]{:S(2)}, u32[]{:S(2)}) collective-permute-start(bf16[32,896]{1,0:T(8,128)(2,1)S(1)} %get-tuple-element.292), channel_id=1, source_target_pairs={{0,3},{1,0},{2,1},{3,2},{4,7},{5,4},{6,5},{7,6},{8,11},{9,8},{10,9... | collective-permute-start | bytes 172040 | tf_op jit(solution)/shard_map/ppermute | solution.py:897
  914.8 8.7 collective-permute-start.30
  914.8 8.8 collective-permute-start.29
  (71 other events, 711.6 us)
Sparse Core Ops, SparseCore 0:
  11.4 79.9 all-gather.2
  94.4 164.3 all-gather.4
  399.7 132.1 reduce-scatter.6
  535.5 51.2 reduce-scatter.8
  590.0 66.8 reduce-scatter.10
  812.0 53.1 reduce-scatter.12
  888.2 20.9 reduce-scatter.16
  911.6 48.9 reduce-scatter.14

commit v4 on v3

--- a/solution.py
+++ b/solution.py
@@ -39,12 +39,16 @@
     return jnp.where(lane < 32, pltpu.roll(values, 96, 1), pltpu.roll(values, 32, 1))
 
 
-def project_kernel(x_ref, gain_ref, w_ref, cos_ref, sin_ref, hidden_ref, q_ref, kv_ref):
+CR = MH * MP + 2 * NS + 128
+FIRST = CR + QH * HD + 2 * KVH * HD + 128
+
+
+def project_kernel(x_ref, gain_ref, w_ref, cos_ref, sin_ref, hidden_ref, cr_ref, q_ref, kv_ref):
     x = x_ref[...].astype(F32)
     scale = lax.rsqrt(jnp.mean(x * x, axis=-1, keepdims=True) + EPSILON)
     hidden = (x * scale * gain_ref[...]).astype(BF16)
     hidden_ref[...] = hidden
-    lin = contract(hidden, w_ref[...], 1, 0)
+    lin = contract(hidden, w_ref[:, CR : CR + QH * HD + 2 * KVH * HD], 1, 0)
     cosine, sine = cos_ref[...], sin_ref[...]
     lane = lanes(cosine.shape)
     for pair in range(QH // 2):
@@ -61,33 +65,97 @@
         kv_ref[:, group * 128 : (group + 1) * 128] = (
             part * cosine + swap_halves(part) * sine
         ).astype(BF16)
+    cr_ref[...] = contract(hidden, w_ref[:, :CR], 1, 0).astype(BF16)
 
 
 def project(x, gain, w_first, cosine, sine):
     rows, width = x.shape
-    tile = 256
+    tile = 256 if rows % 256 == 0 else 128
     block = lambda cols: pl.BlockSpec((tile, cols), lambda i: (i, 0))
-    fixed = lambda shape: pl.BlockSpec(shape, lambda i: (0, 0))
-    kv_width = 2 * KVH * HD
+    fixed = lambda array: pl.BlockSpec(array.shape, lambda i: (0, 0))
+    cols = [width, CR, QH * HD, 2 * KVH * HD]
     return pl.pallas_call(
         project_kernel,
         grid=(rows // tile,),
         in_specs=[
-            block(width),
-            fixed((1, width)),
-            fixed((width, QH * HD + kv_width)),
+            block(width), fixed(gain), pl.BlockSpec((width, FIRST), lambda i: (0, 0)), block(128),
             block(128),
-            block(128),
-        ],
-        out_specs=[block(width), block(QH * HD), block(kv_width)],
-        out_shape=[
-            jax.ShapeDtypeStruct((rows, width), BF16),
-            jax.ShapeDtypeStruct((rows, QH * HD), BF16),
-            jax.ShapeDtypeStruct((rows, kv_width), BF16),
-        ],
+        ],
+        out_specs=[block(size) for size in cols],
+        out_shape=[jax.ShapeDtypeStruct((rows, size), BF16) for size in cols],
         compiler_params=pltpu.CompilerParams(vmem_limit_bytes=VMEM_BYTES),
         name="project",
     )(x, gain, w_first, cosine, sine)
+
+
+def finish_kernel(
+    x_ref, gain_ref, dgate_ref, dcr_ref, dq_ref, dkv_ref, cos_ref, sin_ref, middle_ref, wg_ref,
+    w_ref, dx_ref, dkv_out_ref, dgain_ref, dgain_s,
+):
+    @pl.when(pl.program_id(0) == 0)
+    def _():
+        dgain_s[...] = jnp.zeros(dgain_s.shape, F32)
+
+    dkv = dkv_ref[0, 0].astype(F32)
+    for source in range(1, dkv_ref.shape[0]):
+        dkv = dkv + dkv_ref[source, 0].astype(F32)
+    cosine, sine = cos_ref[...], sin_ref[...]
+    turned = []
+    for group in range(KVH):
+        part = dkv[:, group * 128 : (group + 1) * 128]
+        back = part * cosine + swap_halves(part * sine)
+        turned.append(jnp.where(lanes(part.shape) < HD, back, part))
+    dkv = jnp.concatenate(turned, axis=1).astype(BF16)
+    dkv_out_ref[...] = dkv
+    at = CR + QH * HD
+    grad = (
+        contract(dgate_ref[...], wg_ref[...], 1, 1)
+        + contract(dcr_ref[...], w_ref[:, :CR], 1, 1)
+        + contract(dq_ref[...], w_ref[:, CR:at], 1, 1)
+        + contract(dkv, w_ref[:, at : at + 2 * KVH * HD], 1, 1)
+    )
+    x = x_ref[...].astype(F32)
+    scale = lax.rsqrt(jnp.mean(x * x, axis=-1, keepdims=True) + EPSILON)
+    scaled = grad * gain_ref[...]
+    shrink = jnp.mean(scaled * x, axis=-1, keepdims=True) * (scale * scale * scale)
+    dx_ref[...] = (middle_ref[...] + scaled * scale - x * shrink).astype(BF16)
+    dgain_s[0:1, :] += jnp.sum(grad * x * scale, axis=0, keepdims=True)
+    dgain_ref[...] = dgain_s[...]
+
+
+def finish(x, gain, dgate, dcr, dq, dkv_all, cosine, sine, middle, w_gates, w_first):
+    rows, width = x.shape
+    span = dkv_all.shape[2]
+    tile = min(256, span)
+    per_seq = span // tile
+    block = lambda array: pl.BlockSpec((tile, array.shape[1]), lambda i: (i, 0))
+    fixed = lambda array: pl.BlockSpec(array.shape, lambda i: (0, 0))
+    keys = pl.BlockSpec(
+        (dkv_all.shape[0], 1, tile, dkv_all.shape[3]), lambda i: (0, i // per_seq, i % per_seq, 0)
+    )
+    kv_width = dkv_all.shape[3]
+    return pl.pallas_call(
+        finish_kernel,
+        grid=(rows // tile,),
+        in_specs=[
+            block(x), fixed(gain), block(dgate), block(dcr), block(dq), keys, block(cosine),
+            block(sine), block(middle), fixed(w_gates),
+            pl.BlockSpec((width, FIRST), lambda i: (0, 0)),
+        ],
+        out_specs=[
+            block(x),
+            pl.BlockSpec((tile, kv_width), lambda i: (i, 0)),
+            pl.BlockSpec((8, width), lambda i: (0, 0)),
+        ],
+        out_shape=[
+            jax.ShapeDtypeStruct((rows, width), BF16),
+            jax.ShapeDtypeStruct((rows, kv_width), BF16),
+            jax.ShapeDtypeStruct((8, width), F32),
+        ],
+        scratch_shapes=[pltpu.VMEM((8, width), F32)],
+        compiler_params=pltpu.CompilerParams(vmem_limit_bytes=VMEM_BYTES),
+        name="finish",
+    )(x, gain, dgate, dcr, dq, dkv_all, cosine, sine, middle, w_gates, w_first)
 
 
 def visible(segk_ref, segq, query_row, at, key_rows):
@@ -366,6 +434,10 @@
     return row >= lanes((CHUNK, CHUNK))
 
 
+def token_rows(token_ref):
+    return jnp.concatenate([token_ref[0]] * 16, axis=0).T
+
+
 def decay_rows(rate, head_ref, token):
     raw = rate.astype(F32) + head_ref[1:2, :]
     step = jnp.maximum(raw, 0.0) + jnp.log1p(jnp.exp(-jnp.abs(raw)))
@@ -388,7 +460,7 @@
 
 
 def mixer_scan_kernel(
-    proj_ref, rim_ref, token_ref, head_ref, taps_ref, shift_ref, spread_ref,
+    cr_ref, rim_ref, token_ref, head_ref, taps_ref, shift_ref, spread_ref,
     act_ref, states_ref, gains_ref, final_ref, final_gain_ref,
     ext_s, state_s, gain_s,
 ):
@@ -404,12 +476,12 @@
     def _():
         ext_s[0:8, :] = ext_s[CHUNK : CHUNK + 8, :]
 
-    token = token_ref[0]
-    ext_s[8 : 8 + CHUNK, :] = proj_ref[0, :, DI : DI + CC].astype(F32)
+    token = token_rows(token_ref)
+    ext_s[8 : 8 + CHUNK, :] = cr_ref[0, :, :CC].astype(F32)
     total = conv_total(ext_s, token, taps_ref, shift_ref)
     act = (total * jax.nn.sigmoid(total)).astype(BF16)
     act_ref[0] = act
-    weight_end, _, gain = decay_rows(proj_ref[0, :, DI + CC :], head_ref, token)[-3:]
+    weight_end, _, gain = decay_rows(cr_ref[0, :, CC:], head_ref, token)[-3:]
     states_ref[0, 0] = state_s[...].astype(BF16)
     before = gain_s[...]
     gains_ref[0, 0] = before
@@ -424,8 +496,8 @@
 
     @pl.when(chunk == pl.num_programs(0) - 1)
     def _():
-        final_ref[0] = state
-        final_gain_ref[0] = before * gain_rows
+        final_ref[0] = state.astype(BF16)
+        final_gain_ref[0] = widen(before * gain_rows, spread)
 
 
 def entering_state(local_ref, gains_ref, state_ref, spread):
@@ -458,11 +530,11 @@
 
 
 def mixer_out_kernel(
-    proj_ref, act_ref, token_ref, states_ref, gains_ref, state_ref, head_ref, skip_ref, gain_ref,
+    gate_ref, cr_ref, act_ref, token_ref, states_ref, gains_ref, state_ref, head_ref, skip_ref, gain_ref,
     spread_ref, y_ref, out_ref,
 ):
-    token, spread = token_ref[0], spread_ref[...]
-    _, step, _, running, _, entry, _ = decay_rows(proj_ref[0, :, DI + CC :], head_ref, token)
+    token, spread = token_rows(token_ref), spread_ref[...]
+    _, step, _, running, _, entry, _ = decay_rows(cr_ref[0, :, CC:], head_ref, token)
     b_rows, c_rows = act_ref[0, :, DI : DI + NS], act_ref[0, :, DI + NS :]
     state = entering_state(states_ref, gains_ref, state_ref, spread)
     carried = contract(c_rows, state, 1, 0) * widen(entry, spread)
@@ -485,19 +557,19 @@
             + skip_ref[:, cols] * xs.astype(F32)
         )
         y_ref[0, :, cols] = y
-        gate = proj_ref[0, :, cols].astype(F32)
+        gate = gate_ref[0, :, cols].astype(F32)
         gated = y * (gate * jax.nn.sigmoid(gate))
         square = square + gated * gated
     scale = lax.rsqrt(jnp.sum(square, axis=1, keepdims=True) * (1.0 / DI) + EPSILON)
     for pair in range(MH // 2):
         cols = slice(pair * 128, (pair + 1) * 128)
-        gate = proj_ref[0, :, cols].astype(F32)
+        gate = gate_ref[0, :, cols].astype(F32)
         gated = y_ref[0, :, cols] * (gate * jax.nn.sigmoid(gate))
         out_ref[0, :, cols] = (gated * scale * gain_ref[:, cols]).astype(BF16)
 
 
 def mixer_gate_back_kernel(
-    gmix_ref, y_ref, proj_ref, act_ref, token_ref, head_ref, gain_ref, spread_ref,
+    gmix_ref, y_ref, gate_ref, cr_ref, act_ref, token_ref, head_ref, gain_ref, spread_ref,
     gy_ref, dgate_ref, gstates_ref, gains_ref, final_ref, dgain_ref, dskip_ref,
     state_s, gain_s, dgain_s, dskip_s,
 ):
@@ -513,10 +585,10 @@
         state_s[...] = jnp.zeros(state_s.shape, F32)
         gain_s[...] = jnp.ones(gain_s.shape, F32)
 
-    token, spread = token_ref[0], spread_ref[...]
-    entry, gain = decay_rows(proj_ref[0, :, DI + CC :], head_ref, token)[-2:]
+    token, spread = token_rows(token_ref), spread_ref[...]
+    entry, gain = decay_rows(cr_ref[0, :, CC:], head_ref, token)[-2:]
     y = y_ref[0]
-    gate = proj_ref[0, :, :DI].astype(F32)
+    gate = gate_ref[0].astype(F32)
     sig = jax.nn.sigmoid(gate)
     swish = gate * sig
     gated = y * swish
@@ -544,17 +616,17 @@
 
     @pl.when(chunk == pl.num_programs(0) - 1)
     def _():
-        final_ref[0] = state
+        final_ref[0] = state.astype(BF16)
 
     dgain_ref[...] = dgain_s[...]
     dskip_ref[...] = dskip_s[...]
 
 
 def mixer_back_kernel(
-    gy_ref, y_ref, dgate_ref, proj_ref, halo_ref, rim_ref, act_ref, token_ref,
+    gy_ref, y_ref, cr_ref, halo_ref, rim_ref, act_ref, token_ref,
     states_ref, gains_ref, state_ref, gstates_ref, ggains_ref, gstate_ref,
     head_ref, skip_ref, taps_ref, shift_ref, spread_ref, spread_first_ref,
-    dproj_ref, drim_ref, dconv_ref, dhead_ref,
+    dcr_ref, drim_ref, dconv_ref, dhead_ref,
     ext_s, grad_s, carry_s, dconv_s, dhead_s,
 ):
     step_index = pl.program_id(0)
@@ -575,12 +647,12 @@
 
     @pl.when(step_index < last_step)
     def _():
-        ext_s[0:8, :] = halo_ref[0, :, DI : DI + CC].astype(F32)[8:16]
-
-    ext_s[8 : 8 + CHUNK, :] = proj_ref[0, :, DI : DI + CC].astype(F32)
-    token, spread, spread_first = token_ref[0], spread_ref[...], spread_first_ref[...]
+        ext_s[0:8, :] = halo_ref[0, :, :CC].astype(F32)[8:16]
+
+    ext_s[8 : 8 + CHUNK, :] = cr_ref[0, :, :CC].astype(F32)
+    token, spread, spread_first = token_rows(token_ref), spread_ref[...], spread_first_ref[...]
     raw, step, log_decay, running, weight_end, entry, gain = decay_rows(
-        proj_ref[0, :, DI + CC :], head_ref, token
+        cr_ref[0, :, CC:], head_ref, token
     )
     b_rows, c_rows = act_ref[0, :, DI : DI + NS], act_ref[0, :, DI + NS :]
     state = entering_state(states_ref, gains_ref, state_ref, spread)
@@ -645,9 +717,8 @@
         grad_s[5 + tap : 5 + tap + CHUNK, :] += part * taps_ref[tap : tap + 1, :]
     grad_s[CHUNK : CHUNK + 8, :] += carry_s[...]
     carry_s[...] = grad_s[0:8, :]
-    dproj_ref[0, :, :DI] = dgate_ref[0]
-    dproj_ref[0, :, DI : DI + CC] = grad_s[8 : 8 + CHUNK, :].astype(BF16)
-    dproj_ref[0, :, DI + CC :] = grad_rate.astype(BF16)
+    dcr_ref[0, :, :CC] = grad_s[8 : 8 + CHUNK, :].astype(BF16)
+    dcr_ref[0, :, CC:] = grad_rate.astype(BF16)
 
     @pl.when(step_index == last_step)
     def _():
@@ -666,6 +737,7 @@
         "chunk": lambda array, at: pl.BlockSpec(
             (1, 1) + array.shape[2:], lambda c: (at, place(c), 0, 0)
         ),
+        "token": lambda array, at: pl.BlockSpec((1, 8, CHUNK), lambda c: (at, 0, place(c))),
         "seq": lambda array, at: pl.BlockSpec((1,) + array.shape[1:], lambda c: (at, 0, 0)),
         "own": lambda array, at: pl.BlockSpec((1,) + array.shape[1:], lambda c: (0, 0, 0)),
         "fixed": lambda array, at: pl.BlockSpec(array.shape, lambda c: (0, 0)),
@@ -702,33 +774,33 @@
     )(*arrays)
 
 
-def mixer_scan(seq, earlier, proj, rim, token, heads, taps, shift, spread):
-    seqs, span, _ = proj.shape
+def mixer_scan(seq, earlier, cr, rim, token, heads, taps, shift, spread):
+    seqs, span, _ = cr.shape
     chunks = span // CHUNK
     return mixer_call(
         mixer_scan_kernel, "mixer_scan", seq, chunks, False,
         [
-            ("block", proj), ("seq", rim), ("block", token), ("fixed", heads), ("fixed", taps),
+            ("block", cr), ("seq", rim), ("token", token), ("fixed", heads), ("fixed", taps),
             ("fixed", shift), ("fixed", spread),
         ],
         [
             ("block", jax.ShapeDtypeStruct((seqs, span, CC), BF16)),
             ("chunk", jax.ShapeDtypeStruct((seqs, chunks, NS, DI), BF16)),
             ("chunk", jax.ShapeDtypeStruct((seqs, chunks, 8, 128), F32)),
-            ("own", jax.ShapeDtypeStruct((1, NS, DI), F32)),
-            ("own", jax.ShapeDtypeStruct((1, 8, 128), F32)),
+            ("own", jax.ShapeDtypeStruct((1, NS, DI), BF16)),
+            ("own", jax.ShapeDtypeStruct((1, 8, DI), F32)),
         ],
         [(CHUNK + 8, CC), (NS, DI), (8, 128)],
         earlier,
     )
 
 
-def mixer_out(seq, earlier, proj, act, token, states, gains, state, heads, skip, gain, spread):
-    seqs, span, _ = proj.shape
+def mixer_out(seq, earlier, gate, cr, act, token, states, gains, state, heads, skip, gain, spread):
+    seqs, span, _ = cr.shape
     return mixer_call(
         mixer_out_kernel, "mixer_out", seq, span // CHUNK, False,
         [
-            ("block", proj), ("block", act), ("block", token), ("chunk", states),
+            ("block", gate), ("block", cr), ("block", act), ("token", token), ("chunk", states),
             ("chunk", gains), ("own", state), ("fixed", heads), ("fixed", skip),
             ("fixed", gain), ("fixed", spread),
         ],
@@ -741,13 +813,15 @@
     )
 
 
-def mixer_gate_back(seq, earlier, gmix, y, proj, act, token, heads, gain, spread):
-    seqs, span, _ = proj.shape
+def mixer_gate_back(
+    seq, earlier, gmix, y, gate, cr, act, token, heads, gain, spread
+):
+    seqs, span, _ = cr.shape
     chunks = span // CHUNK
     return mixer_call(
         mixer_gate_back_kernel, "mixer_gate_back", seq, chunks, True,
         [
-            ("block", gmix), ("block", y), ("block", proj), ("block", act), ("block", token),
+            ("block", gmix), ("block", y), ("block", gate), ("block", cr), ("block", act), ("token", token),
             ("fixed", heads), ("fixed", gain), ("fixed", spread),
         ],
         [
@@ -755,7 +829,7 @@
             ("block", jax.ShapeDtypeStruct((seqs, span, DI), BF16)),
             ("chunk", jax.ShapeDtypeStruct((seqs, chunks, NS, DI), BF16)),
             ("chunk", jax.ShapeDtypeStruct((seqs, chunks, 8, 128), F32)),
-            ("own", jax.ShapeDtypeStruct((1, NS, DI), F32)),
+            ("own", jax.ShapeDtypeStruct((1, NS, DI), BF16)),
             ("fixed", jax.ShapeDtypeStruct((8, DI), F32)),
             ("fixed", jax.ShapeDtypeStruct((8, DI), F32)),
         ],
@@ -765,15 +839,15 @@
 
 
 def mixer_back(
-    seq, earlier, gy, y, dgate, proj, rim, act, token, states, gains, state, gstates, ggains,
+    seq, earlier, gy, y, cr, rim, act, token, states, gains, state, gstates, ggains,
     gstate, heads, skip, taps, shift, spread, spread_first,
 ):
-    seqs, span, width = proj.shape
+    seqs, span, width = cr.shape
     return mixer_call(
         mixer_back_kernel, "mixer_back", seq, span // CHUNK, True,
         [
-            ("block", gy), ("block", y), ("block", dgate), ("block", proj), ("halo", proj),
-            ("seq", rim), ("block", act), ("block", token), ("chunk", states), ("chunk", gains),
+            ("block", gy), ("block", y), ("block", cr), ("halo", cr),
+            ("seq", rim), ("block", act), ("token", token), ("chunk", states), ("chunk", gains),
             ("own", state), ("chunk", gstates), ("chunk", ggains), ("own", gstate),
             ("fixed", heads), ("fixed", skip), ("fixed", taps), ("fixed", shift),
             ("fixed", spread), ("fixed", spread_first),
@@ -804,7 +878,7 @@
         seg_own.astype(F32),
         spare,
     ]
-    return jnp.pad(jnp.stack(rows, axis=-1), ((0, 0), (0, 0), (0, 120)))
+    return jnp.stack(rows, axis=1)
 
 
 def from_behind(block, axis, distance):
@@ -828,7 +902,11 @@
             return
         source = self.count - 1 - self.hop if self.reverse else self.hop
         target = source - 1 if self.reverse else source + 1
-        sent = after((self.gain * self.state.astype(F32) + self.local).astype(BF16), *earlier)
+        sent = self.local
+        if self.hop:
+            sent = (self.gain * self.state.astype(F32) + sent.astype(F32)).astype(BF16)
+        if earlier:
+            sent = after(sent, *earlier)
         self.flying = (lax.ppermute(sent, "ctx", [(source, target)]), target)
         self.hop += 1
 
@@ -854,28 +932,6 @@
             values = values + lax.ppermute(values, axis, route)
             distance *= 2
     return values
-
-
-def gather_all(shard):
-    count, place = lax.axis_size("ctx"), lax.axis_index("ctx")
-    devices, me = lax.axis_size("dp"), lax.axis_index("dp")
-    relative = [shard] + [
-        lax.ppermute(shard, "ctx", [(i, (i + d) % count) for i in range(count)])
-        for d in range(1, count)
-    ]
-    ordered = jnp.stack([relative[-k % count] for k in range(count)])
-    whole = lax.dynamic_slice_in_dim(
-        jnp.concatenate([ordered, ordered]), (count - place) % count, count, 0
-    )
-    bits = devices.bit_length() - 1
-    for bit in list(range(1, bits)) + [0]:
-        other = lax.ppermute(whole, "dp", [(i, i ^ (1 << bit)) for i in range(devices)])
-        low = ((me >> bit) & 1) == 0
-        whole = jnp.stack(
-            [jnp.where(low, whole, other), jnp.where(low, other, whole)],
-            axis=0 if bit else bits - 1,
-        )
-    return whole.reshape((-1,) + shard.shape[1:])
 
 
 def scatter_all(grad):
@@ -928,12 +984,19 @@
         [w_k.reshape(own_rows, KVH, HD), w_v.reshape(own_rows, KVH, HD)], axis=2
     ).reshape(own_rows, kv_width)
     gather = lambda shard: lax.all_gather(shard, axes, axis=0, tiled=True)
-    first_all = gather_all(jnp.concatenate([w_q, w_kv, small_block], axis=1))
-    in_width = DI + CC + 128
-    w_in_all = gather(jnp.pad(w_in, ((0, 0), (0, in_width - w_in.shape[1]))))
+    w_cr = jnp.pad(w_in[:, DI:], ((0, 0), (0, CR - (w_in.shape[1] - DI))))
+    first_all = gather(jnp.concatenate([w_cr, w_q, w_kv, small_block, w_in[:, :DI]], axis=1))
     turned_o = w_o.T
     half_rows, ff = own_rows // 2, w_gate.shape[1]
-    rest = [w_down, w_out, jnp.concatenate([turned_o[:half_rows], turned_o[half_rows:]], axis=1)]
+
+    def fold(block, cut):
+        return jnp.concatenate([block[..., :half_rows, cut:], block[..., half_rows:, cut:]], axis=-1)
+
+    def unfold(block):
+        half = block.shape[-1] // 2
+        return jnp.concatenate([block[..., :half], block[..., half:]], axis=-2)
+
+    rest = [w_down, w_out, fold(turned_o, 0)]
     for matrix in (w_gate, w_up):
         rest += [matrix[:, at : at + width] for at in range(0, ff, width)]
     rest_sizes = [part.shape[0] for part in rest]
@@ -943,10 +1006,10 @@
         cuts.append(rest_all[:, at : at + size])
         at += size
     w_down_all, w_out_all = cuts[0].reshape(-1, width), cuts[1].reshape(-1, width)
-    w_o_all = jnp.stack([cuts[2][..., :q_width], cuts[2][..., q_width:]], axis=1)
-    w_o_all = w_o_all.reshape(width, q_width)
+    w_o_all = unfold(cuts[2]).reshape(width, q_width)
+    w_gates = first_all[:, FIRST:]
     w_gu_all = jnp.concatenate([cut.reshape(width, width) for cut in cuts[3:]], axis=1)
-    small_all = first_all[:, q_width + kv_width :].reshape(-1, slots).astype(F32)
+    small_all = first_all[:, FIRST - 128 : FIRST].reshape(-1, slots).astype(F32)
     parts, at = [], 0
     for size in small_sizes:
         parts.append(small_all[:, at : at + size])
@@ -976,25 +1039,22 @@
     small = (token, bounds, segk, segq, cosine, sine, heads, skip, spread, spread_first)
     first_all, small = lax.optimization_barrier((first_all, small))
     token, bounds, segk, segq, cosine, sine, heads, skip, spread, spread_first = small
-    hidden, q, kv = project(
-        tokens, gain1_all, first_all, cosine.reshape(rows, 128), sine.reshape(rows, 128)
-    )
+    cosine, sine = cosine.reshape(rows, 128), sine.reshape(rows, 128)
+    hidden, cr, q, kv = project(tokens, gain1_all, first_all, cosine, sine)
     q = q.reshape(seqs, span, q_width)
     kv = kv.reshape(seqs, span, kv_width)
     exchange = lambda blocks: lax.all_to_all(blocks, "ctx", 0, 0, tiled=True)
     kv_all = exchange(jnp.broadcast_to(kv[None], (count,) + kv.shape))
-    edge = from_behind(hidden.reshape(seqs, span, width)[:, span - (KC - 1) :], "ctx", 1)
-    proj = low_dot(hidden, w_in_all).astype(BF16).reshape(seqs, span, in_width)
-    rim = low_dot(edge.reshape(-1, width), w_in_all[:, DI : DI + CC]).astype(BF16)
-    rim = jnp.pad(rim.reshape(seqs, KC - 1, CC), ((0, 0), (8 - (KC - 1), 0), (0, 0)))
-    wide = lambda gain: jnp.repeat(gain[:, :1, :MH], MP, axis=2)
+    cr = cr.reshape(seqs, span, CR)
+    rim = from_behind(cr[:, span - (KC - 1) :, :CC], "ctx", 1)
+    rim = jnp.pad(rim, ((0, 0), (8 - (KC - 1), 0), (0, 0)))
     scanned, chains, wide_gains = None, [], []
     for seq in range(seqs):
         scanned = mixer_scan(
-            seq, scanned, proj, rim, token, heads, taps_all,
+            seq, scanned, cr, rim, token, heads, taps_all,
             shift_all, spread,
         )
-        wide_gains.append(wide(scanned[4]))
+        wide_gains.append(scanned[4][:, :1])
         chains.append(Chain(scanned[3], wide_gains[seq], False))
         chains[seq].send()
     act, states, gains = scanned[:3]
@@ -1007,11 +1067,12 @@
         att, lse = attend(seq, bounds, after(q, act, *taken), kv_all, segk, segq)
         atts.append(att)
         lses.append(lse)
+    gate = low_dot(hidden, w_gates).astype(BF16).reshape(seqs, span, DI)
     states_in = []
     for seq in range(seqs):
         states_in.append(chains[seq].finish())
         mixed = mixer_out(
-            seq, mixed, proj, act, token, states, gains, states_in[seq], heads, skip, gain_m_all,
+            seq, mixed, gate, cr, act, token, states, gains, states_in[seq], heads, skip, gain_m_all,
             spread,
         )
     mixer_y, mixer_in = mixed
@@ -1029,8 +1090,6 @@
         silu_product, gate_up[:, :ff].astype(F32), gate_up[:, ff:].astype(F32)
     )
     act_rows = act_float.astype(BF16)
-    layer_result = (middle + low_dot(act_rows, w_down_all)).astype(BF16)
-
     def scatter(grad):
         return lax.psum_scatter(grad, "dp", scatter_dimension=0, tiled=True)
 
@@ -1046,7 +1105,6 @@
     grad_wgu = weight_grad(normed_two, grad_gate_up)
     grad_normed = back_dot(grad_gate_up, w_gu_all)
     grad_normed, grad_down, grad_wgu = lax.optimization_barrier((grad_normed, grad_down, grad_wgu))
-    part_down = scatter(grad_down)
     part_gu = scatter(grad_wgu)
     grad_mid_norm, grad_gain_second = norm2_pull(grad_normed)
     grad_middle = cot_rows.astype(F32) + grad_mid_norm
@@ -1062,7 +1120,7 @@
     gated, chains, grad_gain_mix, grad_skip = None, [], 0.0, 0.0
     for seq in range(seqs):
         gated = mixer_gate_back(
-            seq, gated, grad_mixer_in, mixer_y, proj, act, token, heads, gain_m_all, spread
+            seq, gated, grad_mixer_in, mixer_y, gate, cr, act, token, heads, gain_m_all, spread
         )
         grad_gain_mix, grad_skip = grad_gain_mix + gated[5], grad_skip + gated[6]
         chains.append(Chain(gated[4], wide_gains[seq], True))
@@ -1070,18 +1128,15 @@
     grad_y, grad_gate, gstates, ggains = gated[:4]
     grad_wgates = weight_grad(hidden, grad_gate.reshape(rows, DI)).reshape(-1, own_rows, DI)
     blocks = grad_wo.shape[0]
-    grad_out = jnp.concatenate(
+    grad_rest = jnp.concatenate(
         [
-            grad_wout.reshape(blocks, -1, width),
-            jnp.concatenate([grad_wo[:, :half_rows], grad_wo[:, half_rows:]], axis=2),
-            grad_wgates[..., :width],
-            jnp.concatenate(
-                [grad_wgates[:, :half_rows, width:], grad_wgates[:, half_rows:, width:]], axis=2
-            ),
+            grad_down.reshape(blocks, -1, width), grad_wout.reshape(blocks, -1, width),
+            fold(grad_wo, 0), grad_wgates[..., :width], fold(grad_wgates, width),
         ],
         axis=1,
     )
-    part_out = scatter(after(grad_out.reshape(-1, width), part_gu))
+    part_rest = scatter(grad_rest.reshape(-1, width))
+    cos3, sin3 = cosine.reshape(seqs, span, 128), sine.reshape(seqs, span, 128)
     dqs, dkvs = [], []
     for seq in range(seqs):
         for chain in chains[: seq + 1]:
@@ -1089,50 +1144,48 @@
             chain.send(*dqs[-1:])
         taken = [chain.state for chain in chains[: seq + 1]]
         dq, dkv = attend_back(
-            seq, bounds, after(q, part_down if seq < seqs - 1 else part_gu, *taken), kv_all, segk,
-            segq, atts[seq], grad_att, lses[seq], cosine, sine,
+            seq, bounds, after(q, *taken), kv_all, segk,
+            segq, atts[seq], grad_att, lses[seq], cos3, sin3,
         )
         dqs.append(dq)
         dkvs.append(dkv)
     dkv_all = exchange(jnp.concatenate(dkvs, axis=1))
     dq = jnp.concatenate(dqs, axis=0)
     last, rims, grad_conv, grad_heads = None, [], 0.0, 0.0
-    waits = [(grad_out,)] + [()] * (seqs - 1)
+    waits = [(grad_rest, part_gu)] + [()] * (seqs - 1)
     for seq in range(seqs):
         gstate = chains[seq].finish()
+        if seq == seqs - 1:
+            gu_blocks = part_gu.reshape(count, own_rows, 2 * ff)
+            parts = [after(part_rest, *rims).reshape(count, -1, width)]
+            parts += [gu_blocks[..., at : at + width] for at in range(0, 2 * ff, width)]
+            rest_low = jnp.concatenate(parts, axis=1).reshape(-1, width)
+            waits[seq] = (rest_low,)
         last = mixer_back(
-            seq, last, after(grad_y, dqs[-1], *waits[seq]), mixer_y, grad_gate, proj, rim, act, token, states,
+            seq, last, after(grad_y, dqs[-1], *waits[seq]), mixer_y, cr, rim, act, token, states,
             gains, states_in[seq], gstates, ggains, gstate, heads, skip, taps_all, shift_all,
             spread, spread_first,
         )
         rims.append(last[1])
         grad_conv, grad_heads = grad_conv + last[2], grad_heads + last[3]
-    grad_proj, grad_rim = last[0], jnp.concatenate(rims, axis=0)
+    grad_cr, grad_rim = last[0], jnp.concatenate(rims, axis=0)
     back_rim = from_behind(grad_rim[:, 8 - (KC - 1) :].astype(BF16), "ctx", -1)
-    edge = grad_proj[:, span - (KC - 1) :, DI : DI + CC].astype(F32) + back_rim.astype(F32)
-    grad_proj = lax.dynamic_update_slice(
-        grad_proj, after(edge.astype(BF16), part_out), (0, span - (KC - 1), DI)
-    ).reshape(rows, in_width)
-    grad_wconv = weight_grad(hidden, grad_proj[:, DI:])
-    part_conv = scatter(grad_wconv)
-    grad_kv = jnp.sum(after(dkv_all, grad_wconv).astype(F32), axis=0)
-    out_conv = lax.psum_scatter(part_conv, "ctx", scatter_dimension=0, tiled=True).astype(F32)
-    grad_kv = grad_kv.reshape(seqs, span, KVH, 2 * HD)
-    turned = grad_kv[..., :HD] * sine[:, :, None, :HD]
-    turned = jnp.concatenate([turned[..., HD // 2 :], turned[..., : HD // 2]], axis=-1)
-    grad_key = grad_kv[..., :HD] * cosine[:, :, None, :HD] + turned
-    grad_kv = jnp.concatenate([grad_key, grad_kv[..., HD:]], axis=-1).astype(BF16)
-    grad_first = jnp.concatenate(
-        [dq.reshape(rows, q_width), grad_kv.reshape(rows, kv_width)], axis=1
-    )
+    edge = grad_cr[:, span - (KC - 1) :, :CC].astype(F32) + back_rim.astype(F32)
+    grad_cr = lax.dynamic_update_slice(
+        grad_cr, edge.astype(BF16), (0, span - (KC - 1), 0)
+    ).reshape(rows, CR)
+    rest_out = lax.psum_scatter(rest_low, "ctx", scatter_dimension=0, tiled=True).astype(F32)
+    grad_wcr = weight_grad(hidden, grad_cr)
+    part_cr = scatter(grad_wcr)
+    layer_result = (middle + low_dot(after(act_rows, part_cr), w_down_all)).astype(BF16)
+    out_cr = lax.psum_scatter(part_cr, "ctx", scatter_dimension=0, tiled=True).astype(F32)
+    grad_tokens, grad_kv, grad_gain_first = finish(
+        tokens, gain1_all, grad_gate.reshape(rows, DI), after(grad_cr, grad_wcr, rest_out),
+        dq.reshape(rows, q_width), dkv_all, cosine, sine, grad_middle, w_gates, first_all,
+    )
+    grad_first = jnp.concatenate([dq.reshape(rows, q_width), grad_kv], axis=1)
     grad_wfirst = weight_grad(hidden, grad_first)
-    grad_hidden = back_dot(after(grad_proj, grad_wconv), w_in_all) + back_dot(
-        grad_first, first_all[:, : q_width + kv_width]
-    )
-    tokens_f = tokens.astype(F32)
-    _, norm1_pull = jax.vjp(rms_scale, tokens_f, gain1_all)
-    grad_tokens_norm, grad_gain_first = norm1_pull(grad_hidden)
-    grad_tokens = (grad_middle + grad_tokens_norm).astype(BF16)
+    grad_gain_first = grad_gain_first[0]
 
     devices = first_all.shape[0] // own_rows
     small_grads = jnp.concatenate(
@@ -1149,29 +1202,15 @@
     out_first = scatter_all(
         jnp.concatenate([grad_wfirst, small_grads.reshape(-1, 128).astype(BF16)], axis=1)
     )
-    parts = [part_down.reshape(count, -1, width), part_out.reshape(count, -1, width)]
     rest_sizes = rest_sizes[:3] + [own_rows, half_rows] + rest_sizes[3:]
-    part_gu = part_gu.reshape(count, own_rows, 2 * ff)
-    parts += [part_gu[..., at : at + width] for at in range(0, 2 * ff, width)]
-    rest_out = lax.psum_scatter(
-        after(jnp.concatenate(parts, axis=1).reshape(-1, width), part_conv),
-        "ctx",
-        scatter_dimension=0,
-        tiled=True,
-    ).astype(F32)
     outs, at = [], 0
     for size in rest_sizes:
         outs.append(rest_out[at : at + size])
         at += size
     out_down, out_wout = outs[0], outs[1]
-    out_wo = jnp.concatenate([outs[2][:, :q_width], outs[2][:, q_width:]], axis=0)
+    out_wo = unfold(outs[2])
     out_win = jnp.concatenate(
-        [
-            outs[3],
-            jnp.concatenate([outs[4][:, : DI - width], outs[4][:, DI - width :]], axis=0),
-            out_conv[:, : w_in.shape[1] - DI],
-        ],
-        axis=1,
+        [outs[3], unfold(outs[4]), out_cr[:, : w_in.shape[1] - DI]], axis=1
     )
     halves = ff // width
     out_gate = jnp.concatenate(outs[5 : 5 + halves], axis=1)

time: 987 us -> 969 us (0.982)
  other arithmetic: 106 us -> 58.1 us
  waiting for transfers between devices: 220 us -> 263 us
  matrix products: 202 us -> 164 us
  Pallas kernels: 234 us -> 259 us
  local copies, waits for them, and re-layouts: 102 us -> 89.7 us
  starting transfers between devices: 95.5 us -> 107 us
    reduce_scatter x4 -> x3, waiting for transfers between devices: 83 us -> 0.02 us  [scatter(): return lax.psum_scatter(grad, 'dp', scatter_dimension=0, tiled=True)]
    all_gather x2, waiting for transfers between devices: 0.04 us -> 60 us  [body(): gather = lambda shard: lax.all_gather(shard, axes, axis=0, tiled=True)]
    ppermute x18, waiting for transfers between devices: 79.5 us -> 124 us  [send(): self.flying = (lax.ppermute(sent, 'ctx', [(source, target)]), target)]
    ppermute x2, waiting for transfers between devices: 0.01 us -> 42.4 us  [from_behind(): return lax.ppermute(block, axis, route)]
    reduce_scatter x2, waiting for transfers between devices: 31.3 us -> 0.02 us  [the longest x1 0.02 us: body(): lax.psum_scatter(rest_low, 'ctx', scatter_dimension=0, tiled=True)]
    convert_element_type x20 -> x14, other arithmetic: 33.6 us -> 6.22 us  [the longest x12 4.53 us: send(): sent = (self.gain * self.state.astype(F32) + sent.astype(F32)).astype(BF16)]
    dot_general x5 -> x3, matrix products: 71 us -> 46.8 us  [back_dot(): return jnp.einsum('ro,io->ri', grad, weight, preferred_element_type=F32)]
    pallas_call x0 -> x1, Pallas kernels: none -> 22.8 us  [finish(): pl.pallas_call(finish_kernel, grid=(rows // tile,), in_specs=[block(x), f...]
  transfers between devices with their start and end apart: 47 -> 40, of which waited for: 13 -> 16; matrix products, arithmetic and copies ran while one was open for 28% -> 17% of each run, Pallas kernels for 24% -> 27%
where the time goes in v4:
time: 969 us; the launch traced here: 958 us
  waiting for transfers between devices  263 us (27%)
  Pallas kernels  259 us (27%)
  matrix products  164 us (17%)
  starting transfers between devices  107 us (11%)
  local copies, waits for them, and re-layouts  89.7 us (9%)
  other arithmetic  58.1 us (6%)
  between operations  16 us (2%)
    pallas_call x12, Pallas kernels, mixer_call(): pl.pallas_call(run, grid=(chunks,), in_specs=in_specs, out_specs=out_spec...  158 us
    ppermute x18, waiting for transfers between devices, send(): self.flying = (lax.ppermute(sent, 'ctx', [(source, target)]), target)  124 us
    dot_general x7, matrix products, weight_grad(): jnp.einsum('ri,ro->io', left, right, preferred_element_type=F32)  63.7 us
    all_gather x2, waiting for transfers between devices, body(): gather = lambda shard: lax.all_gather(shard, axes, axis=0, tiled=True)  60 us
    dot_general x5, matrix products, body(): low_dot = lambda a, b: jnp.dot(a, b, preferred_element_type=F32)  52 us
    dot_general x3, matrix products, back_dot(): return jnp.einsum('ro,io->ri', grad, weight, preferred_element_type=F32)  46.8 us
    all_to_all x2, starting transfers between devices, body(): exchange = lambda blocks: lax.all_to_all(blocks, 'ctx', 0, 0, tiled=True)  44 us
    ppermute x2, waiting for transfers between devices, from_behind(): return lax.ppermute(block, axis, route)  42.4 us
  transfers between devices with their start and end apart: 40, of which 16 were waited for; matrix products, arithmetic and copies ran while one was open for 17% of the time, Pallas kernels for 27%

profile of v4, /device:TPU:0, one launch (start us, length us, event | category | flops | bytes accessed | tf_op | source)
XLA Modules:
  0.0 957.7 jit_solution(996746233461002644)
XLA Ops:
  11.5 2.8 concatenate.90
  32.4 2.8 fusion.37
  38.5 60.0 %all-gather.3.cloned.1.call-done.w_ref = bf16[1024,4352]{1,0:T(8,128)(2,1)} async-done(((bf16[32,4352]{1,0:T(8,128)(2,1)}), bf16[1024,4352]{1,0:T(8,128)(2,1)}) %all-gather.3.cloned.1.call-update) | async-done | bytes 8912912 | tf_op jit(solution)/shard_map/all_gather | solution.py:986
  100.3 15.3 %project.1 = (bf16[1536,1024]{1,0:T(8,128)(2,1)}, bf16[1536,1920]{1,0:T(8,128)(2,1)}, bf16[1536,512]{1,0:T(8,128)(2,1)}, bf16[1536,256]{1,0:T(8,128)(2,1)}) custom-call(bf16[1536,1024]{1,0:T(8,128)(2,1)} %bitcast.209, f32[1,1024]{1,0:T(1,128)} %reshape.273.gain_ref, bf16[1024,4352]{1,0:T(8,128)(2,1)} %all-gather.3.cloned.1.call-done.w_ref, ...), custom_call_target="tpu_custom_call" | custom-call | tf_op jit(solution)/shard_map/project/pallas_call | solution.py:77
  116.5 3.4 collective-permute-start
  124.5 3.1 broadcast_in_dim.59
  127.6 3.8 all-to-all-start
  132.1 9.4 mixer_scan.3
  141.5 4.1 collective-permute-start.7
  145.6 8.6 convolution_convert_fusion.2
  155.7 9.1 mixer_scan.4
  166.1 9.2 mixer_scan.5
  179.3 56.7 %collective-permute-done.7 = bf16[1,128,1536]{2,1,0:T(8,128)(2,1)S(1)} collective-permute-done((bf16[1,128,1536]{2,1,0:T(8,128)(2,1)}, bf16[1,128,1536]{2,1,0:T(8,128)(2,1)S(1)}, u32[]{:S(2)}, u32[]{:S(2)}) %collective-permute-start.7) | collective-permute-done | bytes 393248 | tf_op jit(solution)/shard_map/ppermute | solution.py:910
  236.9 16.0 %collective-permute-done.4 = bf16[1,128,1536]{2,1,0:T(8,128)(2,1)S(1)} collective-permute-done((bf16[1,128,1536]{2,1,0:T(8,128)(2,1)}, bf16[1,128,1536]{2,1,0:T(8,128)(2,1)S(1)}, u32[]{:S(2)}, u32[]{:S(2)}) %collective-permute-start.4) | collective-permute-done | bytes 393248 | tf_op jit(solution)/shard_map/ppermute | solution.py:910
  253.7 15.8 %collective-permute-done.1 = bf16[1,128,1536]{2,1,0:T(8,128)(2,1)S(1)} collective-permute-done((bf16[1,128,1536]{2,1,0:T(8,128)(2,1)}, bf16[1,128,1536]{2,1,0:T(8,128)(2,1)S(1)}, u32[]{:S(2)}, u32[]{:S(2)}) %collective-permute-start.1) | collective-permute-done | bytes 393248 | tf_op jit(solution)/shard_map/ppermute | solution.py:910
  275.3 9.0 mixer_out.3
  285.0 8.9 mixer_out.4
  294.8 9.0 mixer_out.5
  305.5 7.4 attend.5
  312.9 7.4 attend.3
  320.4 7.5 attend.4
  333.3 6.0 slice.388
  339.3 6.3 fusion.68
  349.3 7.2 multiply_reduce_fusion.2
  356.6 20.9 %convolution_convert_fusion = bf16[1536,4096]{1,0:T(8,128)(2,1)} fusion(bf16[1024,1024]{1,0:T(8,128)(2,1)} %bitcast.227, bf16[1024,1024]{1,0:T(8,128)(2,1)} %bitcast.229, bf16[1024,1024]{1,0:T(8,128)(2,1)} %bitcast.231, bf16[1024,1024]{1,0:T(8,128)(2,1)} %bitcast.225, f32[1536,1024]{1,0:T(8,128)} %get-tuple-element.308, f32[1024]{0:T(1024)S(1)} %copy-done.39, ...), kind=kOutput, calls=%fused_computation.6 | convolution fusion | flops 12929466368 | bytes 27273216 | tf_op jit(solution)/shard_map/dot_general | solution.py:976
  377.5 18.9 %fusion.6 = (bf16[1536,2048]{1,0:T(8,128)(2,1)}, bf16[1536,2048]{1,0:T(8,128)(2,1)}, bf16[1536,2048]{1,0:T(8,128)(2,1)}) fusion(bf16[1536,4096]{1,0:T(8,128)(2,1)} %convolution_convert_fusion, bf16[2048,1024]{1,0:T(8,128)(2,1)} %bitcast.215, bf16[1536,1024]{1,0:T(8,128)(2,1)S(1)} %bitcast.218), kind=kOutput, calls=%fused_computation.13 | convolution fusion | flops 6499074048 | bytes 38797312 | tf_op jit(solution)/shard_map/ro,io->ri/dot_general | solution.py:1100
  396.5 21.0 %fusion.9 = f32[1536,1024]{1,0:T(8,128)} fusion(bf16[1536,2048]{1,0:T(8,128)(2,1)} %get-tuple-element.266, bf16[1536,2048]{1,0:T(8,128)(2,1)} %get-tuple-element.265, bf16[1024,1024]{1,0:T(8,128)(2,1)S(1)} %bitcast.228, bf16[1024,1024]{1,0:T(8,128)(2,1)S(1)} %bitcast.230, bf16[1024,1024]{1,0:T(8,128)(2,1)} %bitcast.232, bf16[1024,1024]{1,0:T(8,128)(2,1)S(1)} %bitcast.226), kind=kOutput, calls=%fused_computation.20 | convolution fusion | flops 12943622144 | bytes 27262976 | tf_op jit(solution)/shard_map/ro,io->ri/dot_general | solution.py:1100
  417.5 21.5 %fusion.10 = bf16[1024,4096]{1,0:T(8,128)(2,1)} fusion(bf16[1536,2048]{1,0:T(8,128)(2,1)} %get-tuple-element.266, bf16[1536,2048]{1,0:T(8,128)(2,1)} %get-tuple-element.265, f32[1536,1024]{1,0:T(8,128)} %get-tuple-element.308, f32[1024]{0:T(1024)S(1)} %copy-done.39, f32[1536]{0:T(1024)S(1)} %fusion.52), kind=kOutput, calls=%fused_computation.23 | convolution fusion | flops 12918980608 | bytes 27273216 | tf_op jit(solution)/shard_map/ri,ro->io/dot_general | solution.py:1097
  439.0 11.1 %convolution_convert_fusion.3 = bf16[2048,1024]{1,0:T(8,128)(2,1)} fusion(bf16[1536,2048]{1,0:T(8,128)(2,1)} %get-tuple-element.215, bf16[1536,1024]{1,0:T(8,128)(2,1)S(1)} %bitcast.219), kind=kOutput, calls=%fused_computation.31 | convolution fusion | flops 6444548096 | bytes 13631488 | tf_op jit(solution)/shard_map/ri,ro->io/dot_general | solution.py:1097
  450.2 6.4 multiply_reduce_fusion
  456.6 7.3 fusion.65
  463.9 3.0 convolution_convert_fusion.7
  466.9 2.8 convolution_convert_fusion.8
  469.8 6.9 convolution_convert_fusion.1
  476.6 5.4 convolution_convert_fusion.6
  482.0 10.0 %mixer_gate_back.3 = (bf16[3,512,1536]{2,1,0:T(8,128)(2,1)}, bf16[3,512,1536]{2,1,0:T(8,128)(2,1)}, bf16[3,4,128,1536]{3,2,1,0:T(8,128)(2,1)}, f32[3,4,8,128]{3,...) custom-call(bf16[3,512,1536]{2,1,0:T(8,128)(2,1)} %bitcast.187, ...), custom_call_target="tpu_custom_call" | custom-call | tf_op jit(solution)/shard_map/mixer_gate_back/pallas_call | solution.py:764
  492.1 11.8 %mixer_gate_back.4 = (bf16[3,512,1536]{2,1,0:T(8,128)(2,1)}, bf16[3,512,1536]{2,1,0:T(8,128)(2,1)}, bf16[3,4,128,1536]{3,2,1,0:T(8,128)(2,1)}, f32[3,4,8,128]{3,...) custom-call(bf16[3,512,1536]{2,1,0:T(8,128)(2,1)} %bitcast.188, ...), custom_call_target="tpu_custom_call", output_to_operand_aliasing={{0}: (9, {}), {1}: (10, {}), {2}: (11, {}), {3}: (12, {})} | custom-call | tf_op jit(solution)/shard_map/mixer_gate_back/pallas_call | solution.py:764
  503.9 10.3 %mixer_gate_back.5 = (bf16[3,512,1536]{2,1,0:T(8,128)(2,1)}, bf16[3,512,1536]{2,1,0:T(8,128)(2,1)}, bf16[3,4,128,1536]{3,2,1,0:T(8,128)(2,1)}, f32[3,4,8,128]{3,...) custom-call(bf16[3,512,1536]{2,1,0:T(8,128)(2,1)} %bitcast.189, ...), custom_call_target="tpu_custom_call", output_to_operand_aliasing={{0}: (9, {}), {1}: (10, {}), {2}: (11, {}), {3}: (12, {})} | custom-call | tf_op jit(solution)/shard_map/mixer_gate_back/pallas_call | solution.py:764
  514.2 2.7 constant_dynamic-update-slice_fusion.7
  522.0 5.6 convolution_convert_fusion.5
  534.4 13.5 %attend_back.3 = (bf16[1,512,512]{2,1,0:T(8,128)(2,1)}, bf16[4,1,512,256]{3,2,1,0:T(8,128)(2,1)}) custom-call(s32[6]{0:T(128)} %and_select_fusion.1.low_ref, s32[6]{0:T(128)} %reshape.275.high_ref, s32[1]{0:T(128)} %bitcast.7.base_ref, bf16[3,512,512]{2,1,0:T(8,128)(2,1)} %bitcast.178, bf16[4,3,512,256]{3,2,1,0:T(8,128)(2,1)} %copy-done, ...), custom_call_target="tpu_custom_call" | custom-call | tf_op jit(solution)/shard_map/attend_back/pallas_call | solution.py:336
  551.2 13.8 %attend_back.5 = (bf16[1,512,512]{2,1,0:T(8,128)(2,1)}, bf16[4,1,512,256]{3,2,1,0:T(8,128)(2,1)}) custom-call(s32[6]{0:T(128)} %and_select_fusion.1.low_ref, s32[6]{0:T(128)} %reshape.275.high_ref, s32[1]{0:T(128)} %bitcast.7.base_ref, bf16[3,512,512]{2,1,0:T(8,128)(2,1)} %bitcast.179, bf16[4,3,512,256]{3,2,1,0:T(8,128)(2,1)} %copy-done, ...), custom_call_target="tpu_custom_call" | custom-call | tf_op jit(solution)/shard_map/attend_back/pallas_call | solution.py:336
  566.5 27.3 %collective-permute-done.12 = bf16[1,128,1536]{2,1,0:T(8,128)(2,1)S(1)} collective-permute-done((bf16[1,128,1536]{2,1,0:T(8,128)(2,1)S(1)}, bf16[1,128,1536]{2,1,0:T(8,128)(2,1)S(1)}, u32[]{:S(2)}, u32[]{:S(2)}) %collective-permute-start.12) | collective-permute-done | bytes 393248 | tf_op jit(solution)/shard_map/ppermute | solution.py:910
  594.6 13.3 %attend_back.4 = (bf16[1,512,512]{2,1,0:T(8,128)(2,1)}, bf16[4,1,512,256]{3,2,1,0:T(8,128)(2,1)}) custom-call(s32[6]{0:T(128)} %and_select_fusion.1.low_ref, s32[6]{0:T(128)} %reshape.275.high_ref, s32[1]{0:T(128)} %bitcast.7.base_ref, bf16[3,512,512]{2,1,0:T(8,128)(2,1)} %bitcast.180, bf16[4,3,512,256]{3,2,1,0:T(8,128)(2,1)} %copy-done, ...), custom_call_target="tpu_custom_call" | custom-call | tf_op jit(solution)/shard_map/attend_back/pallas_call | solution.py:336
  608.0 8.1 collective-permute-done.16
  616.9 23.7 %mixer_back.3 = (bf16[3,512,1920]{2,1,0:T(8,128)(2,1)}, f32[1,8,1792]{2,1,0:T(8,128)}, f32[8,1792]{1,0:T(8,128)}, f32[8,128]{1,0:T(8,128)}) custom-call(bf16[3,512,1536]{2,1,0:T(8,128)(2,1)} %get-tuple-element.210.refs_0_, f32[3,512,1536]{2,1,0:T(8,128)} %get-tuple-element.170.refs_1_, bf16[3,512,1920]{2,1,0:T(8,128)(2,1)} %bitcast.163, ...), custom_call_target="tpu_custom_call" | custom-call | tf_op jit(solution)/shard_map/mixer_back/pallas_call | solution.py:764
  640.6 23.9 %mixer_back.4 = (bf16[3,512,1920]{2,1,0:T(8,128)(2,1)}, f32[1,8,1792]{2,1,0:T(8,128)}, f32[8,1792]{1,0:T(8,128)}, f32[8,128]{1,0:T(8,128)}) custom-call(bf16[3,512,1536]{2,1,0:T(8,128)(2,1)} %get-tuple-element.210.refs_0_, f32[3,512,1536]{2,1,0:T(8,128)} %get-tuple-element.170.refs_1_, ...), custom_call_target="tpu_custom_call", output_to_operand_aliasing={{0}: (19, {})} | custom-call | tf_op jit(solution)/shard_map/mixer_back/pallas_call | solution.py:764
  674.2 3.9 pad_maximum_fusion.6
  678.1 40.2 %all-to-all-start.1 = ((bf16[4,3,512,256]{3,2,1,0:T(8,128)(2,1)}), bf16[4,3,512,256]{3,2,1,0:T(8,128)(2,1)S(1)}, u32[]{:S(2)}, u32[]{:S(2)}) async-start(bf16[4,3,512,256]{3,2,1,0:T(8,128)(2,1)} %pad_maximum_fusion.6), calls=%async_computation.5 | async-start | bytes 6291456 | tf_op jit(solution)/shard_map/all_to_all | solution.py:1046
  721.9 23.8 %mixer_back.5 = (bf16[3,512,1920]{2,1,0:T(8,128)(2,1)}, f32[1,8,1792]{2,1,0:T(8,128)}, f32[8,1792]{1,0:T(8,128)}, f32[8,128]{1,0:T(8,128)}) custom-call(bf16[3,512,1536]{2,1,0:T(8,128)(2,1)} %get-tuple-element.210.refs_0_, f32[3,512,1536]{2,1,0:T(8,128)} %get-tuple-element.170.refs_1_, ...), custom_call_target="tpu_custom_call", output_to_operand_aliasing={{0}: (19, {})} | custom-call | tf_op jit(solution)/shard_map/mixer_back/pallas_call | solution.py:764
  747.9 42.4 %collective-permute-done.19 = bf16[3,3,1792]{2,1,0:T(4,128)(2,1)S(1)} collective-permute-done((bf16[3,3,1792]{2,1,0:T(4,128)(2,1)S(1)}, bf16[3,3,1792]{2,1,0:T(4,128)(2,1)S(1)}, u32[]{:S(2)}, u32[]{:S(2)}) %collective-permute-start.19) | collective-permute-done | bytes 32288 | tf_op jit(solution)/shard_map/ppermute | solution.py:887
  793.4 11.4 %convolution_convert_fusion.4 = bf16[1024,1920]{1,0:T(8,128)(2,1)} fusion(bf16[1536,1024]{1,0:T(8,128)(2,1)} %get-tuple-element.129, bf16[1536,1920]{1,0:T(8,128)(2,1)} %bitcast.181), kind=kOutput, calls=%fused_computation.32 | convolution fusion | flops 6041763840 | bytes 12976128 | tf_op jit(solution)/shard_map/ri,ro->io/dot_general | solution.py:1097
  804.9 3.8 slice.371.wg_ref
  809.8 2.7 pad_maximum_fusion.9
  812.9 16.4 %all-to-all-done.1.dkv_ref = bf16[4,3,512,256]{3,2,1,0:T(8,128)(2,1)S(1)} async-done(((bf16[4,3,512,256]{3,2,1,0:T(8,128)(2,1)}), bf16[4,3,512,256]{3,2,1,0:T(8,128)(2,1)S(1)}, u32[]{:S(2)}, u32[]{:S(2)}) %all-to-all-start.1) | async-done | bytes 3145760 | tf_op jit(solution)/shard_map/all_to_all | solution.py:1046
  831.0 22.8 %finish.1 = (bf16[1536,1024]{1,0:T(8,128)(2,1)}, bf16[1536,256]{1,0:T(8,128)(2,1)}, f32[8,1024]{1,0:T(8,128)}) custom-call(bf16[1536,1024]{1,0:T(8,128)(2,1)} %bitcast.210, f32[1,1024]{1,0:T(1,128)} %reshape.273.gain_ref, bf16[1536,1536]{1,0:T(8,128)(2,1)} %bitcast.183, bf16[1536,1920]{1,0:T(8,128)(2,1)} %bitcast.182, bf16[1536,512]{1,0:T(8,128)(2,1)} %bitcast.212, ...), custom_call_target="tpu_custom_call" | custom-call | tf_op jit(solution)/shard_map/finish/pallas_call | solution.py:137
  855.1 5.8 fusion.16
  862.2 3.1 copy.159
  873.8 5.2 collective-permute-start.28
  880.5 22.7 %collective-permute-start.29 = (f32[3,24]{1,0:T(4,128)S(1)}, f32[3,24]{1,0:T(4,128)S(1)}, u32[]{:S(2)}, u32[]{:S(2)}) collective-permute-start(f32[3,24]{1,0:T(4,128)S(1)} %add.241), channel_id=1, source_target_pairs={{0,1},{1,0},{2,3},{3,2},{4,5},{5,4},{6,7},{7,6},{8,9},{9,8},{10,11... | collective-permute-start | bytes 872 | tf_op jit(solution)/shard_map/ppermute | solution.py:932
  906.6 2.7 collective-permute-done.30
  915.2 5.9 collective-permute-done.21
  922.4 5.0 collective-permute-done.22
  931.5 12.3 %add_convert_fusion = bf16[1536,1024]{1,0:T(8,128)(2,1)} fusion(f32[1536,1024]{1,0:T(8,128)} %get-tuple-element.308, bf16[1536,2048]{1,0:T(8,128)(2,1)} %get-tuple-element.215, bf16[2048,1024]{1,0:T(8,128)(2,1)} %bitcast.216), kind=kOutput, calls=%fused_computation.26 | convolution fusion | flops 6445596672 | bytes 19922944 | tf_op jit(solution)/shard_map/dot_general | solution.py:976
  (361 shorter events, 133.6 us)
Async XLA Ops:
  7.2 91.3 %all-gather.3.cloned.1.call-start = ((), (), s32[]{:S(2)}) async-start(), calls=%async_computation.7 | async-start | bytes 9191424 | tf_op jit(solution)/shard_map/all_gather | solution.py:986
  15.9 313.3 %all-gather.5.cloned.1.call-start = ((), (), s32[]{:S(2)}) async-start(), calls=%async_computation.8 | async-start | bytes 17301504 | tf_op jit(solution)/shard_map/all_gather | solution.py:986
  99.5 20.5 %copy-start.27 = (f32[32,4096]{1,0:T(8,128)}, f32[32,4096]{1,0:T(8,128)S(1)}, u32[]{:S(2)}) copy-start(f32[32,4096]{1,0:T(8,128)S(1)} %reshape.318) | copy-start | bytes 1572868
  100.3 22.0 %copy-start.35 = (s32[3,2048]{1,0:T(4,128)S(1)}, s32[3,2048]{1,0:T(4,128)}, u32[]{:S(2)}) copy-start(s32[3,2048]{1,0:T(4,128)} %param.20) | copy-start | bytes 73732
  116.5 15.0 %collective-permute-start = (bf16[3,3,1792]{2,1,0:T(4,128)(2,1)S(1)}, bf16[3,3,1792]{2,1,0:T(4,128)(2,1)S(1)}, u32[]{:S(2)}, u32[]{:S(2)}) collective-permute-start(bf16[3,3,1792]{2,1,0:T(4,128)(2,1)S(1)} %slice.372), channel_id=1, source_target_pairs={{0,1},{1,2},{2,3},{4,5},{5,6},{6,7},{8,9},{9,10},{10,11},{12,13},{... | collective-permute-start | bytes 96776 | tf_op jit(solution)/shard_map/ppermute | solution.py:887
  127.6 176.2 %all-to-all-start = ((bf16[4,3,512,256]{3,2,1,0:T(8,128)(2,1)}), bf16[4,3,512,256]{3,2,1,0:T(8,128)(2,1)S(1)}, u32[]{:S(2)}, u32[]{:S(2)}) async-start(bf16[4,3,512,256]{3,2,1,0:T(8,128)(2,1)} %broadcast_in_dim.59), calls=%async_computation | async-start | bytes 6291456 | tf_op jit(solution)/shard_map/all_to_all | solution.py:1046
  131.4 485.5 %reduce-scatter.8.cloned.1.call-start = ((), (), s32[]{:S(2)}) async-start(), calls=%async_computation.10 | async-start | bytes 9437184 | tf_op jit(solution)/shard_map/reduce_scatter | solution.py:1094
  131.4 14.2 %copy-start.44 = (bf16[1536,1024]{1,0:T(8,128)(2,1)S(1)}, bf16[1536,1024]{1,0:T(8,128)(2,1)}, u32[]{:S(2)}) copy-start(bf16[1536,1024]{1,0:T(8,128)(2,1)} %get-tuple-element.129) | copy-start | bytes 9437188
  141.5 94.5 %collective-permute-start.7 = (bf16[1,128,1536]{2,1,0:T(8,128)(2,1)}, bf16[1,128,1536]{2,1,0:T(8,128)(2,1)S(1)}, u32[]{:S(2)}, u32[]{:S(2)}) collective-permute-start(bf16[1,128,1536]{2,1,0:T(8,128)(2,1)} %get-tuple-element.149), channel_id=1, source_target_pairs={{0,1},{4,5},{8,9},{12,13},{16,17},{20,21},{24,25},{28,29}} | collective-permute-start | bytes 1179656 | tf_op jit(solution)/shard_map/ppermute | solution.py:910
  164.8 88.1 %collective-permute-start.4 = (bf16[1,128,1536]{2,1,0:T(8,128)(2,1)}, bf16[1,128,1536]{2,1,0:T(8,128)(2,1)S(1)}, u32[]{:S(2)}, u32[]{:S(2)}) collective-permute-start(bf16[1,128,1536]{2,1,0:T(8,128)(2,1)} %get-tuple-element.147), channel_id=1, source_target_pairs={{0,1},{4,5},{8,9},{12,13},{16,17},{20,21},{24,25},{28,29}} | collective-permute-start | bytes 1179656 | tf_op jit(solution)/shard_map/ppermute | solution.py:910
  166.1 69.9 %copy-start.20 = (bf16[1,128,1536]{2,1,0:T(8,128)(2,1)S(1)}, bf16[1,128,1536]{2,1,0:T(8,128)(2,1)}, u32[]{:S(2)}) copy-start(bf16[1,128,1536]{2,1,0:T(8,128)(2,1)} %get-tuple-element.149) | copy-start | bytes 1179652
  166.1 86.7 %copy-start.21 = (bf16[1,128,1536]{2,1,0:T(8,128)(2,1)S(1)}, bf16[1,128,1536]{2,1,0:T(8,128)(2,1)}, u32[]{:S(2)}) copy-start(bf16[1,128,1536]{2,1,0:T(8,128)(2,1)} %get-tuple-element.147) | copy-start | bytes 1179652
  175.3 97.8 %copy-start.19 = (bf16[1,128,1536]{2,1,0:T(8,128)(2,1)S(1)}, bf16[1,128,1536]{2,1,0:T(8,128)(2,1)}, u32[]{:S(2)}) copy-start(bf16[1,128,1536]{2,1,0:T(8,128)(2,1)} %get-tuple-element.144) | copy-start | bytes 1179652
  175.4 94.2 %collective-permute-start.1 = (bf16[1,128,1536]{2,1,0:T(8,128)(2,1)}, bf16[1,128,1536]{2,1,0:T(8,128)(2,1)S(1)}, u32[]{:S(2)}, u32[]{:S(2)}) collective-permute-start(bf16[1,128,1536]{2,1,0:T(8,128)(2,1)} %get-tuple-element.144), channel_id=1, source_target_pairs={{0,1},{4,5},{8,9},{12,13},{16,17},{20,21},{24,25},{28,29}} | collective-permute-start | bytes 1179656 | tf_op jit(solution)/shard_map/ppermute | solution.py:910
  177.6 95.7 %copy-start.33 = (f32[1536]{0:T(1024)}, f32[1536]{0:T(1024)S(1)}, u32[]{:S(2)}) copy-start(f32[1536]{0:T(1024)S(1)} %slice_reduce_fusion.4) | copy-start | bytes 18436
  178.5 94.9 %copy-start.31 = (f32[1536]{0:T(1024)}, f32[1536]{0:T(1024)S(1)}, u32[]{:S(2)}) copy-start(f32[1536]{0:T(1024)S(1)} %slice_reduce_fusion.5) | copy-start | bytes 18436
  179.3 94.1 %copy-start.29 = (f32[1536]{0:T(1024)}, f32[1536]{0:T(1024)S(1)}, u32[]{:S(2)}) copy-start(f32[1536]{0:T(1024)S(1)} %slice_reduce_fusion.6) | copy-start | bytes 18436
  236.2 35.2 %collective-permute-start.8 = (bf16[1,128,1536]{2,1,0:T(8,128)(2,1)S(1)}, bf16[1,128,1536]{2,1,0:T(8,128)(2,1)S(1)}, u32[]{:S(2)}, u32[]{:S(2)}) collective-permute-start(bf16[1,128,1536]{2,1,0:T(8,128)(2,1)S(1)} %get-tuple-element.261), channel_id=1, source_target_pairs={{1,2},{5,6},{9,10},{13,14},{17,18},{21,22},{25,26},{29,30}} | collective-permute-start | bytes 1179656 | tf_op jit(solution)/shard_map/ppermute | solution.py:910
  253.0 19.3 %collective-permute-start.5 = (bf16[1,128,1536]{2,1,0:T(8,128)(2,1)S(1)}, bf16[1,128,1536]{2,1,0:T(8,128)(2,1)S(1)}, u32[]{:S(2)}, u32[]{:S(2)}) collective-permute-start(bf16[1,128,1536]{2,1,0:T(8,128)(2,1)S(1)} %get-tuple-element.257), channel_id=1, source_target_pairs={{1,2},{5,6},{9,10},{13,14},{17,18},{21,22},{25,26},{29,30}} | collective-permute-start | bytes 1179656 | tf_op jit(solution)/shard_map/ppermute | solution.py:910
  270.7 2.5 collective-permute-start.2
  271.6 2.9 collective-permute-start.9
  272.5 11.8 %collective-permute-start.6 = (bf16[1,128,1536]{2,1,0:T(8,128)(2,1)S(1)}, bf16[1,128,1536]{2,1,0:T(8,128)(2,1)S(1)}, u32[]{:S(2)}, u32[]{:S(2)}) collective-permute-start(bf16[1,128,1536]{2,1,0:T(8,128)(2,1)S(1)} %get-tuple-element.253), channel_id=1, source_target_pairs={{2,3},{6,7},{10,11},{14,15},{18,19},{22,23},{26,27},{30,31}} | collective-permute-start | bytes 1179656 | tf_op jit(solution)/shard_map/ppermute | solution.py:910
  273.4 20.6 %collective-permute-start.3 = (bf16[1,128,1536]{2,1,0:T(8,128)(2,1)S(1)}, bf16[1,128,1536]{2,1,0:T(8,128)(2,1)S(1)}, u32[]{:S(2)}, u32[]{:S(2)}) collective-permute-start(bf16[1,128,1536]{2,1,0:T(8,128)(2,1)S(1)} %fusion.22), channel_id=1, source_target_pairs={{2,3},{6,7},{10,11},{14,15},{18,19},{22,23},{26,27},{30,31}} | collective-permute-start | bytes 1179656 | tf_op jit(solution)/shard_map/ppermute | solution.py:910
  329.1 16.6 %copy-start.14 = (bf16[3,512,512]{2,1,0:T(8,128)(2,1)}, bf16[3,512,512]{2,1,0:T(8,128)(2,1)S(1)}, u32[]{:S(2)}) copy-start(bf16[3,512,512]{2,1,0:T(8,128)(2,1)S(1)} %pad_maximum_fusion.8) | copy-start | bytes 4718596
  333.3 14.4 %copy-start.6 = (bf16[32,48,1024]{2,1,0:T(8,128)(2,1)}, bf16[32,48,1024]{2,1,0:T(8,128)(2,1)S(1)}, u32[]{:S(2)}) copy-start(bf16[32,48,1024]{2,1,0:T(8,128)(2,1)S(1)} %slice.378) | copy-start | bytes 9437188
  356.6 20.9 %copy-start.5 = (bf16[3,512,1024]{2,1,0:T(8,128)(2,1)S(1)}, bf16[3,512,1024]{2,1,0:T(8,128)(2,1)}, u32[]{:S(2)}) copy-start(bf16[3,512,1024]{2,1,0:T(8,128)(2,1)} %param.37) | copy-start | bytes 9437188
  377.5 19.0 %copy-start.11 = (bf16[32,32,1024]{2,1,0:T(8,128)(2,1)S(1)}, bf16[32,32,1024]{2,1,0:T(8,128)(2,1)}, u32[]{:S(2)}) copy-start(bf16[32,32,1024]{2,1,0:T(8,128)(2,1)} %get-tuple-element.267) | copy-start | bytes 6291460
  377.5 19.0 %copy-start.12 = (bf16[32,32,1024]{2,1,0:T(8,128)(2,1)S(1)}, bf16[32,32,1024]{2,1,0:T(8,128)(2,1)}, u32[]{:S(2)}) copy-start(bf16[32,32,1024]{2,1,0:T(8,128)(2,1)} %get-tuple-element.268) | copy-start | bytes 6291460
  377.5 19.0 %copy-start.13 = (bf16[32,32,1024]{2,1,0:T(8,128)(2,1)S(1)}, bf16[32,32,1024]{2,1,0:T(8,128)(2,1)}, u32[]{:S(2)}) copy-start(bf16[32,32,1024]{2,1,0:T(8,128)(2,1)} %get-tuple-element.269) | copy-start | bytes 6291460
  450.2 214.3 %reduce-scatter.6.cloned.1.call-start = ((), (), s32[]{:S(2)}) async-start(), calls=%async_computation.9 | async-start | bytes 12976128 | tf_op jit(solution)/shard_map/reduce_scatter | solution.py:1094
  466.9 9.7 %slice-start.4 = ((s8[4718592]{0:T(1024)(128)(4,1)}), s8[4194304]{0:T(1024)(128)(4,1)S(1)}, s32[]{:S(2)}) async-start(s8[4718592]{0:T(1024)(128)(4,1)} %bitcast.197), calls=%async_computation.18 | async-start | bytes 8388608
  503.9 10.3 %copy-start.4 = (bf16[2048,1024]{1,0:T(8,128)(2,1)S(1)}, bf16[2048,1024]{1,0:T(8,128)(2,1)}, u32[]{:S(2)}) copy-start(bf16[2048,1024]{1,0:T(8,128)(2,1)} %convolution_convert_fusion.3) | copy-start | bytes 12582916
  530.5 282.4 %reduce-scatter.12.cloned.1.call-start = ((), (), s32[]{:S(2)}) async-start(), calls=%async_computation.12 | async-start | bytes 3112960 | tf_op jit(solution)/shard_map/reduce_scatter | solution.py:1177
  531.4 2.1 collective-permute-start.10
  532.1 16.7 %collective-permute-start.15 = (bf16[1,128,1536]{2,1,0:T(8,128)(2,1)S(1)}, bf16[1,128,1536]{2,1,0:T(8,128)(2,1)S(1)}, u32[]{:S(2)}, u32[]{:S(2)}) collective-permute-start(bf16[1,128,1536]{2,1,0:T(8,128)(2,1)S(1)} %copy-done.16), channel_id=1, source_target_pairs={{3,2},{7,6},{11,10},{15,14},{19,18},{23,22},{27,26},{31,30}} | collective-permute-start | bytes 1179656 | tf_op jit(solution)/shard_map/ppermute | solution.py:910
  532.8 15.1 %collective-permute-start.13 = (bf16[1,128,1536]{2,1,0:T(8,128)(2,1)S(1)}, bf16[1,128,1536]{2,1,0:T(8,128)(2,1)S(1)}, u32[]{:S(2)}, u32[]{:S(2)}) collective-permute-start(bf16[1,128,1536]{2,1,0:T(8,128)(2,1)S(1)} %copy-done.17), channel_id=1, source_target_pairs={{3,2},{7,6},{11,10},{15,14},{19,18},{23,22},{27,26},{31,30}} | collective-permute-start | bytes 1179656 | tf_op jit(solution)/shard_map/ppermute | solution.py:910
  533.7 16.0 %collective-permute-start.11 = (bf16[1,128,1536]{2,1,0:T(8,128)(2,1)S(1)}, bf16[1,128,1536]{2,1,0:T(8,128)(2,1)S(1)}, u32[]{:S(2)}, u32[]{:S(2)}) collective-permute-start(bf16[1,128,1536]{2,1,0:T(8,128)(2,1)S(1)} %get-tuple-element.249), channel_id=1, source_target_pairs={{2,1},{6,5},{10,9},{14,13},{18,17},{22,21},{26,25},{30,29}} | collective-permute-start | bytes 1179656 | tf_op jit(solution)/shard_map/ppermute | solution.py:910
  534.4 13.5 %copy-start.32 = (f32[1536]{0:T(1024)S(1)}, f32[1536]{0:T(1024)}, u32[]{:S(2)}) copy-start(f32[1536]{0:T(1024)} %copy-done.31) | copy-start | bytes 18436
  534.4 14.4 %copy-start.30 = (f32[1536]{0:T(1024)S(1)}, f32[1536]{0:T(1024)}, u32[]{:S(2)}) copy-start(f32[1536]{0:T(1024)} %copy-done.29) | copy-start | bytes 18436
  548.1 16.9 %collective-permute-start.14 = (bf16[1,128,1536]{2,1,0:T(8,128)(2,1)S(1)}, bf16[1,128,1536]{2,1,0:T(8,128)(2,1)S(1)}, u32[]{:S(2)}, u32[]{:S(2)}) collective-permute-start(bf16[1,128,1536]{2,1,0:T(8,128)(2,1)S(1)} %get-tuple-element.187), channel_id=1, source_target_pairs={{2,1},{6,5},{10,9},{14,13},{18,17},{22,21},{26,25},{30,29}} | collective-permute-start | bytes 1179656 | tf_op jit(solution)/shard_map/ppermute | solution.py:910
  549.9 43.9 %collective-permute-start.12 = (bf16[1,128,1536]{2,1,0:T(8,128)(2,1)S(1)}, bf16[1,128,1536]{2,1,0:T(8,128)(2,1)S(1)}, u32[]{:S(2)}, u32[]{:S(2)}) collective-permute-start(bf16[1,128,1536]{2,1,0:T(8,128)(2,1)S(1)} %get-tuple-element.185), channel_id=1, source_target_pairs={{1,0},{5,4},{9,8},{13,12},{17,16},{21,20},{25,24},{29,28}} | collective-permute-start | bytes 1179656 | tf_op jit(solution)/shard_map/ppermute | solution.py:910
  565.2 50.9 %collective-permute-start.16 = (bf16[1,128,1536]{2,1,0:T(8,128)(2,1)S(1)}, bf16[1,128,1536]{2,1,0:T(8,128)(2,1)S(1)}, u32[]{:S(2)}, u32[]{:S(2)}) collective-permute-start(bf16[1,128,1536]{2,1,0:T(8,128)(2,1)S(1)} %get-tuple-element.206), channel_id=1, source_target_pairs={{1,0},{5,4},{9,8},{13,12},{17,16},{21,20},{25,24},{29,28}} | collective-permute-start | bytes 1179656 | tf_op jit(solution)/shard_map/ppermute | solution.py:910
  671.3 0.7 collective-permute-start.17
  672.9 45.6 %collective-permute-start.18 = (bf16[1,128,1536]{2,1,0:T(8,128)(2,1)}, bf16[1,128,1536]{2,1,0:T(8,128)(2,1)}, u32[]{:S(2)}, u32[]{:S(2)}) collective-permute-start(bf16[1,128,1536]{2,1,0:T(8,128)(2,1)} %fusion.32), channel_id=1, source_target_pairs={{1,0},{5,4},{9,8},{13,12},{17,16},{21,20},{25,24},{29,28}} | collective-permute-start | bytes 1179656 | tf_op jit(solution)/shard_map/ppermute | solution.py:910
  678.1 151.2 %all-to-all-start.1 = ((bf16[4,3,512,256]{3,2,1,0:T(8,128)(2,1)}), bf16[4,3,512,256]{3,2,1,0:T(8,128)(2,1)S(1)}, u32[]{:S(2)}, u32[]{:S(2)}) async-start(bf16[4,3,512,256]{3,2,1,0:T(8,128)(2,1)} %pad_maximum_fusion.6), calls=%async_computation.5 | async-start | bytes 6291456 | tf_op jit(solution)/shard_map/all_to_all | solution.py:1046
  718.3 204.1 %reduce-scatter.10.cloned.1.call-start = ((), (), s32[]{:S(2)}) async-start(), calls=%async_computation.11 | async-start | bytes 4423680 | tf_op jit(solution)/shard_map/reduce_scatter | solution.py:1094
  746.6 43.7 %collective-permute-start.19 = (bf16[3,3,1792]{2,1,0:T(4,128)(2,1)S(1)}, bf16[3,3,1792]{2,1,0:T(4,128)(2,1)S(1)}, u32[]{:S(2)}, u32[]{:S(2)}) collective-permute-start(bf16[3,3,1792]{2,1,0:T(4,128)(2,1)S(1)} %pad_maximum_fusion.16), channel_id=1, source_target_pairs={{1,0},{2,1},{3,2},{5,4},{6,5},{7,6},{9,8},{10,9},{11,10},{13,12},{... | collective-permute-start | bytes 96776 | tf_op jit(solution)/shard_map/ppermute | solution.py:887
  804.8 143.9 %reduce-scatter.14.cloned.1.call-start = ((), (), s32[]{:S(2)}) async-start(), calls=%async_computation.13 | async-start | bytes 614400 | tf_op jit(solution)/shard_map/reduce_scatter | solution.py:1181
  804.9 7.6 copy-start.36
  860.8 8.0 copy-start.41
  860.8 8.0 copy-start.42
  860.8 8.0 copy-start.43
  860.9 49.0 %copy-start.8 = (bf16[304,1024]{1,0:T(8,128)(2,1)S(1)}, bf16[304,1024]{1,0:T(8,128)(2,1)}, u32[]{:S(2)}) copy-start(bf16[304,1024]{1,0:T(8,128)(2,1)} %reduce-scatter.12.cloned.1.call-done) | copy-start | bytes 1867780
  866.3 45.6 %collective-permute-start.20 = (bf16[2,2,4,32,896]{4,3,2,1,0:T(8,128)(2,1)}, bf16[2,2,4,32,896]{4,3,2,1,0:T(8,128)(2,1)S(1)}, u32[]{:S(2)}, u32[]{:S(2)}) collective-permute-start(bf16[2,2,4,32,896]{4,3,2,1,0:T(8,128)(2,1)} %fusion.19), channel_id=1, source_target_pairs={{0,4},{4,0},{8,12},{12,8},{16,20},{20,16},{24,28},{28,24},{1,5},{5... | collective-permute-start | bytes 2752520 | tf_op jit(solution)/shard_map/ppermute | solution.py:947
  868.9 1.2 collective-permute-start.26
  870.1 3.7 collective-permute-start.27
  873.8 6.7 collective-permute-start.28
  880.5 24.3 %collective-permute-start.29 = (f32[3,24]{1,0:T(4,128)S(1)}, f32[3,24]{1,0:T(4,128)S(1)}, u32[]{:S(2)}, u32[]{:S(2)}) collective-permute-start(f32[3,24]{1,0:T(4,128)S(1)} %add.241), channel_id=1, source_target_pairs={{0,1},{1,0},{2,3},{3,2},{4,5},{5,4},{6,7},{7,6},{8,9},{9,8},{10,11... | collective-permute-start | bytes 872 | tf_op jit(solution)/shard_map/ppermute | solution.py:932
  904.8 4.5 collective-permute-start.30
  912.3 8.8 collective-permute-start.21
  921.3 6.1 collective-permute-start.22
  927.6 16.2 %collective-permute-start.23 = (bf16[32,896]{1,0:T(8,128)(2,1)S(1)}, bf16[32,896]{1,0:T(8,128)(2,1)S(1)}, u32[]{:S(2)}, u32[]{:S(2)}) collective-permute-start(bf16[32,896]{1,0:T(8,128)(2,1)S(1)} %get-tuple-element.289), channel_id=1, source_target_pairs={{0,1},{1,2},{2,3},{3,0},{4,5},{5,6},{6,7},{7,4},{8,9},{9,10},{10,1... | collective-permute-start | bytes 172040 | tf_op jit(solution)/shard_map/ppermute | solution.py:953
  929.4 14.4 %collective-permute-start.25 = (bf16[32,896]{1,0:T(8,128)(2,1)S(1)}, bf16[32,896]{1,0:T(8,128)(2,1)S(1)}, u32[]{:S(2)}, u32[]{:S(2)}) collective-permute-start(bf16[32,896]{1,0:T(8,128)(2,1)S(1)} %get-tuple-element.290), channel_id=1, source_target_pairs={{0,3},{1,0},{2,1},{3,2},{4,7},{5,4},{6,5},{7,6},{8,11},{9,8},{10,9... | collective-permute-start | bytes 172040 | tf_op jit(solution)/shard_map/ppermute | solution.py:953
  931.5 12.3 %collective-permute-start.24 = (bf16[32,896]{1,0:T(8,128)(2,1)S(1)}, bf16[32,896]{1,0:T(8,128)(2,1)S(1)}, u32[]{:S(2)}, u32[]{:S(2)}) collective-permute-start(bf16[32,896]{1,0:T(8,128)(2,1)S(1)} %get-tuple-element.291), channel_id=1, source_target_pairs={{0,2},{1,3},{2,0},{3,1},{4,6},{5,7},{6,4},{7,5},{8,10},{9,11},{10,... | collective-permute-start | bytes 172040 | tf_op jit(solution)/shard_map/ppermute | solution.py:953
  (28 other events, 105.0 us)
Sparse Core Ops, SparseCore 0:
  16.0 82.4 all-gather.2
  101.4 171.7 all-gather.4
  450.3 105.5 reduce-scatter.7
  559.6 94.5 reduce-scatter.5
  671.4 131.5 reduce-scatter.11
  806.7 88.9 reduce-scatter.9
  922.5 22.2 reduce-scatter.13

commit v5 on v4

--- a/solution.py
+++ b/solution.py
@@ -926,11 +926,9 @@
 
 def sum_everywhere(values, axes):
     for axis in axes:
-        count, distance = lax.axis_size(axis), 1
-        while distance < count:
-            route = [(i, i ^ distance) for i in range(count)]
-            values = values + lax.ppermute(values, axis, route)
-            distance *= 2
+        count = lax.axis_size(axis)
+        copies = jnp.broadcast_to(values[None], (count,) + values.shape)
+        values = jnp.sum(lax.all_to_all(copies, axis, 0, 0, tiled=True), axis=0)
     return values
 
 
@@ -983,9 +981,14 @@
     w_kv = jnp.stack(
         [w_k.reshape(own_rows, KVH, HD), w_v.reshape(own_rows, KVH, HD)], axis=2
     ).reshape(own_rows, kv_width)
-    gather = lambda shard: lax.all_gather(shard, axes, axis=0, tiled=True)
+    count = lax.axis_size("ctx")
+    exchange = lambda blocks: lax.all_to_all(blocks, "ctx", 0, 0, tiled=True)
+    copies = lambda block: jnp.broadcast_to(block[None], (count,) + block.shape)
+    gather = lambda part: lax.all_gather(part, "dp", axis=0, tiled=True)
     w_cr = jnp.pad(w_in[:, DI:], ((0, 0), (0, CR - (w_in.shape[1] - DI))))
-    first_all = gather(jnp.concatenate([w_cr, w_q, w_kv, small_block, w_in[:, :DI]], axis=1))
+    first = jnp.concatenate([w_cr, w_q, w_kv, small_block, w_in[:, :DI]], axis=1)
+    first_part = lax.all_gather(first, "ctx", axis=0, tiled=True)
+    first_all = gather(first_part)
     turned_o = w_o.T
     half_rows, ff = own_rows // 2, w_gate.shape[1]
 
@@ -1000,7 +1003,8 @@
     for matrix in (w_gate, w_up):
         rest += [matrix[:, at : at + width] for at in range(0, ff, width)]
     rest_sizes = [part.shape[0] for part in rest]
-    rest_all = gather(jnp.concatenate(rest, axis=0)).reshape(-1, sum(rest_sizes), width)
+    rest_part = exchange(after(copies(jnp.concatenate(rest, axis=0)), first_part))
+    rest_all = gather(rest_part.reshape(-1, width)).reshape(-1, sum(rest_sizes), width)
     cuts, at = [], 0
     for size in rest_sizes:
         cuts.append(rest_all[:, at : at + size])
@@ -1027,7 +1031,6 @@
         -1,
     )
     token = token_table(seg_own, seg_rim)
-    count = lax.axis_size("ctx")
     bounds = attention_bounds(segments, seg_own, span_start)
     segk, segq = segments[:, :, None], seg_own[:, None, :]
     cosine, sine = rope_tables(positions)
@@ -1043,8 +1046,7 @@
     hidden, cr, q, kv = project(tokens, gain1_all, first_all, cosine, sine)
     q = q.reshape(seqs, span, q_width)
     kv = kv.reshape(seqs, span, kv_width)
-    exchange = lambda blocks: lax.all_to_all(blocks, "ctx", 0, 0, tiled=True)
-    kv_all = exchange(jnp.broadcast_to(kv[None], (count,) + kv.shape))
+    kv_all = exchange(copies(kv))
     cr = cr.reshape(seqs, span, CR)
     rim = from_behind(cr[:, span - (KC - 1) :, :CC], "ctx", 1)
     rim = jnp.pad(rim, ((0, 0), (8 - (KC - 1), 0), (0, 0)))
@@ -1058,15 +1060,17 @@
         chains.append(Chain(scanned[3], wide_gains[seq], False))
         chains[seq].send()
     act, states, gains = scanned[:3]
-    atts, lses, mixed = [], [], None
+    for chain in chains:
+        chain.take()
+        chain.send()
+    atts, lses, mixed, mark = [], [], None, act
     for seq in range(seqs):
-        for chain in chains[: seq + 1]:
-            chain.take()
-            chain.send()
-        taken = [chain.state for chain in chains[: seq + 1]]
-        att, lse = attend(seq, bounds, after(q, act, *taken), kv_all, segk, segq)
+        att, lse = attend(seq, bounds, after(q, mark), kv_all, segk, segq)
         atts.append(att)
         lses.append(lse)
+        chains[seq].take()
+        chains[seq].send(lse)
+        mark = lse
     gate = low_dot(hidden, w_gates).astype(BF16).reshape(seqs, span, DI)
     states_in = []
     for seq in range(seqs):
@@ -1139,12 +1143,13 @@
     cos3, sin3 = cosine.reshape(seqs, span, 128), sine.reshape(seqs, span, 128)
     dqs, dkvs = [], []
     for seq in range(seqs):
-        for chain in chains[: seq + 1]:
-            chain.take()
-            chain.send(*dqs[-1:])
-        taken = [chain.state for chain in chains[: seq + 1]]
+        if seq:
+            for chain in chains:
+                chain.take()
+                chain.send(dqs[-1])
+        mark = dqs[-1:] + [chain.state for chain in chains] if seq else []
         dq, dkv = attend_back(
-            seq, bounds, after(q, *taken), kv_all, segk,
+            seq, bounds, after(q, grad_y, *mark), kv_all, segk,
             segq, atts[seq], grad_att, lses[seq], cos3, sin3,
         )
         dqs.append(dq)
@@ -1153,8 +1158,10 @@
     dq = jnp.concatenate(dqs, axis=0)
     last, rims, grad_conv, grad_heads = None, [], 0.0, 0.0
     waits = [(grad_rest, part_gu)] + [()] * (seqs - 1)
+    finals = [chain.finish() for chain in chains]
+    waits[1 % seqs] += tuple(finals)
     for seq in range(seqs):
-        gstate = chains[seq].finish()
+        gstate = finals[seq]
         if seq == seqs - 1:
             gu_blocks = part_gu.reshape(count, own_rows, 2 * ff)
             parts = [after(part_rest, *rims).reshape(count, -1, width)]
@@ -1172,7 +1179,7 @@
     back_rim = from_behind(grad_rim[:, 8 - (KC - 1) :].astype(BF16), "ctx", -1)
     edge = grad_cr[:, span - (KC - 1) :, :CC].astype(F32) + back_rim.astype(F32)
     grad_cr = lax.dynamic_update_slice(
-        grad_cr, edge.astype(BF16), (0, span - (KC - 1), 0)
+        grad_cr, after(edge.astype(BF16), dkv_all), (0, span - (KC - 1), 0)
     ).reshape(rows, CR)
     rest_out = lax.psum_scatter(rest_low, "ctx", scatter_dimension=0, tiled=True).astype(F32)
     grad_wcr = weight_grad(hidden, grad_cr)

time: 969 us -> 934 us (0.964)
  waiting for transfers between devices: 263 us -> 149 us
  blocking collectives: 0 us -> 66.6 us
  starting transfers between devices: 107 us -> 121 us
    ppermute x18, waiting for transfers between devices: 124 us -> 46.5 us  [send(): self.flying = (lax.ppermute(sent, 'ctx', [(source, target)]), target)]
    all_to_all x0 -> x2, blocking collectives: none -> 66.6 us  [the longest x1 51.5 us: body(): exchange = lambda blocks: lax.all_to_all(blocks, 'ctx', 0, 0, tiled=True)]
    ppermute x5 -> x0, starting transfers between devices: 31.2 us -> none  [sum_everywhere(): values = values + lax.ppermute(values, axis, route)]
    all_gather x2 -> x3, waiting for transfers between devices: 60 us -> 31.8 us  [the longest x1 31.8 us: body(): first_part = lax.all_gather(first, 'ctx', axis=0, tiled=True)]
    all_to_all x2, starting transfers between devices: 44 us -> 70.3 us  [body(): exchange = lambda blocks: lax.all_to_all(blocks, 'ctx', 0, 0, tiled=True)]
    ppermute x18, starting transfers between devices: 19.3 us -> 37 us  [send(): self.flying = (lax.ppermute(sent, 'ctx', [(source, target)]), target)]
    all_to_all x2, waiting for transfers between devices: 16.4 us -> 0.01 us  [body(): exchange = lambda blocks: lax.all_to_all(blocks, 'ctx', 0, 0, tiled=True)]
    unnamed x122 -> x154, local copies, waits for them, and re-layouts: 26.8 us -> 27.3 us
  transfers between devices with their start and end apart: 40 -> 37, of which waited for: 16 -> 10; matrix products, arithmetic and copies ran while one was open for 17% -> 19% of each run, Pallas kernels for 27% -> 28%
where the time goes in v5:
time: 934 us; the launch traced here: 924 us
  Pallas kernels  258 us (28%)
  matrix products  164 us (18%)
  waiting for transfers between devices  149 us (16%)
  starting transfers between devices  121 us (13%)
  local copies, waits for them, and re-layouts  92.9 us (10%)
  blocking collectives  66.6 us (7%)
  other arithmetic  55.9 us (6%)
  between operations  15.9 us (2%)
    pallas_call x12, Pallas kernels, mixer_call(): pl.pallas_call(run, grid=(chunks,), in_specs=in_specs, out_specs=out_spec...  157 us
    all_to_all x2, starting transfers between devices, body(): exchange = lambda blocks: lax.all_to_all(blocks, 'ctx', 0, 0, tiled=True)  70.3 us
    dot_general x7, matrix products, weight_grad(): jnp.einsum('ri,ro->io', left, right, preferred_element_type=F32)  63.4 us
    dot_general x5, matrix products, body(): low_dot = lambda a, b: jnp.dot(a, b, preferred_element_type=F32)  52.2 us
    all_to_all x1, blocking collectives, body(): exchange = lambda blocks: lax.all_to_all(blocks, 'ctx', 0, 0, tiled=True)  51.5 us
    ppermute x2, waiting for transfers between devices, from_behind(): return lax.ppermute(block, axis, route)  49.6 us
    ppermute x18, waiting for transfers between devices, send(): self.flying = (lax.ppermute(sent, 'ctx', [(source, target)]), target)  46.5 us
    dot_general x3, matrix products, back_dot(): return jnp.einsum('ro,io->ri', grad, weight, preferred_element_type=F32)  46.4 us
  transfers between devices with their start and end apart: 37, of which 10 were waited for; matrix products, arithmetic and copies ran while one was open for 19% of the time, Pallas kernels for 28%

profile of v5, /device:TPU:0, one launch (start us, length us, event | category | flops | bytes accessed | tf_op | source)
XLA Modules:
  0.0 923.6 jit_solution(17213747312037916241)
XLA Ops:
  11.5 2.8 concatenate.90
  15.9 31.8 %all-gather.4.cloned.1.call-done = bf16[128,4352]{1,0:T(8,128)(2,1)} async-done(((bf16[32,4352]{1,0:T(8,128)(2,1)}), bf16[128,4352]{1,0:T(8,128)(2,1)}) %all-gather.4.cloned.1.call-update) | async-done | bytes 1114128 | tf_op jit(solution)/shard_map/all_gather | solution.py:990
  54.1 51.5 %all_to_all.25 = bf16[4,256,1024]{2,1,0:T(8,128)(2,1)} all-to-all(bf16[4,256,1024]{2,1,0:T(8,128)(2,1)S(1)} %broadcast_in_dim.78), channel_id=1, replica_groups=mesh['dp'=8,'ctx'=4] {'ctx'}, dimensions={0} | all-to-all | bytes 4194304 | tf_op jit(solution)/shard_map/all_to_all | solution.py:985
  111.2 2.8 fusion.37
  119.8 15.3 %project.1 = (bf16[1536,1024]{1,0:T(8,128)(2,1)}, bf16[1536,1920]{1,0:T(8,128)(2,1)}, bf16[1536,512]{1,0:T(8,128)(2,1)}, bf16[1536,256]{1,0:T(8,128)(2,1)}) custom-call(bf16[1536,1024]{1,0:T(8,128)(2,1)} %bitcast.210, f32[1,1024]{1,0:T(1,128)} %reshape.279.gain_ref, bf16[1024,4352]{1,0:T(8,128)(2,1)} %all-gather.6.cloned.1.call-done.w_ref, ...), custom_call_target="tpu_custom_call" | custom-call | tf_op jit(solution)/shard_map/project/pallas_call | solution.py:77
  135.1 3.1 broadcast_in_dim.77
  138.2 3.7 all-to-all-start
  142.9 3.8 collective-permute-start
  150.0 43.3 %collective-permute-done = bf16[3,3,1792]{2,1,0:T(4,128)(2,1)S(1)} collective-permute-done((bf16[3,3,1792]{2,1,0:T(4,128)(2,1)S(1)}, bf16[3,3,1792]{2,1,0:T(4,128)(2,1)S(1)}, u32[]{:S(2)}, u32[]{:S(2)}) %collective-permute-start) | collective-permute-done | bytes 32288 | tf_op jit(solution)/shard_map/ppermute | solution.py:887
  194.0 9.1 mixer_scan.3
  203.1 20.7 %collective-permute-start.7 = (bf16[1,128,1536]{2,1,0:T(8,128)(2,1)}, bf16[1,128,1536]{2,1,0:T(8,128)(2,1)S(1)}, u32[]{:S(2)}, u32[]{:S(2)}) collective-permute-start(bf16[1,128,1536]{2,1,0:T(8,128)(2,1)} %get-tuple-element.171), channel_id=1, source_target_pairs={{0,1},{4,5},{8,9},{12,13},{16,17},{20,21},{24,25},{28,29}} | collective-permute-start | bytes 1179656 | tf_op jit(solution)/shard_map/ppermute | solution.py:910
  223.8 8.6 convolution_convert_fusion.2
  234.6 2.9 copy.174.segk_ref
  237.5 9.1 mixer_scan.4
  248.0 9.2 mixer_scan.5
  262.7 3.0 collective-permute-done.1
  273.5 7.6 attend.3
  282.1 7.4 attend.4
  290.9 7.4 attend.5
  301.2 9.0 mixer_out.3
  311.0 8.9 mixer_out.4
  320.8 9.0 mixer_out.5
  333.4 6.0 slice.388
  339.4 6.2 fusion.67
  349.3 7.2 multiply_reduce_fusion.2
  356.5 21.1 %convolution_convert_fusion = bf16[1536,4096]{1,0:T(8,128)(2,1)} fusion(bf16[1024,1024]{1,0:T(8,128)(2,1)} %bitcast.228, bf16[1024,1024]{1,0:T(8,128)(2,1)} %bitcast.230, bf16[1024,1024]{1,0:T(8,128)(2,1)} %bitcast.232, bf16[1024,1024]{1,0:T(8,128)(2,1)} %bitcast.226, f32[1536,1024]{1,0:T(8,128)} %get-tuple-element.314, f32[1024]{0:T(1024)S(1)} %mul.214, ...), kind=kOutput, calls=%fused_computation.6 | convolution fusion | flops 12929466368 | bytes 27273216 | tf_op jit(solution)/shard_map/dot_general | solution.py:974
  377.6 19.0 %fusion.6 = (bf16[1536,2048]{1,0:T(8,128)(2,1)}, bf16[1536,2048]{1,0:T(8,128)(2,1)}, bf16[1536,2048]{1,0:T(8,128)(2,1)}) fusion(bf16[1536,4096]{1,0:T(8,128)(2,1)} %convolution_convert_fusion, bf16[2048,1024]{1,0:T(8,128)(2,1)} %bitcast.216, bf16[1536,1024]{1,0:T(8,128)(2,1)S(1)} %bitcast.219), kind=kOutput, calls=%fused_computation.13 | convolution fusion | flops 6499074048 | bytes 38797312 | tf_op jit(solution)/shard_map/ro,io->ri/dot_general | solution.py:1104
  396.6 20.6 %fusion.9 = f32[1536,1024]{1,0:T(8,128)} fusion(bf16[1536,2048]{1,0:T(8,128)(2,1)} %get-tuple-element.272, bf16[1536,2048]{1,0:T(8,128)(2,1)} %get-tuple-element.271, bf16[1024,1024]{1,0:T(8,128)(2,1)S(1)} %bitcast.229, bf16[1024,1024]{1,0:T(8,128)(2,1)S(1)} %bitcast.231, bf16[1024,1024]{1,0:T(8,128)(2,1)} %bitcast.233, bf16[1024,1024]{1,0:T(8,128)(2,1)S(1)} %bitcast.227), kind=kOutput, calls=%fused_computation.20 | convolution fusion | flops 12943622144 | bytes 27262976 | tf_op jit(solution)/shard_map/ro,io->ri/dot_general | solution.py:1104
  417.2 21.7 %fusion.10 = bf16[1024,4096]{1,0:T(8,128)(2,1)} fusion(bf16[1536,2048]{1,0:T(8,128)(2,1)} %get-tuple-element.272, bf16[1536,2048]{1,0:T(8,128)(2,1)} %get-tuple-element.271, f32[1536,1024]{1,0:T(8,128)} %get-tuple-element.314, f32[1024]{0:T(1024)S(1)} %mul.214, f32[1536]{0:T(1024)S(1)} %fusion.52), kind=kOutput, calls=%fused_computation.23 | convolution fusion | flops 12918980608 | bytes 27273216 | tf_op jit(solution)/shard_map/ri,ro->io/dot_general | solution.py:1101
  438.9 11.1 %convolution_convert_fusion.3 = bf16[2048,1024]{1,0:T(8,128)(2,1)} fusion(bf16[1536,2048]{1,0:T(8,128)(2,1)} %get-tuple-element.232, bf16[1536,1024]{1,0:T(8,128)(2,1)S(1)} %bitcast.220), kind=kOutput, calls=%fused_computation.31 | convolution fusion | flops 6444548096 | bytes 13631488 | tf_op jit(solution)/shard_map/ri,ro->io/dot_general | solution.py:1101
  450.2 6.6 multiply_reduce_fusion
  456.8 7.3 fusion.64
  464.1 3.0 convolution_convert_fusion.7
  467.1 2.8 convolution_convert_fusion.8
  469.9 6.8 convolution_convert_fusion.1
  476.8 5.4 convolution_convert_fusion.6
  482.2 10.2 %mixer_gate_back.3 = (bf16[3,512,1536]{2,1,0:T(8,128)(2,1)}, bf16[3,512,1536]{2,1,0:T(8,128)(2,1)}, bf16[3,4,128,1536]{3,2,1,0:T(8,128)(2,1)}, f32[3,4,8,128]{3,...) custom-call(bf16[3,512,1536]{2,1,0:T(8,128)(2,1)} %bitcast.188, ...), custom_call_target="tpu_custom_call" | custom-call | tf_op jit(solution)/shard_map/mixer_gate_back/pallas_call | solution.py:764
  492.4 11.1 %mixer_gate_back.4 = (bf16[3,512,1536]{2,1,0:T(8,128)(2,1)}, bf16[3,512,1536]{2,1,0:T(8,128)(2,1)}, bf16[3,4,128,1536]{3,2,1,0:T(8,128)(2,1)}, f32[3,4,8,128]{3,...) custom-call(bf16[3,512,1536]{2,1,0:T(8,128)(2,1)} %bitcast.189, ...), custom_call_target="tpu_custom_call", output_to_operand_aliasing={{0}: (9, {}), {1}: (10, {}), {2}: (11, {}), {3}: (12, {})} | custom-call | tf_op jit(solution)/shard_map/mixer_gate_back/pallas_call | solution.py:764
  503.5 10.2 %mixer_gate_back.5 = (bf16[3,512,1536]{2,1,0:T(8,128)(2,1)}, bf16[3,512,1536]{2,1,0:T(8,128)(2,1)}, bf16[3,4,128,1536]{3,2,1,0:T(8,128)(2,1)}, f32[3,4,8,128]{3,...) custom-call(bf16[3,512,1536]{2,1,0:T(8,128)(2,1)} %bitcast.190, ...), custom_call_target="tpu_custom_call", output_to_operand_aliasing={{0}: (9, {}), {1}: (10, {}), {2}: (11, {}), {3}: (12, {})} | custom-call | tf_op jit(solution)/shard_map/mixer_gate_back/pallas_call | solution.py:764
  513.7 2.7 constant_dynamic-update-slice_fusion.7
  521.8 5.6 convolution_convert_fusion.5
  533.4 13.3 %attend_back.3 = (bf16[1,512,512]{2,1,0:T(8,128)(2,1)}, bf16[4,1,512,256]{3,2,1,0:T(8,128)(2,1)}) custom-call(s32[6]{0:T(128)} %and_select_fusion.1.low_ref, s32[6]{0:T(128)} %reshape.281.high_ref, s32[1]{0:T(128)} %bitcast.7.base_ref, bf16[3,512,512]{2,1,0:T(8,128)(2,1)} %bitcast.179, bf16[4,3,512,256]{3,2,1,0:T(8,128)(2,1)} %copy-done, ...), custom_call_target="tpu_custom_call" | custom-call | tf_op jit(solution)/shard_map/attend_back/pallas_call | solution.py:336
  549.4 13.6 %attend_back.4 = (bf16[1,512,512]{2,1,0:T(8,128)(2,1)}, bf16[4,1,512,256]{3,2,1,0:T(8,128)(2,1)}) custom-call(s32[6]{0:T(128)} %and_select_fusion.1.low_ref, s32[6]{0:T(128)} %reshape.281.high_ref, s32[1]{0:T(128)} %bitcast.7.base_ref, bf16[3,512,512]{2,1,0:T(8,128)(2,1)} %bitcast.180, bf16[4,3,512,256]{3,2,1,0:T(8,128)(2,1)} %copy-done, ...), custom_call_target="tpu_custom_call" | custom-call | tf_op jit(solution)/shard_map/attend_back/pallas_call | solution.py:336
  567.4 13.4 %attend_back.5 = (bf16[1,512,512]{2,1,0:T(8,128)(2,1)}, bf16[4,1,512,256]{3,2,1,0:T(8,128)(2,1)}) custom-call(s32[6]{0:T(128)} %and_select_fusion.1.low_ref, s32[6]{0:T(128)} %reshape.281.high_ref, s32[1]{0:T(128)} %bitcast.7.base_ref, bf16[3,512,512]{2,1,0:T(8,128)(2,1)} %bitcast.181, bf16[4,3,512,256]{3,2,1,0:T(8,128)(2,1)} %copy-done, ...), custom_call_target="tpu_custom_call" | custom-call | tf_op jit(solution)/shard_map/attend_back/pallas_call | solution.py:336
  580.8 3.5 pad_maximum_fusion.6
  584.3 66.6 %all-to-all-start.2 = ((bf16[4,3,512,256]{3,2,1,0:T(8,128)(2,1)}), bf16[4,3,512,256]{3,2,1,0:T(8,128)(2,1)S(1)}, u32[]{:S(2)}, u32[]{:S(2)}) async-start(bf16[4,3,512,256]{3,2,1,0:T(8,128)(2,1)} %pad_maximum_fusion.6), calls=%async_computation.4 | async-start | bytes 6291456 | tf_op jit(solution)/shard_map/all_to_all | solution.py:985
  655.4 37.9 %collective-permute-done.17 = bf16[1,128,1536]{2,1,0:T(8,128)(2,1)S(1)} collective-permute-done((bf16[1,128,1536]{2,1,0:T(8,128)(2,1)}, bf16[1,128,1536]{2,1,0:T(8,128)(2,1)S(1)}, u32[]{:S(2)}, u32[]{:S(2)}) %collective-permute-start.17) | collective-permute-done | bytes 393248 | tf_op jit(solution)/shard_map/ppermute | solution.py:910
  694.1 5.6 collective-permute-done.18
  700.5 24.0 %mixer_back.3 = (bf16[3,512,1920]{2,1,0:T(8,128)(2,1)}, f32[1,8,1792]{2,1,0:T(8,128)}, f32[8,1792]{1,0:T(8,128)}, f32[8,128]{1,0:T(8,128)}) custom-call(bf16[3,512,1536]{2,1,0:T(8,128)(2,1)} %get-tuple-element.224.refs_0_, f32[3,512,1536]{2,1,0:T(8,128)} %get-tuple-element.184.refs_1_, bf16[3,512,1920]{2,1,0:T(8,128)(2,1)} %bitcast.164, ...), custom_call_target="tpu_custom_call" | custom-call | tf_op jit(solution)/shard_map/mixer_back/pallas_call | solution.py:764
  724.5 23.6 %mixer_back.4 = (bf16[3,512,1920]{2,1,0:T(8,128)(2,1)}, f32[1,8,1792]{2,1,0:T(8,128)}, f32[8,1792]{1,0:T(8,128)}, f32[8,128]{1,0:T(8,128)}) custom-call(bf16[3,512,1536]{2,1,0:T(8,128)(2,1)} %get-tuple-element.224.refs_0_, f32[3,512,1536]{2,1,0:T(8,128)} %get-tuple-element.184.refs_1_, ...), custom_call_target="tpu_custom_call", output_to_operand_aliasing={{0}: (19, {})} | custom-call | tf_op jit(solution)/shard_map/mixer_back/pallas_call | solution.py:764
  757.5 23.6 %mixer_back.5 = (bf16[3,512,1920]{2,1,0:T(8,128)(2,1)}, f32[1,8,1792]{2,1,0:T(8,128)}, f32[8,1792]{1,0:T(8,128)}, f32[8,128]{1,0:T(8,128)}) custom-call(bf16[3,512,1536]{2,1,0:T(8,128)(2,1)} %get-tuple-element.224.refs_0_, f32[3,512,1536]{2,1,0:T(8,128)} %get-tuple-element.184.refs_1_, ...), custom_call_target="tpu_custom_call", output_to_operand_aliasing={{0}: (19, {})} | custom-call | tf_op jit(solution)/shard_map/mixer_back/pallas_call | solution.py:764
  783.2 6.3 collective-permute-done.19
  792.6 11.4 %convolution_convert_fusion.4 = bf16[1024,1920]{1,0:T(8,128)(2,1)} fusion(bf16[1536,1024]{1,0:T(8,128)(2,1)} %get-tuple-element.136, bf16[1536,1920]{1,0:T(8,128)(2,1)} %bitcast.182), kind=kOutput, calls=%fused_computation.32 | convolution fusion | flops 6041763840 | bytes 12976128 | tf_op jit(solution)/shard_map/ri,ro->io/dot_general | solution.py:1101
  804.1 3.9 slice.371.wg_ref
  812.4 22.9 %finish.1 = (bf16[1536,1024]{1,0:T(8,128)(2,1)}, bf16[1536,256]{1,0:T(8,128)(2,1)}, f32[8,1024]{1,0:T(8,128)}) custom-call(bf16[1536,1024]{1,0:T(8,128)(2,1)} %bitcast.211, f32[1,1024]{1,0:T(1,128)} %reshape.279.gain_ref, bf16[1536,1536]{1,0:T(8,128)(2,1)} %bitcast.184, bf16[1536,1920]{1,0:T(8,128)(2,1)} %bitcast.183, bf16[1536,512]{1,0:T(8,128)(2,1)} %bitcast.214, ...), custom_call_target="tpu_custom_call" | custom-call | tf_op jit(solution)/shard_map/finish/pallas_call | solution.py:137
  836.5 5.4 fusion.16
  843.3 3.1 copy.183
  848.6 15.1 %all_to_all.26 = f32[8,3,24]{2,1,0:T(4,128)S(1)} all-to-all(f32[8,3,24]{2,1,0:T(4,128)S(1)} %broadcast_in_dim.81), channel_id=1, replica_groups=mesh['dp'=8,'ctx'=4] {'dp'}, dimensions={0} | all-to-all | bytes 4608 | tf_op jit(solution)/shard_map/all_to_all | solution.py:931
  864.3 3.2 all-to-all-start.4
  867.6 5.5 all-to-all-done.4
  877.6 9.7 %collective-permute-done.21 = bf16[2,4,32,896]{3,2,1,0:T(8,128)(2,1)S(1)} collective-permute-done((bf16[2,4,32,896]{3,2,1,0:T(8,128)(2,1)S(1)}, bf16[2,4,32,896]{3,2,1,0:T(8,128)(2,1)S(1)}, u32[]{:S(2)}, u32[]{:S(2)}) %collective-permute-start.21) | collective-permute-done | bytes 458784 | tf_op jit(solution)/shard_map/ppermute | solution.py:945
  889.2 4.4 collective-permute-done.22
  894.4 3.2 collective-permute-start.25
  897.6 12.3 %add_convert_fusion = bf16[1536,1024]{1,0:T(8,128)(2,1)} fusion(f32[1536,1024]{1,0:T(8,128)} %get-tuple-element.314, bf16[1536,2048]{1,0:T(8,128)(2,1)} %get-tuple-element.232, bf16[2048,1024]{1,0:T(8,128)(2,1)} %bitcast.217), kind=kOutput, calls=%fused_computation.26 | convolution fusion | flops 6445596672 | bytes 19922944 | tf_op jit(solution)/shard_map/dot_general | solution.py:974
  (390 shorter events, 121.6 us)
Async XLA Ops:
  7.2 40.5 %all-gather.4.cloned.1.call-start = ((), (), s32[]{:S(2)}) async-start(), calls=%async_computation.10 | async-start | bytes 1392640 | tf_op jit(solution)/shard_map/all_gather | solution.py:990
  15.9 101.4 %all-gather.6.cloned.1.call-start = ((), (), s32[]{:S(2)}) async-start(), calls=%async_computation.11 | async-start | bytes 10027008 | tf_op jit(solution)/shard_map/all_gather | solution.py:987
  47.8 282.1 %all-gather.8.cloned.1.call-start = ((), (), s32[]{:S(2)}) async-start(), calls=%async_computation.12 | async-start | bytes 18874368 | tf_op jit(solution)/shard_map/all_gather | solution.py:987
  50.4 55.2 %copy-start.48 = (s32[3,2048]{1,0:T(4,128)S(1)}, s32[3,2048]{1,0:T(4,128)}, u32[]{:S(2)}) copy-start(s32[3,2048]{1,0:T(4,128)} %param.20) | copy-start | bytes 73732
  51.2 56.2 %copy-start.59 = (f32[3,24]{1,0:T(4,128)S(1)}, f32[3,24]{1,0:T(4,128)}, u32[]{:S(2)}) copy-start(f32[3,24]{1,0:T(4,128)} %param.26) | copy-start | bytes 868
  51.2 56.8 %copy-start.55 = (s32[3,512]{1,0:T(4,128)S(1)}, s32[3,512]{1,0:T(4,128)}, u32[]{:S(2)}) copy-start(s32[3,512]{1,0:T(4,128)} %param.21) | copy-start | bytes 18436
  118.3 16.8 %copy-start.35 = (f32[32,4096]{1,0:T(8,128)}, f32[32,4096]{1,0:T(8,128)S(1)}, u32[]{:S(2)}) copy-start(f32[32,4096]{1,0:T(8,128)S(1)} %reshape.325) | copy-start | bytes 1572868
  138.2 133.6 %all-to-all-start = ((bf16[4,3,512,256]{3,2,1,0:T(8,128)(2,1)}), bf16[4,3,512,256]{3,2,1,0:T(8,128)(2,1)S(1)}, u32[]{:S(2)}, u32[]{:S(2)}) async-start(bf16[4,3,512,256]{3,2,1,0:T(8,128)(2,1)} %broadcast_in_dim.77), calls=%async_computation | async-start | bytes 6291456 | tf_op jit(solution)/shard_map/all_to_all | solution.py:985
  141.9 558.6 %reduce-scatter.8.cloned.1.call-start = ((), (), s32[]{:S(2)}) async-start(), calls=%async_computation.14 | async-start | bytes 9437184 | tf_op jit(solution)/shard_map/reduce_scatter | solution.py:1098
  142.9 50.5 %collective-permute-start = (bf16[3,3,1792]{2,1,0:T(4,128)(2,1)S(1)}, bf16[3,3,1792]{2,1,0:T(4,128)(2,1)S(1)}, u32[]{:S(2)}, u32[]{:S(2)}) collective-permute-start(bf16[3,3,1792]{2,1,0:T(4,128)(2,1)S(1)} %slice.372), channel_id=1, source_target_pairs={{0,1},{1,2},{2,3},{4,5},{5,6},{6,7},{8,9},{9,10},{10,11},{12,13},{... | collective-permute-start | bytes 96776 | tf_op jit(solution)/shard_map/ppermute | solution.py:887
  149.4 74.4 %copy-start.60 = (bf16[1536,1024]{1,0:T(8,128)(2,1)S(1)}, bf16[1536,1024]{1,0:T(8,128)(2,1)}, u32[]{:S(2)}) copy-start(bf16[1536,1024]{1,0:T(8,128)(2,1)} %get-tuple-element.136) | copy-start | bytes 9437188
  203.1 57.9 %collective-permute-start.7 = (bf16[1,128,1536]{2,1,0:T(8,128)(2,1)}, bf16[1,128,1536]{2,1,0:T(8,128)(2,1)S(1)}, u32[]{:S(2)}, u32[]{:S(2)}) collective-permute-start(bf16[1,128,1536]{2,1,0:T(8,128)(2,1)} %get-tuple-element.171), channel_id=1, source_target_pairs={{0,1},{4,5},{8,9},{12,13},{16,17},{20,21},{24,25},{28,29}} | collective-permute-start | bytes 1179656 | tf_op jit(solution)/shard_map/ppermute | solution.py:910
  246.6 15.2 %collective-permute-start.4 = (bf16[1,128,1536]{2,1,0:T(8,128)(2,1)}, bf16[1,128,1536]{2,1,0:T(8,128)(2,1)S(1)}, u32[]{:S(2)}, u32[]{:S(2)}) collective-permute-start(bf16[1,128,1536]{2,1,0:T(8,128)(2,1)} %get-tuple-element.168), channel_id=1, source_target_pairs={{0,1},{4,5},{8,9},{12,13},{16,17},{20,21},{24,25},{28,29}} | collective-permute-start | bytes 1179656 | tf_op jit(solution)/shard_map/ppermute | solution.py:910
  247.9 13.0 %copy-start.23 = (bf16[1,128,1536]{2,1,0:T(8,128)(2,1)S(1)}, bf16[1,128,1536]{2,1,0:T(8,128)(2,1)}, u32[]{:S(2)}) copy-start(bf16[1,128,1536]{2,1,0:T(8,128)(2,1)} %get-tuple-element.171) | copy-start | bytes 1179652
  247.9 13.9 %copy-start.29 = (bf16[1,128,1536]{2,1,0:T(8,128)(2,1)S(1)}, bf16[1,128,1536]{2,1,0:T(8,128)(2,1)}, u32[]{:S(2)}) copy-start(bf16[1,128,1536]{2,1,0:T(8,128)(2,1)} %get-tuple-element.168) | copy-start | bytes 1179652
  257.1 8.5 collective-permute-start.1
  259.3 10.8 %copy-start.46 = (f32[1536]{0:T(1024)}, f32[1536]{0:T(1024)S(1)}, u32[]{:S(2)}) copy-start(f32[1536]{0:T(1024)S(1)} %slice_reduce_fusion.4) | copy-start | bytes 18436
  260.1 10.0 %copy-start.44 = (f32[1536]{0:T(1024)}, f32[1536]{0:T(1024)S(1)}, u32[]{:S(2)}) copy-start(f32[1536]{0:T(1024)S(1)} %slice_reduce_fusion.5) | copy-start | bytes 18436
  260.9 20.9 %copy-start.42 = (f32[1536]{0:T(1024)}, f32[1536]{0:T(1024)S(1)}, u32[]{:S(2)}) copy-start(f32[1536]{0:T(1024)S(1)} %slice_reduce_fusion.6) | copy-start | bytes 18436
  261.1 8.0 collective-permute-start.8
  262.0 8.1 collective-permute-start.5
  267.7 14.2 %collective-permute-start.2 = (bf16[1,128,1536]{2,1,0:T(8,128)(2,1)}, bf16[1,128,1536]{2,1,0:T(8,128)(2,1)}, u32[]{:S(2)}, u32[]{:S(2)}) collective-permute-start(bf16[1,128,1536]{2,1,0:T(8,128)(2,1)} %fusion.21), channel_id=1, source_target_pairs={{1,2},{5,6},{9,10},{13,14},{17,18},{21,22},{25,26},{29,30}} | collective-permute-start | bytes 1179656 | tf_op jit(solution)/shard_map/ppermute | solution.py:910
  281.0 19.2 %collective-permute-start.9 = (bf16[1,128,1536]{2,1,0:T(8,128)(2,1)S(1)}, bf16[1,128,1536]{2,1,0:T(8,128)(2,1)S(1)}, u32[]{:S(2)}, u32[]{:S(2)}) collective-permute-start(bf16[1,128,1536]{2,1,0:T(8,128)(2,1)S(1)} %copy-done.41), channel_id=1, source_target_pairs={{2,3},{6,7},{10,11},{14,15},{18,19},{22,23},{26,27},{30,31}} | collective-permute-start | bytes 1179656 | tf_op jit(solution)/shard_map/ppermute | solution.py:910
  289.6 10.7 %copy-start.28 = (bf16[1,128,1536]{2,1,0:T(8,128)(2,1)S(1)}, bf16[1,128,1536]{2,1,0:T(8,128)(2,1)}, u32[]{:S(2)}) copy-start(bf16[1,128,1536]{2,1,0:T(8,128)(2,1)} %copy-done.27) | copy-start | bytes 1179652
  289.6 20.6 %collective-permute-start.6 = (bf16[1,128,1536]{2,1,0:T(8,128)(2,1)S(1)}, bf16[1,128,1536]{2,1,0:T(8,128)(2,1)S(1)}, u32[]{:S(2)}, u32[]{:S(2)}) collective-permute-start(bf16[1,128,1536]{2,1,0:T(8,128)(2,1)S(1)} %copy-done.40), channel_id=1, source_target_pairs={{2,3},{6,7},{10,11},{14,15},{18,19},{22,23},{26,27},{30,31}} | collective-permute-start | bytes 1179656 | tf_op jit(solution)/shard_map/ppermute | solution.py:910
  298.3 21.7 %collective-permute-start.3 = (bf16[1,128,1536]{2,1,0:T(8,128)(2,1)S(1)}, bf16[1,128,1536]{2,1,0:T(8,128)(2,1)S(1)}, u32[]{:S(2)}, u32[]{:S(2)}) collective-permute-start(bf16[1,128,1536]{2,1,0:T(8,128)(2,1)S(1)} %fusion.22), channel_id=1, source_target_pairs={{2,3},{6,7},{10,11},{14,15},{18,19},{22,23},{26,27},{30,31}} | collective-permute-start | bytes 1179656 | tf_op jit(solution)/shard_map/ppermute | solution.py:910
  300.2 45.5 %copy-start.18 = (bf16[3,512,512]{2,1,0:T(8,128)(2,1)}, bf16[3,512,512]{2,1,0:T(8,128)(2,1)S(1)}, u32[]{:S(2)}) copy-start(bf16[3,512,512]{2,1,0:T(8,128)(2,1)S(1)} %pad_maximum_fusion.8) | copy-start | bytes 4718596
  333.4 14.2 %copy-start.10 = (bf16[32,48,1024]{2,1,0:T(8,128)(2,1)}, bf16[32,48,1024]{2,1,0:T(8,128)(2,1)S(1)}, u32[]{:S(2)}) copy-start(bf16[32,48,1024]{2,1,0:T(8,128)(2,1)S(1)} %slice.378) | copy-start | bytes 9437188
  356.5 21.1 %copy-start.9 = (bf16[3,512,1024]{2,1,0:T(8,128)(2,1)S(1)}, bf16[3,512,1024]{2,1,0:T(8,128)(2,1)}, u32[]{:S(2)}) copy-start(bf16[3,512,1024]{2,1,0:T(8,128)(2,1)} %param.37) | copy-start | bytes 9437188
  377.6 19.0 %copy-start.15 = (bf16[32,32,1024]{2,1,0:T(8,128)(2,1)S(1)}, bf16[32,32,1024]{2,1,0:T(8,128)(2,1)}, u32[]{:S(2)}) copy-start(bf16[32,32,1024]{2,1,0:T(8,128)(2,1)} %get-tuple-element.273) | copy-start | bytes 6291460
  377.6 19.0 %copy-start.16 = (bf16[32,32,1024]{2,1,0:T(8,128)(2,1)S(1)}, bf16[32,32,1024]{2,1,0:T(8,128)(2,1)}, u32[]{:S(2)}) copy-start(bf16[32,32,1024]{2,1,0:T(8,128)(2,1)} %get-tuple-element.274) | copy-start | bytes 6291460
  377.6 19.0 %copy-start.17 = (bf16[32,32,1024]{2,1,0:T(8,128)(2,1)S(1)}, bf16[32,32,1024]{2,1,0:T(8,128)(2,1)}, u32[]{:S(2)}) copy-start(bf16[32,32,1024]{2,1,0:T(8,128)(2,1)} %get-tuple-element.275) | copy-start | bytes 6291460
  450.1 298.0 %reduce-scatter.6.cloned.1.call-start = ((), (), s32[]{:S(2)}) async-start(), calls=%async_computation.13 | async-start | bytes 12976128 | tf_op jit(solution)/shard_map/reduce_scatter | solution.py:1098
  467.1 9.6 %slice-start.4 = ((s8[4718592]{0:T(1024)(128)(4,1)}), s8[4194304]{0:T(1024)(128)(4,1)S(1)}, s32[]{:S(2)}) async-start(s8[4718592]{0:T(1024)(128)(4,1)} %bitcast.198), calls=%async_computation.22 | async-start | bytes 8388608
  503.5 10.2 %copy-start.4 = (bf16[2048,1024]{1,0:T(8,128)(2,1)S(1)}, bf16[2048,1024]{1,0:T(8,128)(2,1)}, u32[]{:S(2)}) copy-start(bf16[2048,1024]{1,0:T(8,128)(2,1)} %convolution_convert_fusion.3) | copy-start | bytes 12582916
  531.2 15.6 %collective-permute-start.12 = (bf16[1,128,1536]{2,1,0:T(8,128)(2,1)S(1)}, bf16[1,128,1536]{2,1,0:T(8,128)(2,1)S(1)}, u32[]{:S(2)}, u32[]{:S(2)}) collective-permute-start(bf16[1,128,1536]{2,1,0:T(8,128)(2,1)S(1)} %copy-done.20), channel_id=1, source_target_pairs={{3,2},{7,6},{11,10},{15,14},{19,18},{23,22},{27,26},{31,30}} | collective-permute-start | bytes 1179656 | tf_op jit(solution)/shard_map/ppermute | solution.py:910
  531.9 15.1 %collective-permute-start.10 = (bf16[1,128,1536]{2,1,0:T(8,128)(2,1)S(1)}, bf16[1,128,1536]{2,1,0:T(8,128)(2,1)S(1)}, u32[]{:S(2)}, u32[]{:S(2)}) collective-permute-start(bf16[1,128,1536]{2,1,0:T(8,128)(2,1)S(1)} %copy-done.22), channel_id=1, source_target_pairs={{3,2},{7,6},{11,10},{15,14},{19,18},{23,22},{27,26},{31,30}} | collective-permute-start | bytes 1179656 | tf_op jit(solution)/shard_map/ppermute | solution.py:910
  532.6 14.2 %copy-start.43 = (f32[1536]{0:T(1024)S(1)}, f32[1536]{0:T(1024)}, u32[]{:S(2)}) copy-start(f32[1536]{0:T(1024)} %copy-done.42) | copy-start | bytes 18436
  532.6 14.4 %copy-start.47 = (f32[1536]{0:T(1024)S(1)}, f32[1536]{0:T(1024)}, u32[]{:S(2)}) copy-start(f32[1536]{0:T(1024)} %copy-done.46) | copy-start | bytes 18436
  532.6 15.2 %copy-start.45 = (f32[1536]{0:T(1024)S(1)}, f32[1536]{0:T(1024)}, u32[]{:S(2)}) copy-start(f32[1536]{0:T(1024)} %copy-done.44) | copy-start | bytes 18436
  532.6 15.2 %collective-permute-start.11 = (bf16[1,128,1536]{2,1,0:T(8,128)(2,1)S(1)}, bf16[1,128,1536]{2,1,0:T(8,128)(2,1)S(1)}, u32[]{:S(2)}, u32[]{:S(2)}) collective-permute-start(bf16[1,128,1536]{2,1,0:T(8,128)(2,1)S(1)} %copy-done.21), channel_id=1, source_target_pairs={{3,2},{7,6},{11,10},{15,14},{19,18},{23,22},{27,26},{31,30}} | collective-permute-start | bytes 1179656 | tf_op jit(solution)/shard_map/ppermute | solution.py:910
  547.1 15.9 %collective-permute-start.13 = (bf16[1,128,1536]{2,1,0:T(8,128)(2,1)S(1)}, bf16[1,128,1536]{2,1,0:T(8,128)(2,1)S(1)}, u32[]{:S(2)}, u32[]{:S(2)}) collective-permute-start(bf16[1,128,1536]{2,1,0:T(8,128)(2,1)S(1)} %get-tuple-element.202), channel_id=1, source_target_pairs={{2,1},{6,5},{10,9},{14,13},{18,17},{22,21},{26,25},{30,29}} | collective-permute-start | bytes 1179656 | tf_op jit(solution)/shard_map/ppermute | solution.py:910
  548.0 17.2 %collective-permute-start.14 = (bf16[1,128,1536]{2,1,0:T(8,128)(2,1)S(1)}, bf16[1,128,1536]{2,1,0:T(8,128)(2,1)S(1)}, u32[]{:S(2)}, u32[]{:S(2)}) collective-permute-start(bf16[1,128,1536]{2,1,0:T(8,128)(2,1)S(1)} %get-tuple-element.203), channel_id=1, source_target_pairs={{2,1},{6,5},{10,9},{14,13},{18,17},{22,21},{26,25},{30,29}} | collective-permute-start | bytes 1179656 | tf_op jit(solution)/shard_map/ppermute | solution.py:910
  548.7 17.6 %collective-permute-start.15 = (bf16[1,128,1536]{2,1,0:T(8,128)(2,1)S(1)}, bf16[1,128,1536]{2,1,0:T(8,128)(2,1)S(1)}, u32[]{:S(2)}, u32[]{:S(2)}) collective-permute-start(bf16[1,128,1536]{2,1,0:T(8,128)(2,1)S(1)} %get-tuple-element.204), channel_id=1, source_target_pairs={{2,1},{6,5},{10,9},{14,13},{18,17},{22,21},{26,25},{30,29}} | collective-permute-start | bytes 1179656 | tf_op jit(solution)/shard_map/ppermute | solution.py:910
  563.9 89.6 %collective-permute-start.16 = (bf16[1,128,1536]{2,1,0:T(8,128)(2,1)}, bf16[1,128,1536]{2,1,0:T(8,128)(2,1)}, u32[]{:S(2)}, u32[]{:S(2)}) collective-permute-start(bf16[1,128,1536]{2,1,0:T(8,128)(2,1)} %get-tuple-element.215), channel_id=1, source_target_pairs={{1,0},{5,4},{9,8},{13,12},{17,16},{21,20},{25,24},{29,28}} | collective-permute-start | bytes 1179656 | tf_op jit(solution)/shard_map/ppermute | solution.py:910
  567.4 13.4 %copy-start.33 = (bf16[4,1,512,256]{3,2,1,0:T(8,128)(2,1)S(1)}, bf16[4,1,512,256]{3,2,1,0:T(8,128)(2,1)}, u32[]{:S(2)}) copy-start(bf16[4,1,512,256]{3,2,1,0:T(8,128)(2,1)} %get-tuple-element.228) | copy-start | bytes 3145732
  567.4 13.4 %copy-start.34 = (bf16[4,1,512,256]{3,2,1,0:T(8,128)(2,1)S(1)}, bf16[4,1,512,256]{3,2,1,0:T(8,128)(2,1)}, u32[]{:S(2)}) copy-start(bf16[4,1,512,256]{3,2,1,0:T(8,128)(2,1)} %get-tuple-element.229) | copy-start | bytes 3145732
  584.3 206.1 %all-to-all-start.2 = ((bf16[4,3,512,256]{3,2,1,0:T(8,128)(2,1)}), bf16[4,3,512,256]{3,2,1,0:T(8,128)(2,1)S(1)}, u32[]{:S(2)}, u32[]{:S(2)}) async-start(bf16[4,3,512,256]{3,2,1,0:T(8,128)(2,1)} %pad_maximum_fusion.6), calls=%async_computation.4 | async-start | bytes 6291456 | tf_op jit(solution)/shard_map/all_to_all | solution.py:985
  651.0 161.4 %reduce-scatter.12.cloned.1.call-start = ((), (), s32[]{:S(2)}) async-start(), calls=%async_computation.16 | async-start | bytes 3112960 | tf_op jit(solution)/shard_map/reduce_scatter | solution.py:1184
  651.0 42.3 %collective-permute-start.17 = (bf16[1,128,1536]{2,1,0:T(8,128)(2,1)}, bf16[1,128,1536]{2,1,0:T(8,128)(2,1)S(1)}, u32[]{:S(2)}, u32[]{:S(2)}) collective-permute-start(bf16[1,128,1536]{2,1,0:T(8,128)(2,1)} %get-tuple-element.218), channel_id=1, source_target_pairs={{1,0},{5,4},{9,8},{13,12},{17,16},{21,20},{25,24},{29,28}} | collective-permute-start | bytes 1179656 | tf_op jit(solution)/shard_map/ppermute | solution.py:910
  652.2 47.5 %collective-permute-start.18 = (bf16[1,128,1536]{2,1,0:T(8,128)(2,1)}, bf16[1,128,1536]{2,1,0:T(8,128)(2,1)S(1)}, u32[]{:S(2)}, u32[]{:S(2)}) collective-permute-start(bf16[1,128,1536]{2,1,0:T(8,128)(2,1)} %get-tuple-element.219), channel_id=1, source_target_pairs={{1,0},{5,4},{9,8},{13,12},{17,16},{21,20},{25,24},{29,28}} | collective-permute-start | bytes 1179656 | tf_op jit(solution)/shard_map/ppermute | solution.py:910
  757.4 131.7 %reduce-scatter.10.cloned.1.call-start = ((), (), s32[]{:S(2)}) async-start(), calls=%async_computation.15 | async-start | bytes 4423680 | tf_op jit(solution)/shard_map/reduce_scatter | solution.py:1098
  781.9 7.6 collective-permute-start.19
  790.5 13.6 %copy-start.1 = (bf16[4,3,512,256]{3,2,1,0:T(8,128)(2,1)}, bf16[4,3,512,256]{3,2,1,0:T(8,128)(2,1)S(1)}, u32[]{:S(2)}) copy-start(bf16[4,3,512,256]{3,2,1,0:T(8,128)(2,1)S(1)} %all-to-all-done.2.dkv_ref) | copy-start | bytes 9437188
  812.4 24.1 %copy-start.3 = (bf16[3,512,512]{2,1,0:T(8,128)(2,1)S(1)}, bf16[3,512,512]{2,1,0:T(8,128)(2,1)}, u32[]{:S(2)}) copy-start(bf16[3,512,512]{2,1,0:T(8,128)(2,1)} %pad_maximum_fusion.9) | copy-start | bytes 4718596
  842.0 31.7 %copy-start.12 = (bf16[304,1024]{1,0:T(8,128)(2,1)S(1)}, bf16[304,1024]{1,0:T(8,128)(2,1)}, u32[]{:S(2)}) copy-start(bf16[304,1024]{1,0:T(8,128)(2,1)} %reduce-scatter.12.cloned.1.call-done) | copy-start | bytes 1867780
  847.5 28.3 %collective-permute-start.20 = (bf16[2,2,4,32,896]{4,3,2,1,0:T(8,128)(2,1)}, bf16[2,2,4,32,896]{4,3,2,1,0:T(8,128)(2,1)S(1)}, u32[]{:S(2)}, u32[]{:S(2)}) collective-permute-start(bf16[2,2,4,32,896]{4,3,2,1,0:T(8,128)(2,1)} %fusion.19), channel_id=1, source_target_pairs={{0,4},{4,0},{8,12},{12,8},{16,20},{20,16},{24,28},{28,24},{1,5},{5... | collective-permute-start | bytes 2752520 | tf_op jit(solution)/shard_map/ppermute | solution.py:945
  864.3 8.8 all-to-all-start.4
  867.6 47.3 %reduce-scatter.14.cloned.1.call-start = ((), (), s32[]{:S(2)}) async-start(), calls=%async_computation.17 | async-start | bytes 614400 | tf_op jit(solution)/shard_map/reduce_scatter | solution.py:1188
  876.2 11.1 %collective-permute-start.21 = (bf16[2,4,32,896]{3,2,1,0:T(8,128)(2,1)S(1)}, bf16[2,4,32,896]{3,2,1,0:T(8,128)(2,1)S(1)}, u32[]{:S(2)}, u32[]{:S(2)}) collective-permute-start(bf16[2,4,32,896]{3,2,1,0:T(8,128)(2,1)S(1)} %fusion.35), channel_id=1, source_target_pairs={{0,16},{4,20},{8,24},{12,28},{16,0},{20,4},{24,8},{28,12},{1,17},{... | collective-permute-start | bytes 1376264 | tf_op jit(solution)/shard_map/ppermute | solution.py:945
  887.5 6.1 collective-permute-start.22
  893.8 16.2 %collective-permute-start.23 = (bf16[32,896]{1,0:T(8,128)(2,1)S(1)}, bf16[32,896]{1,0:T(8,128)(2,1)S(1)}, u32[]{:S(2)}, u32[]{:S(2)}) collective-permute-start(bf16[32,896]{1,0:T(8,128)(2,1)S(1)} %get-tuple-element.295), channel_id=1, source_target_pairs={{0,1},{1,2},{2,3},{3,0},{4,5},{5,6},{6,7},{7,4},{8,9},{9,10},{10,1... | collective-permute-start | bytes 172040 | tf_op jit(solution)/shard_map/ppermute | solution.py:951
  894.4 15.5 %collective-permute-start.25 = (bf16[32,896]{1,0:T(8,128)(2,1)S(1)}, bf16[32,896]{1,0:T(8,128)(2,1)S(1)}, u32[]{:S(2)}, u32[]{:S(2)}) collective-permute-start(bf16[32,896]{1,0:T(8,128)(2,1)S(1)} %get-tuple-element.296), channel_id=1, source_target_pairs={{0,3},{1,0},{2,1},{3,2},{4,7},{5,4},{6,5},{7,6},{8,11},{9,8},{10,9... | collective-permute-start | bytes 172040 | tf_op jit(solution)/shard_map/ppermute | solution.py:951
  897.6 12.3 %collective-permute-start.24 = (bf16[32,896]{1,0:T(8,128)(2,1)S(1)}, bf16[32,896]{1,0:T(8,128)(2,1)S(1)}, u32[]{:S(2)}, u32[]{:S(2)}) collective-permute-start(bf16[32,896]{1,0:T(8,128)(2,1)S(1)} %get-tuple-element.297), channel_id=1, source_target_pairs={{0,2},{1,3},{2,0},{3,1},{4,6},{5,7},{6,4},{7,5},{8,10},{9,11},{10,... | collective-permute-start | bytes 172040 | tf_op jit(solution)/shard_map/ppermute | solution.py:951
  (41 other events, 217.3 us)
Sparse Core Ops, SparseCore 0:
  16.0 31.6 all-gather.3
  49.6 56.0 all-gather.5
  107.6 89.9 all-gather.7
  450.2 103.5 reduce-scatter.7
  557.6 94.7 reduce-scatter.5
  757.5 54.8 reduce-scatter.11
  816.3 49.6 reduce-scatter.9
  889.3 19.6 reduce-scatter.13

commit v6 on v5

--- a/solution.py
+++ b/solution.py
@@ -78,8 +78,7 @@
         project_kernel,
         grid=(rows // tile,),
         in_specs=[
-            block(width), fixed(gain), pl.BlockSpec((width, FIRST), lambda i: (0, 0)), block(128),
-            block(128),
+            block(width), fixed(gain), fixed(w_first), block(128), block(128),
         ],
         out_specs=[block(size) for size in cols],
         out_shape=[jax.ShapeDtypeStruct((rows, size), BF16) for size in cols],
@@ -89,7 +88,7 @@
 
 
 def finish_kernel(
-    x_ref, gain_ref, dgate_ref, dcr_ref, dq_ref, dkv_ref, cos_ref, sin_ref, middle_ref, wg_ref,
+    x_ref, gain_ref, dgate_ref, dcr_ref, dq_ref, dkv_ref, cos_ref, sin_ref, middle_ref,
     w_ref, dx_ref, dkv_out_ref, dgain_ref, dgain_s,
 ):
     @pl.when(pl.program_id(0) == 0)
@@ -109,7 +108,7 @@
     dkv_out_ref[...] = dkv
     at = CR + QH * HD
     grad = (
-        contract(dgate_ref[...], wg_ref[...], 1, 1)
+        contract(dgate_ref[...], w_ref[:, FIRST:], 1, 1)
         + contract(dcr_ref[...], w_ref[:, :CR], 1, 1)
         + contract(dq_ref[...], w_ref[:, CR:at], 1, 1)
         + contract(dkv, w_ref[:, at : at + 2 * KVH * HD], 1, 1)
@@ -123,7 +122,7 @@
     dgain_ref[...] = dgain_s[...]
 
 
-def finish(x, gain, dgate, dcr, dq, dkv_all, cosine, sine, middle, w_gates, w_first):
+def finish(x, gain, dgate, dcr, dq, dkv_all, cosine, sine, middle, w_first):
     rows, width = x.shape
     span = dkv_all.shape[2]
     tile = min(256, span)
@@ -139,8 +138,7 @@
         grid=(rows // tile,),
         in_specs=[
             block(x), fixed(gain), block(dgate), block(dcr), block(dq), keys, block(cosine),
-            block(sine), block(middle), fixed(w_gates),
-            pl.BlockSpec((width, FIRST), lambda i: (0, 0)),
+            block(sine), block(middle), fixed(w_first),
         ],
         out_specs=[
             block(x),
@@ -155,7 +153,7 @@
         scratch_shapes=[pltpu.VMEM((8, width), F32)],
         compiler_params=pltpu.CompilerParams(vmem_limit_bytes=VMEM_BYTES),
         name="finish",
-    )(x, gain, dgate, dcr, dq, dkv_all, cosine, sine, middle, w_gates, w_first)
+    )(x, gain, dgate, dcr, dq, dkv_all, cosine, sine, middle, w_first)
 
 
 def visible(segk_ref, segq, query_row, at, key_rows):
@@ -1003,7 +1001,26 @@
     for matrix in (w_gate, w_up):
         rest += [matrix[:, at : at + width] for at in range(0, ff, width)]
     rest_sizes = [part.shape[0] for part in rest]
-    rest_part = exchange(after(copies(jnp.concatenate(rest, axis=0)), first_part))
+    place = lax.axis_index("ctx")
+    span_start = place * span
+    seg_own = lax.dynamic_slice_in_dim(segments, span_start, span, 1)
+    seg_rim = jnp.where(
+        place > 0,
+        lax.dynamic_slice_in_dim(segments, jnp.maximum(span_start - (KC - 1), 0), KC - 1, 1),
+        -1,
+    )
+    token = token_table(seg_own, seg_rim)
+    bounds = attention_bounds(segments, seg_own, span_start)
+    segk, segq = segments[:, :, None], seg_own[:, None, :]
+    cosine, sine = rope_tables(positions)
+    heads = jnp.pad(head_params, ((0, 5), (0, 128 - MH)))
+    skip = jnp.repeat(head_params[2], MP)[None]
+    spread, spread_first = spread_matrix(), spread_first_matrix()
+
+    tokens = layer_input.reshape(rows, width)
+    small = (token, bounds, segk, segq, cosine, sine, heads, skip, spread, spread_first)
+    cosine, sine = cosine.reshape(rows, 128), sine.reshape(rows, 128)
+    rest_part = exchange(after(copies(jnp.concatenate(rest, axis=0)), first_part, small))
     rest_all = gather(rest_part.reshape(-1, width)).reshape(-1, sum(rest_sizes), width)
     cuts, at = [], 0
     for size in rest_sizes:
@@ -1022,33 +1039,13 @@
     taps_all = jnp.swapaxes(parts[4].reshape(-1, KC, small_sizes[3]), 0, 1).reshape(KC, CC)
     taps_all = jnp.pad(taps_all, ((0, 8 - KC), (0, 0)))
 
-    place = lax.axis_index("ctx")
-    span_start = place * span
-    seg_own = lax.dynamic_slice_in_dim(segments, span_start, span, 1)
-    seg_rim = jnp.where(
-        place > 0,
-        lax.dynamic_slice_in_dim(segments, jnp.maximum(span_start - (KC - 1), 0), KC - 1, 1),
-        -1,
-    )
-    token = token_table(seg_own, seg_rim)
-    bounds = attention_bounds(segments, seg_own, span_start)
-    segk, segq = segments[:, :, None], seg_own[:, None, :]
-    cosine, sine = rope_tables(positions)
-    heads = jnp.pad(head_params, ((0, 5), (0, 128 - MH)))
-    skip = jnp.repeat(head_params[2], MP)[None]
-    spread, spread_first = spread_matrix(), spread_first_matrix()
-
-    tokens = layer_input.reshape(rows, width)
-    small = (token, bounds, segk, segq, cosine, sine, heads, skip, spread, spread_first)
-    first_all, small = lax.optimization_barrier((first_all, small))
-    token, bounds, segk, segq, cosine, sine, heads, skip, spread, spread_first = small
-    cosine, sine = cosine.reshape(rows, 128), sine.reshape(rows, 128)
+
     hidden, cr, q, kv = project(tokens, gain1_all, first_all, cosine, sine)
     q = q.reshape(seqs, span, q_width)
     kv = kv.reshape(seqs, span, kv_width)
-    kv_all = exchange(copies(kv))
     cr = cr.reshape(seqs, span, CR)
     rim = from_behind(cr[:, span - (KC - 1) :, :CC], "ctx", 1)
+    kv_all = exchange(after(copies(kv), rim))
     rim = jnp.pad(rim, ((0, 0), (8 - (KC - 1), 0), (0, 0)))
     scanned, chains, wide_gains = None, [], []
     for seq in range(seqs):
@@ -1063,7 +1060,8 @@
     for chain in chains:
         chain.take()
         chain.send()
-    atts, lses, mixed, mark = [], [], None, act
+    atts, lses, mixed = [], [], None
+    mark = (act, w_down_all, w_out_all, w_o_all, w_gu_all)
     for seq in range(seqs):
         att, lse = attend(seq, bounds, after(q, mark), kv_all, segk, segq)
         atts.append(att)
@@ -1130,11 +1128,13 @@
         chains.append(Chain(gated[4], wide_gains[seq], True))
         chains[seq].send()
     grad_y, grad_gate, gstates, ggains = gated[:4]
-    grad_wgates = weight_grad(hidden, grad_gate.reshape(rows, DI)).reshape(-1, own_rows, DI)
+    chains[0].take()
+    chains[1 % seqs].take()
+    grad_wgates = weight_grad(after(hidden, chains[0].state), grad_gate.reshape(rows, DI)).reshape(-1, own_rows, DI)
     blocks = grad_wo.shape[0]
     grad_rest = jnp.concatenate(
         [
-            grad_down.reshape(blocks, -1, width), grad_wout.reshape(blocks, -1, width),
+            after(grad_down, chains[0].state, chains[1 % seqs].state).reshape(blocks, -1, width), grad_wout.reshape(blocks, -1, width),
             fold(grad_wo, 0), grad_wgates[..., :width], fold(grad_wgates, width),
         ],
         axis=1,
@@ -1143,22 +1143,22 @@
     cos3, sin3 = cosine.reshape(seqs, span, 128), sine.reshape(seqs, span, 128)
     dqs, dkvs = [], []
     for seq in range(seqs):
-        if seq:
+        if seq < 2:
             for chain in chains:
                 chain.take()
-                chain.send(dqs[-1])
-        mark = dqs[-1:] + [chain.state for chain in chains] if seq else []
+                chain.send(*dqs[-1:])
+        mark = dqs[-1:] + [chain.state for chain in chains] + ([] if seq else [grad_rest])
         dq, dkv = attend_back(
             seq, bounds, after(q, grad_y, *mark), kv_all, segk,
             segq, atts[seq], grad_att, lses[seq], cos3, sin3,
         )
         dqs.append(dq)
         dkvs.append(dkv)
-    dkv_all = exchange(jnp.concatenate(dkvs, axis=1))
     dq = jnp.concatenate(dqs, axis=0)
     last, rims, grad_conv, grad_heads = None, [], 0.0, 0.0
     waits = [(grad_rest, part_gu)] + [()] * (seqs - 1)
     finals = [chain.finish() for chain in chains]
+    dkv_all = exchange(after(jnp.concatenate(dkvs, axis=1), *finals))
     waits[1 % seqs] += tuple(finals)
     for seq in range(seqs):
         gstate = finals[seq]
@@ -1188,7 +1188,7 @@
     out_cr = lax.psum_scatter(part_cr, "ctx", scatter_dimension=0, tiled=True).astype(F32)
     grad_tokens, grad_kv, grad_gain_first = finish(
         tokens, gain1_all, grad_gate.reshape(rows, DI), after(grad_cr, grad_wcr, rest_out),
-        dq.reshape(rows, q_width), dkv_all, cosine, sine, grad_middle, w_gates, first_all,
+        dq.reshape(rows, q_width), dkv_all, cosine, sine, grad_middle, first_all,
     )
     grad_first = jnp.concatenate([dq.reshape(rows, q_width), grad_kv], axis=1)
     grad_wfirst = weight_grad(hidden, grad_first)

time: 934 us -> 873 us (0.935)
  waiting for transfers between devices: 149 us -> 111 us
  starting transfers between devices: 121 us -> 95.2 us
    ppermute x2, waiting for transfers between devices: 49.6 us -> 6.98 us  [from_behind(): return lax.ppermute(block, axis, route)]
    all_to_all x2, starting transfers between devices: 70.3 us -> 50.8 us  [body(): exchange = lambda blocks: lax.all_to_all(blocks, 'ctx', 0, 0, tiled=True)]
    unnamed x154 -> x142, local copies, waits for them, and re-layouts: 27.3 us -> 26.7 us
  transfers between devices with their start and end apart: 37 -> 37, of which waited for: 10 -> 12; matrix products, arithmetic and copies ran while one was open for 19% -> 23% of each run, Pallas kernels for 28% -> 29%
where the time goes in v6:
time: 873 us; the launch traced here: 859 us
  Pallas kernels  261 us (30%)
  matrix products  169 us (19%)
  waiting for transfers between devices  111 us (13%)
  starting transfers between devices  95.2 us (11%)
  local copies, waits for them, and re-layouts  86 us (10%)
  other arithmetic  61.1 us (7%)
  blocking collectives  59.3 us (7%)
  between operations  15.8 us (2%)
    pallas_call x12, Pallas kernels, mixer_call(): pl.pallas_call(run, grid=(chunks,), in_specs=in_specs, out_specs=out_spec...  158 us
    dot_general x7, matrix products, weight_grad(): jnp.einsum('ri,ro->io', left, right, preferred_element_type=F32)  62.5 us
    dot_general x5, matrix products, body(): low_dot = lambda a, b: jnp.dot(a, b, preferred_element_type=F32)  55.4 us
    all_to_all x1, blocking collectives, body(): exchange = lambda blocks: lax.all_to_all(blocks, 'ctx', 0, 0, tiled=True)  51.5 us
    all_to_all x2, starting transfers between devices, body(): exchange = lambda blocks: lax.all_to_all(blocks, 'ctx', 0, 0, tiled=True)  50.8 us
    ppermute x18, waiting for transfers between devices, send(): self.flying = (lax.ppermute(sent, 'ctx', [(source, target)]), target)  49.8 us
    dot_general x3, matrix products, back_dot(): return jnp.einsum('ro,io->ri', grad, weight, preferred_element_type=F32)  46.9 us
    pallas_call x3, Pallas kernels, attend_back(): pl.pallas_call(functools.partial(attend_back_kernel, seq * (span // rows)...  40.6 us
  transfers between devices with their start and end apart: 37, of which 12 were waited for; matrix products, arithmetic and copies ran while one was open for 23% of the time, Pallas kernels for 29%

profile of v6, /device:TPU:0, one launch (start us, length us, event | category | flops | bytes accessed | tf_op | source)
XLA Modules:
  0.0 859.2 jit_solution(17411032989904246891)
XLA Ops:
  15.9 31.8 %all-gather.4.cloned.1.call-done = bf16[128,4352]{1,0:T(8,128)(2,1)} async-done(((bf16[32,4352]{1,0:T(8,128)(2,1)}), bf16[128,4352]{1,0:T(8,128)(2,1)}) %all-gather.4.cloned.1.call-update) | async-done | bytes 1114128 | tf_op jit(solution)/shard_map/all_gather | solution.py:988
  69.9 51.5 %all_to_all.25 = bf16[4,256,1024]{2,1,0:T(8,128)(2,1)} all-to-all(bf16[4,256,1024]{2,1,0:T(8,128)(2,1)S(1)} %broadcast_in_dim.77), channel_id=1, replica_groups=mesh['dp'=8,'ctx'=4] {'ctx'}, dimensions={0} | all-to-all | bytes 4194304 | tf_op jit(solution)/shard_map/all_to_all | solution.py:983
  121.5 2.8 fusion.38
  128.5 17.4 %project.1 = (bf16[1536,1024]{1,0:T(8,128)(2,1)}, bf16[1536,1920]{1,0:T(8,128)(2,1)}, bf16[1536,512]{1,0:T(8,128)(2,1)}, bf16[1536,256]{1,0:T(8,128)(2,1)}) custom-call(bf16[1536,1024]{1,0:T(8,128)(2,1)} %bitcast.202, f32[1,1024]{1,0:T(1,128)} %reshape.286.gain_ref, bf16[1024,4352]{1,0:T(8,128)(2,1)} %all-gather.6.cloned.1.call-done.w_ref, ...), custom_call_target="tpu_custom_call" | custom-call | tf_op jit(solution)/shard_map/project/pallas_call | solution.py:77
  153.0 3.1 broadcast_in_dim.84
  156.0 3.7 all-to-all-start.1
  160.9 10.6 %mixer_scan.3 = (bf16[3,512,1792]{2,1,0:T(8,128)(2,1)}, bf16[3,4,128,1536]{3,2,1,0:T(8,128)(2,1)}, f32[3,4,8,128]{3,2,1,0:T(8,128)}, bf16[1,128,1536]{2,1,0:T(8,128)(2,1)}, f32[1,8,1536]{2,1,0:T(8,128)}) custom-call(bf16[3,512,1920]{2,1,0:T(8,128)(2,1)} %bitcast.153, bf16[3,8,1792]{2,1,0:T(8,128)(2,1)} %pad.27.refs_1_.refs_4_, ...), custom_call_target="tpu_custom_call" | custom-call | tf_op jit(solution)/shard_map/mixer_scan/pallas_call | solution.py:762
  171.5 3.9 collective-permute-start.7
  175.4 8.6 convolution_convert_fusion.2
  186.2 9.4 %mixer_scan.4 = (bf16[3,512,1792]{2,1,0:T(8,128)(2,1)}, bf16[3,4,128,1536]{3,2,1,0:T(8,128)(2,1)}, f32[3,4,8,128]{3,2,1,0:T(8,128)}, bf16[1,128,1536]{2,1,0:T(8,128)(2,1)}, f32[1,8,1536]{2,1,0:T(8,128)}) custom-call(bf16[3,512,1920]{2,1,0:T(8,128)(2,1)} %bitcast.154, ...), custom_call_target="tpu_custom_call", output_to_operand_aliasing={{0}: (7, {}), {1}: (8, {}), {2}: (9, {})} | custom-call | tf_op jit(solution)/shard_map/mixer_scan/pallas_call | solution.py:762
  197.0 9.2 %mixer_scan.5 = (bf16[3,512,1792]{2,1,0:T(8,128)(2,1)}, bf16[3,4,128,1536]{3,2,1,0:T(8,128)(2,1)}, f32[3,4,8,128]{3,2,1,0:T(8,128)}, bf16[1,128,1536]{2,1,0:T(8,128)(2,1)}, f32[1,8,1536]{2,1,0:T(8,128)}) custom-call(bf16[3,512,1920]{2,1,0:T(8,128)(2,1)} %bitcast.155, ...), custom_call_target="tpu_custom_call", output_to_operand_aliasing={{0}: (7, {}), {1}: (8, {}), {2}: (9, {})} | custom-call | tf_op jit(solution)/shard_map/mixer_scan/pallas_call | solution.py:762
  210.1 10.1 %collective-permute-done.7 = bf16[1,128,1536]{2,1,0:T(8,128)(2,1)S(1)} collective-permute-done((bf16[1,128,1536]{2,1,0:T(8,128)(2,1)}, bf16[1,128,1536]{2,1,0:T(8,128)(2,1)S(1)}, u32[]{:S(2)}, u32[]{:S(2)}) %collective-permute-start.7) | collective-permute-done | bytes 393248 | tf_op jit(solution)/shard_map/ppermute | solution.py:908
  221.1 7.6 collective-permute-done.4
  229.5 5.1 collective-permute-done.1
  240.3 4.2 slice.378
  244.5 5.6 slice.377
  252.5 3.3 fusion.67
  257.4 7.4 attend.3
  264.9 12.3 %collective-permute-start.9 = (bf16[1,128,1536]{2,1,0:T(8,128)(2,1)}, bf16[1,128,1536]{2,1,0:T(8,128)(2,1)S(1)}, u32[]{:S(2)}, u32[]{:S(2)}) collective-permute-start(bf16[1,128,1536]{2,1,0:T(8,128)(2,1)} %fusion.27), channel_id=1, source_target_pairs={{2,3},{6,7},{10,11},{14,15},{18,19},{22,23},{26,27},{30,31}} | collective-permute-start | bytes 1179656 | tf_op jit(solution)/shard_map/ppermute | solution.py:908
  277.2 7.4 attend.4
  285.4 7.5 attend.5
  294.9 4.4 fusion.76
  300.1 9.0 %mixer_out.3 = (f32[3,512,1536]{2,1,0:T(8,128)}, bf16[3,512,1536]{2,1,0:T(8,128)(2,1)}) custom-call(bf16[3,512,1536]{2,1,0:T(8,128)(2,1)} %bitcast.168, bf16[3,512,1920]{2,1,0:T(8,128)(2,1)} %bitcast.156, bf16[3,512,1792]{2,1,0:T(8,128)(2,1)} %get-tuple-element.129.refs_2_.refs_4_.refs_5_, f32[3,8,512]{2,1,0:T(8,128)} %stack.51.refs_2_.refs_3_.refs_5_.refs_6_, ...), custom_call_target="tpu_custom_call" | custom-call | tf_op jit(solution)/shard_map/mixer_out/pallas_call | solution.py:762
  310.0 9.0 %mixer_out.4 = (f32[3,512,1536]{2,1,0:T(8,128)}, bf16[3,512,1536]{2,1,0:T(8,128)(2,1)}) custom-call(bf16[3,512,1536]{2,1,0:T(8,128)(2,1)} %bitcast.169, bf16[3,512,1920]{2,1,0:T(8,128)(2,1)} %bitcast.157, bf16[3,512,1792]{2,1,0:T(8,128)(2,1)} %get-tuple-element.129.refs_2_.refs_4_.refs_5_, ...), custom_call_target="tpu_custom_call", output_to_operand_aliasing={{0}: (11, {}), {1}: (12, {})} | custom-call | tf_op jit(solution)/shard_map/mixer_out/pallas_call | solution.py:762
  319.8 9.1 %mixer_out.5 = (f32[3,512,1536]{2,1,0:T(8,128)}, bf16[3,512,1536]{2,1,0:T(8,128)(2,1)}) custom-call(bf16[3,512,1536]{2,1,0:T(8,128)(2,1)} %bitcast.170, bf16[3,512,1920]{2,1,0:T(8,128)(2,1)} %bitcast.158, bf16[3,512,1792]{2,1,0:T(8,128)(2,1)} %get-tuple-element.129.refs_2_.refs_4_.refs_5_, ...), custom_call_target="tpu_custom_call", output_to_operand_aliasing={{0}: (11, {}), {1}: (12, {})} | custom-call | tf_op jit(solution)/shard_map/mixer_out/pallas_call | solution.py:762
  328.9 10.8 %multiply_reduce_fusion.2 = (f32[1536]{0:T(1024)S(1)}, f32[1536,1024]{1,0:T(8,128)}) fusion(f32[1536,1024]{1,0:T(8,128)} %fusion.76, bf16[1536,1536]{1,0:T(8,128)(2,1)} %bitcast.189, bf16[1536,1024]{1,0:T(8,128)(2,1)S(1)} %bitcast.213, bf16[1536,1024]{1,0:T(8,128)(2,1)S(1)} %bitcast.204), kind=kOutput, calls=%fused_computation.29 | convolution fusion | flops 4839700992 | bytes 23599104 | tf_op jit(solution)/shard_map/dot_general | solution.py:972
  339.7 20.9 %convolution_convert_fusion = bf16[1536,4096]{1,0:T(8,128)(2,1)} fusion(f32[1536,1024]{1,0:T(8,128)} %get-tuple-element.293, f32[1024]{0:T(1024)S(1)} %mul.230, f32[1536]{0:T(1024)S(1)} %fusion.54, bf16[1024,1024]{1,0:T(8,128)(2,1)} %bitcast.220, bf16[1024,1024]{1,0:T(8,128)(2,1)} %bitcast.222, bf16[1024,1024]{1,0:T(8,128)(2,1)} %bitcast.224, ...), kind=kOutput, calls=%fused_computation.6 | convolution fusion | flops 12929466368 | bytes 27273216 | tf_op jit(solution)/shard_map/dot_general | solution.py:972
  360.7 19.4 %fusion.6 = (bf16[1536,2048]{1,0:T(8,128)(2,1)}, bf16[1536,2048]{1,0:T(8,128)(2,1)}, bf16[1536,2048]{1,0:T(8,128)(2,1)}) fusion(bf16[1536,4096]{1,0:T(8,128)(2,1)} %convolution_convert_fusion, bf16[2048,1024]{1,0:T(8,128)(2,1)} %bitcast.208, bf16[1536,1024]{1,0:T(8,128)(2,1)S(1)} %bitcast.211), kind=kOutput, calls=%fused_computation.13 | convolution fusion | flops 6499074048 | bytes 38797312 | tf_op jit(solution)/shard_map/ro,io->ri/dot_general | solution.py:1102
  380.1 20.6 %fusion.9 = f32[1536,1024]{1,0:T(8,128)} fusion(bf16[1536,2048]{1,0:T(8,128)(2,1)} %get-tuple-element.248, bf16[1536,2048]{1,0:T(8,128)(2,1)} %get-tuple-element.247, bf16[1024,1024]{1,0:T(8,128)(2,1)S(1)} %bitcast.221, bf16[1024,1024]{1,0:T(8,128)(2,1)S(1)} %bitcast.223, bf16[1024,1024]{1,0:T(8,128)(2,1)} %bitcast.225, bf16[1024,1024]{1,0:T(8,128)(2,1)S(1)} %bitcast.219), kind=kOutput, calls=%fused_computation.20 | convolution fusion | flops 12943622144 | bytes 27262976 | tf_op jit(solution)/shard_map/ro,io->ri/dot_general | solution.py:1102
  400.7 21.7 %fusion.10 = bf16[1024,4096]{1,0:T(8,128)(2,1)} fusion(bf16[1536,2048]{1,0:T(8,128)(2,1)} %get-tuple-element.248, bf16[1536,2048]{1,0:T(8,128)(2,1)} %get-tuple-element.247, f32[1536,1024]{1,0:T(8,128)} %get-tuple-element.293, f32[1024]{0:T(1024)S(1)} %mul.230, f32[1536]{0:T(1024)S(1)} %fusion.54), kind=kOutput, calls=%fused_computation.23 | convolution fusion | flops 12918980608 | bytes 27273216 | tf_op jit(solution)/shard_map/ri,ro->io/dot_general | solution.py:1099
  422.4 11.2 %convolution_convert_fusion.3 = bf16[2048,1024]{1,0:T(8,128)(2,1)} fusion(bf16[1536,2048]{1,0:T(8,128)(2,1)} %get-tuple-element.208, bf16[1536,1024]{1,0:T(8,128)(2,1)S(1)} %bitcast.212), kind=kOutput, calls=%fused_computation.31 | convolution fusion | flops 6444548096 | bytes 13631488 | tf_op jit(solution)/shard_map/ri,ro->io/dot_general | solution.py:1099
  433.6 5.8 multiply_reduce_fusion
  439.5 7.3 fusion.64
  446.8 3.0 convolution_convert_fusion.7
  451.7 6.9 convolution_convert_fusion.1
  458.6 5.4 convolution_convert_fusion.6
  464.0 10.1 %mixer_gate_back.3 = (bf16[3,512,1536]{2,1,0:T(8,128)(2,1)}, bf16[3,512,1536]{2,1,0:T(8,128)(2,1)}, bf16[3,4,128,1536]{3,2,1,0:T(8,128)(2,1)}, f32[3,4,8,128]{3,...) custom-call(bf16[3,512,1536]{2,1,0:T(8,128)(2,1)} %bitcast.186, ...), custom_call_target="tpu_custom_call" | custom-call | tf_op jit(solution)/shard_map/mixer_gate_back/pallas_call | solution.py:762
  474.9 11.1 %mixer_gate_back.4 = (bf16[3,512,1536]{2,1,0:T(8,128)(2,1)}, bf16[3,512,1536]{2,1,0:T(8,128)(2,1)}, bf16[3,4,128,1536]{3,2,1,0:T(8,128)(2,1)}, f32[3,4,8,128]{3,...) custom-call(bf16[3,512,1536]{2,1,0:T(8,128)(2,1)} %bitcast.187, ...), custom_call_target="tpu_custom_call", output_to_operand_aliasing={{0}: (9, {}), {1}: (10, {}), {2}: (11, {}), {3}: (12, {})} | custom-call | tf_op jit(solution)/shard_map/mixer_gate_back/pallas_call | solution.py:762
  486.7 10.0 %mixer_gate_back.5 = (bf16[3,512,1536]{2,1,0:T(8,128)(2,1)}, bf16[3,512,1536]{2,1,0:T(8,128)(2,1)}, bf16[3,4,128,1536]{3,2,1,0:T(8,128)(2,1)}, f32[3,4,8,128]{3,...) custom-call(bf16[3,512,1536]{2,1,0:T(8,128)(2,1)} %bitcast.188, ...), custom_call_target="tpu_custom_call", output_to_operand_aliasing={{0}: (9, {}), {1}: (10, {}), {2}: (11, {}), {3}: (12, {})} | custom-call | tf_op jit(solution)/shard_map/mixer_gate_back/pallas_call | solution.py:762
  506.2 5.6 convolution_convert_fusion.5
  518.6 13.9 %attend_back.3 = (bf16[1,512,512]{2,1,0:T(8,128)(2,1)}, bf16[4,1,512,256]{3,2,1,0:T(8,128)(2,1)}) custom-call(s32[6]{0:T(128)} %and_select_fusion.1.low_ref, s32[6]{0:T(128)} %reshape.293.high_ref, s32[1]{0:T(128)} %bitcast.10.base_ref, bf16[3,512,512]{2,1,0:T(8,128)(2,1)} %bitcast.177, bf16[4,3,512,256]{3,2,1,0:T(8,128)(2,1)} %copy-done, ...), custom_call_target="tpu_custom_call" | custom-call | tf_op jit(solution)/shard_map/attend_back/pallas_call | solution.py:334
  537.3 13.3 %attend_back.4 = (bf16[1,512,512]{2,1,0:T(8,128)(2,1)}, bf16[4,1,512,256]{3,2,1,0:T(8,128)(2,1)}) custom-call(s32[6]{0:T(128)} %and_select_fusion.1.low_ref, s32[6]{0:T(128)} %reshape.293.high_ref, s32[1]{0:T(128)} %bitcast.10.base_ref, bf16[3,512,512]{2,1,0:T(8,128)(2,1)} %bitcast.178, bf16[4,3,512,256]{3,2,1,0:T(8,128)(2,1)} %copy-done, ...), custom_call_target="tpu_custom_call" | custom-call | tf_op jit(solution)/shard_map/attend_back/pallas_call | solution.py:334
  550.6 13.4 %attend_back.5 = (bf16[1,512,512]{2,1,0:T(8,128)(2,1)}, bf16[4,1,512,256]{3,2,1,0:T(8,128)(2,1)}) custom-call(s32[6]{0:T(128)} %and_select_fusion.1.low_ref, s32[6]{0:T(128)} %reshape.293.high_ref, s32[1]{0:T(128)} %bitcast.10.base_ref, bf16[3,512,512]{2,1,0:T(8,128)(2,1)} %bitcast.179, bf16[4,3,512,256]{3,2,1,0:T(8,128)(2,1)} %copy-done, ...), custom_call_target="tpu_custom_call" | custom-call | tf_op jit(solution)/shard_map/attend_back/pallas_call | solution.py:334
  564.0 3.5 pad_maximum_fusion.6
  567.5 3.5 collective-permute-done.16
  571.8 19.3 %collective-permute-done.17 = bf16[1,128,1536]{2,1,0:T(8,128)(2,1)S(1)} collective-permute-done((bf16[1,128,1536]{2,1,0:T(8,128)(2,1)S(1)}, bf16[1,128,1536]{2,1,0:T(8,128)(2,1)S(1)}, u32[]{:S(2)}, u32[]{:S(2)}) %collective-permute-start.17) | collective-permute-done | bytes 393248 | tf_op jit(solution)/shard_map/ppermute | solution.py:908
  591.9 4.2 collective-permute-done.18
  596.9 47.1 %all-to-all-start.2 = ((bf16[4,3,512,256]{3,2,1,0:T(8,128)(2,1)}), bf16[4,3,512,256]{3,2,1,0:T(8,128)(2,1)S(1)}, u32[]{:S(2)}, u32[]{:S(2)}) async-start(bf16[4,3,512,256]{3,2,1,0:T(8,128)(2,1)} %pad_maximum_fusion.6), calls=%async_computation.4 | async-start | bytes 6291456 | tf_op jit(solution)/shard_map/all_to_all | solution.py:983
  644.3 23.6 %mixer_back.3 = (bf16[3,512,1920]{2,1,0:T(8,128)(2,1)}, f32[1,8,1792]{2,1,0:T(8,128)}, f32[8,1792]{1,0:T(8,128)}, f32[8,128]{1,0:T(8,128)}) custom-call(bf16[3,512,1536]{2,1,0:T(8,128)(2,1)} %get-tuple-element.199.refs_0_, f32[3,512,1536]{2,1,0:T(8,128)} %get-tuple-element.161.refs_1_, bf16[3,512,1920]{2,1,0:T(8,128)(2,1)} %bitcast.162, ...), custom_call_target="tpu_custom_call" | custom-call | tf_op jit(solution)/shard_map/mixer_back/pallas_call | solution.py:762
  667.9 23.6 %mixer_back.4 = (bf16[3,512,1920]{2,1,0:T(8,128)(2,1)}, f32[1,8,1792]{2,1,0:T(8,128)}, f32[8,1792]{1,0:T(8,128)}, f32[8,128]{1,0:T(8,128)}) custom-call(bf16[3,512,1536]{2,1,0:T(8,128)(2,1)} %get-tuple-element.199.refs_0_, f32[3,512,1536]{2,1,0:T(8,128)} %get-tuple-element.161.refs_1_, ...), custom_call_target="tpu_custom_call", output_to_operand_aliasing={{0}: (19, {})} | custom-call | tf_op jit(solution)/shard_map/mixer_back/pallas_call | solution.py:762
  700.8 23.6 %mixer_back.5 = (bf16[3,512,1920]{2,1,0:T(8,128)(2,1)}, f32[1,8,1792]{2,1,0:T(8,128)}, f32[8,1792]{1,0:T(8,128)}, f32[8,128]{1,0:T(8,128)}) custom-call(bf16[3,512,1536]{2,1,0:T(8,128)(2,1)} %get-tuple-element.199.refs_0_, f32[3,512,1536]{2,1,0:T(8,128)} %get-tuple-element.161.refs_1_, ...), custom_call_target="tpu_custom_call", output_to_operand_aliasing={{0}: (19, {})} | custom-call | tf_op jit(solution)/shard_map/mixer_back/pallas_call | solution.py:762
  727.0 7.0 collective-permute-done.19
  736.9 11.5 %convolution_convert_fusion.4 = bf16[1024,1920]{1,0:T(8,128)(2,1)} fusion(bf16[1536,1024]{1,0:T(8,128)(2,1)} %get-tuple-element.178, bf16[1536,1920]{1,0:T(8,128)(2,1)} %bitcast.180), kind=kOutput, calls=%fused_computation.32 | convolution fusion | flops 6041763840 | bytes 12976128 | tf_op jit(solution)/shard_map/ri,ro->io/dot_general | solution.py:1099
  752.5 2.8 reduce-scatter.12.cloned.1.call-done
  755.4 22.8 %finish.1 = (bf16[1536,1024]{1,0:T(8,128)(2,1)}, bf16[1536,256]{1,0:T(8,128)(2,1)}, f32[8,1024]{1,0:T(8,128)}) custom-call(bf16[1536,1024]{1,0:T(8,128)(2,1)} %bitcast.203, f32[1,1024]{1,0:T(1,128)} %reshape.286.gain_ref, bf16[1536,1536]{1,0:T(8,128)(2,1)} %bitcast.182, bf16[1536,1920]{1,0:T(8,128)(2,1)} %bitcast.181, bf16[1536,512]{1,0:T(8,128)(2,1)} %bitcast.206, ...), custom_call_target="tpu_custom_call" | custom-call | tf_op jit(solution)/shard_map/finish/pallas_call | solution.py:136
  779.5 5.4 fusion.17
  786.3 3.1 copy.210
  791.5 7.8 all_to_all.26
  800.0 3.2 all-to-all-start.4
  803.3 5.5 all-to-all-done.4
  813.3 9.7 %collective-permute-done.21 = bf16[2,4,32,896]{3,2,1,0:T(8,128)(2,1)S(1)} collective-permute-done((bf16[2,4,32,896]{3,2,1,0:T(8,128)(2,1)S(1)}, bf16[2,4,32,896]{3,2,1,0:T(8,128)(2,1)S(1)}, u32[]{:S(2)}, u32[]{:S(2)}) %collective-permute-start.21) | collective-permute-done | bytes 458784 | tf_op jit(solution)/shard_map/ppermute | solution.py:943
  824.9 4.4 collective-permute-done.22
  830.2 3.3 collective-permute-start.25
  833.5 12.1 %add_convert_fusion = bf16[1536,1024]{1,0:T(8,128)(2,1)} fusion(f32[1536,1024]{1,0:T(8,128)} %get-tuple-element.293, bf16[1536,2048]{1,0:T(8,128)(2,1)} %get-tuple-element.208, bf16[2048,1024]{1,0:T(8,128)(2,1)} %bitcast.209), kind=kOutput, calls=%fused_computation.26 | convolution fusion | flops 6445596672 | bytes 19922944 | tf_op jit(solution)/shard_map/dot_general | solution.py:972
  (379 shorter events, 132.0 us)
Async XLA Ops:
  7.2 40.5 %all-gather.4.cloned.1.call-start = ((), (), s32[]{:S(2)}) async-start(), calls=%async_computation.10 | async-start | bytes 1392640 | tf_op jit(solution)/shard_map/all_gather | solution.py:988
  15.9 110.0 %all-gather.6.cloned.1.call-start = ((), (), s32[]{:S(2)}) async-start(), calls=%async_computation.11 | async-start | bytes 10027008 | tf_op jit(solution)/shard_map/all_gather | solution.py:985
  47.8 192.5 %all-gather.8.cloned.1.call-start = ((), (), s32[]{:S(2)}) async-start(), calls=%async_computation.12 | async-start | bytes 18874368 | tf_op jit(solution)/shard_map/all_gather | solution.py:985
  127.0 24.3 %copy-start.37 = (f32[32,4096]{1,0:T(8,128)}, f32[32,4096]{1,0:T(8,128)S(1)}, u32[]{:S(2)}) copy-start(f32[32,4096]{1,0:T(8,128)S(1)} %reshape.330) | copy-start | bytes 1572868
  128.5 20.6 %copy-start.47 = (s32[3,2048]{1,0:T(4,128)S(1)}, s32[3,2048]{1,0:T(4,128)}, u32[]{:S(2)}) copy-start(s32[3,2048]{1,0:T(4,128)} %param.20) | copy-start | bytes 73732
  146.8 6.2 collective-permute-start
  156.0 99.7 %all-to-all-start.1 = ((bf16[4,3,512,256]{3,2,1,0:T(8,128)(2,1)}), bf16[4,3,512,256]{3,2,1,0:T(8,128)(2,1)S(1)}, u32[]{:S(2)}, u32[]{:S(2)}) async-start(bf16[4,3,512,256]{3,2,1,0:T(8,128)(2,1)} %broadcast_in_dim.84), calls=%async_computation.1 | async-start | bytes 6291456 | tf_op jit(solution)/shard_map/all_to_all | solution.py:983
  159.8 484.5 %reduce-scatter.8.cloned.1.call-start = ((), (), s32[]{:S(2)}) async-start(), calls=%async_computation.14 | async-start | bytes 9437184 | tf_op jit(solution)/shard_map/reduce_scatter | solution.py:1096
  160.2 15.2 %copy-start.56 = (bf16[1536,1024]{1,0:T(8,128)(2,1)S(1)}, bf16[1536,1024]{1,0:T(8,128)(2,1)}, u32[]{:S(2)}) copy-start(bf16[1536,1024]{1,0:T(8,128)(2,1)} %get-tuple-element.178) | copy-start | bytes 9437188
  171.5 48.7 %collective-permute-start.7 = (bf16[1,128,1536]{2,1,0:T(8,128)(2,1)}, bf16[1,128,1536]{2,1,0:T(8,128)(2,1)S(1)}, u32[]{:S(2)}, u32[]{:S(2)}) collective-permute-start(bf16[1,128,1536]{2,1,0:T(8,128)(2,1)} %get-tuple-element.149), channel_id=1, source_target_pairs={{0,1},{4,5},{8,9},{12,13},{16,17},{20,21},{24,25},{28,29}} | collective-permute-start | bytes 1179656 | tf_op jit(solution)/shard_map/ppermute | solution.py:908
  195.6 33.0 %collective-permute-start.4 = (bf16[1,128,1536]{2,1,0:T(8,128)(2,1)}, bf16[1,128,1536]{2,1,0:T(8,128)(2,1)S(1)}, u32[]{:S(2)}, u32[]{:S(2)}) collective-permute-start(bf16[1,128,1536]{2,1,0:T(8,128)(2,1)} %get-tuple-element.146), channel_id=1, source_target_pairs={{0,1},{4,5},{8,9},{12,13},{16,17},{20,21},{24,25},{28,29}} | collective-permute-start | bytes 1179656 | tf_op jit(solution)/shard_map/ppermute | solution.py:908
  196.9 23.3 %copy-start.30 = (bf16[1,128,1536]{2,1,0:T(8,128)(2,1)S(1)}, bf16[1,128,1536]{2,1,0:T(8,128)(2,1)}, u32[]{:S(2)}) copy-start(bf16[1,128,1536]{2,1,0:T(8,128)(2,1)} %get-tuple-element.149) | copy-start | bytes 1179652
  197.0 31.7 %copy-start.31 = (bf16[1,128,1536]{2,1,0:T(8,128)(2,1)S(1)}, bf16[1,128,1536]{2,1,0:T(8,128)(2,1)}, u32[]{:S(2)}) copy-start(bf16[1,128,1536]{2,1,0:T(8,128)(2,1)} %get-tuple-element.146) | copy-start | bytes 1179652
  206.2 33.2 %copy-start.32 = (bf16[1,128,1536]{2,1,0:T(8,128)(2,1)S(1)}, bf16[1,128,1536]{2,1,0:T(8,128)(2,1)}, u32[]{:S(2)}) copy-start(bf16[1,128,1536]{2,1,0:T(8,128)(2,1)} %get-tuple-element.133) | copy-start | bytes 1179652
  206.2 28.4 %collective-permute-start.1 = (bf16[1,128,1536]{2,1,0:T(8,128)(2,1)}, bf16[1,128,1536]{2,1,0:T(8,128)(2,1)S(1)}, u32[]{:S(2)}, u32[]{:S(2)}) collective-permute-start(bf16[1,128,1536]{2,1,0:T(8,128)(2,1)} %get-tuple-element.133), channel_id=1, source_target_pairs={{0,1},{4,5},{8,9},{12,13},{16,17},{20,21},{24,25},{28,29}} | collective-permute-start | bytes 1179656 | tf_op jit(solution)/shard_map/ppermute | solution.py:908
  208.5 30.1 %copy-start.45 = (f32[1536]{0:T(1024)}, f32[1536]{0:T(1024)S(1)}, u32[]{:S(2)}) copy-start(f32[1536]{0:T(1024)S(1)} %slice_reduce_fusion.4) | copy-start | bytes 18436
  209.3 29.3 %copy-start.41 = (f32[1536]{0:T(1024)}, f32[1536]{0:T(1024)S(1)}, u32[]{:S(2)}) copy-start(f32[1536]{0:T(1024)S(1)} %slice_reduce_fusion.5) | copy-start | bytes 18436
  210.1 28.4 %copy-start.43 = (f32[1536]{0:T(1024)}, f32[1536]{0:T(1024)S(1)}, u32[]{:S(2)}) copy-start(f32[1536]{0:T(1024)S(1)} %slice_reduce_fusion.6) | copy-start | bytes 18436
  220.4 16.2 %collective-permute-start.8 = (bf16[1,128,1536]{2,1,0:T(8,128)(2,1)S(1)}, bf16[1,128,1536]{2,1,0:T(8,128)(2,1)S(1)}, u32[]{:S(2)}, u32[]{:S(2)}) collective-permute-start(bf16[1,128,1536]{2,1,0:T(8,128)(2,1)S(1)} %fusion.26), channel_id=1, source_target_pairs={{1,2},{5,6},{9,10},{13,14},{17,18},{21,22},{25,26},{29,30}} | collective-permute-start | bytes 1179656 | tf_op jit(solution)/shard_map/ppermute | solution.py:908
  228.8 8.8 %collective-permute-start.5 = (bf16[1,128,1536]{2,1,0:T(8,128)(2,1)S(1)}, bf16[1,128,1536]{2,1,0:T(8,128)(2,1)S(1)}, u32[]{:S(2)}, u32[]{:S(2)}) collective-permute-start(bf16[1,128,1536]{2,1,0:T(8,128)(2,1)S(1)} %fusion.24), channel_id=1, source_target_pairs={{1,2},{5,6},{9,10},{13,14},{17,18},{21,22},{25,26},{29,30}} | collective-permute-start | bytes 1179656 | tf_op jit(solution)/shard_map/ppermute | solution.py:908
  235.9 2.6 collective-permute-start.2
  240.3 12.2 %copy-start.1 = (bf16[8192,1024]{1,0:T(8,128)(2,1)S(1)}, bf16[8192,1024]{1,0:T(8,128)(2,1)}, u32[]{:S(2)}) copy-start(bf16[8192,1024]{1,0:T(8,128)(2,1)} %all-gather.8.cloned.1.call-done) | copy-start | bytes 50331652
  264.8 19.8 %copy-start.40 = (bf16[1,128,1536]{2,1,0:T(8,128)(2,1)S(1)}, bf16[1,128,1536]{2,1,0:T(8,128)(2,1)}, u32[]{:S(2)}) copy-start(bf16[1,128,1536]{2,1,0:T(8,128)(2,1)} %fusion.25) | copy-start | bytes 1179652
  264.9 34.4 %collective-permute-start.9 = (bf16[1,128,1536]{2,1,0:T(8,128)(2,1)}, bf16[1,128,1536]{2,1,0:T(8,128)(2,1)S(1)}, u32[]{:S(2)}, u32[]{:S(2)}) collective-permute-start(bf16[1,128,1536]{2,1,0:T(8,128)(2,1)} %fusion.27), channel_id=1, source_target_pairs={{2,3},{6,7},{10,11},{14,15},{18,19},{22,23},{26,27},{30,31}} | collective-permute-start | bytes 1179656 | tf_op jit(solution)/shard_map/ppermute | solution.py:908
  284.6 10.2 %copy-start.33 = (bf16[32,32,512]{2,1,0:T(8,128)(2,1)S(1)}, bf16[32,32,512]{2,1,0:T(8,128)(2,1)}, u32[]{:S(2)}) copy-start(bf16[32,32,512]{2,1,0:T(8,128)(2,1)} %pad_maximum_fusion.10) | copy-start | bytes 3145732
  284.6 24.5 %collective-permute-start.6 = (bf16[1,128,1536]{2,1,0:T(8,128)(2,1)S(1)}, bf16[1,128,1536]{2,1,0:T(8,128)(2,1)S(1)}, u32[]{:S(2)}, u32[]{:S(2)}) collective-permute-start(bf16[1,128,1536]{2,1,0:T(8,128)(2,1)S(1)} %copy-done.40), channel_id=1, source_target_pairs={{2,3},{6,7},{10,11},{14,15},{18,19},{22,23},{26,27},{30,31}} | collective-permute-start | bytes 1179656 | tf_op jit(solution)/shard_map/ppermute | solution.py:908
  292.9 26.1 %collective-permute-start.3 = (bf16[1,128,1536]{2,1,0:T(8,128)(2,1)S(1)}, bf16[1,128,1536]{2,1,0:T(8,128)(2,1)S(1)}, u32[]{:S(2)}, u32[]{:S(2)}) collective-permute-start(bf16[1,128,1536]{2,1,0:T(8,128)(2,1)S(1)} %copy-done.39), channel_id=1, source_target_pairs={{2,3},{6,7},{10,11},{14,15},{18,19},{22,23},{26,27},{30,31}} | collective-permute-start | bytes 1179656 | tf_op jit(solution)/shard_map/ppermute | solution.py:908
  339.7 20.9 %copy-start.10 = (bf16[3,512,1024]{2,1,0:T(8,128)(2,1)S(1)}, bf16[3,512,1024]{2,1,0:T(8,128)(2,1)}, u32[]{:S(2)}) copy-start(bf16[3,512,1024]{2,1,0:T(8,128)(2,1)} %param.37) | copy-start | bytes 9437188
  360.7 19.4 %copy-start.16 = (bf16[32,32,1024]{2,1,0:T(8,128)(2,1)S(1)}, bf16[32,32,1024]{2,1,0:T(8,128)(2,1)}, u32[]{:S(2)}) copy-start(bf16[32,32,1024]{2,1,0:T(8,128)(2,1)} %get-tuple-element.249) | copy-start | bytes 6291460
  360.7 19.4 %copy-start.17 = (bf16[32,32,1024]{2,1,0:T(8,128)(2,1)S(1)}, bf16[32,32,1024]{2,1,0:T(8,128)(2,1)}, u32[]{:S(2)}) copy-start(bf16[32,32,1024]{2,1,0:T(8,128)(2,1)} %get-tuple-element.250) | copy-start | bytes 6291460
  360.7 19.4 %copy-start.18 = (bf16[32,32,1024]{2,1,0:T(8,128)(2,1)S(1)}, bf16[32,32,1024]{2,1,0:T(8,128)(2,1)}, u32[]{:S(2)}) copy-start(bf16[32,32,1024]{2,1,0:T(8,128)(2,1)} %get-tuple-element.251) | copy-start | bytes 6291460
  433.6 257.9 %reduce-scatter.6.cloned.1.call-start = ((), (), s32[]{:S(2)}) async-start(), calls=%async_computation.13 | async-start | bytes 12976128 | tf_op jit(solution)/shard_map/reduce_scatter | solution.py:1096
  474.2 22.6 %collective-permute-start.10 = (bf16[1,128,1536]{2,1,0:T(8,128)(2,1)}, bf16[1,128,1536]{2,1,0:T(8,128)(2,1)S(1)}, u32[]{:S(2)}, u32[]{:S(2)}) collective-permute-start(bf16[1,128,1536]{2,1,0:T(8,128)(2,1)} %get-tuple-element.171), channel_id=1, source_target_pairs={{3,2},{7,6},{11,10},{15,14},{19,18},{23,22},{27,26},{31,30}} | collective-permute-start | bytes 1179656 | tf_op jit(solution)/shard_map/ppermute | solution.py:908
  485.9 11.1 %collective-permute-start.11 = (bf16[1,128,1536]{2,1,0:T(8,128)(2,1)}, bf16[1,128,1536]{2,1,0:T(8,128)(2,1)S(1)}, u32[]{:S(2)}, u32[]{:S(2)}) collective-permute-start(bf16[1,128,1536]{2,1,0:T(8,128)(2,1)} %get-tuple-element.172), channel_id=1, source_target_pairs={{3,2},{7,6},{11,10},{15,14},{19,18},{23,22},{27,26},{31,30}} | collective-permute-start | bytes 1179656 | tf_op jit(solution)/shard_map/ppermute | solution.py:908
  486.6 10.2 %copy-start.22 = (bf16[1,128,1536]{2,1,0:T(8,128)(2,1)S(1)}, bf16[1,128,1536]{2,1,0:T(8,128)(2,1)}, u32[]{:S(2)}) copy-start(bf16[1,128,1536]{2,1,0:T(8,128)(2,1)} %get-tuple-element.171) | copy-start | bytes 1179652
  486.7 10.2 %copy-start.46 = (f32[1536]{0:T(1024)S(1)}, f32[1536]{0:T(1024)}, u32[]{:S(2)}) copy-start(f32[1536]{0:T(1024)} %copy-done.45) | copy-start | bytes 18436
  486.7 10.4 %copy-start.21 = (bf16[1,128,1536]{2,1,0:T(8,128)(2,1)S(1)}, bf16[1,128,1536]{2,1,0:T(8,128)(2,1)}, u32[]{:S(2)}) copy-start(bf16[1,128,1536]{2,1,0:T(8,128)(2,1)} %get-tuple-element.172) | copy-start | bytes 1179652
  486.7 10.4 %copy-start.42 = (f32[1536]{0:T(1024)S(1)}, f32[1536]{0:T(1024)}, u32[]{:S(2)}) copy-start(f32[1536]{0:T(1024)} %copy-done.41) | copy-start | bytes 18436
  515.7 1.4 collective-permute-start.12
  516.4 16.2 %collective-permute-start.13 = (bf16[1,128,1536]{2,1,0:T(8,128)(2,1)S(1)}, bf16[1,128,1536]{2,1,0:T(8,128)(2,1)S(1)}, u32[]{:S(2)}, u32[]{:S(2)}) collective-permute-start(bf16[1,128,1536]{2,1,0:T(8,128)(2,1)S(1)} %get-tuple-element.241), channel_id=1, source_target_pairs={{2,1},{6,5},{10,9},{14,13},{18,17},{22,21},{26,25},{30,29}} | collective-permute-start | bytes 1179656 | tf_op jit(solution)/shard_map/ppermute | solution.py:908
  517.3 17.0 %collective-permute-start.15 = (bf16[1,128,1536]{2,1,0:T(8,128)(2,1)S(1)}, bf16[1,128,1536]{2,1,0:T(8,128)(2,1)S(1)}, u32[]{:S(2)}, u32[]{:S(2)}) collective-permute-start(bf16[1,128,1536]{2,1,0:T(8,128)(2,1)S(1)} %get-tuple-element.237), channel_id=1, source_target_pairs={{2,1},{6,5},{10,9},{14,13},{18,17},{22,21},{26,25},{30,29}} | collective-permute-start | bytes 1179656 | tf_op jit(solution)/shard_map/ppermute | solution.py:908
  517.9 16.5 %collective-permute-start.14 = (bf16[1,128,1536]{2,1,0:T(8,128)(2,1)S(1)}, bf16[1,128,1536]{2,1,0:T(8,128)(2,1)S(1)}, u32[]{:S(2)}, u32[]{:S(2)}) collective-permute-start(bf16[1,128,1536]{2,1,0:T(8,128)(2,1)S(1)} %get-tuple-element.239), channel_id=1, source_target_pairs={{2,1},{6,5},{10,9},{14,13},{18,17},{22,21},{26,25},{30,29}} | collective-permute-start | bytes 1179656 | tf_op jit(solution)/shard_map/ppermute | solution.py:908
  532.8 38.2 %collective-permute-start.16 = (bf16[1,128,1536]{2,1,0:T(8,128)(2,1)S(1)}, bf16[1,128,1536]{2,1,0:T(8,128)(2,1)S(1)}, u32[]{:S(2)}, u32[]{:S(2)}) collective-permute-start(bf16[1,128,1536]{2,1,0:T(8,128)(2,1)S(1)} %get-tuple-element.191), channel_id=1, source_target_pairs={{1,0},{5,4},{9,8},{13,12},{17,16},{21,20},{25,24},{29,28}} | collective-permute-start | bytes 1179656 | tf_op jit(solution)/shard_map/ppermute | solution.py:908
  534.7 56.4 %collective-permute-start.17 = (bf16[1,128,1536]{2,1,0:T(8,128)(2,1)S(1)}, bf16[1,128,1536]{2,1,0:T(8,128)(2,1)S(1)}, u32[]{:S(2)}, u32[]{:S(2)}) collective-permute-start(bf16[1,128,1536]{2,1,0:T(8,128)(2,1)S(1)} %get-tuple-element.193), channel_id=1, source_target_pairs={{1,0},{5,4},{9,8},{13,12},{17,16},{21,20},{25,24},{29,28}} | collective-permute-start | bytes 1179656 | tf_op jit(solution)/shard_map/ppermute | solution.py:908
  536.0 60.2 %collective-permute-start.18 = (bf16[1,128,1536]{2,1,0:T(8,128)(2,1)S(1)}, bf16[1,128,1536]{2,1,0:T(8,128)(2,1)S(1)}, u32[]{:S(2)}, u32[]{:S(2)}) collective-permute-start(bf16[1,128,1536]{2,1,0:T(8,128)(2,1)S(1)} %get-tuple-element.194), channel_id=1, source_target_pairs={{1,0},{5,4},{9,8},{13,12},{17,16},{21,20},{25,24},{29,28}} | collective-permute-start | bytes 1179656 | tf_op jit(solution)/shard_map/ppermute | solution.py:908
  550.5 13.4 %copy-start.35 = (bf16[4,1,512,256]{3,2,1,0:T(8,128)(2,1)S(1)}, bf16[4,1,512,256]{3,2,1,0:T(8,128)(2,1)}, u32[]{:S(2)}) copy-start(bf16[4,1,512,256]{3,2,1,0:T(8,128)(2,1)} %get-tuple-element.203) | copy-start | bytes 3145732
  550.6 13.4 %copy-start.36 = (bf16[4,1,512,256]{3,2,1,0:T(8,128)(2,1)S(1)}, bf16[4,1,512,256]{3,2,1,0:T(8,128)(2,1)}, u32[]{:S(2)}) copy-start(bf16[4,1,512,256]{3,2,1,0:T(8,128)(2,1)} %get-tuple-element.204) | copy-start | bytes 3145732
  596.9 138.0 %all-to-all-start.2 = ((bf16[4,3,512,256]{3,2,1,0:T(8,128)(2,1)}), bf16[4,3,512,256]{3,2,1,0:T(8,128)(2,1)S(1)}, u32[]{:S(2)}, u32[]{:S(2)}) async-start(bf16[4,3,512,256]{3,2,1,0:T(8,128)(2,1)} %pad_maximum_fusion.6), calls=%async_computation.4 | async-start | bytes 6291456 | tf_op jit(solution)/shard_map/all_to_all | solution.py:983
  644.0 111.3 %reduce-scatter.12.cloned.1.call-start = ((), (), s32[]{:S(2)}) async-start(), calls=%async_computation.16 | async-start | bytes 3112960 | tf_op jit(solution)/shard_map/reduce_scatter | solution.py:1184
  691.4 9.4 %copy-start.52 = (f32[1,8,1792]{2,1,0:T(8,128)S(1)}, f32[1,8,1792]{2,1,0:T(8,128)}, u32[]{:S(2)}) copy-start(f32[1,8,1792]{2,1,0:T(8,128)} %get-tuple-element.197) | copy-start | bytes 172036
  691.4 9.4 %copy-start.51 = (f32[1,8,1792]{2,1,0:T(8,128)S(1)}, f32[1,8,1792]{2,1,0:T(8,128)}, u32[]{:S(2)}) copy-start(f32[1,8,1792]{2,1,0:T(8,128)} %get-tuple-element.192) | copy-start | bytes 172036
  700.7 124.1 %reduce-scatter.10.cloned.1.call-start = ((), (), s32[]{:S(2)}) async-start(), calls=%async_computation.15 | async-start | bytes 4423680 | tf_op jit(solution)/shard_map/reduce_scatter | solution.py:1096
  725.3 8.7 %collective-permute-start.19 = (bf16[3,3,1792]{2,1,0:T(4,128)(2,1)S(1)}, bf16[3,3,1792]{2,1,0:T(4,128)(2,1)S(1)}, u32[]{:S(2)}, u32[]{:S(2)}) collective-permute-start(bf16[3,3,1792]{2,1,0:T(4,128)(2,1)S(1)} %pad_maximum_fusion.14), channel_id=1, source_target_pairs={{1,0},{2,1},{3,2},{5,4},{6,5},{7,6},{9,8},{10,9},{11,10},{13,12},{... | collective-permute-start | bytes 96776 | tf_op jit(solution)/shard_map/ppermute | solution.py:885
  734.9 13.4 %copy-start.2 = (bf16[4,3,512,256]{3,2,1,0:T(8,128)(2,1)}, bf16[4,3,512,256]{3,2,1,0:T(8,128)(2,1)S(1)}, u32[]{:S(2)}) copy-start(bf16[4,3,512,256]{3,2,1,0:T(8,128)(2,1)S(1)} %all-to-all-done.2.dkv_ref) | copy-start | bytes 9437188
  755.4 24.1 %copy-start.4 = (bf16[3,512,512]{2,1,0:T(8,128)(2,1)S(1)}, bf16[3,512,512]{2,1,0:T(8,128)(2,1)}, u32[]{:S(2)}) copy-start(bf16[3,512,512]{2,1,0:T(8,128)(2,1)} %pad_maximum_fusion.9) | copy-start | bytes 4718596
  784.9 24.5 %copy-start.13 = (bf16[304,1024]{1,0:T(8,128)(2,1)S(1)}, bf16[304,1024]{1,0:T(8,128)(2,1)}, u32[]{:S(2)}) copy-start(bf16[304,1024]{1,0:T(8,128)(2,1)} %reduce-scatter.12.cloned.1.call-done) | copy-start | bytes 1867780
  790.4 21.1 %collective-permute-start.20 = (bf16[2,2,4,32,896]{4,3,2,1,0:T(8,128)(2,1)}, bf16[2,2,4,32,896]{4,3,2,1,0:T(8,128)(2,1)S(1)}, u32[]{:S(2)}, u32[]{:S(2)}) collective-permute-start(bf16[2,2,4,32,896]{4,3,2,1,0:T(8,128)(2,1)} %fusion.20), channel_id=1, source_target_pairs={{0,4},{4,0},{8,12},{12,8},{16,20},{20,16},{24,28},{28,24},{1,5},{5... | collective-permute-start | bytes 2752520 | tf_op jit(solution)/shard_map/ppermute | solution.py:943
  800.0 8.8 %all-to-all-start.4 = ((f32[4,3,24]{2,1,0:T(4,128)}), f32[4,3,24]{2,1,0:T(4,128)S(1)}, u32[]{:S(2)}, u32[]{:S(2)}) async-start(f32[4,3,24]{2,1,0:T(4,128)} %broadcast_in_dim.88), calls=%async_computation.9 | async-start | bytes 16384 | tf_op jit(solution)/shard_map/all_to_all | solution.py:929
  803.2 47.2 %reduce-scatter.14.cloned.1.call-start = ((), (), s32[]{:S(2)}) async-start(), calls=%async_computation.17 | async-start | bytes 614400 | tf_op jit(solution)/shard_map/reduce_scatter | solution.py:1188
  811.9 11.1 %collective-permute-start.21 = (bf16[2,4,32,896]{3,2,1,0:T(8,128)(2,1)S(1)}, bf16[2,4,32,896]{3,2,1,0:T(8,128)(2,1)S(1)}, u32[]{:S(2)}, u32[]{:S(2)}) collective-permute-start(bf16[2,4,32,896]{3,2,1,0:T(8,128)(2,1)S(1)} %fusion.36), channel_id=1, source_target_pairs={{0,16},{4,20},{8,24},{12,28},{16,0},{20,4},{24,8},{28,12},{1,17},{... | collective-permute-start | bytes 1376264 | tf_op jit(solution)/shard_map/ppermute | solution.py:943
  823.2 6.1 collective-permute-start.22
  829.5 16.1 %collective-permute-start.23 = (bf16[32,896]{1,0:T(8,128)(2,1)S(1)}, bf16[32,896]{1,0:T(8,128)(2,1)S(1)}, u32[]{:S(2)}, u32[]{:S(2)}) collective-permute-start(bf16[32,896]{1,0:T(8,128)(2,1)S(1)} %get-tuple-element.271), channel_id=1, source_target_pairs={{0,1},{1,2},{2,3},{3,0},{4,5},{5,6},{6,7},{7,4},{8,9},{9,10},{10,1... | collective-permute-start | bytes 172040 | tf_op jit(solution)/shard_map/ppermute | solution.py:949
  830.2 15.4 %collective-permute-start.25 = (bf16[32,896]{1,0:T(8,128)(2,1)S(1)}, bf16[32,896]{1,0:T(8,128)(2,1)S(1)}, u32[]{:S(2)}, u32[]{:S(2)}) collective-permute-start(bf16[32,896]{1,0:T(8,128)(2,1)S(1)} %get-tuple-element.272), channel_id=1, source_target_pairs={{0,3},{1,0},{2,1},{3,2},{4,7},{5,4},{6,5},{7,6},{8,11},{9,8},{10,9... | collective-permute-start | bytes 172040 | tf_op jit(solution)/shard_map/ppermute | solution.py:949
  833.5 12.1 %collective-permute-start.24 = (bf16[32,896]{1,0:T(8,128)(2,1)S(1)}, bf16[32,896]{1,0:T(8,128)(2,1)S(1)}, u32[]{:S(2)}, u32[]{:S(2)}) collective-permute-start(bf16[32,896]{1,0:T(8,128)(2,1)S(1)} %get-tuple-element.273), channel_id=1, source_target_pairs={{0,2},{1,3},{2,0},{3,1},{4,6},{5,7},{6,4},{7,5},{8,10},{9,11},{10,... | collective-permute-start | bytes 172040 | tf_op jit(solution)/shard_map/ppermute | solution.py:949
  (35 other events, 187.0 us)
Sparse Core Ops, SparseCore 0:
  16.0 31.6 all-gather.3
  49.6 56.0 all-gather.5
  121.6 89.0 all-gather.7
  433.7 101.7 reduce-scatter.7
  539.2 98.2 reduce-scatter.5
  700.9 54.4 reduce-scatter.11
  759.3 49.5 reduce-scatter.9
  825.0 19.7 reduce-scatter.13

commit v7 on v6

--- a/solution.py
+++ b/solution.py
@@ -432,6 +432,10 @@
     return row >= lanes((CHUNK, CHUNK))
 
 
+def saved_terms(terms_ref):
+    return [terms_ref[0, :, at * 128 : (at + 1) * 128] for at in range(6)]
+
+
 def token_rows(token_ref):
     return jnp.concatenate([token_ref[0]] * 16, axis=0).T
 
@@ -459,7 +463,7 @@
 
 def mixer_scan_kernel(
     cr_ref, rim_ref, token_ref, head_ref, taps_ref, shift_ref, spread_ref,
-    act_ref, states_ref, gains_ref, final_ref, final_gain_ref,
+    act_ref, states_ref, gains_ref, final_ref, final_gain_ref, terms_ref,
     ext_s, state_s, gain_s,
 ):
     chunk = pl.program_id(0)
@@ -479,10 +483,15 @@
     total = conv_total(ext_s, token, taps_ref, shift_ref)
     act = (total * jax.nn.sigmoid(total)).astype(BF16)
     act_ref[0] = act
-    weight_end, _, gain = decay_rows(cr_ref[0, :, CC:], head_ref, token)[-3:]
+    raw, step, log_decay, running, weight_end, entry, gain = decay_rows(
+        cr_ref[0, :, CC:], head_ref, token
+    )
+    for at, term in enumerate((raw, step, log_decay, running, weight_end, entry)):
+        terms_ref[0, :, at * 128 : (at + 1) * 128] = term
     states_ref[0, 0] = state_s[...].astype(BF16)
     before = gain_s[...]
-    gains_ref[0, 0] = before
+    row = lax.broadcasted_iota(jnp.int32, before.shape, 0)
+    gains_ref[0, 0] = jnp.where(row == 1, jnp.broadcast_to(gain, before.shape), before)
     spread = spread_ref[...]
     scaled = (act[:, :DI].astype(F32) * widen(weight_end, spread)).astype(BF16)
     gain_rows = jnp.broadcast_to(gain, (8, 128))
@@ -528,11 +537,11 @@
 
 
 def mixer_out_kernel(
-    gate_ref, cr_ref, act_ref, token_ref, states_ref, gains_ref, state_ref, head_ref, skip_ref, gain_ref,
+    gate_ref, terms_ref, act_ref, token_ref, states_ref, gains_ref, state_ref, skip_ref, gain_ref,
     spread_ref, y_ref, out_ref,
 ):
     token, spread = token_rows(token_ref), spread_ref[...]
-    _, step, _, running, _, entry, _ = decay_rows(cr_ref[0, :, CC:], head_ref, token)
+    _, step, _, running, _, entry = saved_terms(terms_ref)
     b_rows, c_rows = act_ref[0, :, DI : DI + NS], act_ref[0, :, DI + NS :]
     state = entering_state(states_ref, gains_ref, state_ref, spread)
     carried = contract(c_rows, state, 1, 0) * widen(entry, spread)
@@ -567,7 +576,7 @@
 
 
 def mixer_gate_back_kernel(
-    gmix_ref, y_ref, gate_ref, cr_ref, act_ref, token_ref, head_ref, gain_ref, spread_ref,
+    gmix_ref, y_ref, gate_ref, terms_ref, act_ref, fgains_ref, gain_ref, spread_ref,
     gy_ref, dgate_ref, gstates_ref, gains_ref, final_ref, dgain_ref, dskip_ref,
     state_s, gain_s, dgain_s, dskip_s,
 ):
@@ -583,8 +592,8 @@
         state_s[...] = jnp.zeros(state_s.shape, F32)
         gain_s[...] = jnp.ones(gain_s.shape, F32)
 
-    token, spread = token_rows(token_ref), spread_ref[...]
-    entry, gain = decay_rows(cr_ref[0, :, CC:], head_ref, token)[-2:]
+    spread = spread_ref[...]
+    entry, gain = saved_terms(terms_ref)[-1], fgains_ref[0, 0, 1:2, :]
     y = y_ref[0]
     gate = gate_ref[0].astype(F32)
     sig = jax.nn.sigmoid(gate)
@@ -621,7 +630,7 @@
 
 
 def mixer_back_kernel(
-    gy_ref, y_ref, cr_ref, halo_ref, rim_ref, act_ref, token_ref,
+    gy_ref, y_ref, terms_ref, cr_ref, halo_ref, rim_ref, act_ref, token_ref,
     states_ref, gains_ref, state_ref, gstates_ref, ggains_ref, gstate_ref,
     head_ref, skip_ref, taps_ref, shift_ref, spread_ref, spread_first_ref,
     dcr_ref, drim_ref, dconv_ref, dhead_ref,
@@ -649,9 +658,8 @@
 
     ext_s[8 : 8 + CHUNK, :] = cr_ref[0, :, :CC].astype(F32)
     token, spread, spread_first = token_rows(token_ref), spread_ref[...], spread_first_ref[...]
-    raw, step, log_decay, running, weight_end, entry, gain = decay_rows(
-        cr_ref[0, :, CC:], head_ref, token
-    )
+    raw, step, log_decay, running, weight_end, entry = saved_terms(terms_ref)
+    gain = gains_ref[0, 0, 1:2, :]
     b_rows, c_rows = act_ref[0, :, DI : DI + NS], act_ref[0, :, DI + NS :]
     state = entering_state(states_ref, gains_ref, state_ref, spread)
     gstate = entering_state(gstates_ref, ggains_ref, gstate_ref, spread)
@@ -787,19 +795,20 @@
             ("chunk", jax.ShapeDtypeStruct((seqs, chunks, 8, 128), F32)),
             ("own", jax.ShapeDtypeStruct((1, NS, DI), BF16)),
             ("own", jax.ShapeDtypeStruct((1, 8, DI), F32)),
+            ("block", jax.ShapeDtypeStruct((seqs, span, 6 * 128), F32)),
         ],
         [(CHUNK + 8, CC), (NS, DI), (8, 128)],
         earlier,
     )
 
 
-def mixer_out(seq, earlier, gate, cr, act, token, states, gains, state, heads, skip, gain, spread):
-    seqs, span, _ = cr.shape
+def mixer_out(seq, earlier, gate, terms, act, token, states, gains, state, skip, gain, spread):
+    seqs, span, _ = gate.shape
     return mixer_call(
         mixer_out_kernel, "mixer_out", seq, span // CHUNK, False,
         [
-            ("block", gate), ("block", cr), ("block", act), ("token", token), ("chunk", states),
-            ("chunk", gains), ("own", state), ("fixed", heads), ("fixed", skip),
+            ("block", gate), ("block", terms), ("block", act), ("token", token), ("chunk", states),
+            ("chunk", gains), ("own", state), ("fixed", skip),
             ("fixed", gain), ("fixed", spread),
         ],
         [
@@ -812,15 +821,15 @@
 
 
 def mixer_gate_back(
-    seq, earlier, gmix, y, gate, cr, act, token, heads, gain, spread
+    seq, earlier, gmix, y, gate, terms, act, gains, gain, spread
 ):
-    seqs, span, _ = cr.shape
+    seqs, span, _ = gate.shape
     chunks = span // CHUNK
     return mixer_call(
         mixer_gate_back_kernel, "mixer_gate_back", seq, chunks, True,
         [
-            ("block", gmix), ("block", y), ("block", gate), ("block", cr), ("block", act), ("token", token),
-            ("fixed", heads), ("fixed", gain), ("fixed", spread),
+            ("block", gmix), ("block", y), ("block", gate), ("block", terms), ("block", act), ("chunk", gains),
+            ("fixed", gain), ("fixed", spread),
         ],
         [
             ("block", jax.ShapeDtypeStruct((seqs, span, DI), BF16)),
@@ -837,14 +846,14 @@
 
 
 def mixer_back(
-    seq, earlier, gy, y, cr, rim, act, token, states, gains, state, gstates, ggains,
+    seq, earlier, gy, y, terms, cr, rim, act, token, states, gains, state, gstates, ggains,
     gstate, heads, skip, taps, shift, spread, spread_first,
 ):
     seqs, span, width = cr.shape
     return mixer_call(
         mixer_back_kernel, "mixer_back", seq, span // CHUNK, True,
         [
-            ("block", gy), ("block", y), ("block", cr), ("halo", cr),
+            ("block", gy), ("block", y), ("block", terms), ("block", cr), ("halo", cr),
             ("seq", rim), ("block", act), ("token", token), ("chunk", states), ("chunk", gains),
             ("own", state), ("chunk", gstates), ("chunk", ggains), ("own", gstate),
             ("fixed", heads), ("fixed", skip), ("fixed", taps), ("fixed", shift),
@@ -930,7 +939,7 @@
     return values
 
 
-def scatter_all(grad):
+def scatter_all(grad, *late):
     count, place = lax.axis_size("ctx"), lax.axis_index("ctx")
     devices, me = lax.axis_size("dp"), lax.axis_index("dp")
     bits = devices.bit_length() - 1
@@ -943,7 +952,7 @@
         received = lax.ppermute(sent, "dp", [(i, i ^ (1 << bit)) for i in range(devices)])
         part = jnp.where(low, first, second).astype(F32) + received.astype(F32)
     relative = lax.dynamic_slice_in_dim(jnp.concatenate([part, part]), place, count, 0)
-    total, rounded = relative[0], relative.astype(BF16)
+    total, rounded = relative[0], after(relative.astype(BF16), *late)
     for d in range(1, count):
         route = [(i, (i + d) % count) for i in range(count)]
         total = total + lax.ppermute(rounded[d], "ctx", route).astype(F32)
@@ -986,7 +995,6 @@
     w_cr = jnp.pad(w_in[:, DI:], ((0, 0), (0, CR - (w_in.shape[1] - DI))))
     first = jnp.concatenate([w_cr, w_q, w_kv, small_block, w_in[:, :DI]], axis=1)
     first_part = lax.all_gather(first, "ctx", axis=0, tiled=True)
-    first_all = gather(first_part)
     turned_o = w_o.T
     half_rows, ff = own_rows // 2, w_gate.shape[1]
 
@@ -1019,8 +1027,10 @@
 
     tokens = layer_input.reshape(rows, width)
     small = (token, bounds, segk, segq, cosine, sine, heads, skip, spread, spread_first)
+    rest_copies = copies(jnp.concatenate(rest, axis=0))
+    first_all = gather(after(first_part, small, rest_copies))
     cosine, sine = cosine.reshape(rows, 128), sine.reshape(rows, 128)
-    rest_part = exchange(after(copies(jnp.concatenate(rest, axis=0)), first_part, small))
+    rest_part = exchange(after(rest_copies, first_part))
     rest_all = gather(rest_part.reshape(-1, width)).reshape(-1, sum(rest_sizes), width)
     cuts, at = [], 0
     for size in rest_sizes:
@@ -1056,7 +1066,7 @@
         wide_gains.append(scanned[4][:, :1])
         chains.append(Chain(scanned[3], wide_gains[seq], False))
         chains[seq].send()
-    act, states, gains = scanned[:3]
+    act, states, gains, terms = scanned[0], scanned[1], scanned[2], scanned[5]
     for chain in chains:
         chain.take()
         chain.send()
@@ -1074,7 +1084,7 @@
     for seq in range(seqs):
         states_in.append(chains[seq].finish())
         mixed = mixer_out(
-            seq, mixed, gate, cr, act, token, states, gains, states_in[seq], heads, skip, gain_m_all,
+            seq, mixed, gate, terms, act, token, states, gains, states_in[seq], skip, gain_m_all,
             spread,
         )
     mixer_y, mixer_in = mixed
@@ -1122,7 +1132,7 @@
     gated, chains, grad_gain_mix, grad_skip = None, [], 0.0, 0.0
     for seq in range(seqs):
         gated = mixer_gate_back(
-            seq, gated, grad_mixer_in, mixer_y, gate, cr, act, token, heads, gain_m_all, spread
+            seq, gated, grad_mixer_in, mixer_y, gate, terms, act, gains, gain_m_all, spread
         )
         grad_gain_mix, grad_skip = grad_gain_mix + gated[5], grad_skip + gated[6]
         chains.append(Chain(gated[4], wide_gains[seq], True))
@@ -1162,14 +1172,14 @@
     waits[1 % seqs] += tuple(finals)
     for seq in range(seqs):
         gstate = finals[seq]
-        if seq == seqs - 1:
+        if seq == min(1, seqs - 1):
             gu_blocks = part_gu.reshape(count, own_rows, 2 * ff)
             parts = [after(part_rest, *rims).reshape(count, -1, width)]
             parts += [gu_blocks[..., at : at + width] for at in range(0, 2 * ff, width)]
             rest_low = jnp.concatenate(parts, axis=1).reshape(-1, width)
-            waits[seq] = (rest_low,)
+            waits[seq] += (rest_low,)
         last = mixer_back(
-            seq, last, after(grad_y, dqs[-1], *waits[seq]), mixer_y, cr, rim, act, token, states,
+            seq, last, after(grad_y, dqs[-1], *waits[seq]), mixer_y, terms, cr, rim, act, token, states,
             gains, states_in[seq], gstates, ggains, gstate, heads, skip, taps_all, shift_all,
             spread, spread_first,
         )
@@ -1183,15 +1193,15 @@
     ).reshape(rows, CR)
     rest_out = lax.psum_scatter(rest_low, "ctx", scatter_dimension=0, tiled=True).astype(F32)
     grad_wcr = weight_grad(hidden, grad_cr)
-    part_cr = scatter(grad_wcr)
+    grad_wq = weight_grad(hidden, dq.reshape(rows, q_width))
+    part_cr = scatter(jnp.concatenate([grad_wcr, grad_wq], axis=1))
     layer_result = (middle + low_dot(after(act_rows, part_cr), w_down_all)).astype(BF16)
     out_cr = lax.psum_scatter(part_cr, "ctx", scatter_dimension=0, tiled=True).astype(F32)
     grad_tokens, grad_kv, grad_gain_first = finish(
         tokens, gain1_all, grad_gate.reshape(rows, DI), after(grad_cr, grad_wcr, rest_out),
         dq.reshape(rows, q_width), dkv_all, cosine, sine, grad_middle, first_all,
     )
-    grad_first = jnp.concatenate([dq.reshape(rows, q_width), grad_kv], axis=1)
-    grad_wfirst = weight_grad(hidden, grad_first)
+    grad_wfirst = weight_grad(hidden, grad_kv)
     grad_gain_first = grad_gain_first[0]
 
     devices = first_all.shape[0] // own_rows
@@ -1207,7 +1217,7 @@
     )
     small_grads = jnp.pad(small_grads, ((0, 0), (0, slots - small_grads.shape[1])))
     out_first = scatter_all(
-        jnp.concatenate([grad_wfirst, small_grads.reshape(-1, 128).astype(BF16)], axis=1)
+        jnp.concatenate([grad_wfirst, small_grads.reshape(-1, 128).astype(BF16)], axis=1), part_cr
     )
     rest_sizes = rest_sizes[:3] + [own_rows, half_rows] + rest_sizes[3:]
     outs, at = [], 0
@@ -1222,12 +1232,12 @@
     halves = ff // width
     out_gate = jnp.concatenate(outs[5 : 5 + halves], axis=1)
     out_up = jnp.concatenate(outs[5 + halves :], axis=1)
-    out_small = out_first[:, q_width + kv_width :].reshape(-1)
+    out_small = out_first[:, kv_width:].reshape(-1)
     pieces, at = [], 0
     for size in small_sizes:
         pieces.append(out_small[at : at + size])
         at += size
-    out_kv = out_first[:, q_width : q_width + kv_width].reshape(own_rows, KVH, 2, HD)
+    out_kv = out_first[:, :kv_width].reshape(own_rows, KVH, 2, HD)
     head_grad = sum_everywhere(
         jnp.concatenate(
             [grad_heads[:2, :MH], grad_skip[0].reshape(MH, MP).sum(axis=1)[None]], axis=0
@@ -1244,7 +1254,7 @@
         head_grad,
         pieces[2],
         out_wout,
-        out_first[:, :q_width],
+        out_cr[:, CR:],
         out_kv[:, :, 0].reshape(own_rows, -1),
         out_kv[:, :, 1].reshape(own_rows, -1),
         out_wo.T,

time: 873 us -> 854 us (0.978)
    all_gather x1, waiting for transfers between devices: 31.8 us -> 10 us  [body(): first_part = lax.all_gather(first, 'ctx', axis=0, tiled=True)]
    all_to_all x1 -> x2, starting transfers between devices: 3.25 us -> 14.2 us  [sum_everywhere(): values = jnp.sum(lax.all_to_all(copies, axis, 0, 0, tiled=True), axis=0)]
    ppermute x18, starting transfers between devices: 30.7 us -> 19.9 us  [send(): self.flying = (lax.ppermute(sent, 'ctx', [(source, target)]), target)]
    ppermute x18, waiting for transfers between devices: 49.8 us -> 58.9 us  [send(): self.flying = (lax.ppermute(sent, 'ctx', [(source, target)]), target)]
    dot_general x7 -> x8, matrix products: 62.5 us -> 63.8 us  [weight_grad(): jnp.einsum('ri,ro->io', left, right, preferred_element_type=F32)]
    unnamed x142 -> x148, local copies, waits for them, and re-layouts: 26.7 us -> 27.4 us
  transfers between devices with their start and end apart: 37 -> 38, of which waited for: 12 -> 15; matrix products, arithmetic and copies ran while one was open for 23% -> 23% of each run, Pallas kernels for 29% -> 29%
where the time goes in v7:
time: 854 us; the launch traced here: 840 us
  Pallas kernels  258 us (30%)
  matrix products  170 us (20%)
  waiting for transfers between devices  108 us (13%)
  starting transfers between devices  90 us (11%)
  local copies, waits for them, and re-layouts  86.1 us (10%)
  other arithmetic  60.3 us (7%)
  blocking collectives  51.6 us (6%)
  between operations  15.9 us (2%)
    pallas_call x12, Pallas kernels, mixer_call(): pl.pallas_call(run, grid=(chunks,), in_specs=in_specs, out_specs=out_spec...  156 us
    dot_general x8, matrix products, weight_grad(): jnp.einsum('ri,ro->io', left, right, preferred_element_type=F32)  63.8 us
    ppermute x18, waiting for transfers between devices, send(): self.flying = (lax.ppermute(sent, 'ctx', [(source, target)]), target)  58.9 us
    dot_general x5, matrix products, body(): low_dot = lambda a, b: jnp.dot(a, b, preferred_element_type=F32)  55.4 us
    all_to_all x1, blocking collectives, body(): exchange = lambda blocks: lax.all_to_all(blocks, 'ctx', 0, 0, tiled=True)  51.6 us
    dot_general x3, matrix products, back_dot(): return jnp.einsum('ro,io->ri', grad, weight, preferred_element_type=F32)  46.6 us
    all_to_all x2, starting transfers between devices, body(): exchange = lambda blocks: lax.all_to_all(blocks, 'ctx', 0, 0, tiled=True)  44.3 us
    pallas_call x3, Pallas kernels, attend_back(): pl.pallas_call(functools.partial(attend_back_kernel, seq * (span // rows)...  40.5 us
  transfers between devices with their start and end apart: 38, of which 15 were waited for; matrix products, arithmetic and copies ran while one was open for 23% of the time, Pallas kernels for 29%

profile of v7, /device:TPU:0, one launch (start us, length us, event | category | flops | bytes accessed | tf_op | source)
XLA Modules:
  0.0 840.4 jit_solution(15464319213820698752)
XLA Ops:
  37.7 10.0 %all-gather.4.cloned.1.call-done = bf16[128,4352]{1,0:T(8,128)(2,1)} async-done(((bf16[32,4352]{1,0:T(8,128)(2,1)}), bf16[128,4352]{1,0:T(8,128)(2,1)}) %all-gather.4.cloned.1.call-update) | async-done | bytes 1114128 | tf_op jit(solution)/shard_map/all_gather | solution.py:997
  48.0 51.6 %all_to_all.25 = bf16[4,256,1024]{2,1,0:T(8,128)(2,1)} all-to-all(bf16[4,256,1024]{2,1,0:T(8,128)(2,1)S(1)} %broadcast_in_dim.80), channel_id=1, replica_groups=mesh['dp'=8,'ctx'=4] {'ctx'}, dimensions={0} | all-to-all | bytes 4194304 | tf_op jit(solution)/shard_map/all_to_all | solution.py:992
  108.3 16.2 %project.1 = (bf16[1536,1024]{1,0:T(8,128)(2,1)}, bf16[1536,1920]{1,0:T(8,128)(2,1)}, bf16[1536,512]{1,0:T(8,128)(2,1)}, bf16[1536,256]{1,0:T(8,128)(2,1)}) custom-call(bf16[1536,1024]{1,0:T(8,128)(2,1)} %bitcast.197, f32[1,1024]{1,0:T(1,128)} %reshape.287.gain_ref, bf16[1024,4352]{1,0:T(8,128)(2,1)} %all-gather.6.cloned.1.call-done.w_ref, ...), custom_call_target="tpu_custom_call" | custom-call | tf_op jit(solution)/shard_map/project/pallas_call | solution.py:77
  125.4 3.4 collective-permute-start
  132.7 3.1 broadcast_in_dim.84
  135.8 3.7 all-to-all-start.1
  140.4 9.5 %mixer_scan.3 = (bf16[3,512,1792]{2,1,0:T(8,128)(2,1)}, bf16[3,4,128,1536]{3,2,1,0:T(8,128)(2,1)}, f32[3,4,8,128]{3,2,1,0:T(8,128)}, bf16[1,128,1536]{2,1,0:T(8,...) custom-call(bf16[3,512,1920]{2,1,0:T(8,128)(2,1)} %bitcast.156, bf16[3,8,1792]{2,1,0:T(8,128)(2,1)} %pad.28.refs_1_.refs_5_, ...), custom_call_target="tpu_custom_call" | custom-call | tf_op jit(solution)/shard_map/mixer_scan/pallas_call | solution.py:770
  150.0 3.9 collective-permute-start.7
  153.8 8.6 %convolution_convert_fusion.2 = bf16[1536,1536]{1,0:T(8,128)(2,1)} fusion(bf16[1536,1024]{1,0:T(8,128)(2,1)S(1)} %copy-done.59, bf16[1024,4352]{1,0:T(8,128)(2,1)} %all-gather.6.cloned.1.call-done.w_ref), kind=kOutput, calls=%fused_computation.22 | convolution fusion | flops 4834197504 | bytes 11010048 | tf_op jit(solution)/shard_map/dot_general | solution.py:981
  164.7 9.3 %mixer_scan.4 = (bf16[3,512,1792]{2,1,0:T(8,128)(2,1)}, bf16[3,4,128,1536]{3,2,1,0:T(8,128)(2,1)}, f32[3,4,8,128]{3,2,1,0:T(8,128)}, bf16[1,128,1536]{2,1,0:T(8,...) custom-call(bf16[3,512,1920]{2,1,0:T(8,128)(2,1)} %bitcast.157, ...), custom_call_target="tpu_custom_call", output_to_operand_aliasing={{0}: (7, {}), {1}: (8, {}), {2}: (9, {}), {5}: (10, {})} | custom-call | tf_op jit(solution)/shard_map/mixer_scan/pallas_call | solution.py:770
  175.3 9.3 %mixer_scan.5 = (bf16[3,512,1792]{2,1,0:T(8,128)(2,1)}, bf16[3,4,128,1536]{3,2,1,0:T(8,128)(2,1)}, f32[3,4,8,128]{3,2,1,0:T(8,128)}, bf16[1,128,1536]{2,1,0:T(8,...) custom-call(bf16[3,512,1920]{2,1,0:T(8,128)(2,1)} %bitcast.158, ...), custom_call_target="tpu_custom_call", output_to_operand_aliasing={{0}: (7, {}), {1}: (8, {}), {2}: (9, {}), {5}: (10, {})} | custom-call | tf_op jit(solution)/shard_map/mixer_scan/pallas_call | solution.py:770
  188.8 11.1 %collective-permute-done.7 = bf16[1,128,1536]{2,1,0:T(8,128)(2,1)S(1)} collective-permute-done((bf16[1,128,1536]{2,1,0:T(8,128)(2,1)}, bf16[1,128,1536]{2,1,0:T(8,128)(2,1)S(1)}, u32[]{:S(2)}, u32[]{:S(2)}) %collective-permute-start.7) | collective-permute-done | bytes 393248 | tf_op jit(solution)/shard_map/ppermute | solution.py:917
  200.7 7.6 collective-permute-done.4
  209.1 6.9 collective-permute-done.1
  221.8 4.2 slice.374
  225.9 5.6 slice.373
  233.9 3.3 fusion.59
  238.8 7.4 attend.3
  247.5 7.4 attend.4
  255.8 7.4 attend.5
  265.2 4.4 fusion.68
  270.4 8.6 %mixer_out.3 = (f32[3,512,1536]{2,1,0:T(8,128)}, bf16[3,512,1536]{2,1,0:T(8,128)(2,1)}) custom-call(bf16[3,512,1536]{2,1,0:T(8,128)(2,1)} %bitcast.165, f32[3,512,768]{2,1,0:T(8,128)} %get-tuple-element.137.refs_1_.refs_3_.refs_2_, bf16[3,512,1792]{2,1,0:T(8,128)(2,1)} %get-tuple-element.138.refs_2_.refs_4_.refs_6_, ...), custom_call_target="tpu_custom_call" | custom-call | tf_op jit(solution)/shard_map/mixer_out/pallas_call | solution.py:770
  279.9 8.6 %mixer_out.4 = (f32[3,512,1536]{2,1,0:T(8,128)}, bf16[3,512,1536]{2,1,0:T(8,128)(2,1)}) custom-call(bf16[3,512,1536]{2,1,0:T(8,128)(2,1)} %bitcast.166, f32[3,512,768]{2,1,0:T(8,128)} %get-tuple-element.137.refs_1_.refs_3_.refs_2_, bf16[3,512,1792]{2,1,0:T(8,128)(2,1)} %get-tuple-element.138.refs_2_.refs_4_.refs_6_, ...), custom_call_target="tpu_custom_call", output_to_operand_aliasing={{0}: (10, {}), {1}: (11, {})} | custom-call | tf_op jit(solution)/shard_map/mixer_out/pallas_call | solution.py:770
  289.4 8.7 %mixer_out.5 = (f32[3,512,1536]{2,1,0:T(8,128)}, bf16[3,512,1536]{2,1,0:T(8,128)(2,1)}) custom-call(bf16[3,512,1536]{2,1,0:T(8,128)(2,1)} %bitcast.167, f32[3,512,768]{2,1,0:T(8,128)} %get-tuple-element.137.refs_1_.refs_3_.refs_2_, bf16[3,512,1792]{2,1,0:T(8,128)(2,1)} %get-tuple-element.138.refs_2_.refs_4_.refs_6_, ...), custom_call_target="tpu_custom_call", output_to_operand_aliasing={{0}: (10, {}), {1}: (11, {})} | custom-call | tf_op jit(solution)/shard_map/mixer_out/pallas_call | solution.py:770
  298.1 10.8 %multiply_reduce_fusion.2 = (f32[1536]{0:T(1024)S(1)}, f32[1536,1024]{1,0:T(8,128)}) fusion(f32[1536,1024]{1,0:T(8,128)} %fusion.68, bf16[1536,1536]{1,0:T(8,128)(2,1)} %bitcast.186, bf16[1536,1024]{1,0:T(8,128)(2,1)S(1)} %bitcast.210, bf16[1536,1024]{1,0:T(8,128)(2,1)S(1)} %bitcast.199), kind=kOutput, calls=%fused_computation.29 | convolution fusion | flops 4839700992 | bytes 23599104 | tf_op jit(solution)/shard_map/dot_general | solution.py:981
  308.9 20.9 %convolution_convert_fusion = bf16[1536,4096]{1,0:T(8,128)(2,1)} fusion(f32[1536,1024]{1,0:T(8,128)} %get-tuple-element.303, f32[1024]{0:T(1024)S(1)} %mul.230, f32[1536]{0:T(1024)S(1)} %fusion.47, bf16[1024,1024]{1,0:T(8,128)(2,1)} %bitcast.217, bf16[1024,1024]{1,0:T(8,128)(2,1)} %bitcast.219, bf16[1024,1024]{1,0:T(8,128)(2,1)} %bitcast.221, ...), kind=kOutput, calls=%fused_computation.6 | convolution fusion | flops 12929466368 | bytes 27273216 | tf_op jit(solution)/shard_map/dot_general | solution.py:981
  329.9 19.1 %fusion.6 = (bf16[1536,2048]{1,0:T(8,128)(2,1)}, bf16[1536,2048]{1,0:T(8,128)(2,1)}, bf16[1536,2048]{1,0:T(8,128)(2,1)}) fusion(bf16[1536,4096]{1,0:T(8,128)(2,1)} %convolution_convert_fusion, bf16[2048,1024]{1,0:T(8,128)(2,1)} %bitcast.205, bf16[1536,1024]{1,0:T(8,128)(2,1)S(1)} %bitcast.208), kind=kOutput, calls=%fused_computation.13 | convolution fusion | flops 6499074048 | bytes 38797312 | tf_op jit(solution)/shard_map/ro,io->ri/dot_general | solution.py:1112
  349.0 20.7 %fusion.9 = f32[1536,1024]{1,0:T(8,128)} fusion(bf16[1536,2048]{1,0:T(8,128)(2,1)} %get-tuple-element.258, bf16[1536,2048]{1,0:T(8,128)(2,1)} %get-tuple-element.257, bf16[1024,1024]{1,0:T(8,128)(2,1)S(1)} %bitcast.218, bf16[1024,1024]{1,0:T(8,128)(2,1)S(1)} %bitcast.220, bf16[1024,1024]{1,0:T(8,128)(2,1)} %bitcast.222, bf16[1024,1024]{1,0:T(8,128)(2,1)S(1)} %bitcast.216), kind=kOutput, calls=%fused_computation.20 | convolution fusion | flops 12943622144 | bytes 27262976 | tf_op jit(solution)/shard_map/ro,io->ri/dot_general | solution.py:1112
  369.6 21.7 %fusion.10 = bf16[1024,4096]{1,0:T(8,128)(2,1)} fusion(bf16[1536,2048]{1,0:T(8,128)(2,1)} %get-tuple-element.258, bf16[1536,2048]{1,0:T(8,128)(2,1)} %get-tuple-element.257, f32[1536,1024]{1,0:T(8,128)} %get-tuple-element.303, f32[1024]{0:T(1024)S(1)} %mul.230, f32[1536]{0:T(1024)S(1)} %fusion.47), kind=kOutput, calls=%fused_computation.23 | convolution fusion | flops 12918980608 | bytes 27273216 | tf_op jit(solution)/shard_map/ri,ro->io/dot_general | solution.py:1109
  391.3 11.2 %convolution_convert_fusion.3 = bf16[2048,1024]{1,0:T(8,128)(2,1)} fusion(bf16[1536,2048]{1,0:T(8,128)(2,1)} %get-tuple-element.217, bf16[1536,1024]{1,0:T(8,128)(2,1)S(1)} %bitcast.209), kind=kOutput, calls=%fused_computation.32 | convolution fusion | flops 6444548096 | bytes 13631488 | tf_op jit(solution)/shard_map/ri,ro->io/dot_general | solution.py:1109
  402.6 6.6 multiply_reduce_fusion
  409.1 7.3 fusion.56
  421.4 6.8 convolution_convert_fusion.1
  428.2 5.4 convolution_convert_fusion.6
  433.7 9.6 %mixer_gate_back.3 = (bf16[3,512,1536]{2,1,0:T(8,128)(2,1)}, bf16[3,512,1536]{2,1,0:T(8,128)(2,1)}, bf16[3,4,128,1536]{3,2,1,0:T(8,128)(2,1)}, f32[3,4,8,128]{3,...) custom-call(bf16[3,512,1536]{2,1,0:T(8,128)(2,1)} %bitcast.183, ...), custom_call_target="tpu_custom_call" | custom-call | tf_op jit(solution)/shard_map/mixer_gate_back/pallas_call | solution.py:770
  444.0 10.0 %mixer_gate_back.4 = (bf16[3,512,1536]{2,1,0:T(8,128)(2,1)}, bf16[3,512,1536]{2,1,0:T(8,128)(2,1)}, bf16[3,4,128,1536]{3,2,1,0:T(8,128)(2,1)}, f32[3,4,8,128]{3,...) custom-call(bf16[3,512,1536]{2,1,0:T(8,128)(2,1)} %bitcast.184, ...), custom_call_target="tpu_custom_call", output_to_operand_aliasing={{0}: (8, {}), {1}: (9, {}), {2}: (10, {}), {3}: (11, {})} | custom-call | tf_op jit(solution)/shard_map/mixer_gate_back/pallas_call | solution.py:770
  455.0 9.5 %mixer_gate_back.5 = (bf16[3,512,1536]{2,1,0:T(8,128)(2,1)}, bf16[3,512,1536]{2,1,0:T(8,128)(2,1)}, bf16[3,4,128,1536]{3,2,1,0:T(8,128)(2,1)}, f32[3,4,8,128]{3,...) custom-call(bf16[3,512,1536]{2,1,0:T(8,128)(2,1)} %bitcast.185, ...), custom_call_target="tpu_custom_call", output_to_operand_aliasing={{0}: (8, {}), {1}: (9, {}), {2}: (10, {}), {3}: (11, {})} | custom-call | tf_op jit(solution)/shard_map/mixer_gate_back/pallas_call | solution.py:770
  474.0 5.6 convolution_convert_fusion.5
  487.2 13.8 %attend_back.3 = (bf16[1,512,512]{2,1,0:T(8,128)(2,1)}, bf16[4,1,512,256]{3,2,1,0:T(8,128)(2,1)}) custom-call(s32[6]{0:T(128)} %and_select_fusion.1.low_ref, s32[6]{0:T(128)} %reshape.286.high_ref, s32[1]{0:T(128)} %bitcast.7.base_ref, bf16[3,512,512]{2,1,0:T(8,128)(2,1)} %bitcast.174, bf16[4,3,512,256]{3,2,1,0:T(8,128)(2,1)} %copy-done, ...), custom_call_target="tpu_custom_call" | custom-call | tf_op jit(solution)/shard_map/attend_back/pallas_call | solution.py:334
  505.8 13.3 %attend_back.4 = (bf16[1,512,512]{2,1,0:T(8,128)(2,1)}, bf16[4,1,512,256]{3,2,1,0:T(8,128)(2,1)}) custom-call(s32[6]{0:T(128)} %and_select_fusion.1.low_ref, s32[6]{0:T(128)} %reshape.286.high_ref, s32[1]{0:T(128)} %bitcast.7.base_ref, bf16[3,512,512]{2,1,0:T(8,128)(2,1)} %bitcast.175, bf16[4,3,512,256]{3,2,1,0:T(8,128)(2,1)} %copy-done, ...), custom_call_target="tpu_custom_call" | custom-call | tf_op jit(solution)/shard_map/attend_back/pallas_call | solution.py:334
  519.1 13.4 %attend_back.5 = (bf16[1,512,512]{2,1,0:T(8,128)(2,1)}, bf16[4,1,512,256]{3,2,1,0:T(8,128)(2,1)}) custom-call(s32[6]{0:T(128)} %and_select_fusion.1.low_ref, s32[6]{0:T(128)} %reshape.286.high_ref, s32[1]{0:T(128)} %bitcast.7.base_ref, bf16[3,512,512]{2,1,0:T(8,128)(2,1)} %bitcast.176, bf16[4,3,512,256]{3,2,1,0:T(8,128)(2,1)} %copy-done, ...), custom_call_target="tpu_custom_call" | custom-call | tf_op jit(solution)/shard_map/attend_back/pallas_call | solution.py:334
  532.5 3.5 pad_maximum_fusion.7
  536.0 13.3 %collective-permute-done.16 = bf16[1,128,1536]{2,1,0:T(8,128)(2,1)S(1)} collective-permute-done((bf16[1,128,1536]{2,1,0:T(8,128)(2,1)S(1)}, bf16[1,128,1536]{2,1,0:T(8,128)(2,1)S(1)}, u32[]{:S(2)}, u32[]{:S(2)}) %collective-permute-start.16) | collective-permute-done | bytes 393248 | tf_op jit(solution)/shard_map/ppermute | solution.py:917
  550.1 16.6 %collective-permute-done.17 = bf16[1,128,1536]{2,1,0:T(8,128)(2,1)S(1)} collective-permute-done((bf16[1,128,1536]{2,1,0:T(8,128)(2,1)S(1)}, bf16[1,128,1536]{2,1,0:T(8,128)(2,1)S(1)}, u32[]{:S(2)}, u32[]{:S(2)}) %collective-permute-start.17) | collective-permute-done | bytes 393248 | tf_op jit(solution)/shard_map/ppermute | solution.py:917
  567.5 3.4 collective-permute-done.18
  571.7 40.6 %all-to-all-start.2 = ((bf16[4,3,512,256]{3,2,1,0:T(8,128)(2,1)}), bf16[4,3,512,256]{3,2,1,0:T(8,128)(2,1)S(1)}, u32[]{:S(2)}, u32[]{:S(2)}) async-start(bf16[4,3,512,256]{3,2,1,0:T(8,128)(2,1)} %pad_maximum_fusion.7), calls=%async_computation.4 | async-start | bytes 6291456 | tf_op jit(solution)/shard_map/all_to_all | solution.py:992
  612.3 24.1 %mixer_back.3 = (bf16[3,512,1920]{2,1,0:T(8,128)(2,1)}, f32[1,8,1792]{2,1,0:T(8,128)}, f32[8,1792]{1,0:T(8,128)}, f32[8,128]{1,0:T(8,128)}) custom-call(bf16[3,512,1536]{2,1,0:T(8,128)(2,1)} %get-tuple-element.206.refs_0_, f32[3,512,1536]{2,1,0:T(8,128)} %get-tuple-element.170.refs_1_, f32[3,512,768]{2,1,0:T(8,128)} %get-tuple-element.137.refs_1_.refs_3_.refs_2_, ...), custom_call_target="tpu_custom_call" | custom-call | tf_op jit(solution)/shard_map/mixer_back/pallas_call | solution.py:770
  647.7 24.5 %mixer_back.4 = (bf16[3,512,1920]{2,1,0:T(8,128)(2,1)}, f32[1,8,1792]{2,1,0:T(8,128)}, f32[8,1792]{1,0:T(8,128)}, f32[8,128]{1,0:T(8,128)}) custom-call(bf16[3,512,1536]{2,1,0:T(8,128)(2,1)} %get-tuple-element.206.refs_0_, f32[3,512,1536]{2,1,0:T(8,128)} %get-tuple-element.170.refs_1_, ...), custom_call_target="tpu_custom_call", output_to_operand_aliasing={{0}: (20, {})} | custom-call | tf_op jit(solution)/shard_map/mixer_back/pallas_call | solution.py:770
  672.3 24.1 %mixer_back.5 = (bf16[3,512,1920]{2,1,0:T(8,128)(2,1)}, f32[1,8,1792]{2,1,0:T(8,128)}, f32[8,1792]{1,0:T(8,128)}, f32[8,128]{1,0:T(8,128)}) custom-call(bf16[3,512,1536]{2,1,0:T(8,128)(2,1)} %get-tuple-element.206.refs_0_, f32[3,512,1536]{2,1,0:T(8,128)} %get-tuple-element.170.refs_1_, ...), custom_call_target="tpu_custom_call", output_to_operand_aliasing={{0}: (20, {})} | custom-call | tf_op jit(solution)/shard_map/mixer_back/pallas_call | solution.py:770
  698.7 4.7 convolution_convert_fusion.8
  703.4 4.0 collective-permute-done.19
  708.4 8.7 %all-to-all-done.2.dkv_ref = bf16[4,3,512,256]{3,2,1,0:T(8,128)(2,1)S(1)} async-done(((bf16[4,3,512,256]{3,2,1,0:T(8,128)(2,1)}), bf16[4,3,512,256]{3,2,1,0:T(8,128)(2,1)S(1)}, u32[]{:S(2)}, u32[]{:S(2)}) %all-to-all-start.2) | async-done | bytes 3145760 | tf_op jit(solution)/shard_map/all_to_all | solution.py:992
  719.1 10.2 %convolution_convert_fusion.4 = bf16[1024,1920]{1,0:T(8,128)(2,1)S(1)} fusion(bf16[1536,1024]{1,0:T(8,128)(2,1)} %get-tuple-element.187, bf16[1536,1920]{1,0:T(8,128)(2,1)} %bitcast.177), kind=kOutput, calls=%fused_computation.33 | convolution fusion | flops 6041763840 | bytes 12976128 | tf_op jit(solution)/shard_map/ri,ro->io/dot_general | solution.py:1109
  735.3 9.6 %all-to-all-start.3 = ((f32[8,3,24]{2,1,0:T(4,128)}), f32[8,3,24]{2,1,0:T(4,128)S(1)}, u32[]{:S(2)}, u32[]{:S(2)}) async-start(f32[8,3,24]{2,1,0:T(4,128)} %broadcast_in_dim.87), calls=%async_computation.8 | async-start | bytes 32768 | tf_op jit(solution)/shard_map/all_to_all | solution.py:938
  745.0 4.7 all-to-all-done.3
  750.3 4.6 all-to-all-start.4
  755.3 5.2 all-to-all-done.4
  761.1 23.4 %finish.1 = (bf16[1536,1024]{1,0:T(8,128)(2,1)}, bf16[1536,256]{1,0:T(8,128)(2,1)}, f32[8,1024]{1,0:T(8,128)}) custom-call(bf16[1536,1024]{1,0:T(8,128)(2,1)} %bitcast.198, f32[1,1024]{1,0:T(1,128)} %reshape.287.gain_ref, bf16[1536,1536]{1,0:T(8,128)(2,1)} %bitcast.179, bf16[1536,1920]{1,0:T(8,128)(2,1)} %bitcast.178, bf16[1536,512]{1,0:T(8,128)(2,1)} %bitcast.204, ...), custom_call_target="tpu_custom_call" | custom-call | tf_op jit(solution)/shard_map/finish/pallas_call | solution.py:136
  785.8 3.2 convolution_convert_fusion.10
  793.5 6.5 collective-permute-done.21
  801.6 3.2 collective-permute-done.22
  805.8 3.2 collective-permute-start.25
  809.0 12.1 %add_convert_fusion = bf16[1536,1024]{1,0:T(8,128)(2,1)} fusion(f32[1536,1024]{1,0:T(8,128)} %get-tuple-element.303, bf16[1536,2048]{1,0:T(8,128)(2,1)} %get-tuple-element.217, bf16[2048,1024]{1,0:T(8,128)(2,1)} %bitcast.206), kind=kOutput, calls=%fused_computation.26 | convolution fusion | flops 6445596672 | bytes 19922944 | tf_op jit(solution)/shard_map/dot_general | solution.py:981
  825.3 4.9 reduce-scatter.14.cloned.1.call-done
  (388 shorter events, 140.6 us)
Async XLA Ops:
  7.2 40.5 %all-gather.4.cloned.1.call-start = ((), (), s32[]{:S(2)}) async-start(), calls=%async_computation.10 | async-start | bytes 1392640 | tf_op jit(solution)/shard_map/all_gather | solution.py:997
  15.9 89.9 %all-gather.6.cloned.1.call-start = ((), (), s32[]{:S(2)}) async-start(), calls=%async_computation.11 | async-start | bytes 10027008 | tf_op jit(solution)/shard_map/all_gather | solution.py:994
  48.0 173.8 %all-gather.8.cloned.1.call-start = ((), (), s32[]{:S(2)}) async-start(), calls=%async_computation.12 | async-start | bytes 18874368 | tf_op jit(solution)/shard_map/all_gather | solution.py:994
  106.9 24.2 %copy-start.38 = (f32[32,4096]{1,0:T(8,128)}, f32[32,4096]{1,0:T(8,128)S(1)}, u32[]{:S(2)}) copy-start(f32[32,4096]{1,0:T(8,128)S(1)} %reshape.334) | copy-start | bytes 1572868
  108.3 20.5 %copy-start.49 = (s32[3,2048]{1,0:T(4,128)S(1)}, s32[3,2048]{1,0:T(4,128)}, u32[]{:S(2)}) copy-start(s32[3,2048]{1,0:T(4,128)} %param.20) | copy-start | bytes 73732
  125.4 7.3 collective-permute-start
  135.8 101.4 %all-to-all-start.1 = ((bf16[4,3,512,256]{3,2,1,0:T(8,128)(2,1)}), bf16[4,3,512,256]{3,2,1,0:T(8,128)(2,1)S(1)}, u32[]{:S(2)}, u32[]{:S(2)}) async-start(bf16[4,3,512,256]{3,2,1,0:T(8,128)(2,1)} %broadcast_in_dim.84), calls=%async_computation.1 | async-start | bytes 6291456 | tf_op jit(solution)/shard_map/all_to_all | solution.py:992
  139.5 472.8 %reduce-scatter.8.cloned.1.call-start = ((), (), s32[]{:S(2)}) async-start(), calls=%async_computation.14 | async-start | bytes 9437184 | tf_op jit(solution)/shard_map/reduce_scatter | solution.py:1106
  139.7 14.1 %copy-start.59 = (bf16[1536,1024]{1,0:T(8,128)(2,1)S(1)}, bf16[1536,1024]{1,0:T(8,128)(2,1)}, u32[]{:S(2)}) copy-start(bf16[1536,1024]{1,0:T(8,128)(2,1)} %get-tuple-element.187) | copy-start | bytes 9437188
  150.0 49.9 %collective-permute-start.7 = (bf16[1,128,1536]{2,1,0:T(8,128)(2,1)}, bf16[1,128,1536]{2,1,0:T(8,128)(2,1)S(1)}, u32[]{:S(2)}, u32[]{:S(2)}) collective-permute-start(bf16[1,128,1536]{2,1,0:T(8,128)(2,1)} %get-tuple-element.158), channel_id=1, source_target_pairs={{0,1},{4,5},{8,9},{12,13},{16,17},{20,21},{24,25},{28,29}} | collective-permute-start | bytes 1179656 | tf_op jit(solution)/shard_map/ppermute | solution.py:917
  174.0 34.3 %collective-permute-start.4 = (bf16[1,128,1536]{2,1,0:T(8,128)(2,1)}, bf16[1,128,1536]{2,1,0:T(8,128)(2,1)S(1)}, u32[]{:S(2)}, u32[]{:S(2)}) collective-permute-start(bf16[1,128,1536]{2,1,0:T(8,128)(2,1)} %get-tuple-element.155), channel_id=1, source_target_pairs={{0,1},{4,5},{8,9},{12,13},{16,17},{20,21},{24,25},{28,29}} | collective-permute-start | bytes 1179656 | tf_op jit(solution)/shard_map/ppermute | solution.py:917
  175.3 24.6 %copy-start.30 = (bf16[1,128,1536]{2,1,0:T(8,128)(2,1)S(1)}, bf16[1,128,1536]{2,1,0:T(8,128)(2,1)}, u32[]{:S(2)}) copy-start(bf16[1,128,1536]{2,1,0:T(8,128)(2,1)} %get-tuple-element.158) | copy-start | bytes 1179652
  175.3 33.0 %copy-start.31 = (bf16[1,128,1536]{2,1,0:T(8,128)(2,1)S(1)}, bf16[1,128,1536]{2,1,0:T(8,128)(2,1)}, u32[]{:S(2)}) copy-start(bf16[1,128,1536]{2,1,0:T(8,128)(2,1)} %get-tuple-element.155) | copy-start | bytes 1179652
  184.6 36.2 %copy-start.32 = (bf16[1,128,1536]{2,1,0:T(8,128)(2,1)S(1)}, bf16[1,128,1536]{2,1,0:T(8,128)(2,1)}, u32[]{:S(2)}) copy-start(bf16[1,128,1536]{2,1,0:T(8,128)(2,1)} %get-tuple-element.142) | copy-start | bytes 1179652
  184.6 31.4 %collective-permute-start.1 = (bf16[1,128,1536]{2,1,0:T(8,128)(2,1)}, bf16[1,128,1536]{2,1,0:T(8,128)(2,1)S(1)}, u32[]{:S(2)}, u32[]{:S(2)}) collective-permute-start(bf16[1,128,1536]{2,1,0:T(8,128)(2,1)} %get-tuple-element.142), channel_id=1, source_target_pairs={{0,1},{4,5},{8,9},{12,13},{16,17},{20,21},{24,25},{28,29}} | collective-permute-start | bytes 1179656 | tf_op jit(solution)/shard_map/ppermute | solution.py:917
  187.1 32.9 %copy-start.44 = (f32[1536]{0:T(1024)}, f32[1536]{0:T(1024)S(1)}, u32[]{:S(2)}) copy-start(f32[1536]{0:T(1024)S(1)} %slice_reduce_fusion.4) | copy-start | bytes 18436
  188.0 32.1 %copy-start.42 = (f32[1536]{0:T(1024)}, f32[1536]{0:T(1024)S(1)}, u32[]{:S(2)}) copy-start(f32[1536]{0:T(1024)S(1)} %slice_reduce_fusion.5) | copy-start | bytes 18436
  188.8 31.2 %copy-start.46 = (f32[1536]{0:T(1024)}, f32[1536]{0:T(1024)S(1)}, u32[]{:S(2)}) copy-start(f32[1536]{0:T(1024)S(1)} %slice_reduce_fusion.6) | copy-start | bytes 18436
  200.0 18.0 %collective-permute-start.8 = (bf16[1,128,1536]{2,1,0:T(8,128)(2,1)S(1)}, bf16[1,128,1536]{2,1,0:T(8,128)(2,1)S(1)}, u32[]{:S(2)}, u32[]{:S(2)}) collective-permute-start(bf16[1,128,1536]{2,1,0:T(8,128)(2,1)S(1)} %fusion.17), channel_id=1, source_target_pairs={{1,2},{5,6},{9,10},{13,14},{17,18},{21,22},{25,26},{29,30}} | collective-permute-start | bytes 1179656 | tf_op jit(solution)/shard_map/ppermute | solution.py:917
  208.3 10.7 %copy-start.6 = (bf16[1,128,1536]{2,1,0:T(8,128)(2,1)}, bf16[1,128,1536]{2,1,0:T(8,128)(2,1)S(1)}, u32[]{:S(2)}) copy-start(bf16[1,128,1536]{2,1,0:T(8,128)(2,1)S(1)} %collective-permute-done.4) | copy-start | bytes 1179652
  208.4 10.6 %collective-permute-start.5 = (bf16[1,128,1536]{2,1,0:T(8,128)(2,1)S(1)}, bf16[1,128,1536]{2,1,0:T(8,128)(2,1)S(1)}, u32[]{:S(2)}, u32[]{:S(2)}) collective-permute-start(bf16[1,128,1536]{2,1,0:T(8,128)(2,1)S(1)} %fusion.15), channel_id=1, source_target_pairs={{1,2},{5,6},{9,10},{13,14},{17,18},{21,22},{25,26},{29,30}} | collective-permute-start | bytes 1179656 | tf_op jit(solution)/shard_map/ppermute | solution.py:917
  217.3 2.7 collective-permute-start.2
  221.8 12.1 %copy-start.1 = (bf16[8192,1024]{1,0:T(8,128)(2,1)S(1)}, bf16[8192,1024]{1,0:T(8,128)(2,1)}, u32[]{:S(2)}) copy-start(bf16[8192,1024]{1,0:T(8,128)(2,1)} %all-gather.8.cloned.1.call-done) | copy-start | bytes 50331652
  246.3 23.3 %collective-permute-start.9 = (bf16[1,128,1536]{2,1,0:T(8,128)(2,1)}, bf16[1,128,1536]{2,1,0:T(8,128)(2,1)S(1)}, u32[]{:S(2)}, u32[]{:S(2)}) collective-permute-start(bf16[1,128,1536]{2,1,0:T(8,128)(2,1)} %fusion.18), channel_id=1, source_target_pairs={{2,3},{6,7},{10,11},{14,15},{18,19},{22,23},{26,27},{30,31}} | collective-permute-start | bytes 1179656 | tf_op jit(solution)/shard_map/ppermute | solution.py:917
  255.0 24.1 %collective-permute-start.6 = (bf16[1,128,1536]{2,1,0:T(8,128)(2,1)S(1)}, bf16[1,128,1536]{2,1,0:T(8,128)(2,1)S(1)}, u32[]{:S(2)}, u32[]{:S(2)}) collective-permute-start(bf16[1,128,1536]{2,1,0:T(8,128)(2,1)S(1)} %copy-done.41), channel_id=1, source_target_pairs={{2,3},{6,7},{10,11},{14,15},{18,19},{22,23},{26,27},{30,31}} | collective-permute-start | bytes 1179656 | tf_op jit(solution)/shard_map/ppermute | solution.py:917
  263.2 25.3 %collective-permute-start.3 = (bf16[1,128,1536]{2,1,0:T(8,128)(2,1)S(1)}, bf16[1,128,1536]{2,1,0:T(8,128)(2,1)S(1)}, u32[]{:S(2)}, u32[]{:S(2)}) collective-permute-start(bf16[1,128,1536]{2,1,0:T(8,128)(2,1)S(1)} %copy-done.40), channel_id=1, source_target_pairs={{2,3},{6,7},{10,11},{14,15},{18,19},{22,23},{26,27},{30,31}} | collective-permute-start | bytes 1179656 | tf_op jit(solution)/shard_map/ppermute | solution.py:917
  308.9 20.9 %copy-start.10 = (bf16[3,512,1024]{2,1,0:T(8,128)(2,1)S(1)}, bf16[3,512,1024]{2,1,0:T(8,128)(2,1)}, u32[]{:S(2)}) copy-start(bf16[3,512,1024]{2,1,0:T(8,128)(2,1)} %param.37) | copy-start | bytes 9437188
  329.8 19.1 %copy-start.16 = (bf16[32,32,1024]{2,1,0:T(8,128)(2,1)S(1)}, bf16[32,32,1024]{2,1,0:T(8,128)(2,1)}, u32[]{:S(2)}) copy-start(bf16[32,32,1024]{2,1,0:T(8,128)(2,1)} %get-tuple-element.259) | copy-start | bytes 6291460
  329.8 19.1 %copy-start.17 = (bf16[32,32,1024]{2,1,0:T(8,128)(2,1)S(1)}, bf16[32,32,1024]{2,1,0:T(8,128)(2,1)}, u32[]{:S(2)}) copy-start(bf16[32,32,1024]{2,1,0:T(8,128)(2,1)} %get-tuple-element.260) | copy-start | bytes 6291460
  329.9 19.1 %copy-start.18 = (bf16[32,32,1024]{2,1,0:T(8,128)(2,1)S(1)}, bf16[32,32,1024]{2,1,0:T(8,128)(2,1)}, u32[]{:S(2)}) copy-start(bf16[32,32,1024]{2,1,0:T(8,128)(2,1)} %get-tuple-element.261) | copy-start | bytes 6291460
  402.5 233.9 %reduce-scatter.6.cloned.1.call-start = ((), (), s32[]{:S(2)}) async-start(), calls=%async_computation.13 | async-start | bytes 12976128 | tf_op jit(solution)/shard_map/reduce_scatter | solution.py:1106
  443.3 21.2 %collective-permute-start.10 = (bf16[1,128,1536]{2,1,0:T(8,128)(2,1)}, bf16[1,128,1536]{2,1,0:T(8,128)(2,1)S(1)}, u32[]{:S(2)}, u32[]{:S(2)}) collective-permute-start(bf16[1,128,1536]{2,1,0:T(8,128)(2,1)} %get-tuple-element.180), channel_id=1, source_target_pairs={{3,2},{7,6},{11,10},{15,14},{19,18},{23,22},{27,26},{31,30}} | collective-permute-start | bytes 1179656 | tf_op jit(solution)/shard_map/ppermute | solution.py:917
  454.0 10.7 %collective-permute-start.11 = (bf16[1,128,1536]{2,1,0:T(8,128)(2,1)}, bf16[1,128,1536]{2,1,0:T(8,128)(2,1)S(1)}, u32[]{:S(2)}, u32[]{:S(2)}) collective-permute-start(bf16[1,128,1536]{2,1,0:T(8,128)(2,1)} %get-tuple-element.181), channel_id=1, source_target_pairs={{3,2},{7,6},{11,10},{15,14},{19,18},{23,22},{27,26},{31,30}} | collective-permute-start | bytes 1179656 | tf_op jit(solution)/shard_map/ppermute | solution.py:917
  483.5 0.7 collective-permute-start.12
  485.1 15.9 %collective-permute-start.15 = (bf16[1,128,1536]{2,1,0:T(8,128)(2,1)}, bf16[1,128,1536]{2,1,0:T(8,128)(2,1)S(1)}, u32[]{:S(2)}, u32[]{:S(2)}) collective-permute-start(bf16[1,128,1536]{2,1,0:T(8,128)(2,1)} %get-tuple-element.247), channel_id=1, source_target_pairs={{2,1},{6,5},{10,9},{14,13},{18,17},{22,21},{26,25},{30,29}} | collective-permute-start | bytes 1179656 | tf_op jit(solution)/shard_map/ppermute | solution.py:917
  485.8 16.8 %collective-permute-start.13 = (bf16[1,128,1536]{2,1,0:T(8,128)(2,1)S(1)}, bf16[1,128,1536]{2,1,0:T(8,128)(2,1)S(1)}, u32[]{:S(2)}, u32[]{:S(2)}) collective-permute-start(bf16[1,128,1536]{2,1,0:T(8,128)(2,1)S(1)} %get-tuple-element.251), channel_id=1, source_target_pairs={{2,1},{6,5},{10,9},{14,13},{18,17},{22,21},{26,25},{30,29}} | collective-permute-start | bytes 1179656 | tf_op jit(solution)/shard_map/ppermute | solution.py:917
  486.5 16.3 %collective-permute-start.14 = (bf16[1,128,1536]{2,1,0:T(8,128)(2,1)S(1)}, bf16[1,128,1536]{2,1,0:T(8,128)(2,1)S(1)}, u32[]{:S(2)}, u32[]{:S(2)}) collective-permute-start(bf16[1,128,1536]{2,1,0:T(8,128)(2,1)S(1)} %get-tuple-element.249), channel_id=1, source_target_pairs={{2,1},{6,5},{10,9},{14,13},{18,17},{22,21},{26,25},{30,29}} | collective-permute-start | bytes 1179656 | tf_op jit(solution)/shard_map/ppermute | solution.py:917
  487.2 13.9 %copy-start.48 = (f32[1536]{0:T(1024)S(1)}, f32[1536]{0:T(1024)}, u32[]{:S(2)}) copy-start(f32[1536]{0:T(1024)} %copy-done.46) | copy-start | bytes 18436
  501.3 48.0 %collective-permute-start.16 = (bf16[1,128,1536]{2,1,0:T(8,128)(2,1)S(1)}, bf16[1,128,1536]{2,1,0:T(8,128)(2,1)S(1)}, u32[]{:S(2)}, u32[]{:S(2)}) collective-permute-start(bf16[1,128,1536]{2,1,0:T(8,128)(2,1)S(1)} %get-tuple-element.199), channel_id=1, source_target_pairs={{1,0},{5,4},{9,8},{13,12},{17,16},{21,20},{25,24},{29,28}} | collective-permute-start | bytes 1179656 | tf_op jit(solution)/shard_map/ppermute | solution.py:917
  503.0 63.7 %collective-permute-start.17 = (bf16[1,128,1536]{2,1,0:T(8,128)(2,1)S(1)}, bf16[1,128,1536]{2,1,0:T(8,128)(2,1)S(1)}, u32[]{:S(2)}, u32[]{:S(2)}) collective-permute-start(bf16[1,128,1536]{2,1,0:T(8,128)(2,1)S(1)} %get-tuple-element.200), channel_id=1, source_target_pairs={{1,0},{5,4},{9,8},{13,12},{17,16},{21,20},{25,24},{29,28}} | collective-permute-start | bytes 1179656 | tf_op jit(solution)/shard_map/ppermute | solution.py:917
  504.3 66.6 %collective-permute-start.18 = (bf16[1,128,1536]{2,1,0:T(8,128)(2,1)S(1)}, bf16[1,128,1536]{2,1,0:T(8,128)(2,1)S(1)}, u32[]{:S(2)}, u32[]{:S(2)}) collective-permute-start(bf16[1,128,1536]{2,1,0:T(8,128)(2,1)S(1)} %get-tuple-element.201), channel_id=1, source_target_pairs={{1,0},{5,4},{9,8},{13,12},{17,16},{21,20},{25,24},{29,28}} | collective-permute-start | bytes 1179656 | tf_op jit(solution)/shard_map/ppermute | solution.py:917
  519.1 13.4 %copy-start.36 = (bf16[4,1,512,256]{3,2,1,0:T(8,128)(2,1)S(1)}, bf16[4,1,512,256]{3,2,1,0:T(8,128)(2,1)}, u32[]{:S(2)}) copy-start(bf16[4,1,512,256]{3,2,1,0:T(8,128)(2,1)} %get-tuple-element.212) | copy-start | bytes 3145732
  519.1 13.4 %copy-start.37 = (bf16[4,1,512,256]{3,2,1,0:T(8,128)(2,1)S(1)}, bf16[4,1,512,256]{3,2,1,0:T(8,128)(2,1)}, u32[]{:S(2)}) copy-start(bf16[4,1,512,256]{3,2,1,0:T(8,128)(2,1)} %get-tuple-element.213) | copy-start | bytes 3145732
  571.7 145.5 %all-to-all-start.2 = ((bf16[4,3,512,256]{3,2,1,0:T(8,128)(2,1)}), bf16[4,3,512,256]{3,2,1,0:T(8,128)(2,1)S(1)}, u32[]{:S(2)}, u32[]{:S(2)}) async-start(bf16[4,3,512,256]{3,2,1,0:T(8,128)(2,1)} %pad_maximum_fusion.7), calls=%async_computation.4 | async-start | bytes 6291456 | tf_op jit(solution)/shard_map/all_to_all | solution.py:992
  612.3 148.9 %reduce-scatter.12.cloned.1.call-start = ((), (), s32[]{:S(2)}) async-start(), calls=%async_computation.16 | async-start | bytes 3112960 | tf_op jit(solution)/shard_map/reduce_scatter | solution.py:1194
  636.4 11.3 %copy-start.53 = (f32[1,8,1792]{2,1,0:T(8,128)S(1)}, f32[1,8,1792]{2,1,0:T(8,128)}, u32[]{:S(2)}) copy-start(f32[1,8,1792]{2,1,0:T(8,128)} %get-tuple-element.204) | copy-start | bytes 172036
  645.7 159.2 %reduce-scatter.10.cloned.1.call-start = ((), (), s32[]{:S(2)}) async-start(), calls=%async_computation.15 | async-start | bytes 5603328 | tf_op jit(solution)/shard_map/reduce_scatter | solution.py:1106
  647.7 51.0 %copy-start.4 = (bf16[3,512,512]{2,1,0:T(8,128)(2,1)}, bf16[3,512,512]{2,1,0:T(8,128)(2,1)S(1)}, u32[]{:S(2)}) copy-start(bf16[3,512,512]{2,1,0:T(8,128)(2,1)S(1)} %pad_maximum_fusion.9) | copy-start | bytes 4718596
  672.3 24.9 %copy-start.54 = (f32[1,8,1792]{2,1,0:T(8,128)S(1)}, f32[1,8,1792]{2,1,0:T(8,128)}, u32[]{:S(2)}) copy-start(f32[1,8,1792]{2,1,0:T(8,128)} %get-tuple-element.210) | copy-start | bytes 172036
  697.2 10.2 %collective-permute-start.19 = (bf16[3,3,1792]{2,1,0:T(4,128)(2,1)S(1)}, bf16[3,3,1792]{2,1,0:T(4,128)(2,1)S(1)}, u32[]{:S(2)}, u32[]{:S(2)}) collective-permute-start(bf16[3,3,1792]{2,1,0:T(4,128)(2,1)S(1)} %pad_maximum_fusion.15), channel_id=1, source_target_pairs={{1,0},{2,1},{3,2},{5,4},{6,5},{7,6},{9,8},{10,9},{11,10},{13,12},{... | collective-permute-start | bytes 96776 | tf_op jit(solution)/shard_map/ppermute | solution.py:894
  717.1 12.2 %copy-start.2 = (bf16[4,3,512,256]{3,2,1,0:T(8,128)(2,1)}, bf16[4,3,512,256]{3,2,1,0:T(8,128)(2,1)S(1)}, u32[]{:S(2)}) copy-start(bf16[4,3,512,256]{3,2,1,0:T(8,128)(2,1)S(1)} %all-to-all-done.2.dkv_ref) | copy-start | bytes 9437188
  719.1 10.2 %copy-start.33 = (bf16[1024,512]{1,0:T(8,128)(2,1)S(1)}, bf16[1024,512]{1,0:T(8,128)(2,1)}, u32[]{:S(2)}) copy-start(bf16[1024,512]{1,0:T(8,128)(2,1)} %convolution_convert_fusion.8) | copy-start | bytes 3145732
  731.9 13.0 %copy-start.50 = (f32[8,1792]{1,0:T(8,128)S(1)}, f32[8,1792]{1,0:T(8,128)}, u32[]{:S(2)}) copy-start(f32[8,1792]{1,0:T(8,128)} %get-tuple-element.225) | copy-start | bytes 172036
  731.9 13.0 %copy-start.51 = (f32[8,1792]{1,0:T(8,128)S(1)}, f32[8,1792]{1,0:T(8,128)}, u32[]{:S(2)}) copy-start(f32[8,1792]{1,0:T(8,128)} %get-tuple-element.226) | copy-start | bytes 172036
  731.9 13.0 %copy-start.52 = (f32[8,1792]{1,0:T(8,128)S(1)}, f32[8,1792]{1,0:T(8,128)}, u32[]{:S(2)}) copy-start(f32[8,1792]{1,0:T(8,128)} %get-tuple-element.227) | copy-start | bytes 172036
  735.3 14.3 %all-to-all-start.3 = ((f32[8,3,24]{2,1,0:T(4,128)}), f32[8,3,24]{2,1,0:T(4,128)S(1)}, u32[]{:S(2)}, u32[]{:S(2)}) async-start(f32[8,3,24]{2,1,0:T(4,128)} %broadcast_in_dim.87), calls=%async_computation.8 | async-start | bytes 32768 | tf_op jit(solution)/shard_map/all_to_all | solution.py:938
  750.3 10.2 %all-to-all-start.4 = ((f32[4,3,24]{2,1,0:T(4,128)}), f32[4,3,24]{2,1,0:T(4,128)S(1)}, u32[]{:S(2)}, u32[]{:S(2)}) async-start(f32[4,3,24]{2,1,0:T(4,128)} %broadcast_in_dim.88), calls=%async_computation.9 | async-start | bytes 16384 | tf_op jit(solution)/shard_map/all_to_all | solution.py:938
  754.9 75.2 %reduce-scatter.14.cloned.1.call-start = ((), (), s32[]{:S(2)}) async-start(), calls=%async_computation.17 | async-start | bytes 778240 | tf_op jit(solution)/shard_map/reduce_scatter | solution.py:1199
  789.4 3.0 collective-permute-start.20
  792.6 7.4 collective-permute-start.21
  800.1 4.7 collective-permute-start.22
  804.9 16.2 %collective-permute-start.23 = (bf16[32,384]{1,0:T(8,128)(2,1)S(1)}, bf16[32,384]{1,0:T(8,128)(2,1)S(1)}, u32[]{:S(2)}, u32[]{:S(2)}) collective-permute-start(bf16[32,384]{1,0:T(8,128)(2,1)S(1)} %get-tuple-element.281), channel_id=1, source_target_pairs={{0,1},{1,2},{2,3},{3,0},{4,5},{5,6},{6,7},{7,4},{8,9},{9,10},{10,1... | collective-permute-start | bytes 73736 | tf_op jit(solution)/shard_map/ppermute | solution.py:958
  805.8 15.3 %collective-permute-start.25 = (bf16[32,384]{1,0:T(8,128)(2,1)S(1)}, bf16[32,384]{1,0:T(8,128)(2,1)S(1)}, u32[]{:S(2)}, u32[]{:S(2)}) collective-permute-start(bf16[32,384]{1,0:T(8,128)(2,1)S(1)} %get-tuple-element.282), channel_id=1, source_target_pairs={{0,3},{1,0},{2,1},{3,2},{4,7},{5,4},{6,5},{7,6},{8,11},{9,8},{10,9... | collective-permute-start | bytes 73736 | tf_op jit(solution)/shard_map/ppermute | solution.py:958
  809.0 12.1 %collective-permute-start.24 = (bf16[32,384]{1,0:T(8,128)(2,1)S(1)}, bf16[32,384]{1,0:T(8,128)(2,1)S(1)}, u32[]{:S(2)}, u32[]{:S(2)}) collective-permute-start(bf16[32,384]{1,0:T(8,128)(2,1)S(1)} %get-tuple-element.283), channel_id=1, source_target_pairs={{0,2},{1,3},{2,0},{3,1},{4,6},{5,7},{6,4},{7,5},{8,10},{9,11},{10,... | collective-permute-start | bytes 73736 | tf_op jit(solution)/shard_map/ppermute | solution.py:958
  (39 other events, 214.7 us)
Sparse Core Ops, SparseCore 0:
  16.0 31.6 all-gather.3
  49.6 56.1 all-gather.5
  107.7 89.8 all-gather.7
  402.6 100.7 reduce-scatter.7
  507.2 97.7 reduce-scatter.5
  645.8 73.7 reduce-scatter.11
  732.1 62.0 reduce-scatter.9
  809.1 21.0 reduce-scatter.13

commit v8 on v7

--- a/solution.py
+++ b/solution.py
@@ -62,26 +62,29 @@
     for group in range(KVH):
         at = QH * HD + group * 128
         part = lin[:, at : at + 128]
-        kv_ref[:, group * 128 : (group + 1) * 128] = (
-            part * cosine + swap_halves(part) * sine
-        ).astype(BF16)
+        turned = (part * cosine + swap_halves(part) * sine).astype(BF16)
+        for copy in range(kv_ref.shape[0]):
+            kv_ref[copy, :, group * 128 : (group + 1) * 128] = turned
     cr_ref[...] = contract(hidden, w_ref[:, :CR], 1, 0).astype(BF16)
 
 
-def project(x, gain, w_first, cosine, sine):
+def project(x, gain, w_first, cosine, sine, copies):
     rows, width = x.shape
     tile = 256 if rows % 256 == 0 else 128
     block = lambda cols: pl.BlockSpec((tile, cols), lambda i: (i, 0))
     fixed = lambda array: pl.BlockSpec(array.shape, lambda i: (0, 0))
-    cols = [width, CR, QH * HD, 2 * KVH * HD]
+    cols = [width, CR, QH * HD]
+    kv_width = 2 * KVH * HD
     return pl.pallas_call(
         project_kernel,
         grid=(rows // tile,),
         in_specs=[
             block(width), fixed(gain), fixed(w_first), block(128), block(128),
         ],
-        out_specs=[block(size) for size in cols],
-        out_shape=[jax.ShapeDtypeStruct((rows, size), BF16) for size in cols],
+        out_specs=[block(size) for size in cols]
+        + [pl.BlockSpec((copies, tile, kv_width), lambda i: (0, i, 0))],
+        out_shape=[jax.ShapeDtypeStruct((rows, size), BF16) for size in cols]
+        + [jax.ShapeDtypeStruct((copies, rows, kv_width), BF16)],
         compiler_params=pltpu.CompilerParams(vmem_limit_bytes=VMEM_BYTES),
         name="project",
     )(x, gain, w_first, cosine, sine)
@@ -1050,12 +1053,12 @@
     taps_all = jnp.pad(taps_all, ((0, 8 - KC), (0, 0)))
 
 
-    hidden, cr, q, kv = project(tokens, gain1_all, first_all, cosine, sine)
+    hidden, cr, q, kv = project(tokens, gain1_all, first_all, cosine, sine, count)
     q = q.reshape(seqs, span, q_width)
-    kv = kv.reshape(seqs, span, kv_width)
+    kv = kv.reshape(count, seqs, span, kv_width)
     cr = cr.reshape(seqs, span, CR)
     rim = from_behind(cr[:, span - (KC - 1) :, :CC], "ctx", 1)
-    kv_all = exchange(after(copies(kv), rim))
+    kv_all = exchange(after(kv, rim))
     rim = jnp.pad(rim, ((0, 0), (8 - (KC - 1), 0), (0, 0)))
     scanned, chains, wide_gains = None, [], []
     for seq in range(seqs):
@@ -1240,7 +1243,11 @@
     out_kv = out_first[:, :kv_width].reshape(own_rows, KVH, 2, HD)
     head_grad = sum_everywhere(
         jnp.concatenate(
-            [grad_heads[:2, :MH], grad_skip[0].reshape(MH, MP).sum(axis=1)[None]], axis=0
+            [
+                after(grad_heads, grad_kv)[:2, :MH],
+                grad_skip[0].reshape(MH, MP).sum(axis=1)[None],
+            ],
+            axis=0,
         ),
         axes,
     )

time: 854 us -> 845 us (0.989)
    ppermute x3, waiting for transfers between devices: 9.67 us -> 0.69 us  [scatter_all(): lax.ppermute(sent, 'dp', [(i, i ^ 1 << bit) for i in range(devices)])]
  transfers between devices with their start and end apart: 38 -> 38, of which waited for: 15 -> 14; matrix products, arithmetic and copies ran while one was open for 23% -> 23% of each run, Pallas kernels for 29% -> 29%
where the time goes in v8:
time: 845 us; the launch traced here: 833 us
  Pallas kernels  259 us (31%)
  matrix products  170 us (20%)
  waiting for transfers between devices  99.6 us (12%)
  starting transfers between devices  93.6 us (11%)
  local copies, waits for them, and re-layouts  83.2 us (10%)
  other arithmetic  60.3 us (7%)
  blocking collectives  51.6 us (6%)
  between operations  15.9 us (2%)
    pallas_call x12, Pallas kernels, mixer_call(): pl.pallas_call(run, grid=(chunks,), in_specs=in_specs, out_specs=out_spec...  157 us
    dot_general x8, matrix products, weight_grad(): jnp.einsum('ri,ro->io', left, right, preferred_element_type=F32)  63.9 us
    ppermute x18, waiting for transfers between devices, send(): self.flying = (lax.ppermute(sent, 'ctx', [(source, target)]), target)  61.1 us
    dot_general x5, matrix products, body(): low_dot = lambda a, b: jnp.dot(a, b, preferred_element_type=F32)  55.4 us
    all_to_all x1, blocking collectives, body(): exchange = lambda blocks: lax.all_to_all(blocks, 'ctx', 0, 0, tiled=True)  51.6 us
    dot_general x3, matrix products, back_dot(): return jnp.einsum('ro,io->ri', grad, weight, preferred_element_type=F32)  46.6 us
    all_to_all x2, starting transfers between devices, body(): exchange = lambda blocks: lax.all_to_all(blocks, 'ctx', 0, 0, tiled=True)  41.8 us
    pallas_call x3, Pallas kernels, attend_back(): pl.pallas_call(functools.partial(attend_back_kernel, seq * (span // rows)...  40.1 us
  transfers between devices with their start and end apart: 38, of which 14 were waited for; matrix products, arithmetic and copies ran while one was open for 23% of the time, Pallas kernels for 29%

profile of v8, /device:TPU:0, one launch (start us, length us, event | category | flops | bytes accessed | tf_op | source)
XLA Modules:
  0.0 832.9 jit_solution(16339135176449235196)
XLA Ops:
  11.5 2.8 concatenate.96
  31.6 2.8 fusion.29
  37.7 10.0 %all-gather.4.cloned.1.call-done = bf16[128,4352]{1,0:T(8,128)(2,1)} async-done(((bf16[32,4352]{1,0:T(8,128)(2,1)}), bf16[128,4352]{1,0:T(8,128)(2,1)}) %all-gather.4.cloned.1.call-update) | async-done | bytes 1114128 | tf_op jit(solution)/shard_map/all_gather | solution.py:1000
  48.0 51.6 %all_to_all.25 = bf16[4,256,1024]{2,1,0:T(8,128)(2,1)} all-to-all(bf16[4,256,1024]{2,1,0:T(8,128)(2,1)S(1)} %broadcast_in_dim.73), channel_id=1, replica_groups=mesh['dp'=8,'ctx'=4] {'ctx'}, dimensions={0} | all-to-all | bytes 4194304 | tf_op jit(solution)/shard_map/all_to_all | solution.py:995
  99.7 2.8 fusion.30
  108.4 16.4 %project.1 = (bf16[1536,1024]{1,0:T(8,128)(2,1)}, bf16[1536,1920]{1,0:T(8,128)(2,1)}, bf16[1536,512]{1,0:T(8,128)(2,1)}, bf16[4,1536,256]{2,1,0:T(8,128)(2,1)}) custom-call(bf16[1536,1024]{1,0:T(8,128)(2,1)} %bitcast.197, f32[1,1024]{1,0:T(1,128)} %reshape.289.gain_ref, bf16[1024,4352]{1,0:T(8,128)(2,1)} %all-gather.6.cloned.1.call-done.w_ref, ...), custom_call_target="tpu_custom_call" | custom-call | tf_op jit(solution)/shard_map/project/pallas_call | solution.py:78
  125.7 3.4 collective-permute-start
  133.0 3.7 all-to-all-start.1
  137.7 9.5 %mixer_scan.3 = (bf16[3,512,1792]{2,1,0:T(8,128)(2,1)}, bf16[3,4,128,1536]{3,2,1,0:T(8,128)(2,1)}, f32[3,4,8,128]{3,2,1,0:T(8,128)}, bf16[1,128,1536]{2,1,0:T(8,...) custom-call(bf16[3,512,1920]{2,1,0:T(8,128)(2,1)} %bitcast.156, bf16[3,8,1792]{2,1,0:T(8,128)(2,1)} %pad.28.refs_1_.refs_5_, ...), custom_call_target="tpu_custom_call" | custom-call | tf_op jit(solution)/shard_map/mixer_scan/pallas_call | solution.py:773
  147.2 3.9 collective-permute-start.7
  151.1 8.6 %convolution_convert_fusion.2 = bf16[1536,1536]{1,0:T(8,128)(2,1)} fusion(bf16[1536,1024]{1,0:T(8,128)(2,1)S(1)} %copy-done.59, bf16[1024,4352]{1,0:T(8,128)(2,1)} %all-gather.6.cloned.1.call-done.w_ref), kind=kOutput, calls=%fused_computation.22 | convolution fusion | flops 4834197504 | bytes 11010048 | tf_op jit(solution)/shard_map/dot_general | solution.py:984
  161.9 9.5 %mixer_scan.4 = (bf16[3,512,1792]{2,1,0:T(8,128)(2,1)}, bf16[3,4,128,1536]{3,2,1,0:T(8,128)(2,1)}, f32[3,4,8,128]{3,2,1,0:T(8,128)}, bf16[1,128,1536]{2,1,0:T(8,...) custom-call(bf16[3,512,1920]{2,1,0:T(8,128)(2,1)} %bitcast.157, ...), custom_call_target="tpu_custom_call", output_to_operand_aliasing={{0}: (7, {}), {1}: (8, {}), {2}: (9, {}), {5}: (10, {})} | custom-call | tf_op jit(solution)/shard_map/mixer_scan/pallas_call | solution.py:773
  173.5 9.4 %mixer_scan.5 = (bf16[3,512,1792]{2,1,0:T(8,128)(2,1)}, bf16[3,4,128,1536]{3,2,1,0:T(8,128)(2,1)}, f32[3,4,8,128]{3,2,1,0:T(8,128)}, bf16[1,128,1536]{2,1,0:T(8,...) custom-call(bf16[3,512,1920]{2,1,0:T(8,128)(2,1)} %bitcast.158, ...), custom_call_target="tpu_custom_call", output_to_operand_aliasing={{0}: (7, {}), {1}: (8, {}), {2}: (9, {}), {5}: (10, {})} | custom-call | tf_op jit(solution)/shard_map/mixer_scan/pallas_call | solution.py:773
  186.8 10.3 %collective-permute-done.7 = bf16[1,128,1536]{2,1,0:T(8,128)(2,1)S(1)} collective-permute-done((bf16[1,128,1536]{2,1,0:T(8,128)(2,1)}, bf16[1,128,1536]{2,1,0:T(8,128)(2,1)S(1)}, u32[]{:S(2)}, u32[]{:S(2)}) %collective-permute-start.7) | collective-permute-done | bytes 393248 | tf_op jit(solution)/shard_map/ppermute | solution.py:920
  198.0 7.6 collective-permute-done.4
  206.4 6.9 collective-permute-done.1
  219.0 4.2 slice.374
  223.2 5.6 slice.373
  231.1 3.3 fusion.59
  236.1 7.4 attend.3
  244.7 7.4 attend.4
  253.0 7.4 attend.5
  262.4 4.4 fusion.68
  267.6 8.6 %mixer_out.3 = (f32[3,512,1536]{2,1,0:T(8,128)}, bf16[3,512,1536]{2,1,0:T(8,128)(2,1)}) custom-call(bf16[3,512,1536]{2,1,0:T(8,128)(2,1)} %bitcast.165, f32[3,512,768]{2,1,0:T(8,128)} %get-tuple-element.138.refs_1_.refs_3_.refs_2_, bf16[3,512,1792]{2,1,0:T(8,128)(2,1)} %get-tuple-element.139.refs_2_.refs_4_.refs_6_, ...), custom_call_target="tpu_custom_call" | custom-call | tf_op jit(solution)/shard_map/mixer_out/pallas_call | solution.py:773
  277.1 8.6 %mixer_out.4 = (f32[3,512,1536]{2,1,0:T(8,128)}, bf16[3,512,1536]{2,1,0:T(8,128)(2,1)}) custom-call(bf16[3,512,1536]{2,1,0:T(8,128)(2,1)} %bitcast.166, f32[3,512,768]{2,1,0:T(8,128)} %get-tuple-element.138.refs_1_.refs_3_.refs_2_, bf16[3,512,1792]{2,1,0:T(8,128)(2,1)} %get-tuple-element.139.refs_2_.refs_4_.refs_6_, ...), custom_call_target="tpu_custom_call", output_to_operand_aliasing={{0}: (10, {}), {1}: (11, {})} | custom-call | tf_op jit(solution)/shard_map/mixer_out/pallas_call | solution.py:773
  286.6 8.7 %mixer_out.5 = (f32[3,512,1536]{2,1,0:T(8,128)}, bf16[3,512,1536]{2,1,0:T(8,128)(2,1)}) custom-call(bf16[3,512,1536]{2,1,0:T(8,128)(2,1)} %bitcast.167, f32[3,512,768]{2,1,0:T(8,128)} %get-tuple-element.138.refs_1_.refs_3_.refs_2_, bf16[3,512,1792]{2,1,0:T(8,128)(2,1)} %get-tuple-element.139.refs_2_.refs_4_.refs_6_, ...), custom_call_target="tpu_custom_call", output_to_operand_aliasing={{0}: (10, {}), {1}: (11, {})} | custom-call | tf_op jit(solution)/shard_map/mixer_out/pallas_call | solution.py:773
  295.3 10.8 %multiply_reduce_fusion.2 = (f32[1536]{0:T(1024)S(1)}, f32[1536,1024]{1,0:T(8,128)}) fusion(f32[1536,1024]{1,0:T(8,128)} %fusion.68, bf16[1536,1536]{1,0:T(8,128)(2,1)} %bitcast.186, bf16[1536,1024]{1,0:T(8,128)(2,1)S(1)} %bitcast.211, bf16[1536,1024]{1,0:T(8,128)(2,1)S(1)} %bitcast.199), kind=kOutput, calls=%fused_computation.29 | convolution fusion | flops 4839700992 | bytes 23599104 | tf_op jit(solution)/shard_map/dot_general | solution.py:984
  306.1 20.9 %convolution_convert_fusion = bf16[1536,4096]{1,0:T(8,128)(2,1)} fusion(f32[1536,1024]{1,0:T(8,128)} %get-tuple-element.305, f32[1024]{0:T(1024)S(1)} %mul.230, f32[1536]{0:T(1024)S(1)} %fusion.47, bf16[1024,1024]{1,0:T(8,128)(2,1)} %bitcast.218, bf16[1024,1024]{1,0:T(8,128)(2,1)} %bitcast.220, bf16[1024,1024]{1,0:T(8,128)(2,1)} %bitcast.222, ...), kind=kOutput, calls=%fused_computation.6 | convolution fusion | flops 12929466368 | bytes 27273216 | tf_op jit(solution)/shard_map/dot_general | solution.py:984
  327.1 19.1 %fusion.6 = (bf16[1536,2048]{1,0:T(8,128)(2,1)}, bf16[1536,2048]{1,0:T(8,128)(2,1)}, bf16[1536,2048]{1,0:T(8,128)(2,1)}) fusion(bf16[1536,4096]{1,0:T(8,128)(2,1)} %convolution_convert_fusion, bf16[2048,1024]{1,0:T(8,128)(2,1)} %bitcast.205, bf16[1536,1024]{1,0:T(8,128)(2,1)S(1)} %bitcast.208), kind=kOutput, calls=%fused_computation.13 | convolution fusion | flops 6499074048 | bytes 38797312 | tf_op jit(solution)/shard_map/ro,io->ri/dot_general | solution.py:1115
  346.2 20.7 %fusion.9 = f32[1536,1024]{1,0:T(8,128)} fusion(bf16[1536,2048]{1,0:T(8,128)(2,1)} %get-tuple-element.260, bf16[1536,2048]{1,0:T(8,128)(2,1)} %get-tuple-element.259, bf16[1024,1024]{1,0:T(8,128)(2,1)S(1)} %bitcast.219, bf16[1024,1024]{1,0:T(8,128)(2,1)S(1)} %bitcast.221, bf16[1024,1024]{1,0:T(8,128)(2,1)} %bitcast.223, bf16[1024,1024]{1,0:T(8,128)(2,1)S(1)} %bitcast.217), kind=kOutput, calls=%fused_computation.20 | convolution fusion | flops 12943622144 | bytes 27262976 | tf_op jit(solution)/shard_map/ro,io->ri/dot_general | solution.py:1115
  366.8 21.7 %fusion.10 = bf16[1024,4096]{1,0:T(8,128)(2,1)} fusion(bf16[1536,2048]{1,0:T(8,128)(2,1)} %get-tuple-element.260, bf16[1536,2048]{1,0:T(8,128)(2,1)} %get-tuple-element.259, f32[1536,1024]{1,0:T(8,128)} %get-tuple-element.305, f32[1024]{0:T(1024)S(1)} %mul.230, f32[1536]{0:T(1024)S(1)} %fusion.47), kind=kOutput, calls=%fused_computation.23 | convolution fusion | flops 12918980608 | bytes 27273216 | tf_op jit(solution)/shard_map/ri,ro->io/dot_general | solution.py:1112
  388.5 11.2 %convolution_convert_fusion.3 = bf16[2048,1024]{1,0:T(8,128)(2,1)} fusion(bf16[1536,2048]{1,0:T(8,128)(2,1)} %get-tuple-element.218, bf16[1536,1024]{1,0:T(8,128)(2,1)S(1)} %bitcast.209), kind=kOutput, calls=%fused_computation.32 | convolution fusion | flops 6444548096 | bytes 13631488 | tf_op jit(solution)/shard_map/ri,ro->io/dot_general | solution.py:1112
  399.8 6.6 multiply_reduce_fusion
  406.4 7.3 fusion.56
  413.7 3.0 convolution_convert_fusion.7
  418.6 6.8 convolution_convert_fusion.1
  425.5 5.4 convolution_convert_fusion.6
  430.9 9.8 %mixer_gate_back.3 = (bf16[3,512,1536]{2,1,0:T(8,128)(2,1)}, bf16[3,512,1536]{2,1,0:T(8,128)(2,1)}, bf16[3,4,128,1536]{3,2,1,0:T(8,128)(2,1)}, f32[3,4,8,128]{3,...) custom-call(bf16[3,512,1536]{2,1,0:T(8,128)(2,1)} %bitcast.183, ...), custom_call_target="tpu_custom_call" | custom-call | tf_op jit(solution)/shard_map/mixer_gate_back/pallas_call | solution.py:773
  441.4 10.1 %mixer_gate_back.4 = (bf16[3,512,1536]{2,1,0:T(8,128)(2,1)}, bf16[3,512,1536]{2,1,0:T(8,128)(2,1)}, bf16[3,4,128,1536]{3,2,1,0:T(8,128)(2,1)}, f32[3,4,8,128]{3,...) custom-call(bf16[3,512,1536]{2,1,0:T(8,128)(2,1)} %bitcast.184, ...), custom_call_target="tpu_custom_call", output_to_operand_aliasing={{0}: (8, {}), {1}: (9, {}), {2}: (10, {}), {3}: (11, {})} | custom-call | tf_op jit(solution)/shard_map/mixer_gate_back/pallas_call | solution.py:773
  452.4 9.9 %mixer_gate_back.5 = (bf16[3,512,1536]{2,1,0:T(8,128)(2,1)}, bf16[3,512,1536]{2,1,0:T(8,128)(2,1)}, bf16[3,4,128,1536]{3,2,1,0:T(8,128)(2,1)}, f32[3,4,8,128]{3,...) custom-call(bf16[3,512,1536]{2,1,0:T(8,128)(2,1)} %bitcast.185, ...), custom_call_target="tpu_custom_call", output_to_operand_aliasing={{0}: (8, {}), {1}: (9, {}), {2}: (10, {}), {3}: (11, {})} | custom-call | tf_op jit(solution)/shard_map/mixer_gate_back/pallas_call | solution.py:773
  472.0 5.6 convolution_convert_fusion.5
  485.2 13.4 %attend_back.3 = (bf16[1,512,512]{2,1,0:T(8,128)(2,1)}, bf16[4,1,512,256]{3,2,1,0:T(8,128)(2,1)}) custom-call(s32[6]{0:T(128)} %and_select_fusion.1.low_ref, s32[6]{0:T(128)} %reshape.288.high_ref, s32[1]{0:T(128)} %bitcast.7.base_ref, bf16[3,512,512]{2,1,0:T(8,128)(2,1)} %bitcast.174, bf16[4,3,512,256]{3,2,1,0:T(8,128)(2,1)} %copy-done, ...), custom_call_target="tpu_custom_call" | custom-call | tf_op jit(solution)/shard_map/attend_back/pallas_call | solution.py:337
  503.3 13.3 %attend_back.4 = (bf16[1,512,512]{2,1,0:T(8,128)(2,1)}, bf16[4,1,512,256]{3,2,1,0:T(8,128)(2,1)}) custom-call(s32[6]{0:T(128)} %and_select_fusion.1.low_ref, s32[6]{0:T(128)} %reshape.288.high_ref, s32[1]{0:T(128)} %bitcast.7.base_ref, bf16[3,512,512]{2,1,0:T(8,128)(2,1)} %bitcast.175, bf16[4,3,512,256]{3,2,1,0:T(8,128)(2,1)} %copy-done, ...), custom_call_target="tpu_custom_call" | custom-call | tf_op jit(solution)/shard_map/attend_back/pallas_call | solution.py:337
  516.6 13.4 %attend_back.5 = (bf16[1,512,512]{2,1,0:T(8,128)(2,1)}, bf16[4,1,512,256]{3,2,1,0:T(8,128)(2,1)}) custom-call(s32[6]{0:T(128)} %and_select_fusion.1.low_ref, s32[6]{0:T(128)} %reshape.288.high_ref, s32[1]{0:T(128)} %bitcast.7.base_ref, bf16[3,512,512]{2,1,0:T(8,128)(2,1)} %bitcast.176, bf16[4,3,512,256]{3,2,1,0:T(8,128)(2,1)} %copy-done, ...), custom_call_target="tpu_custom_call" | custom-call | tf_op jit(solution)/shard_map/attend_back/pallas_call | solution.py:337
  530.1 3.5 pad_maximum_fusion.7
  533.6 13.8 %collective-permute-done.16 = bf16[1,128,1536]{2,1,0:T(8,128)(2,1)S(1)} collective-permute-done((bf16[1,128,1536]{2,1,0:T(8,128)(2,1)S(1)}, bf16[1,128,1536]{2,1,0:T(8,128)(2,1)S(1)}, u32[]{:S(2)}, u32[]{:S(2)}) %collective-permute-start.16) | collective-permute-done | bytes 393248 | tf_op jit(solution)/shard_map/ppermute | solution.py:920
  548.2 17.8 %collective-permute-done.17 = bf16[1,128,1536]{2,1,0:T(8,128)(2,1)S(1)} collective-permute-done((bf16[1,128,1536]{2,1,0:T(8,128)(2,1)S(1)}, bf16[1,128,1536]{2,1,0:T(8,128)(2,1)S(1)}, u32[]{:S(2)}, u32[]{:S(2)}) %collective-permute-start.17) | collective-permute-done | bytes 393248 | tf_op jit(solution)/shard_map/ppermute | solution.py:920
  566.8 4.6 collective-permute-done.18
  572.2 38.1 %all-to-all-start.2 = ((bf16[4,3,512,256]{3,2,1,0:T(8,128)(2,1)}), bf16[4,3,512,256]{3,2,1,0:T(8,128)(2,1)S(1)}, u32[]{:S(2)}, u32[]{:S(2)}) async-start(bf16[4,3,512,256]{3,2,1,0:T(8,128)(2,1)} %pad_maximum_fusion.7), calls=%async_computation.4 | async-start | bytes 6291456 | tf_op jit(solution)/shard_map/all_to_all | solution.py:995
  610.3 24.1 %mixer_back.3 = (bf16[3,512,1920]{2,1,0:T(8,128)(2,1)}, f32[1,8,1792]{2,1,0:T(8,128)}, f32[8,1792]{1,0:T(8,128)}, f32[8,128]{1,0:T(8,128)}) custom-call(bf16[3,512,1536]{2,1,0:T(8,128)(2,1)} %get-tuple-element.207.refs_0_, f32[3,512,1536]{2,1,0:T(8,128)} %get-tuple-element.171.refs_1_, f32[3,512,768]{2,1,0:T(8,128)} %get-tuple-element.138.refs_1_.refs_3_.refs_2_, ...), custom_call_target="tpu_custom_call" | custom-call | tf_op jit(solution)/shard_map/mixer_back/pallas_call | solution.py:773
  634.4 2.6 constant_dynamic-update-slice_fusion.8
  645.8 24.5 %mixer_back.4 = (bf16[3,512,1920]{2,1,0:T(8,128)(2,1)}, f32[1,8,1792]{2,1,0:T(8,128)}, f32[8,1792]{1,0:T(8,128)}, f32[8,128]{1,0:T(8,128)}) custom-call(bf16[3,512,1536]{2,1,0:T(8,128)(2,1)} %get-tuple-element.207.refs_0_, f32[3,512,1536]{2,1,0:T(8,128)} %get-tuple-element.171.refs_1_, ...), custom_call_target="tpu_custom_call", output_to_operand_aliasing={{0}: (20, {})} | custom-call | tf_op jit(solution)/shard_map/mixer_back/pallas_call | solution.py:773
  670.3 24.1 %mixer_back.5 = (bf16[3,512,1920]{2,1,0:T(8,128)(2,1)}, f32[1,8,1792]{2,1,0:T(8,128)}, f32[8,1792]{1,0:T(8,128)}, f32[8,128]{1,0:T(8,128)}) custom-call(bf16[3,512,1536]{2,1,0:T(8,128)(2,1)} %get-tuple-element.207.refs_0_, f32[3,512,1536]{2,1,0:T(8,128)} %get-tuple-element.171.refs_1_, ...), custom_call_target="tpu_custom_call", output_to_operand_aliasing={{0}: (20, {})} | custom-call | tf_op jit(solution)/shard_map/mixer_back/pallas_call | solution.py:773
  696.8 4.8 convolution_convert_fusion.8
  701.6 5.6 collective-permute-done.19
  708.2 7.8 all-to-all-done.2.dkv_ref
  717.9 10.2 %convolution_convert_fusion.4 = bf16[1024,1920]{1,0:T(8,128)(2,1)S(1)} fusion(bf16[1536,1024]{1,0:T(8,128)(2,1)} %get-tuple-element.188, bf16[1536,1920]{1,0:T(8,128)(2,1)} %bitcast.177), kind=kOutput, calls=%fused_computation.33 | convolution fusion | flops 6041763840 | bytes 12976128 | tf_op jit(solution)/shard_map/ri,ro->io/dot_general | solution.py:1112
  734.0 22.8 %finish.1 = (bf16[1536,1024]{1,0:T(8,128)(2,1)}, bf16[1536,256]{1,0:T(8,128)(2,1)}, f32[8,1024]{1,0:T(8,128)}) custom-call(bf16[1536,1024]{1,0:T(8,128)(2,1)} %bitcast.198, f32[1,1024]{1,0:T(1,128)} %reshape.289.gain_ref, bf16[1536,1536]{1,0:T(8,128)(2,1)} %bitcast.179, bf16[1536,1920]{1,0:T(8,128)(2,1)} %bitcast.178, bf16[1536,512]{1,0:T(8,128)(2,1)} %bitcast.204, ...), custom_call_target="tpu_custom_call" | custom-call | tf_op jit(solution)/shard_map/finish/pallas_call | solution.py:139
  758.3 10.9 %all-to-all-start.3 = ((f32[8,3,24]{2,1,0:T(4,128)}), f32[8,3,24]{2,1,0:T(4,128)S(1)}, u32[]{:S(2)}, u32[]{:S(2)}) async-start(f32[8,3,24]{2,1,0:T(4,128)} %broadcast_in_dim.78), calls=%async_computation.8 | async-start | bytes 32768 | tf_op jit(solution)/shard_map/all_to_all | solution.py:941
  769.6 3.2 convolution_convert_fusion.10
  778.2 5.9 all-to-all-start.4
  791.1 5.4 reduce-scatter.10.cloned.1.call-done
  801.5 12.1 %add_convert_fusion = bf16[1536,1024]{1,0:T(8,128)(2,1)} fusion(f32[1536,1024]{1,0:T(8,128)} %get-tuple-element.305, bf16[1536,2048]{1,0:T(8,128)(2,1)} %get-tuple-element.218, bf16[2048,1024]{1,0:T(8,128)(2,1)} %bitcast.206), kind=kOutput, calls=%fused_computation.26 | convolution fusion | flops 6445596672 | bytes 19922944 | tf_op jit(solution)/shard_map/dot_general | solution.py:984
  817.8 5.0 reduce-scatter.14.cloned.1.call-done
  (387 shorter events, 136.2 us)
Async XLA Ops:
  7.2 40.5 %all-gather.4.cloned.1.call-start = ((), (), s32[]{:S(2)}) async-start(), calls=%async_computation.10 | async-start | bytes 1392640 | tf_op jit(solution)/shard_map/all_gather | solution.py:1000
  15.9 89.9 %all-gather.6.cloned.1.call-start = ((), (), s32[]{:S(2)}) async-start(), calls=%async_computation.11 | async-start | bytes 10027008 | tf_op jit(solution)/shard_map/all_gather | solution.py:997
  48.0 171.0 %all-gather.8.cloned.1.call-start = ((), (), s32[]{:S(2)}) async-start(), calls=%async_computation.12 | async-start | bytes 18874368 | tf_op jit(solution)/shard_map/all_gather | solution.py:997
  106.9 24.5 %copy-start.38 = (f32[32,4096]{1,0:T(8,128)}, f32[32,4096]{1,0:T(8,128)S(1)}, u32[]{:S(2)}) copy-start(f32[32,4096]{1,0:T(8,128)S(1)} %reshape.337) | copy-start | bytes 1572868
  108.4 20.8 %copy-start.49 = (s32[3,2048]{1,0:T(4,128)S(1)}, s32[3,2048]{1,0:T(4,128)}, u32[]{:S(2)}) copy-start(s32[3,2048]{1,0:T(4,128)} %param.20) | copy-start | bytes 73732
  125.7 7.3 collective-permute-start
  133.0 101.4 %all-to-all-start.1 = ((bf16[4,3,512,256]{3,2,1,0:T(8,128)(2,1)}), bf16[4,3,512,256]{3,2,1,0:T(8,128)(2,1)S(1)}, u32[]{:S(2)}, u32[]{:S(2)}) async-start(bf16[4,3,512,256]{3,2,1,0:T(8,128)(2,1)} %bitcast.210), calls=%async_computation.1 | async-start | bytes 6291456 | tf_op jit(solution)/shard_map/all_to_all | solution.py:995
  136.7 473.6 %reduce-scatter.8.cloned.1.call-start = ((), (), s32[]{:S(2)}) async-start(), calls=%async_computation.14 | async-start | bytes 9437184 | tf_op jit(solution)/shard_map/reduce_scatter | solution.py:1109
  137.0 14.1 %copy-start.59 = (bf16[1536,1024]{1,0:T(8,128)(2,1)S(1)}, bf16[1536,1024]{1,0:T(8,128)(2,1)}, u32[]{:S(2)}) copy-start(bf16[1536,1024]{1,0:T(8,128)(2,1)} %get-tuple-element.188) | copy-start | bytes 9437188
  147.2 49.9 %collective-permute-start.7 = (bf16[1,128,1536]{2,1,0:T(8,128)(2,1)}, bf16[1,128,1536]{2,1,0:T(8,128)(2,1)S(1)}, u32[]{:S(2)}, u32[]{:S(2)}) collective-permute-start(bf16[1,128,1536]{2,1,0:T(8,128)(2,1)} %get-tuple-element.159), channel_id=1, source_target_pairs={{0,1},{4,5},{8,9},{12,13},{16,17},{20,21},{24,25},{28,29}} | collective-permute-start | bytes 1179656 | tf_op jit(solution)/shard_map/ppermute | solution.py:920
  171.4 34.1 %collective-permute-start.4 = (bf16[1,128,1536]{2,1,0:T(8,128)(2,1)}, bf16[1,128,1536]{2,1,0:T(8,128)(2,1)S(1)}, u32[]{:S(2)}, u32[]{:S(2)}) collective-permute-start(bf16[1,128,1536]{2,1,0:T(8,128)(2,1)} %get-tuple-element.156), channel_id=1, source_target_pairs={{0,1},{4,5},{8,9},{12,13},{16,17},{20,21},{24,25},{28,29}} | collective-permute-start | bytes 1179656 | tf_op jit(solution)/shard_map/ppermute | solution.py:920
  173.4 23.7 %copy-start.30 = (bf16[1,128,1536]{2,1,0:T(8,128)(2,1)S(1)}, bf16[1,128,1536]{2,1,0:T(8,128)(2,1)}, u32[]{:S(2)}) copy-start(bf16[1,128,1536]{2,1,0:T(8,128)(2,1)} %get-tuple-element.159) | copy-start | bytes 1179652
  173.4 32.1 %copy-start.31 = (bf16[1,128,1536]{2,1,0:T(8,128)(2,1)S(1)}, bf16[1,128,1536]{2,1,0:T(8,128)(2,1)}, u32[]{:S(2)}) copy-start(bf16[1,128,1536]{2,1,0:T(8,128)(2,1)} %get-tuple-element.156) | copy-start | bytes 1179652
  182.9 35.1 %copy-start.32 = (bf16[1,128,1536]{2,1,0:T(8,128)(2,1)S(1)}, bf16[1,128,1536]{2,1,0:T(8,128)(2,1)}, u32[]{:S(2)}) copy-start(bf16[1,128,1536]{2,1,0:T(8,128)(2,1)} %get-tuple-element.143) | copy-start | bytes 1179652
  182.9 30.4 %collective-permute-start.1 = (bf16[1,128,1536]{2,1,0:T(8,128)(2,1)}, bf16[1,128,1536]{2,1,0:T(8,128)(2,1)S(1)}, u32[]{:S(2)}, u32[]{:S(2)}) collective-permute-start(bf16[1,128,1536]{2,1,0:T(8,128)(2,1)} %get-tuple-element.143), channel_id=1, source_target_pairs={{0,1},{4,5},{8,9},{12,13},{16,17},{20,21},{24,25},{28,29}} | collective-permute-start | bytes 1179656 | tf_op jit(solution)/shard_map/ppermute | solution.py:920
  185.1 32.1 %copy-start.44 = (f32[1536]{0:T(1024)}, f32[1536]{0:T(1024)S(1)}, u32[]{:S(2)}) copy-start(f32[1536]{0:T(1024)S(1)} %slice_reduce_fusion.4) | copy-start | bytes 18436
  186.0 31.2 %copy-start.42 = (f32[1536]{0:T(1024)}, f32[1536]{0:T(1024)S(1)}, u32[]{:S(2)}) copy-start(f32[1536]{0:T(1024)S(1)} %slice_reduce_fusion.5) | copy-start | bytes 18436
  186.8 30.4 %copy-start.46 = (f32[1536]{0:T(1024)}, f32[1536]{0:T(1024)S(1)}, u32[]{:S(2)}) copy-start(f32[1536]{0:T(1024)S(1)} %slice_reduce_fusion.6) | copy-start | bytes 18436
  197.3 18.0 %collective-permute-start.8 = (bf16[1,128,1536]{2,1,0:T(8,128)(2,1)S(1)}, bf16[1,128,1536]{2,1,0:T(8,128)(2,1)S(1)}, u32[]{:S(2)}, u32[]{:S(2)}) collective-permute-start(bf16[1,128,1536]{2,1,0:T(8,128)(2,1)S(1)} %fusion.17), channel_id=1, source_target_pairs={{1,2},{5,6},{9,10},{13,14},{17,18},{21,22},{25,26},{29,30}} | collective-permute-start | bytes 1179656 | tf_op jit(solution)/shard_map/ppermute | solution.py:920
  205.5 10.7 %copy-start.6 = (bf16[1,128,1536]{2,1,0:T(8,128)(2,1)}, bf16[1,128,1536]{2,1,0:T(8,128)(2,1)S(1)}, u32[]{:S(2)}) copy-start(bf16[1,128,1536]{2,1,0:T(8,128)(2,1)S(1)} %collective-permute-done.4) | copy-start | bytes 1179652
  205.7 10.6 %collective-permute-start.5 = (bf16[1,128,1536]{2,1,0:T(8,128)(2,1)S(1)}, bf16[1,128,1536]{2,1,0:T(8,128)(2,1)S(1)}, u32[]{:S(2)}, u32[]{:S(2)}) collective-permute-start(bf16[1,128,1536]{2,1,0:T(8,128)(2,1)S(1)} %fusion.15), channel_id=1, source_target_pairs={{1,2},{5,6},{9,10},{13,14},{17,18},{21,22},{25,26},{29,30}} | collective-permute-start | bytes 1179656 | tf_op jit(solution)/shard_map/ppermute | solution.py:920
  214.6 2.6 collective-permute-start.2
  219.0 12.1 %copy-start.1 = (bf16[8192,1024]{1,0:T(8,128)(2,1)S(1)}, bf16[8192,1024]{1,0:T(8,128)(2,1)}, u32[]{:S(2)}) copy-start(bf16[8192,1024]{1,0:T(8,128)(2,1)} %all-gather.8.cloned.1.call-done) | copy-start | bytes 50331652
  243.5 23.3 %collective-permute-start.9 = (bf16[1,128,1536]{2,1,0:T(8,128)(2,1)}, bf16[1,128,1536]{2,1,0:T(8,128)(2,1)S(1)}, u32[]{:S(2)}, u32[]{:S(2)}) collective-permute-start(bf16[1,128,1536]{2,1,0:T(8,128)(2,1)} %fusion.18), channel_id=1, source_target_pairs={{2,3},{6,7},{10,11},{14,15},{18,19},{22,23},{26,27},{30,31}} | collective-permute-start | bytes 1179656 | tf_op jit(solution)/shard_map/ppermute | solution.py:920
  252.2 10.2 %copy-start.34 = (bf16[32,32,512]{2,1,0:T(8,128)(2,1)S(1)}, bf16[32,32,512]{2,1,0:T(8,128)(2,1)}, u32[]{:S(2)}) copy-start(bf16[32,32,512]{2,1,0:T(8,128)(2,1)} %pad_maximum_fusion.10) | copy-start | bytes 3145732
  252.2 24.1 %collective-permute-start.6 = (bf16[1,128,1536]{2,1,0:T(8,128)(2,1)S(1)}, bf16[1,128,1536]{2,1,0:T(8,128)(2,1)S(1)}, u32[]{:S(2)}, u32[]{:S(2)}) collective-permute-start(bf16[1,128,1536]{2,1,0:T(8,128)(2,1)S(1)} %copy-done.41), channel_id=1, source_target_pairs={{2,3},{6,7},{10,11},{14,15},{18,19},{22,23},{26,27},{30,31}} | collective-permute-start | bytes 1179656 | tf_op jit(solution)/shard_map/ppermute | solution.py:920
  260.5 25.3 %collective-permute-start.3 = (bf16[1,128,1536]{2,1,0:T(8,128)(2,1)S(1)}, bf16[1,128,1536]{2,1,0:T(8,128)(2,1)S(1)}, u32[]{:S(2)}, u32[]{:S(2)}) collective-permute-start(bf16[1,128,1536]{2,1,0:T(8,128)(2,1)S(1)} %copy-done.40), channel_id=1, source_target_pairs={{2,3},{6,7},{10,11},{14,15},{18,19},{22,23},{26,27},{30,31}} | collective-permute-start | bytes 1179656 | tf_op jit(solution)/shard_map/ppermute | solution.py:920
  306.1 20.9 %copy-start.10 = (bf16[3,512,1024]{2,1,0:T(8,128)(2,1)S(1)}, bf16[3,512,1024]{2,1,0:T(8,128)(2,1)}, u32[]{:S(2)}) copy-start(bf16[3,512,1024]{2,1,0:T(8,128)(2,1)} %param.37) | copy-start | bytes 9437188
  327.1 19.1 %copy-start.16 = (bf16[32,32,1024]{2,1,0:T(8,128)(2,1)S(1)}, bf16[32,32,1024]{2,1,0:T(8,128)(2,1)}, u32[]{:S(2)}) copy-start(bf16[32,32,1024]{2,1,0:T(8,128)(2,1)} %get-tuple-element.261) | copy-start | bytes 6291460
  327.1 19.1 %copy-start.17 = (bf16[32,32,1024]{2,1,0:T(8,128)(2,1)S(1)}, bf16[32,32,1024]{2,1,0:T(8,128)(2,1)}, u32[]{:S(2)}) copy-start(bf16[32,32,1024]{2,1,0:T(8,128)(2,1)} %get-tuple-element.262) | copy-start | bytes 6291460
  327.1 19.1 %copy-start.18 = (bf16[32,32,1024]{2,1,0:T(8,128)(2,1)S(1)}, bf16[32,32,1024]{2,1,0:T(8,128)(2,1)}, u32[]{:S(2)}) copy-start(bf16[32,32,1024]{2,1,0:T(8,128)(2,1)} %get-tuple-element.263) | copy-start | bytes 6291460
  399.7 234.7 %reduce-scatter.6.cloned.1.call-start = ((), (), s32[]{:S(2)}) async-start(), calls=%async_computation.13 | async-start | bytes 12976128 | tf_op jit(solution)/shard_map/reduce_scatter | solution.py:1109
  440.7 21.7 %collective-permute-start.10 = (bf16[1,128,1536]{2,1,0:T(8,128)(2,1)}, bf16[1,128,1536]{2,1,0:T(8,128)(2,1)S(1)}, u32[]{:S(2)}, u32[]{:S(2)}) collective-permute-start(bf16[1,128,1536]{2,1,0:T(8,128)(2,1)} %get-tuple-element.181), channel_id=1, source_target_pairs={{3,2},{7,6},{11,10},{15,14},{19,18},{23,22},{27,26},{31,30}} | collective-permute-start | bytes 1179656 | tf_op jit(solution)/shard_map/ppermute | solution.py:920
  451.4 11.1 %collective-permute-start.11 = (bf16[1,128,1536]{2,1,0:T(8,128)(2,1)}, bf16[1,128,1536]{2,1,0:T(8,128)(2,1)S(1)}, u32[]{:S(2)}, u32[]{:S(2)}) collective-permute-start(bf16[1,128,1536]{2,1,0:T(8,128)(2,1)} %get-tuple-element.182), channel_id=1, source_target_pairs={{3,2},{7,6},{11,10},{15,14},{19,18},{23,22},{27,26},{31,30}} | collective-permute-start | bytes 1179656 | tf_op jit(solution)/shard_map/ppermute | solution.py:920
  452.3 10.3 %copy-start.22 = (bf16[1,128,1536]{2,1,0:T(8,128)(2,1)S(1)}, bf16[1,128,1536]{2,1,0:T(8,128)(2,1)}, u32[]{:S(2)}) copy-start(bf16[1,128,1536]{2,1,0:T(8,128)(2,1)} %get-tuple-element.182) | copy-start | bytes 1179652
  452.3 10.3 %copy-start.43 = (f32[1536]{0:T(1024)S(1)}, f32[1536]{0:T(1024)}, u32[]{:S(2)}) copy-start(f32[1536]{0:T(1024)} %copy-done.42) | copy-start | bytes 18436
  481.5 0.7 collective-permute-start.12
  483.1 15.5 %collective-permute-start.15 = (bf16[1,128,1536]{2,1,0:T(8,128)(2,1)}, bf16[1,128,1536]{2,1,0:T(8,128)(2,1)S(1)}, u32[]{:S(2)}, u32[]{:S(2)}) collective-permute-start(bf16[1,128,1536]{2,1,0:T(8,128)(2,1)} %get-tuple-element.249), channel_id=1, source_target_pairs={{2,1},{6,5},{10,9},{14,13},{18,17},{22,21},{26,25},{30,29}} | collective-permute-start | bytes 1179656 | tf_op jit(solution)/shard_map/ppermute | solution.py:920
  483.8 16.3 %collective-permute-start.13 = (bf16[1,128,1536]{2,1,0:T(8,128)(2,1)S(1)}, bf16[1,128,1536]{2,1,0:T(8,128)(2,1)S(1)}, u32[]{:S(2)}, u32[]{:S(2)}) collective-permute-start(bf16[1,128,1536]{2,1,0:T(8,128)(2,1)S(1)} %get-tuple-element.253), channel_id=1, source_target_pairs={{2,1},{6,5},{10,9},{14,13},{18,17},{22,21},{26,25},{30,29}} | collective-permute-start | bytes 1179656 | tf_op jit(solution)/shard_map/ppermute | solution.py:920
  484.5 15.9 %collective-permute-start.14 = (bf16[1,128,1536]{2,1,0:T(8,128)(2,1)S(1)}, bf16[1,128,1536]{2,1,0:T(8,128)(2,1)S(1)}, u32[]{:S(2)}, u32[]{:S(2)}) collective-permute-start(bf16[1,128,1536]{2,1,0:T(8,128)(2,1)S(1)} %get-tuple-element.251), channel_id=1, source_target_pairs={{2,1},{6,5},{10,9},{14,13},{18,17},{22,21},{26,25},{30,29}} | collective-permute-start | bytes 1179656 | tf_op jit(solution)/shard_map/ppermute | solution.py:920
  485.2 13.5 %copy-start.48 = (f32[1536]{0:T(1024)S(1)}, f32[1536]{0:T(1024)}, u32[]{:S(2)}) copy-start(f32[1536]{0:T(1024)} %copy-done.46) | copy-start | bytes 18436
  498.8 48.6 %collective-permute-start.16 = (bf16[1,128,1536]{2,1,0:T(8,128)(2,1)S(1)}, bf16[1,128,1536]{2,1,0:T(8,128)(2,1)S(1)}, u32[]{:S(2)}, u32[]{:S(2)}) collective-permute-start(bf16[1,128,1536]{2,1,0:T(8,128)(2,1)S(1)} %get-tuple-element.200), channel_id=1, source_target_pairs={{1,0},{5,4},{9,8},{13,12},{17,16},{21,20},{25,24},{29,28}} | collective-permute-start | bytes 1179656 | tf_op jit(solution)/shard_map/ppermute | solution.py:920
  500.5 65.5 %collective-permute-start.17 = (bf16[1,128,1536]{2,1,0:T(8,128)(2,1)S(1)}, bf16[1,128,1536]{2,1,0:T(8,128)(2,1)S(1)}, u32[]{:S(2)}, u32[]{:S(2)}) collective-permute-start(bf16[1,128,1536]{2,1,0:T(8,128)(2,1)S(1)} %get-tuple-element.201), channel_id=1, source_target_pairs={{1,0},{5,4},{9,8},{13,12},{17,16},{21,20},{25,24},{29,28}} | collective-permute-start | bytes 1179656 | tf_op jit(solution)/shard_map/ppermute | solution.py:920
  501.8 69.6 %collective-permute-start.18 = (bf16[1,128,1536]{2,1,0:T(8,128)(2,1)S(1)}, bf16[1,128,1536]{2,1,0:T(8,128)(2,1)S(1)}, u32[]{:S(2)}, u32[]{:S(2)}) collective-permute-start(bf16[1,128,1536]{2,1,0:T(8,128)(2,1)S(1)} %get-tuple-element.202), channel_id=1, source_target_pairs={{1,0},{5,4},{9,8},{13,12},{17,16},{21,20},{25,24},{29,28}} | collective-permute-start | bytes 1179656 | tf_op jit(solution)/shard_map/ppermute | solution.py:920
  516.6 13.4 %copy-start.36 = (bf16[4,1,512,256]{3,2,1,0:T(8,128)(2,1)S(1)}, bf16[4,1,512,256]{3,2,1,0:T(8,128)(2,1)}, u32[]{:S(2)}) copy-start(bf16[4,1,512,256]{3,2,1,0:T(8,128)(2,1)} %get-tuple-element.213) | copy-start | bytes 3145732
  516.6 13.4 %copy-start.37 = (bf16[4,1,512,256]{3,2,1,0:T(8,128)(2,1)S(1)}, bf16[4,1,512,256]{3,2,1,0:T(8,128)(2,1)}, u32[]{:S(2)}) copy-start(bf16[4,1,512,256]{3,2,1,0:T(8,128)(2,1)} %get-tuple-element.214) | copy-start | bytes 3145732
  572.2 143.8 %all-to-all-start.2 = ((bf16[4,3,512,256]{3,2,1,0:T(8,128)(2,1)}), bf16[4,3,512,256]{3,2,1,0:T(8,128)(2,1)S(1)}, u32[]{:S(2)}, u32[]{:S(2)}) async-start(bf16[4,3,512,256]{3,2,1,0:T(8,128)(2,1)} %pad_maximum_fusion.7), calls=%async_computation.4 | async-start | bytes 6291456 | tf_op jit(solution)/shard_map/all_to_all | solution.py:995
  610.3 123.7 %reduce-scatter.12.cloned.1.call-start = ((), (), s32[]{:S(2)}) async-start(), calls=%async_computation.16 | async-start | bytes 3112960 | tf_op jit(solution)/shard_map/reduce_scatter | solution.py:1197
  634.4 11.3 %copy-start.53 = (f32[1,8,1792]{2,1,0:T(8,128)S(1)}, f32[1,8,1792]{2,1,0:T(8,128)}, u32[]{:S(2)}) copy-start(f32[1,8,1792]{2,1,0:T(8,128)} %get-tuple-element.205) | copy-start | bytes 172036
  643.7 152.8 %reduce-scatter.10.cloned.1.call-start = ((), (), s32[]{:S(2)}) async-start(), calls=%async_computation.15 | async-start | bytes 5603328 | tf_op jit(solution)/shard_map/reduce_scatter | solution.py:1109
  645.7 51.1 %copy-start.4 = (bf16[3,512,512]{2,1,0:T(8,128)(2,1)}, bf16[3,512,512]{2,1,0:T(8,128)(2,1)S(1)}, u32[]{:S(2)}) copy-start(bf16[3,512,512]{2,1,0:T(8,128)(2,1)S(1)} %pad_maximum_fusion.9) | copy-start | bytes 4718596
  670.3 25.0 %copy-start.54 = (f32[1,8,1792]{2,1,0:T(8,128)S(1)}, f32[1,8,1792]{2,1,0:T(8,128)}, u32[]{:S(2)}) copy-start(f32[1,8,1792]{2,1,0:T(8,128)} %get-tuple-element.211) | copy-start | bytes 172036
  695.3 11.9 %collective-permute-start.19 = (bf16[3,3,1792]{2,1,0:T(4,128)(2,1)S(1)}, bf16[3,3,1792]{2,1,0:T(4,128)(2,1)S(1)}, u32[]{:S(2)}, u32[]{:S(2)}) collective-permute-start(bf16[3,3,1792]{2,1,0:T(4,128)(2,1)S(1)} %pad_maximum_fusion.15), channel_id=1, source_target_pairs={{1,0},{2,1},{3,2},{5,4},{6,5},{7,6},{9,8},{10,9},{11,10},{13,12},{... | collective-permute-start | bytes 96776 | tf_op jit(solution)/shard_map/ppermute | solution.py:897
  716.0 12.2 %copy-start.2 = (bf16[4,3,512,256]{3,2,1,0:T(8,128)(2,1)}, bf16[4,3,512,256]{3,2,1,0:T(8,128)(2,1)S(1)}, u32[]{:S(2)}) copy-start(bf16[4,3,512,256]{3,2,1,0:T(8,128)(2,1)S(1)} %all-to-all-done.2.dkv_ref) | copy-start | bytes 9437188
  717.9 10.3 %copy-start.33 = (bf16[1024,512]{1,0:T(8,128)(2,1)S(1)}, bf16[1024,512]{1,0:T(8,128)(2,1)}, u32[]{:S(2)}) copy-start(bf16[1024,512]{1,0:T(8,128)(2,1)} %convolution_convert_fusion.8) | copy-start | bytes 3145732
  758.3 19.2 %all-to-all-start.3 = ((f32[8,3,24]{2,1,0:T(4,128)}), f32[8,3,24]{2,1,0:T(4,128)S(1)}, u32[]{:S(2)}, u32[]{:S(2)}) async-start(f32[8,3,24]{2,1,0:T(4,128)} %broadcast_in_dim.78), calls=%async_computation.8 | async-start | bytes 32768 | tf_op jit(solution)/shard_map/all_to_all | solution.py:941
  773.3 2.1 collective-permute-start.20
  775.6 8.6 %collective-permute-start.21 = (bf16[2,4,32,384]{3,2,1,0:T(8,128)(2,1)S(1)}, bf16[2,4,32,384]{3,2,1,0:T(8,128)(2,1)S(1)}, u32[]{:S(2)}, u32[]{:S(2)}) collective-permute-start(bf16[2,4,32,384]{3,2,1,0:T(8,128)(2,1)S(1)} %fusion.31), channel_id=1, source_target_pairs={{0,16},{4,20},{8,24},{12,28},{16,0},{20,4},{24,8},{28,12},{1,17},{... | collective-permute-start | bytes 589832 | tf_op jit(solution)/shard_map/ppermute | solution.py:955
  778.2 11.5 %all-to-all-start.4 = ((f32[4,3,24]{2,1,0:T(4,128)}), f32[4,3,24]{2,1,0:T(4,128)S(1)}, u32[]{:S(2)}, u32[]{:S(2)}) async-start(f32[4,3,24]{2,1,0:T(4,128)} %broadcast_in_dim.79), calls=%async_computation.9 | async-start | bytes 16384 | tf_op jit(solution)/shard_map/all_to_all | solution.py:941
  784.1 38.6 %reduce-scatter.14.cloned.1.call-start = ((), (), s32[]{:S(2)}) async-start(), calls=%async_computation.17 | async-start | bytes 778240 | tf_op jit(solution)/shard_map/reduce_scatter | solution.py:1202
  784.2 6.8 collective-permute-start.22
  796.6 17.0 %collective-permute-start.23 = (bf16[32,384]{1,0:T(8,128)(2,1)S(1)}, bf16[32,384]{1,0:T(8,128)(2,1)S(1)}, u32[]{:S(2)}, u32[]{:S(2)}) collective-permute-start(bf16[32,384]{1,0:T(8,128)(2,1)S(1)} %get-tuple-element.283), channel_id=1, source_target_pairs={{0,1},{1,2},{2,3},{3,0},{4,5},{5,6},{6,7},{7,4},{8,9},{9,10},{10,1... | collective-permute-start | bytes 73736 | tf_op jit(solution)/shard_map/ppermute | solution.py:961
  798.6 15.0 %collective-permute-start.25 = (bf16[32,384]{1,0:T(8,128)(2,1)S(1)}, bf16[32,384]{1,0:T(8,128)(2,1)S(1)}, u32[]{:S(2)}, u32[]{:S(2)}) collective-permute-start(bf16[32,384]{1,0:T(8,128)(2,1)S(1)} %get-tuple-element.284), channel_id=1, source_target_pairs={{0,3},{1,0},{2,1},{3,2},{4,7},{5,4},{6,5},{7,6},{8,11},{9,8},{10,9... | collective-permute-start | bytes 73736 | tf_op jit(solution)/shard_map/ppermute | solution.py:961
  800.6 12.9 %collective-permute-start.24 = (bf16[32,384]{1,0:T(8,128)(2,1)S(1)}, bf16[32,384]{1,0:T(8,128)(2,1)S(1)}, u32[]{:S(2)}, u32[]{:S(2)}) collective-permute-start(bf16[32,384]{1,0:T(8,128)(2,1)S(1)} %get-tuple-element.285), channel_id=1, source_target_pairs={{0,2},{1,3},{2,0},{3,1},{4,6},{5,7},{6,4},{7,5},{8,10},{9,11},{10,... | collective-permute-start | bytes 73736 | tf_op jit(solution)/shard_map/ppermute | solution.py:961
  (39 other events, 196.0 us)
Sparse Core Ops, SparseCore 0:
  16.0 31.6 all-gather.3
  49.6 56.1 all-gather.5
  107.7 89.8 all-gather.7
  399.9 100.3 reduce-scatter.7
  504.0 97.7 reduce-scatter.5
  643.9 76.1 reduce-scatter.11
  730.9 65.5 reduce-scatter.9
  801.6 21.0 reduce-scatter.13

commit v9 on v8

--- a/solution.py
+++ b/solution.py
@@ -1160,7 +1160,7 @@
             for chain in chains:
                 chain.take()
                 chain.send(*dqs[-1:])
-        mark = dqs[-1:] + [chain.state for chain in chains] + ([] if seq else [grad_rest])
+        mark = dqs[-1:] + [chain.state for chain in chains] + ([part_gu] if seq == seqs - 1 else [] if seq else [grad_rest])
         dq, dkv = attend_back(
             seq, bounds, after(q, grad_y, *mark), kv_all, segk,
             segq, atts[seq], grad_att, lses[seq], cos3, sin3,
@@ -1175,7 +1175,7 @@
     waits[1 % seqs] += tuple(finals)
     for seq in range(seqs):
         gstate = finals[seq]
-        if seq == min(1, seqs - 1):
+        if seq == 0:
             gu_blocks = part_gu.reshape(count, own_rows, 2 * ff)
             parts = [after(part_rest, *rims).reshape(count, -1, width)]
             parts += [gu_blocks[..., at : at + width] for at in range(0, 2 * ff, width)]

time: 845 us -> 857 us (1.014)
  waiting for transfers between devices: 99.6 us -> 122 us
    ppermute x18, waiting for transfers between devices: 61.1 us -> 78.3 us  [send(): self.flying = (lax.ppermute(sent, 'ctx', [(source, target)]), target)]
    all_to_all x2, starting transfers between devices: 41.8 us -> 24.7 us  [body(): exchange = lambda blocks: lax.all_to_all(blocks, 'ctx', 0, 0, tiled=True)]
    ppermute x18, starting transfers between devices: 20.4 us -> 31.6 us  [send(): self.flying = (lax.ppermute(sent, 'ctx', [(source, target)]), target)]
    all_to_all x2, waiting for transfers between devices: 7.8 us -> 17.1 us  [body(): exchange = lambda blocks: lax.all_to_all(blocks, 'ctx', 0, 0, tiled=True)]
    unnamed x148 -> x146, local copies, waits for them, and re-layouts: 27.4 us -> 27.4 us
  transfers between devices with their start and end apart: 38 -> 38, of which waited for: 14 -> 15; matrix products, arithmetic and copies ran while one was open for 23% -> 22% of each run, Pallas kernels for 29% -> 29%
where the time goes in v9:
time: 857 us; the launch traced here: 847 us
  Pallas kernels  258 us (30%)
  matrix products  171 us (20%)
  waiting for transfers between devices  122 us (14%)
  starting transfers between devices  85.8 us (10%)
  local copies, waits for them, and re-layouts  83.4 us (10%)
  other arithmetic  59 us (7%)
  blocking collectives  51.6 us (6%)
  between operations  16.1 us (2%)
    pallas_call x12, Pallas kernels, mixer_call(): pl.pallas_call(run, grid=(chunks,), in_specs=in_specs, out_specs=out_spec...  157 us
    ppermute x18, waiting for transfers between devices, send(): self.flying = (lax.ppermute(sent, 'ctx', [(source, target)]), target)  78.3 us
    dot_general x8, matrix products, weight_grad(): jnp.einsum('ri,ro->io', left, right, preferred_element_type=F32)  64 us
    dot_general x5, matrix products, body(): low_dot = lambda a, b: jnp.dot(a, b, preferred_element_type=F32)  55.6 us
    all_to_all x1, blocking collectives, body(): exchange = lambda blocks: lax.all_to_all(blocks, 'ctx', 0, 0, tiled=True)  51.6 us
    dot_general x3, matrix products, back_dot(): return jnp.einsum('ro,io->ri', grad, weight, preferred_element_type=F32)  46.7 us
    pallas_call x3, Pallas kernels, attend_back(): pl.pallas_call(functools.partial(attend_back_kernel, seq * (span // rows)...  40 us
    ppermute x18, starting transfers between devices, send(): self.flying = (lax.ppermute(sent, 'ctx', [(source, target)]), target)  31.6 us
  transfers between devices with their start and end apart: 38, of which 15 were waited for; matrix products, arithmetic and copies ran while one was open for 22% of the time, Pallas kernels for 29%

profile of v9, /device:TPU:0, one launch (start us, length us, event | category | flops | bytes accessed | tf_op | source)
XLA Modules:
  0.0 847.0 jit_solution(7916920496205368689)
XLA Ops:
  11.5 2.8 concatenate.96
  31.6 2.8 fusion.29
  37.6 10.0 %all-gather.4.cloned.1.call-done = bf16[128,4352]{1,0:T(8,128)(2,1)} async-done(((bf16[32,4352]{1,0:T(8,128)(2,1)}), bf16[128,4352]{1,0:T(8,128)(2,1)}) %all-gather.4.cloned.1.call-update) | async-done | bytes 1114128 | tf_op jit(solution)/shard_map/all_gather | solution.py:1000
  48.0 51.6 %all_to_all.25 = bf16[4,256,1024]{2,1,0:T(8,128)(2,1)} all-to-all(bf16[4,256,1024]{2,1,0:T(8,128)(2,1)S(1)} %broadcast_in_dim.73), channel_id=1, replica_groups=mesh['dp'=8,'ctx'=4] {'ctx'}, dimensions={0} | all-to-all | bytes 4194304 | tf_op jit(solution)/shard_map/all_to_all | solution.py:995
  99.7 2.8 fusion.30
  108.4 16.4 %project.1 = (bf16[1536,1024]{1,0:T(8,128)(2,1)}, bf16[1536,1920]{1,0:T(8,128)(2,1)}, bf16[1536,512]{1,0:T(8,128)(2,1)}, bf16[4,1536,256]{2,1,0:T(8,128)(2,1)}) custom-call(bf16[1536,1024]{1,0:T(8,128)(2,1)} %bitcast.197, f32[1,1024]{1,0:T(1,128)} %reshape.289.gain_ref, bf16[1024,4352]{1,0:T(8,128)(2,1)} %all-gather.6.cloned.1.call-done.w_ref, ...), custom_call_target="tpu_custom_call" | custom-call | tf_op jit(solution)/shard_map/project/pallas_call | solution.py:78
  125.7 3.4 collective-permute-start
  133.0 3.7 all-to-all-start.1
  137.7 9.5 %mixer_scan.3 = (bf16[3,512,1792]{2,1,0:T(8,128)(2,1)}, bf16[3,4,128,1536]{3,2,1,0:T(8,128)(2,1)}, f32[3,4,8,128]{3,2,1,0:T(8,128)}, bf16[1,128,1536]{2,1,0:T(8,...) custom-call(bf16[3,512,1920]{2,1,0:T(8,128)(2,1)} %bitcast.156, bf16[3,8,1792]{2,1,0:T(8,128)(2,1)} %pad.28.refs_1_.refs_5_, ...), custom_call_target="tpu_custom_call" | custom-call | tf_op jit(solution)/shard_map/mixer_scan/pallas_call | solution.py:773
  147.3 3.9 collective-permute-start.7
  151.2 8.6 %convolution_convert_fusion.2 = bf16[1536,1536]{1,0:T(8,128)(2,1)} fusion(bf16[1536,1024]{1,0:T(8,128)(2,1)S(1)} %copy-done.58, bf16[1024,4352]{1,0:T(8,128)(2,1)} %all-gather.6.cloned.1.call-done.w_ref), kind=kOutput, calls=%fused_computation.22 | convolution fusion | flops 4834197504 | bytes 11010048 | tf_op jit(solution)/shard_map/dot_general | solution.py:984
  162.0 9.5 %mixer_scan.4 = (bf16[3,512,1792]{2,1,0:T(8,128)(2,1)}, bf16[3,4,128,1536]{3,2,1,0:T(8,128)(2,1)}, f32[3,4,8,128]{3,2,1,0:T(8,128)}, bf16[1,128,1536]{2,1,0:T(8,...) custom-call(bf16[3,512,1920]{2,1,0:T(8,128)(2,1)} %bitcast.157, ...), custom_call_target="tpu_custom_call", output_to_operand_aliasing={{0}: (7, {}), {1}: (8, {}), {2}: (9, {}), {5}: (10, {})} | custom-call | tf_op jit(solution)/shard_map/mixer_scan/pallas_call | solution.py:773
  173.5 9.3 %mixer_scan.5 = (bf16[3,512,1792]{2,1,0:T(8,128)(2,1)}, bf16[3,4,128,1536]{3,2,1,0:T(8,128)(2,1)}, f32[3,4,8,128]{3,2,1,0:T(8,128)}, bf16[1,128,1536]{2,1,0:T(8,...) custom-call(bf16[3,512,1920]{2,1,0:T(8,128)(2,1)} %bitcast.158, ...), custom_call_target="tpu_custom_call", output_to_operand_aliasing={{0}: (7, {}), {1}: (8, {}), {2}: (9, {}), {5}: (10, {})} | custom-call | tf_op jit(solution)/shard_map/mixer_scan/pallas_call | solution.py:773
  186.8 10.2 %collective-permute-done.7 = bf16[1,128,1536]{2,1,0:T(8,128)(2,1)S(1)} collective-permute-done((bf16[1,128,1536]{2,1,0:T(8,128)(2,1)}, bf16[1,128,1536]{2,1,0:T(8,128)(2,1)S(1)}, u32[]{:S(2)}, u32[]{:S(2)}) %collective-permute-start.7) | collective-permute-done | bytes 393248 | tf_op jit(solution)/shard_map/ppermute | solution.py:920
  197.9 7.6 collective-permute-done.4
  206.4 6.9 collective-permute-done.1
  219.0 4.2 slice.374
  223.1 5.6 slice.373
  231.1 3.3 fusion.59
  236.0 7.4 attend.3
  243.4 12.1 %collective-permute-start.9 = (bf16[1,128,1536]{2,1,0:T(8,128)(2,1)}, bf16[1,128,1536]{2,1,0:T(8,128)(2,1)S(1)}, u32[]{:S(2)}, u32[]{:S(2)}) collective-permute-start(bf16[1,128,1536]{2,1,0:T(8,128)(2,1)} %fusion.18), channel_id=1, source_target_pairs={{2,3},{6,7},{10,11},{14,15},{18,19},{22,23},{26,27},{30,31}} | collective-permute-start | bytes 1179656 | tf_op jit(solution)/shard_map/ppermute | solution.py:920
  255.5 7.4 attend.4
  263.8 7.4 attend.5
  273.2 4.4 fusion.68
  278.5 8.6 %mixer_out.3 = (f32[3,512,1536]{2,1,0:T(8,128)}, bf16[3,512,1536]{2,1,0:T(8,128)(2,1)}) custom-call(bf16[3,512,1536]{2,1,0:T(8,128)(2,1)} %bitcast.165, f32[3,512,768]{2,1,0:T(8,128)} %get-tuple-element.137.refs_1_.refs_3_.refs_2_, bf16[3,512,1792]{2,1,0:T(8,128)(2,1)} %get-tuple-element.138.refs_2_.refs_4_.refs_6_, ...), custom_call_target="tpu_custom_call" | custom-call | tf_op jit(solution)/shard_map/mixer_out/pallas_call | solution.py:773
  287.9 8.7 %mixer_out.4 = (f32[3,512,1536]{2,1,0:T(8,128)}, bf16[3,512,1536]{2,1,0:T(8,128)(2,1)}) custom-call(bf16[3,512,1536]{2,1,0:T(8,128)(2,1)} %bitcast.166, f32[3,512,768]{2,1,0:T(8,128)} %get-tuple-element.137.refs_1_.refs_3_.refs_2_, bf16[3,512,1792]{2,1,0:T(8,128)(2,1)} %get-tuple-element.138.refs_2_.refs_4_.refs_6_, ...), custom_call_target="tpu_custom_call", output_to_operand_aliasing={{0}: (10, {}), {1}: (11, {})} | custom-call | tf_op jit(solution)/shard_map/mixer_out/pallas_call | solution.py:773
  297.4 8.7 %mixer_out.5 = (f32[3,512,1536]{2,1,0:T(8,128)}, bf16[3,512,1536]{2,1,0:T(8,128)(2,1)}) custom-call(bf16[3,512,1536]{2,1,0:T(8,128)(2,1)} %bitcast.167, f32[3,512,768]{2,1,0:T(8,128)} %get-tuple-element.137.refs_1_.refs_3_.refs_2_, bf16[3,512,1792]{2,1,0:T(8,128)(2,1)} %get-tuple-element.138.refs_2_.refs_4_.refs_6_, ...), custom_call_target="tpu_custom_call", output_to_operand_aliasing={{0}: (10, {}), {1}: (11, {})} | custom-call | tf_op jit(solution)/shard_map/mixer_out/pallas_call | solution.py:773
  306.2 10.8 %multiply_reduce_fusion.2 = (f32[1536]{0:T(1024)S(1)}, f32[1536,1024]{1,0:T(8,128)}) fusion(f32[1536,1024]{1,0:T(8,128)} %fusion.68, bf16[1536,1536]{1,0:T(8,128)(2,1)} %bitcast.186, bf16[1536,1024]{1,0:T(8,128)(2,1)S(1)} %bitcast.211, bf16[1536,1024]{1,0:T(8,128)(2,1)S(1)} %bitcast.199), kind=kOutput, calls=%fused_computation.29 | convolution fusion | flops 4839700992 | bytes 23599104 | tf_op jit(solution)/shard_map/dot_general | solution.py:984
  317.0 20.9 %convolution_convert_fusion = bf16[1536,4096]{1,0:T(8,128)(2,1)} fusion(f32[1536,1024]{1,0:T(8,128)} %get-tuple-element.303, f32[1024]{0:T(1024)S(1)} %mul.230, f32[1536]{0:T(1024)S(1)} %fusion.47, bf16[1024,1024]{1,0:T(8,128)(2,1)} %bitcast.218, bf16[1024,1024]{1,0:T(8,128)(2,1)} %bitcast.220, bf16[1024,1024]{1,0:T(8,128)(2,1)} %bitcast.222, ...), kind=kOutput, calls=%fused_computation.6 | convolution fusion | flops 12929466368 | bytes 27273216 | tf_op jit(solution)/shard_map/dot_general | solution.py:984
  337.9 19.1 %fusion.6 = (bf16[1536,2048]{1,0:T(8,128)(2,1)}, bf16[1536,2048]{1,0:T(8,128)(2,1)}, bf16[1536,2048]{1,0:T(8,128)(2,1)}) fusion(bf16[1536,4096]{1,0:T(8,128)(2,1)} %convolution_convert_fusion, bf16[2048,1024]{1,0:T(8,128)(2,1)} %bitcast.205, bf16[1536,1024]{1,0:T(8,128)(2,1)S(1)} %bitcast.208), kind=kOutput, calls=%fused_computation.13 | convolution fusion | flops 6499074048 | bytes 38797312 | tf_op jit(solution)/shard_map/ro,io->ri/dot_general | solution.py:1115
  357.1 20.6 %fusion.9 = f32[1536,1024]{1,0:T(8,128)} fusion(bf16[1536,2048]{1,0:T(8,128)(2,1)} %get-tuple-element.258, bf16[1536,2048]{1,0:T(8,128)(2,1)} %get-tuple-element.257, bf16[1024,1024]{1,0:T(8,128)(2,1)S(1)} %bitcast.219, bf16[1024,1024]{1,0:T(8,128)(2,1)S(1)} %bitcast.221, bf16[1024,1024]{1,0:T(8,128)(2,1)} %bitcast.223, bf16[1024,1024]{1,0:T(8,128)(2,1)S(1)} %bitcast.217), kind=kOutput, calls=%fused_computation.20 | convolution fusion | flops 12943622144 | bytes 27262976 | tf_op jit(solution)/shard_map/ro,io->ri/dot_general | solution.py:1115
  377.7 21.9 %fusion.10 = bf16[1024,4096]{1,0:T(8,128)(2,1)} fusion(bf16[1536,2048]{1,0:T(8,128)(2,1)} %get-tuple-element.258, bf16[1536,2048]{1,0:T(8,128)(2,1)} %get-tuple-element.257, f32[1536,1024]{1,0:T(8,128)} %get-tuple-element.303, f32[1024]{0:T(1024)S(1)} %mul.230, f32[1536]{0:T(1024)S(1)} %fusion.47), kind=kOutput, calls=%fused_computation.23 | convolution fusion | flops 12918980608 | bytes 27273216 | tf_op jit(solution)/shard_map/ri,ro->io/dot_general | solution.py:1112
  399.6 11.2 %convolution_convert_fusion.3 = bf16[2048,1024]{1,0:T(8,128)(2,1)} fusion(bf16[1536,2048]{1,0:T(8,128)(2,1)} %get-tuple-element.216, bf16[1536,1024]{1,0:T(8,128)(2,1)S(1)} %bitcast.209), kind=kOutput, calls=%fused_computation.32 | convolution fusion | flops 6444548096 | bytes 13631488 | tf_op jit(solution)/shard_map/ri,ro->io/dot_general | solution.py:1112
  410.8 6.3 multiply_reduce_fusion
  417.2 7.3 fusion.56
  424.5 3.0 convolution_convert_fusion.7
  429.4 6.9 convolution_convert_fusion.1
  436.4 5.4 convolution_convert_fusion.6
  441.8 9.9 %mixer_gate_back.3 = (bf16[3,512,1536]{2,1,0:T(8,128)(2,1)}, bf16[3,512,1536]{2,1,0:T(8,128)(2,1)}, bf16[3,4,128,1536]{3,2,1,0:T(8,128)(2,1)}, f32[3,4,8,128]{3,...) custom-call(bf16[3,512,1536]{2,1,0:T(8,128)(2,1)} %bitcast.183, ...), custom_call_target="tpu_custom_call" | custom-call | tf_op jit(solution)/shard_map/mixer_gate_back/pallas_call | solution.py:773
  452.4 10.2 %mixer_gate_back.4 = (bf16[3,512,1536]{2,1,0:T(8,128)(2,1)}, bf16[3,512,1536]{2,1,0:T(8,128)(2,1)}, bf16[3,4,128,1536]{3,2,1,0:T(8,128)(2,1)}, f32[3,4,8,128]{3,...) custom-call(bf16[3,512,1536]{2,1,0:T(8,128)(2,1)} %bitcast.184, ...), custom_call_target="tpu_custom_call", output_to_operand_aliasing={{0}: (8, {}), {1}: (9, {}), {2}: (10, {}), {3}: (11, {})} | custom-call | tf_op jit(solution)/shard_map/mixer_gate_back/pallas_call | solution.py:773
  463.5 9.5 %mixer_gate_back.5 = (bf16[3,512,1536]{2,1,0:T(8,128)(2,1)}, bf16[3,512,1536]{2,1,0:T(8,128)(2,1)}, bf16[3,4,128,1536]{3,2,1,0:T(8,128)(2,1)}, f32[3,4,8,128]{3,...) custom-call(bf16[3,512,1536]{2,1,0:T(8,128)(2,1)} %bitcast.185, ...), custom_call_target="tpu_custom_call", output_to_operand_aliasing={{0}: (8, {}), {1}: (9, {}), {2}: (10, {}), {3}: (11, {})} | custom-call | tf_op jit(solution)/shard_map/mixer_gate_back/pallas_call | solution.py:773
  482.7 5.6 convolution_convert_fusion.5
  495.1 13.3 %attend_back.3 = (bf16[1,512,512]{2,1,0:T(8,128)(2,1)}, bf16[4,1,512,256]{3,2,1,0:T(8,128)(2,1)}) custom-call(s32[6]{0:T(128)} %and_select_fusion.1.low_ref, s32[6]{0:T(128)} %reshape.288.high_ref, s32[1]{0:T(128)} %bitcast.7.base_ref, bf16[3,512,512]{2,1,0:T(8,128)(2,1)} %bitcast.174, bf16[4,3,512,256]{3,2,1,0:T(8,128)(2,1)} %copy-done, ...), custom_call_target="tpu_custom_call" | custom-call | tf_op jit(solution)/shard_map/attend_back/pallas_call | solution.py:337
  513.3 13.3 %attend_back.4 = (bf16[1,512,512]{2,1,0:T(8,128)(2,1)}, bf16[4,1,512,256]{3,2,1,0:T(8,128)(2,1)}) custom-call(s32[6]{0:T(128)} %and_select_fusion.1.low_ref, s32[6]{0:T(128)} %reshape.288.high_ref, s32[1]{0:T(128)} %bitcast.7.base_ref, bf16[3,512,512]{2,1,0:T(8,128)(2,1)} %bitcast.175, bf16[4,3,512,256]{3,2,1,0:T(8,128)(2,1)} %copy-done, ...), custom_call_target="tpu_custom_call" | custom-call | tf_op jit(solution)/shard_map/attend_back/pallas_call | solution.py:337
  526.6 39.6 %collective-permute-done.16 = bf16[1,128,1536]{2,1,0:T(8,128)(2,1)S(1)} collective-permute-done((bf16[1,128,1536]{2,1,0:T(8,128)(2,1)S(1)}, bf16[1,128,1536]{2,1,0:T(8,128)(2,1)S(1)}, u32[]{:S(2)}, u32[]{:S(2)}) %collective-permute-start.16) | collective-permute-done | bytes 393248 | tf_op jit(solution)/shard_map/ppermute | solution.py:920
  567.0 7.6 collective-permute-done.17
  575.4 6.3 collective-permute-done.18
  582.5 13.4 %attend_back.5 = (bf16[1,512,512]{2,1,0:T(8,128)(2,1)}, bf16[4,1,512,256]{3,2,1,0:T(8,128)(2,1)}) custom-call(s32[6]{0:T(128)} %and_select_fusion.1.low_ref, s32[6]{0:T(128)} %reshape.288.high_ref, s32[1]{0:T(128)} %bitcast.7.base_ref, bf16[3,512,512]{2,1,0:T(8,128)(2,1)} %bitcast.176, bf16[4,3,512,256]{3,2,1,0:T(8,128)(2,1)} %copy-done, ...), custom_call_target="tpu_custom_call" | custom-call | tf_op jit(solution)/shard_map/attend_back/pallas_call | solution.py:337
  595.9 3.2 pad_maximum_fusion.7
  599.2 21.0 %all-to-all-start.2 = ((bf16[4,3,512,256]{3,2,1,0:T(8,128)(2,1)}), bf16[4,3,512,256]{3,2,1,0:T(8,128)(2,1)S(1)}, u32[]{:S(2)}, u32[]{:S(2)}) async-start(bf16[4,3,512,256]{3,2,1,0:T(8,128)(2,1)} %pad_maximum_fusion.7), calls=%async_computation.4 | async-start | bytes 6291456 | tf_op jit(solution)/shard_map/all_to_all | solution.py:995
  631.2 24.6 %mixer_back.3 = (bf16[3,512,1920]{2,1,0:T(8,128)(2,1)}, f32[1,8,1792]{2,1,0:T(8,128)}, f32[8,1792]{1,0:T(8,128)}, f32[8,128]{1,0:T(8,128)}) custom-call(bf16[3,512,1536]{2,1,0:T(8,128)(2,1)} %get-tuple-element.204.refs_0_, f32[3,512,1536]{2,1,0:T(8,128)} %get-tuple-element.170.refs_1_, f32[3,512,768]{2,1,0:T(8,128)} %get-tuple-element.137.refs_1_.refs_3_.refs_2_, ...), custom_call_target="tpu_custom_call" | custom-call | tf_op jit(solution)/shard_map/mixer_back/pallas_call | solution.py:773
  655.8 24.0 %mixer_back.4 = (bf16[3,512,1920]{2,1,0:T(8,128)(2,1)}, f32[1,8,1792]{2,1,0:T(8,128)}, f32[8,1792]{1,0:T(8,128)}, f32[8,128]{1,0:T(8,128)}) custom-call(bf16[3,512,1536]{2,1,0:T(8,128)(2,1)} %get-tuple-element.204.refs_0_, f32[3,512,1536]{2,1,0:T(8,128)} %get-tuple-element.170.refs_1_, ...), custom_call_target="tpu_custom_call", output_to_operand_aliasing={{0}: (20, {})} | custom-call | tf_op jit(solution)/shard_map/mixer_back/pallas_call | solution.py:773
  679.9 24.3 %mixer_back.5 = (bf16[3,512,1920]{2,1,0:T(8,128)(2,1)}, f32[1,8,1792]{2,1,0:T(8,128)}, f32[8,1792]{1,0:T(8,128)}, f32[8,128]{1,0:T(8,128)}) custom-call(bf16[3,512,1536]{2,1,0:T(8,128)(2,1)} %get-tuple-element.204.refs_0_, f32[3,512,1536]{2,1,0:T(8,128)} %get-tuple-element.170.refs_1_, ...), custom_call_target="tpu_custom_call", output_to_operand_aliasing={{0}: (20, {})} | custom-call | tf_op jit(solution)/shard_map/mixer_back/pallas_call | solution.py:773
  706.4 4.7 convolution_convert_fusion.8
  714.2 17.1 %all-to-all-done.2.dkv_ref = bf16[4,3,512,256]{3,2,1,0:T(8,128)(2,1)S(1)} async-done(((bf16[4,3,512,256]{3,2,1,0:T(8,128)(2,1)}), bf16[4,3,512,256]{3,2,1,0:T(8,128)(2,1)S(1)}, u32[]{:S(2)}, u32[]{:S(2)}) %all-to-all-start.2) | async-done | bytes 3145760 | tf_op jit(solution)/shard_map/all_to_all | solution.py:995
  733.5 10.2 %convolution_convert_fusion.4 = bf16[1024,1920]{1,0:T(8,128)(2,1)S(1)} fusion(bf16[1536,1024]{1,0:T(8,128)(2,1)} %get-tuple-element.187, bf16[1536,1920]{1,0:T(8,128)(2,1)} %bitcast.177), kind=kOutput, calls=%fused_computation.33 | convolution fusion | flops 6041763840 | bytes 12976128 | tf_op jit(solution)/shard_map/ri,ro->io/dot_general | solution.py:1112
  749.5 22.9 %finish.1 = (bf16[1536,1024]{1,0:T(8,128)(2,1)}, bf16[1536,256]{1,0:T(8,128)(2,1)}, f32[8,1024]{1,0:T(8,128)}) custom-call(bf16[1536,1024]{1,0:T(8,128)(2,1)} %bitcast.198, f32[1,1024]{1,0:T(1,128)} %reshape.289.gain_ref, bf16[1536,1536]{1,0:T(8,128)(2,1)} %bitcast.179, bf16[1536,1920]{1,0:T(8,128)(2,1)} %bitcast.178, bf16[1536,512]{1,0:T(8,128)(2,1)} %bitcast.204, ...), custom_call_target="tpu_custom_call" | custom-call | tf_op jit(solution)/shard_map/finish/pallas_call | solution.py:139
  773.9 12.4 %all-to-all-start.3 = ((f32[8,3,24]{2,1,0:T(4,128)}), f32[8,3,24]{2,1,0:T(4,128)S(1)}, u32[]{:S(2)}, u32[]{:S(2)}) async-start(f32[8,3,24]{2,1,0:T(4,128)} %broadcast_in_dim.78), calls=%async_computation.8 | async-start | bytes 32768 | tf_op jit(solution)/shard_map/all_to_all | solution.py:941
  786.7 3.2 convolution_convert_fusion.10
  795.1 3.2 all-to-all-start.4
  804.5 2.8 collective-permute-done.22
  807.4 3.3 reduce-scatter.10.cloned.1.call-done
  815.2 12.3 %add_convert_fusion = bf16[1536,1024]{1,0:T(8,128)(2,1)} fusion(f32[1536,1024]{1,0:T(8,128)} %get-tuple-element.303, bf16[1536,2048]{1,0:T(8,128)(2,1)} %get-tuple-element.216, bf16[2048,1024]{1,0:T(8,128)(2,1)} %bitcast.206), kind=kOutput, calls=%fused_computation.26 | convolution fusion | flops 6445596672 | bytes 19922944 | tf_op jit(solution)/shard_map/dot_general | solution.py:984
  831.8 4.7 reduce-scatter.14.cloned.1.call-done
  (385 shorter events, 137.7 us)
Async XLA Ops:
  7.2 40.5 %all-gather.4.cloned.1.call-start = ((), (), s32[]{:S(2)}) async-start(), calls=%async_computation.10 | async-start | bytes 1392640 | tf_op jit(solution)/shard_map/all_gather | solution.py:1000
  15.9 89.9 %all-gather.6.cloned.1.call-start = ((), (), s32[]{:S(2)}) async-start(), calls=%async_computation.11 | async-start | bytes 10027008 | tf_op jit(solution)/shard_map/all_gather | solution.py:997
  48.0 171.0 %all-gather.8.cloned.1.call-start = ((), (), s32[]{:S(2)}) async-start(), calls=%async_computation.12 | async-start | bytes 18874368 | tf_op jit(solution)/shard_map/all_gather | solution.py:997
  106.9 24.5 %copy-start.38 = (f32[32,4096]{1,0:T(8,128)}, f32[32,4096]{1,0:T(8,128)S(1)}, u32[]{:S(2)}) copy-start(f32[32,4096]{1,0:T(8,128)S(1)} %reshape.337) | copy-start | bytes 1572868
  108.4 20.7 %copy-start.48 = (s32[3,2048]{1,0:T(4,128)S(1)}, s32[3,2048]{1,0:T(4,128)}, u32[]{:S(2)}) copy-start(s32[3,2048]{1,0:T(4,128)} %param.20) | copy-start | bytes 73732
  125.7 7.3 collective-permute-start
  133.0 101.3 %all-to-all-start.1 = ((bf16[4,3,512,256]{3,2,1,0:T(8,128)(2,1)}), bf16[4,3,512,256]{3,2,1,0:T(8,128)(2,1)S(1)}, u32[]{:S(2)}, u32[]{:S(2)}) async-start(bf16[4,3,512,256]{3,2,1,0:T(8,128)(2,1)} %bitcast.210), calls=%async_computation.1 | async-start | bytes 6291456 | tf_op jit(solution)/shard_map/all_to_all | solution.py:995
  136.7 445.8 %reduce-scatter.6.cloned.1.call-start = ((), (), s32[]{:S(2)}) async-start(), calls=%async_computation.13 | async-start | bytes 9437184 | tf_op jit(solution)/shard_map/reduce_scatter | solution.py:1109
  137.0 14.1 %copy-start.58 = (bf16[1536,1024]{1,0:T(8,128)(2,1)S(1)}, bf16[1536,1024]{1,0:T(8,128)(2,1)}, u32[]{:S(2)}) copy-start(bf16[1536,1024]{1,0:T(8,128)(2,1)} %get-tuple-element.187) | copy-start | bytes 9437188
  147.3 49.8 %collective-permute-start.7 = (bf16[1,128,1536]{2,1,0:T(8,128)(2,1)}, bf16[1,128,1536]{2,1,0:T(8,128)(2,1)S(1)}, u32[]{:S(2)}, u32[]{:S(2)}) collective-permute-start(bf16[1,128,1536]{2,1,0:T(8,128)(2,1)} %get-tuple-element.158), channel_id=1, source_target_pairs={{0,1},{4,5},{8,9},{12,13},{16,17},{20,21},{24,25},{28,29}} | collective-permute-start | bytes 1179656 | tf_op jit(solution)/shard_map/ppermute | solution.py:920
  171.5 34.1 %collective-permute-start.4 = (bf16[1,128,1536]{2,1,0:T(8,128)(2,1)}, bf16[1,128,1536]{2,1,0:T(8,128)(2,1)S(1)}, u32[]{:S(2)}, u32[]{:S(2)}) collective-permute-start(bf16[1,128,1536]{2,1,0:T(8,128)(2,1)} %get-tuple-element.155), channel_id=1, source_target_pairs={{0,1},{4,5},{8,9},{12,13},{16,17},{20,21},{24,25},{28,29}} | collective-permute-start | bytes 1179656 | tf_op jit(solution)/shard_map/ppermute | solution.py:920
  173.5 23.6 %copy-start.30 = (bf16[1,128,1536]{2,1,0:T(8,128)(2,1)S(1)}, bf16[1,128,1536]{2,1,0:T(8,128)(2,1)}, u32[]{:S(2)}) copy-start(bf16[1,128,1536]{2,1,0:T(8,128)(2,1)} %get-tuple-element.158) | copy-start | bytes 1179652
  173.5 32.0 %copy-start.31 = (bf16[1,128,1536]{2,1,0:T(8,128)(2,1)S(1)}, bf16[1,128,1536]{2,1,0:T(8,128)(2,1)}, u32[]{:S(2)}) copy-start(bf16[1,128,1536]{2,1,0:T(8,128)(2,1)} %get-tuple-element.155) | copy-start | bytes 1179652
  182.9 35.1 %copy-start.32 = (bf16[1,128,1536]{2,1,0:T(8,128)(2,1)S(1)}, bf16[1,128,1536]{2,1,0:T(8,128)(2,1)}, u32[]{:S(2)}) copy-start(bf16[1,128,1536]{2,1,0:T(8,128)(2,1)} %get-tuple-element.142) | copy-start | bytes 1179652
  182.9 30.4 %collective-permute-start.1 = (bf16[1,128,1536]{2,1,0:T(8,128)(2,1)}, bf16[1,128,1536]{2,1,0:T(8,128)(2,1)S(1)}, u32[]{:S(2)}, u32[]{:S(2)}) collective-permute-start(bf16[1,128,1536]{2,1,0:T(8,128)(2,1)} %get-tuple-element.142), channel_id=1, source_target_pairs={{0,1},{4,5},{8,9},{12,13},{16,17},{20,21},{24,25},{28,29}} | collective-permute-start | bytes 1179656 | tf_op jit(solution)/shard_map/ppermute | solution.py:920
  185.2 32.0 %copy-start.42 = (f32[1536]{0:T(1024)}, f32[1536]{0:T(1024)S(1)}, u32[]{:S(2)}) copy-start(f32[1536]{0:T(1024)S(1)} %slice_reduce_fusion.4) | copy-start | bytes 18436
  186.0 31.2 %copy-start.46 = (f32[1536]{0:T(1024)}, f32[1536]{0:T(1024)S(1)}, u32[]{:S(2)}) copy-start(f32[1536]{0:T(1024)S(1)} %slice_reduce_fusion.5) | copy-start | bytes 18436
  186.8 30.4 %copy-start.44 = (f32[1536]{0:T(1024)}, f32[1536]{0:T(1024)S(1)}, u32[]{:S(2)}) copy-start(f32[1536]{0:T(1024)S(1)} %slice_reduce_fusion.6) | copy-start | bytes 18436
  197.2 18.0 %collective-permute-start.8 = (bf16[1,128,1536]{2,1,0:T(8,128)(2,1)S(1)}, bf16[1,128,1536]{2,1,0:T(8,128)(2,1)S(1)}, u32[]{:S(2)}, u32[]{:S(2)}) collective-permute-start(bf16[1,128,1536]{2,1,0:T(8,128)(2,1)S(1)} %fusion.17), channel_id=1, source_target_pairs={{1,2},{5,6},{9,10},{13,14},{17,18},{21,22},{25,26},{29,30}} | collective-permute-start | bytes 1179656 | tf_op jit(solution)/shard_map/ppermute | solution.py:920
  205.5 10.7 %copy-start.6 = (bf16[1,128,1536]{2,1,0:T(8,128)(2,1)}, bf16[1,128,1536]{2,1,0:T(8,128)(2,1)S(1)}, u32[]{:S(2)}) copy-start(bf16[1,128,1536]{2,1,0:T(8,128)(2,1)S(1)} %collective-permute-done.4) | copy-start | bytes 1179652
  205.7 10.6 %collective-permute-start.5 = (bf16[1,128,1536]{2,1,0:T(8,128)(2,1)S(1)}, bf16[1,128,1536]{2,1,0:T(8,128)(2,1)S(1)}, u32[]{:S(2)}, u32[]{:S(2)}) collective-permute-start(bf16[1,128,1536]{2,1,0:T(8,128)(2,1)S(1)} %fusion.15), channel_id=1, source_target_pairs={{1,2},{5,6},{9,10},{13,14},{17,18},{21,22},{25,26},{29,30}} | collective-permute-start | bytes 1179656 | tf_op jit(solution)/shard_map/ppermute | solution.py:920
  214.6 2.6 collective-permute-start.2
  219.0 12.1 %copy-start.1 = (bf16[8192,1024]{1,0:T(8,128)(2,1)S(1)}, bf16[8192,1024]{1,0:T(8,128)(2,1)}, u32[]{:S(2)}) copy-start(bf16[8192,1024]{1,0:T(8,128)(2,1)} %all-gather.8.cloned.1.call-done) | copy-start | bytes 50331652
  243.4 19.5 %copy-start.41 = (bf16[1,128,1536]{2,1,0:T(8,128)(2,1)S(1)}, bf16[1,128,1536]{2,1,0:T(8,128)(2,1)}, u32[]{:S(2)}) copy-start(bf16[1,128,1536]{2,1,0:T(8,128)(2,1)} %fusion.16) | copy-start | bytes 1179652
  243.4 34.2 %collective-permute-start.9 = (bf16[1,128,1536]{2,1,0:T(8,128)(2,1)}, bf16[1,128,1536]{2,1,0:T(8,128)(2,1)S(1)}, u32[]{:S(2)}, u32[]{:S(2)}) collective-permute-start(bf16[1,128,1536]{2,1,0:T(8,128)(2,1)} %fusion.18), channel_id=1, source_target_pairs={{2,3},{6,7},{10,11},{14,15},{18,19},{22,23},{26,27},{30,31}} | collective-permute-start | bytes 1179656 | tf_op jit(solution)/shard_map/ppermute | solution.py:920
  263.0 10.2 %copy-start.34 = (bf16[32,32,512]{2,1,0:T(8,128)(2,1)S(1)}, bf16[32,32,512]{2,1,0:T(8,128)(2,1)}, u32[]{:S(2)}) copy-start(bf16[32,32,512]{2,1,0:T(8,128)(2,1)} %pad_maximum_fusion.10) | copy-start | bytes 3145732
  263.0 24.1 %collective-permute-start.6 = (bf16[1,128,1536]{2,1,0:T(8,128)(2,1)S(1)}, bf16[1,128,1536]{2,1,0:T(8,128)(2,1)S(1)}, u32[]{:S(2)}, u32[]{:S(2)}) collective-permute-start(bf16[1,128,1536]{2,1,0:T(8,128)(2,1)S(1)} %copy-done.41), channel_id=1, source_target_pairs={{2,3},{6,7},{10,11},{14,15},{18,19},{22,23},{26,27},{30,31}} | collective-permute-start | bytes 1179656 | tf_op jit(solution)/shard_map/ppermute | solution.py:920
  271.3 25.3 %collective-permute-start.3 = (bf16[1,128,1536]{2,1,0:T(8,128)(2,1)S(1)}, bf16[1,128,1536]{2,1,0:T(8,128)(2,1)S(1)}, u32[]{:S(2)}, u32[]{:S(2)}) collective-permute-start(bf16[1,128,1536]{2,1,0:T(8,128)(2,1)S(1)} %copy-done.40), channel_id=1, source_target_pairs={{2,3},{6,7},{10,11},{14,15},{18,19},{22,23},{26,27},{30,31}} | collective-permute-start | bytes 1179656 | tf_op jit(solution)/shard_map/ppermute | solution.py:920
  317.0 20.9 %copy-start.10 = (bf16[3,512,1024]{2,1,0:T(8,128)(2,1)S(1)}, bf16[3,512,1024]{2,1,0:T(8,128)(2,1)}, u32[]{:S(2)}) copy-start(bf16[3,512,1024]{2,1,0:T(8,128)(2,1)} %param.37) | copy-start | bytes 9437188
  337.9 19.1 %copy-start.16 = (bf16[32,32,1024]{2,1,0:T(8,128)(2,1)S(1)}, bf16[32,32,1024]{2,1,0:T(8,128)(2,1)}, u32[]{:S(2)}) copy-start(bf16[32,32,1024]{2,1,0:T(8,128)(2,1)} %get-tuple-element.259) | copy-start | bytes 6291460
  337.9 19.1 %copy-start.17 = (bf16[32,32,1024]{2,1,0:T(8,128)(2,1)S(1)}, bf16[32,32,1024]{2,1,0:T(8,128)(2,1)}, u32[]{:S(2)}) copy-start(bf16[32,32,1024]{2,1,0:T(8,128)(2,1)} %get-tuple-element.260) | copy-start | bytes 6291460
  337.9 19.1 %copy-start.18 = (bf16[32,32,1024]{2,1,0:T(8,128)(2,1)S(1)}, bf16[32,32,1024]{2,1,0:T(8,128)(2,1)}, u32[]{:S(2)}) copy-start(bf16[32,32,1024]{2,1,0:T(8,128)(2,1)} %get-tuple-element.261) | copy-start | bytes 6291460
  410.8 209.4 %reduce-scatter.8.cloned.1.call-start = ((), (), s32[]{:S(2)}) async-start(), calls=%async_computation.14 | async-start | bytes 12976128 | tf_op jit(solution)/shard_map/reduce_scatter | solution.py:1109
  451.7 21.4 %collective-permute-start.10 = (bf16[1,128,1536]{2,1,0:T(8,128)(2,1)}, bf16[1,128,1536]{2,1,0:T(8,128)(2,1)S(1)}, u32[]{:S(2)}, u32[]{:S(2)}) collective-permute-start(bf16[1,128,1536]{2,1,0:T(8,128)(2,1)} %get-tuple-element.180), channel_id=1, source_target_pairs={{3,2},{7,6},{11,10},{15,14},{19,18},{23,22},{27,26},{31,30}} | collective-permute-start | bytes 1179656 | tf_op jit(solution)/shard_map/ppermute | solution.py:920
  462.6 10.7 %collective-permute-start.11 = (bf16[1,128,1536]{2,1,0:T(8,128)(2,1)}, bf16[1,128,1536]{2,1,0:T(8,128)(2,1)S(1)}, u32[]{:S(2)}, u32[]{:S(2)}) collective-permute-start(bf16[1,128,1536]{2,1,0:T(8,128)(2,1)} %get-tuple-element.181), channel_id=1, source_target_pairs={{3,2},{7,6},{11,10},{15,14},{19,18},{23,22},{27,26},{31,30}} | collective-permute-start | bytes 1179656 | tf_op jit(solution)/shard_map/ppermute | solution.py:920
  463.5 9.8 %copy-start.22 = (bf16[1,128,1536]{2,1,0:T(8,128)(2,1)S(1)}, bf16[1,128,1536]{2,1,0:T(8,128)(2,1)}, u32[]{:S(2)}) copy-start(bf16[1,128,1536]{2,1,0:T(8,128)(2,1)} %get-tuple-element.181) | copy-start | bytes 1179652
  463.5 9.8 %copy-start.47 = (f32[1536]{0:T(1024)S(1)}, f32[1536]{0:T(1024)}, u32[]{:S(2)}) copy-start(f32[1536]{0:T(1024)} %copy-done.46) | copy-start | bytes 18436
  492.2 2.1 collective-permute-start.12
  492.9 17.3 %collective-permute-start.13 = (bf16[1,128,1536]{2,1,0:T(8,128)(2,1)S(1)}, bf16[1,128,1536]{2,1,0:T(8,128)(2,1)S(1)}, u32[]{:S(2)}, u32[]{:S(2)}) collective-permute-start(bf16[1,128,1536]{2,1,0:T(8,128)(2,1)S(1)} %get-tuple-element.251), channel_id=1, source_target_pairs={{2,1},{6,5},{10,9},{14,13},{18,17},{22,21},{26,25},{30,29}} | collective-permute-start | bytes 1179656 | tf_op jit(solution)/shard_map/ppermute | solution.py:920
  493.5 14.9 %collective-permute-start.14 = (bf16[1,128,1536]{2,1,0:T(8,128)(2,1)S(1)}, bf16[1,128,1536]{2,1,0:T(8,128)(2,1)S(1)}, u32[]{:S(2)}, u32[]{:S(2)}) collective-permute-start(bf16[1,128,1536]{2,1,0:T(8,128)(2,1)S(1)} %get-tuple-element.249), channel_id=1, source_target_pairs={{2,1},{6,5},{10,9},{14,13},{18,17},{22,21},{26,25},{30,29}} | collective-permute-start | bytes 1179656 | tf_op jit(solution)/shard_map/ppermute | solution.py:920
  494.4 14.2 %collective-permute-start.15 = (bf16[1,128,1536]{2,1,0:T(8,128)(2,1)S(1)}, bf16[1,128,1536]{2,1,0:T(8,128)(2,1)S(1)}, u32[]{:S(2)}, u32[]{:S(2)}) collective-permute-start(bf16[1,128,1536]{2,1,0:T(8,128)(2,1)S(1)} %get-tuple-element.247), channel_id=1, source_target_pairs={{2,1},{6,5},{10,9},{14,13},{18,17},{22,21},{26,25},{30,29}} | collective-permute-start | bytes 1179656 | tf_op jit(solution)/shard_map/ppermute | solution.py:920
  508.8 57.4 %collective-permute-start.16 = (bf16[1,128,1536]{2,1,0:T(8,128)(2,1)S(1)}, bf16[1,128,1536]{2,1,0:T(8,128)(2,1)S(1)}, u32[]{:S(2)}, u32[]{:S(2)}) collective-permute-start(bf16[1,128,1536]{2,1,0:T(8,128)(2,1)S(1)} %get-tuple-element.200), channel_id=1, source_target_pairs={{1,0},{5,4},{9,8},{13,12},{17,16},{21,20},{25,24},{29,28}} | collective-permute-start | bytes 1179656 | tf_op jit(solution)/shard_map/ppermute | solution.py:920
  510.3 64.3 %collective-permute-start.17 = (bf16[1,128,1536]{2,1,0:T(8,128)(2,1)S(1)}, bf16[1,128,1536]{2,1,0:T(8,128)(2,1)S(1)}, u32[]{:S(2)}, u32[]{:S(2)}) collective-permute-start(bf16[1,128,1536]{2,1,0:T(8,128)(2,1)S(1)} %get-tuple-element.201), channel_id=1, source_target_pairs={{1,0},{5,4},{9,8},{13,12},{17,16},{21,20},{25,24},{29,28}} | collective-permute-start | bytes 1179656 | tf_op jit(solution)/shard_map/ppermute | solution.py:920
  511.6 70.1 %collective-permute-start.18 = (bf16[1,128,1536]{2,1,0:T(8,128)(2,1)S(1)}, bf16[1,128,1536]{2,1,0:T(8,128)(2,1)S(1)}, u32[]{:S(2)}, u32[]{:S(2)}) collective-permute-start(bf16[1,128,1536]{2,1,0:T(8,128)(2,1)S(1)} %get-tuple-element.202), channel_id=1, source_target_pairs={{1,0},{5,4},{9,8},{13,12},{17,16},{21,20},{25,24},{29,28}} | collective-permute-start | bytes 1179656 | tf_op jit(solution)/shard_map/ppermute | solution.py:920
  582.5 13.4 %copy-start.36 = (bf16[4,1,512,256]{3,2,1,0:T(8,128)(2,1)S(1)}, bf16[4,1,512,256]{3,2,1,0:T(8,128)(2,1)}, u32[]{:S(2)}) copy-start(bf16[4,1,512,256]{3,2,1,0:T(8,128)(2,1)} %get-tuple-element.211) | copy-start | bytes 3145732
  582.5 13.4 %copy-start.37 = (bf16[4,1,512,256]{3,2,1,0:T(8,128)(2,1)S(1)}, bf16[4,1,512,256]{3,2,1,0:T(8,128)(2,1)}, u32[]{:S(2)}) copy-start(bf16[4,1,512,256]{3,2,1,0:T(8,128)(2,1)} %get-tuple-element.212) | copy-start | bytes 3145732
  599.2 132.1 %all-to-all-start.2 = ((bf16[4,3,512,256]{3,2,1,0:T(8,128)(2,1)}), bf16[4,3,512,256]{3,2,1,0:T(8,128)(2,1)S(1)}, u32[]{:S(2)}, u32[]{:S(2)}) async-start(bf16[4,3,512,256]{3,2,1,0:T(8,128)(2,1)} %pad_maximum_fusion.7), calls=%async_computation.4 | async-start | bytes 6291456 | tf_op jit(solution)/shard_map/all_to_all | solution.py:995
  620.2 129.3 %reduce-scatter.12.cloned.1.call-start = ((), (), s32[]{:S(2)}) async-start(), calls=%async_computation.16 | async-start | bytes 3112960 | tf_op jit(solution)/shard_map/reduce_scatter | solution.py:1197
  629.5 181.2 %reduce-scatter.10.cloned.1.call-start = ((), (), s32[]{:S(2)}) async-start(), calls=%async_computation.15 | async-start | bytes 5603328 | tf_op jit(solution)/shard_map/reduce_scatter | solution.py:1109
  631.2 75.2 %copy-start.4 = (bf16[3,512,512]{2,1,0:T(8,128)(2,1)}, bf16[3,512,512]{2,1,0:T(8,128)(2,1)S(1)}, u32[]{:S(2)}) copy-start(bf16[3,512,512]{2,1,0:T(8,128)(2,1)S(1)} %pad_maximum_fusion.9) | copy-start | bytes 4718596
  679.9 25.2 %copy-start.53 = (f32[1,8,1792]{2,1,0:T(8,128)S(1)}, f32[1,8,1792]{2,1,0:T(8,128)}, u32[]{:S(2)}) copy-start(f32[1,8,1792]{2,1,0:T(8,128)} %get-tuple-element.209) | copy-start | bytes 172036
  679.9 25.2 %copy-start.52 = (f32[1,8,1792]{2,1,0:T(8,128)S(1)}, f32[1,8,1792]{2,1,0:T(8,128)}, u32[]{:S(2)}) copy-start(f32[1,8,1792]{2,1,0:T(8,128)} %get-tuple-element.208) | copy-start | bytes 172036
  705.1 8.1 collective-permute-start.19
  731.2 12.4 %copy-start.2 = (bf16[4,3,512,256]{3,2,1,0:T(8,128)(2,1)}, bf16[4,3,512,256]{3,2,1,0:T(8,128)(2,1)S(1)}, u32[]{:S(2)}) copy-start(bf16[4,3,512,256]{3,2,1,0:T(8,128)(2,1)S(1)} %all-to-all-done.2.dkv_ref) | copy-start | bytes 9437188
  733.5 10.2 %copy-start.33 = (bf16[1024,512]{1,0:T(8,128)(2,1)S(1)}, bf16[1024,512]{1,0:T(8,128)(2,1)}, u32[]{:S(2)}) copy-start(bf16[1024,512]{1,0:T(8,128)(2,1)} %convolution_convert_fusion.8) | copy-start | bytes 3145732
  773.9 20.5 %all-to-all-start.3 = ((f32[8,3,24]{2,1,0:T(4,128)}), f32[8,3,24]{2,1,0:T(4,128)S(1)}, u32[]{:S(2)}, u32[]{:S(2)}) async-start(f32[8,3,24]{2,1,0:T(4,128)} %broadcast_in_dim.78), calls=%async_computation.8 | async-start | bytes 32768 | tf_op jit(solution)/shard_map/all_to_all | solution.py:941
  790.4 2.1 collective-permute-start.20
  792.6 7.4 collective-permute-start.21
  795.1 8.8 %all-to-all-start.4 = ((f32[4,3,24]{2,1,0:T(4,128)}), f32[4,3,24]{2,1,0:T(4,128)S(1)}, u32[]{:S(2)}, u32[]{:S(2)}) async-start(f32[4,3,24]{2,1,0:T(4,128)} %broadcast_in_dim.79), calls=%async_computation.9 | async-start | bytes 16384 | tf_op jit(solution)/shard_map/all_to_all | solution.py:941
  798.3 38.2 %reduce-scatter.14.cloned.1.call-start = ((), (), s32[]{:S(2)}) async-start(), calls=%async_computation.17 | async-start | bytes 778240 | tf_op jit(solution)/shard_map/reduce_scatter | solution.py:1202
  800.1 7.2 collective-permute-start.22
  810.7 16.9 %collective-permute-start.23 = (bf16[32,384]{1,0:T(8,128)(2,1)S(1)}, bf16[32,384]{1,0:T(8,128)(2,1)S(1)}, u32[]{:S(2)}, u32[]{:S(2)}) collective-permute-start(bf16[32,384]{1,0:T(8,128)(2,1)S(1)} %get-tuple-element.281), channel_id=1, source_target_pairs={{0,1},{1,2},{2,3},{3,0},{4,5},{5,6},{6,7},{7,4},{8,9},{9,10},{10,1... | collective-permute-start | bytes 73736 | tf_op jit(solution)/shard_map/ppermute | solution.py:961
  812.2 15.3 %collective-permute-start.25 = (bf16[32,384]{1,0:T(8,128)(2,1)S(1)}, bf16[32,384]{1,0:T(8,128)(2,1)S(1)}, u32[]{:S(2)}, u32[]{:S(2)}) collective-permute-start(bf16[32,384]{1,0:T(8,128)(2,1)S(1)} %get-tuple-element.282), channel_id=1, source_target_pairs={{0,3},{1,0},{2,1},{3,2},{4,7},{5,4},{6,5},{7,6},{8,11},{9,8},{10,9... | collective-permute-start | bytes 73736 | tf_op jit(solution)/shard_map/ppermute | solution.py:961
  814.6 13.0 %collective-permute-start.24 = (bf16[32,384]{1,0:T(8,128)(2,1)S(1)}, bf16[32,384]{1,0:T(8,128)(2,1)S(1)}, u32[]{:S(2)}, u32[]{:S(2)}) collective-permute-start(bf16[32,384]{1,0:T(8,128)(2,1)S(1)} %get-tuple-element.283), channel_id=1, source_target_pairs={{0,2},{1,3},{2,0},{3,1},{4,6},{5,7},{6,4},{7,5},{8,10},{9,11},{10,... | collective-permute-start | bytes 73736 | tf_op jit(solution)/shard_map/ppermute | solution.py:961
  (38 other events, 188.1 us)
Sparse Core Ops, SparseCore 0:
  16.0 31.6 all-gather.3
  49.6 56.1 all-gather.5
  107.7 89.8 all-gather.7
  410.9 101.8 reduce-scatter.5
  516.5 97.3 reduce-scatter.7
  629.6 97.9 reduce-scatter.11
  746.4 64.2 reduce-scatter.9
  815.3 21.1 reduce-scatter.13
